TPU v7x, 32 devices: a whole 2x2x4 slice. The times are simulated.
32 devices in a mesh: fsdp: 4 (over y, x), rep: 8 (over z, core).
Axes of the slice: x: 2, y: 2, z: 4, core: 2. Of those that a mesh axis runs over, the one named last changes fastest.
Arguments:
- tokens: bfloat16 [64, 256, 384], P(('fsdp', 'rep')), may hold values from -6 to 6
- conditions: bfloat16 [64, 384], P(('fsdp', 'rep')), may hold values from -6 to 6
- assignment: int32 [64], P(('fsdp', 'rep')), may hold values from 0 to 63, each once
- params: float32 [2654208], P('fsdp')
- momentum: float32 [2654208], P('fsdp'), may hold values from -24 to 24
- cotangent: bfloat16 [64, 256, 384], P(('fsdp', 'rep')), may hold values from -6 to 6
Outputs:
- blended: bfloat16 [64, 256, 384], P(('fsdp', 'rep'))
- grad_tokens: float32 [64, 256, 384], P(('fsdp', 'rep'))
- grad_params: float32 [2654208], P('fsdp')
- new_params: float32 [2654208], P('fsdp')
- new_momentum: float32 [2654208], P('fsdp')
Inputs may be any that keep to these rules, and one draw needn't show every extreme that they name: assignment is a permutation of the latent numbers.
All inputs are finite; a program needn't handle non-finite values.
Results may differ from a plain program's by a relative error of at most 0.014.
The roundings to bfloat16 on the way count: a program that leaves them out, or rounds other values in their place, can miss the bound.
Values may be sent and summed in bfloat16 or wider, within the bound.
No kernel may reach another device: no remote copies, remote signals or barrier semaphores. Data moves between devices by JAX's collectives and lax.ppermute only.
A program may use at most 192 MiB of HBM per device.

v0:
```python
import functools
import math

import jax
import jax.numpy as jnp
from jax import lax
from jax.experimental import pallas as pl
from jax.experimental.pallas import tpu as pltpu
from jax.sharding import PartitionSpec as P

D = 384
HEADS = 6
HD = 64
FF = 1536
SEQ = 256
NS_ITERS = 3

LN_EPSILON = 1e-06
MOMENTUM_RATE = 0.95
LEARN_RATE = 0.2
COEFF_A = 3.4445
COEFF_B = -4.775
COEFF_C = 2.0315

F32 = jnp.float32
BF16 = jnp.bfloat16
ANY = pl.ANY
VMEM_LIMIT = 60 * 1024 * 1024

MATS = ((D, 6 * D, 0, True), (D, 3 * D, 6, True), (D, D, 9, True), (D, FF, 10, True), (FF, D, 14, False))
NBLOCKS = 18
ADALN, QKV, OUTW, UP, DOWN = range(5)
P_SIZE = sum(m[0] * m[1] for m in MATS)
GRAD_ROWS = 3584
KEPT_ROWS = 16


def update_scale(mat):
    return LEARN_RATE * 0.2 * math.sqrt(max(MATS[mat][0], MATS[mat][1]))


def shard_pieces(shard, count):
    size = P_SIZE // count
    begin, end = shard * size, (shard + 1) * size
    pieces, crow, offset = [], 0, 0
    for mat, (rows, cols, first, by_cols) in enumerate(MATS):
        lo, hi = max(begin, offset), min(end, offset + rows * cols)
        if lo < hi:
            r0, r1 = (lo - offset) // cols, (hi - offset) // cols
            stride = cols // 128
            base = (offset - begin) // 128
            if by_cols:
                for b in range(cols // D):
                    pieces.append((mat, first + b, r0, r1 - r0, crow, base + r0 * stride + 3 * b, stride))
                    crow += r1 - r0
            else:
                r = r0
                while r < r1:
                    n = min(r1, (r // D + 1) * D) - r
                    pieces.append((mat, first + r // D, r % D, n, crow, base + r * stride, stride))
                    crow += n
                    r += n
        offset += rows * cols
    return pieces


def mm(a, b, ca=1, cb=0):
    return lax.dot_general(a, b, (((ca,), (cb,)), ((), ())), preferred_element_type=F32)


def vspec():
    return pl.BlockSpec(memory_space=pltpu.VMEM)


def aspec():
    return pl.BlockSpec(memory_space=ANY)


def sspec():
    return pl.BlockSpec(memory_space=pltpu.SMEM)


def params_of(**kw):
    return pltpu.CompilerParams(vmem_limit_bytes=VMEM_LIMIT, **kw)


def prep_kernel(count, s_ref, p_ref, m_ref, w_ref, mo_ref):
    for shard in range(count):

        @pl.when(s_ref[0] == shard)
        def _(shard=shard):
            for _, _, _, n, crow, frow, stride in shard_pieces(shard, count):
                for j in range(3):
                    src = pl.ds(frow + j, n, stride=stride)
                    w_ref[crow : crow + n, 128 * j : 128 * j + 128] = p_ref[src, :].astype(BF16)
                    mo_ref[crow : crow + n, 128 * j : 128 * j + 128] = m_ref[src, :].astype(BF16)


def prep(sidx, params, momentum, count):
    rows = P_SIZE // count // D
    out = jax.ShapeDtypeStruct((rows, D), BF16)
    return pl.pallas_call(
        functools.partial(prep_kernel, count),
        out_shape=(out, out),
        in_specs=[sspec(), vspec(), vspec()],
        out_specs=(vspec(), vspec()),
        compiler_params=params_of(),
        name="prep",
    )(sidx, params, momentum)


def layer_norm(h):
    center = jnp.mean(h, axis=-1, keepdims=True)
    cent = h - center
    spread = jnp.mean(jnp.square(cent), axis=-1, keepdims=True)
    rstd = lax.rsqrt(spread + LN_EPSILON)
    return cent * rstd, rstd


def layer_norm_grad(xhat, rstd, gx):
    m1 = jnp.mean(gx, axis=-1, keepdims=True)
    m2 = jnp.mean(gx * xhat, axis=-1, keepdims=True)
    return rstd * (gx - m1 - xhat * m2)


def gather_plan(count):
    plan = []
    half = P_SIZE // count // D // 2
    for shard in range(count):
        for _, block, r0, n, crow, _, _ in shard_pieces(shard, count):
            cuts = sorted({crow, crow + n} | {c for c in range(0, 2 * half + 1, half // 2) if crow < c < crow + n})
            for a, b in zip(cuts[:-1], cuts[1:]):
                plan.append((shard, a // half, a % half, b - a, block, r0 + a - crow))
    return plan


def load_weights_fast(s_ref, bufs, wts, sems, start):
    own, rx, ry, rda, rdb, px, py, pda, pdb = bufs
    me, core = s_ref[0], s_ref[1]
    half = own.shape[0] // 2
    quarter = half // 2
    for q, (shard, h, r, n, block, br) in enumerate(gather_plan(4)):
        dst = wts.at[block, br : br + n]
        if not start:
            pltpu.make_async_copy(own.at[0:n], dst, sems.at[q]).wait()
            continue
        for m in range(4):
            for mine in (True, False):
                if m == 0 and not mine:
                    continue
                cond = me == (shard ^ m)
                if m > 0:
                    cond = jnp.logical_and(cond, (core == h) if mine else (core != h))
                if m == 0:
                    src = own.at[h * half + r : h * half + r + n]
                elif m < 3:
                    src = ((rx, ry) if mine else (px, py))[m - 1].at[r : r + n]
                else:
                    pair = (rda, rdb) if mine else (pda, pdb)
                    k = r // quarter
                    src = pair[k].at[r - k * quarter : r - k * quarter + n]

                @pl.when(cond)
                def _(src=src, dst=dst, q=q):
                    pltpu.make_async_copy(src, dst, sems.at[q]).start()


def main_kernel(nbuf, fast, rows, s_ref, table, tok, cot, *refs):
    bufs = refs[:nbuf]
    (blend, qkv, probs, amix_in, gafter, gmx, mods, gmod, silu, wqkv, grads) = refs[nbuf : nbuf + 11]
    wts, ao_s, aa_s, amix, minp, gmi, mo, sems = refs[nbuf + 11 :]
    lat = rows // SEQ
    if fast:
        load_weights_fast(s_ref, bufs, wts, sems, True)
    else:
        whole = pltpu.make_async_copy(bufs[0], wts, sems.at[0])
        whole.start()
    nt = table.shape[0]
    lanes = lax.broadcasted_iota(jnp.int32, (16, nt), 1)
    rws = lax.broadcasted_iota(jnp.int32, (16, nt), 0)
    pick = jnp.zeros((16, nt), jnp.bool_)
    for l in range(lat):
        pick = pick | ((rws == l) & (lanes == s_ref[3 + l]))
    cond = mm(pick.astype(F32).astype(BF16), table[...])
    sc = (cond * (1.0 / (1.0 + jnp.exp(-cond)))).astype(BF16)
    silu[...] = sc.astype(F32)
    if fast:
        load_weights_fast(s_ref, bufs, wts, sems, False)
    else:
        whole.wait()
    for b in range(6):
        mods[b] = mm(sc, wts[b])[:8]
    for j in range(3):
        wqkv[j] = wts[6 + j]
    grads[9 * D :, :] = jnp.zeros((GRAD_ROWS - 9 * D, D), F32)

    def mod(b, l):
        return mods[b, l : l + 1, :]

    for l in range(lat):
        rs = slice(l * SEQ, (l + 1) * SEQ)
        xhat, _ = layer_norm(tok[rs, :].astype(F32))
        amix_in[rs, :] = (xhat * (1.0 + mod(1, l)) + mod(0, l)).astype(BF16)
    ai = amix_in[...]
    for j in range(3):
        qkv[j] = mm(ai, wts[6 + j]).astype(BF16)

    low = lax.broadcasted_iota(jnp.int32, (SEQ, 128), 1) < HD
    zero = jnp.zeros((SEQ, 128), BF16)

    def attend(l, carry):
        rs = pl.ds(pl.multiple_of(l * SEQ, SEQ), SEQ)
        for hp in range(HEADS // 2):
            cs = slice(hp * 128, hp * 128 + 128)
            q, k, v = qkv[0, rs, cs], qkv[1, rs, cs], qkv[2, rs, cs]
            outs = []
            for h in range(2):
                qm = jnp.where(low if h == 0 else jnp.logical_not(low), q, zero)
                s = mm(qm, k, 1, 1) * HD ** (-0.5)
                top = jnp.max(s, axis=-1, keepdims=True)
                e = jnp.exp(s - top)
                pr = e * (1.0 / jnp.sum(e, axis=-1, keepdims=True))
                probs[l * HEADS + hp * 2 + h] = pr
                outs.append(mm(pr.astype(BF16), v))
            amix[rs, cs] = jnp.where(low, outs[0], outs[1]).astype(BF16)
        return carry

    lax.fori_loop(0, lat, attend, 0)

    ao = mm(amix[...], wts[9])
    ao_s[...] = ao
    for l in range(lat):
        rs = slice(l * SEQ, (l + 1) * SEQ)
        aa = tok[rs, :].astype(F32) + mod(2, l) * ao_s[rs, :]
        aa_s[rs, :] = aa
        xhat, _ = layer_norm(aa)
        minp[rs, :] = (xhat * (1.0 + mod(4, l)) + mod(3, l)).astype(BF16)
        gmx[rs, :] = (cot[rs, :].astype(F32) * mod(5, l)).astype(BF16)
    gmi[...] = jnp.zeros_like(gmi)
    mo[...] = jnp.zeros_like(mo)

    def mlp(j, carry):
        wu, wd = wts[10 + j], wts[14 + j]
        u = mm(minp[...], wu)
        c = math.sqrt(2.0 / math.pi)
        u2 = u * u
        t = jnp.tanh(c * (u + 0.044715 * (u2 * u)))
        half = 0.5 * (1.0 + t)
        act = (u * half).astype(BF16)
        slope = half + 0.5 * u * (1.0 - t * t) * (c * (1.0 + 3.0 * 0.044715 * u2))
        mo[...] += mm(act, wd)
        gmo = gmx[...]
        gp = (mm(gmo, wd, 1, 1) * slope).astype(BF16)
        grads[pl.ds(pl.multiple_of((5 + j) * D, D), D), :] = mm(act, gmo, 0, 0)
        grads[pl.ds(pl.multiple_of((1 + j) * D, D), D), :] = mm(minp[...], gp, 0, 0)
        gmi[...] += mm(gp, wu, 1, 1)
        return carry

    lax.fori_loop(0, FF // D, mlp, 0)

    gmod[...] = jnp.zeros_like(gmod)
    for l in range(lat):
        rs = slice(l * SEQ, (l + 1) * SEQ)
        up = cot[rs, :].astype(F32)
        blend[rs, :] = (aa_s[rs, :] + mod(5, l) * mo[rs, :]).astype(BF16)
        gmod[5, l : l + 1, :] = jnp.sum(up * mo[rs, :], axis=0, keepdims=True)
        xhat, rstd = layer_norm(aa_s[rs, :])
        g = gmi[rs, :]
        gmod[3, l : l + 1, :] = jnp.sum(g, axis=0, keepdims=True)
        gmod[4, l : l + 1, :] = jnp.sum(g * xhat, axis=0, keepdims=True)
        ga = up + layer_norm_grad(xhat, rstd, g * (1.0 + mod(4, l)))
        gafter[rs, :] = ga
        gmod[2, l : l + 1, :] = jnp.sum(ga * ao_s[rs, :], axis=0, keepdims=True)
        minp[rs, :] = (ga * mod(2, l)).astype(BF16)
    gao = minp[...]
    grads[0:D, :] = mm(amix[...], gao, 0, 0)
    gmx[...] = mm(gao, wts[9], 1, 1).astype(BF16)


def main_call(sidx, table, tokens, cotangent, bufs, fast):
    rows = tokens.shape[0]
    lat = rows // SEQ
    sd = jax.ShapeDtypeStruct
    outs = (
        sd((rows, D), BF16),
        sd((3, rows, D), BF16),
        sd((lat * HEADS, SEQ, SEQ), F32),
        sd((rows, D), BF16),
        sd((rows, D), F32),
        sd((rows, D), BF16),
        sd((6, 8, D), F32),
        sd((6, 8, D), F32),
        sd((16, D), F32),
        sd((3, D, D), BF16),
        sd((GRAD_ROWS, D), F32),
    )
    nsem = len(gather_plan(4)) if fast else 1
    return pl.pallas_call(
        functools.partial(main_kernel, len(bufs), fast, rows),
        out_shape=outs,
        in_specs=[sspec(), vspec(), vspec(), vspec()] + [aspec()] * len(bufs),
        out_specs=(vspec(),) * len(outs),
        scratch_shapes=[
            pltpu.VMEM((NBLOCKS, D, D), BF16),
            pltpu.VMEM((rows, D), F32),
            pltpu.VMEM((rows, D), F32),
            pltpu.VMEM((rows, D), BF16),
            pltpu.VMEM((rows, D), BF16),
            pltpu.VMEM((rows, D), F32),
            pltpu.VMEM((rows, D), F32),
            pltpu.SemaphoreType.DMA((nsem,)),
        ],
        compiler_params=params_of(),
        cost_estimate=pl.CostEstimate(flops=20_000_000_000, bytes_accessed=30_000_000, transcendentals=0),
        name="main",
    )(sidx, table, tokens, cotangent, *bufs)


def heads_kernel(rows, tok, qkv, probs, ai, gafter, gmx, mods, gmod1, silu, wqkv, gtok, gq, keep, gqkv, srow):
    lat = rows // SEQ
    low = lax.broadcasted_iota(jnp.int32, (SEQ, 128), 1) < HD
    zero = jnp.zeros((SEQ, 128), BF16)

    def back(l, carry):
        rs = pl.ds(pl.multiple_of(l * SEQ, SEQ), SEQ)
        for hp in range(HEADS // 2):
            cs = slice(hp * 128, hp * 128 + 128)
            q, k, v = qkv[0, rs, cs], qkv[1, rs, cs], qkv[2, rs, cs]
            g = gmx[rs, cs]
            res = []
            for h in range(2):
                p = probs[l * HEADS + hp * 2 + h]
                gm = jnp.where(low if h == 0 else jnp.logical_not(low), g, zero)
                gv = mm(p.astype(BF16), g, 0, 0)
                gpr = mm(gm, v, 1, 1)
                dots = jnp.sum(p * gpr, axis=-1, keepdims=True)
                gs = (p * (gpr - dots) * HD ** (-0.5)).astype(BF16)
                res.append((mm(gs, k), mm(gs, q, 0, 0), gv))
            for j in range(3):
                gqkv[j, rs, cs] = jnp.where(low, res[0][j], res[1][j]).astype(BF16)
        return carry

    lax.fori_loop(0, lat, back, 0)
    gai = None
    for j in range(3):
        part = mm(gqkv[j], wqkv[j], 1, 1)
        gai = part if gai is None else gai + part
        gq[j * D : (j + 1) * D, :] = mm(ai[...], gqkv[j], 0, 0)
    srow[...] = jnp.zeros_like(srow)
    for l in range(lat):
        rs = slice(l * SEQ, (l + 1) * SEQ)
        xhat, rstd = layer_norm(tok[rs, :].astype(F32))
        g = gai[rs, :]
        srow[l : l + 1, :] = jnp.sum(g, axis=0, keepdims=True)
        srow[lat + l : lat + l + 1, :] = jnp.sum(g * xhat, axis=0, keepdims=True)
        gtok[rs, :] = gafter[rs, :] + layer_norm_grad(xhat, rstd, g * (1.0 + mods[1, l : l + 1, :]))
        for b in range(2, 6):
            srow[lat * b + l : lat * b + l + 1, :] = gmod1[b, l : l + 1, :]
        srow[lat * 6 + l : lat * 6 + l + 1, :] = silu[l : l + 1, :]
    keep[...] = srow[...].astype(BF16)


def heads_call(tokens, qkv, probs, ai, gafter, gmx, mods, gmod1, silu, wqkv):
    rows = tokens.shape[0]
    sd = jax.ShapeDtypeStruct
    outs = (sd((rows, D), F32), sd((3 * D, D), F32), sd((KEPT_ROWS, D), BF16))
    return pl.pallas_call(
        functools.partial(heads_kernel, rows),
        out_shape=outs,
        in_specs=[vspec()] * 10,
        out_specs=(vspec(),) * 3,
        scratch_shapes=[pltpu.VMEM((3, rows, D), BF16), pltpu.VMEM((KEPT_ROWS, D), F32)],
        compiler_params=params_of(),
        cost_estimate=pl.CostEstimate(flops=12_000_000_000, bytes_accessed=12_000_000, transcendentals=0),
        name="heads",
    )(tokens, qkv, probs, ai, gafter, gmx, mods, gmod1, silu, wqkv)


def split(x):
    hi = x.astype(BF16)
    return hi, (x - hi.astype(F32)).astype(BF16)


POLY = (COEFF_C, COEFF_B, COEFF_A)
PLAIN = (1.0, 0.0, 0.0)
STEPS = (
    (0, 0, 2, POLY),
    (2, 0, 3, PLAIN),
    (3, 2, 0, PLAIN),
    (0, 0, 1, POLY),
    (1, 2, 2, PLAIN),
    (1, 0, 3, PLAIN),
    (3, 1, 0, PLAIN),
    (0, 0, 1, POLY),
    (1, 2, 2, PLAIN),
)


def step_tables():
    ints = jnp.array([x for st in STEPS for x in st[:3]], jnp.int32)
    coeffs = jnp.array([x for st in STEPS for x in st[3]], F32)
    return ints, coeffs


def newton_schulz(ints, coeffs, mat_ref, upd_ref, bufs, npairs, flipped, factor):
    bufs[0] = jnp.zeros((D, D), F32)

    def gram(b, carry):
        x0, x1 = mat_ref[2 * b].astype(BF16), mat_ref[2 * b + 1].astype(BF16)

        @pl.when(flipped)
        def _():
            x = jnp.concatenate([x0, x1], axis=0)
            bufs[0] += mm(x, x, 0, 0)

        @pl.when(jnp.logical_not(flipped))
        def _():
            x = jnp.concatenate([x0, x1], axis=1)
            bufs[0] += mm(x, x, 1, 1)

        return carry

    lax.fori_loop(0, npairs, gram, 0)
    g = bufs[0]
    ri = lax.broadcasted_iota(jnp.int32, (D, D), 0)
    ci = lax.broadcasted_iota(jnp.int32, (D, D), 1)
    eye = jnp.where(ri == ci, 1.0, 0.0)
    diag = jnp.sum(g * eye, axis=1, keepdims=True)
    total = jnp.sum(diag, axis=0, keepdims=True)
    inv = 1.0 / (jnp.sqrt(total) + 1e-07)
    bufs[0] = g * (inv * inv)

    def step(k, carry):
        i, j, d = ints[3 * k], ints[3 * k + 1], ints[3 * k + 2]
        x = bufs[i]
        xh, xl = split(x)
        yh, yl = split(bufs[j])
        prod = mm(jnp.concatenate([xh, xl, xh], axis=1), jnp.concatenate([yh, yh, yl], axis=0))
        r0 = lax.broadcasted_iota(jnp.int32, (D, D), 0)
        r1 = lax.broadcasted_iota(jnp.int32, (D, D), 1)
        ident = jnp.where(r0 == r1, coeffs[3 * k + 2], 0.0)
        bufs[d] = coeffs[3 * k] * prod + (coeffs[3 * k + 1] * x + ident)
        return carry

    lax.fori_loop(0, len(STEPS), step, 0)
    bufs[0] = bufs[2] * (inv * factor)

    def apply(b, carry):
        wh, wl = split(bufs[0])
        xs = [mat_ref[2 * b + i] for i in range(2)]

        @pl.when(flipped)
        def _():
            for i in range(2):
                xh, xl = split(xs[i])
                upd_ref[2 * b + i] = mm(
                    jnp.concatenate([xh, xl, xh], axis=1), jnp.concatenate([wh, wh, wl], axis=0)
                )

        @pl.when(jnp.logical_not(flipped))
        def _():
            (h0, l0), (h1, l1) = split(xs[0]), split(xs[1])
            xh = jnp.concatenate([h0, h1], axis=1)
            xl = jnp.concatenate([l0, l1], axis=1)
            out = mm(jnp.concatenate([wh, wl, wh], axis=1), jnp.concatenate([xh, xh, xl], axis=0))
            upd_ref[2 * b] = out[:, :D]
            upd_ref[2 * b + 1] = out[:, D:]

        return carry

    lax.fori_loop(0, npairs, apply, 0)


def first_chunks():
    for q in range(32):
        size = GRAD_ROWS // 32
        row = q * size
        while row < min((q + 1) * size, 9 * D):
            n = min((q + 1) * size, (row // D + 1) * D) - row
            yield (q // 16, q // 4 % 4, q % 4), row // D, row % D, n, row - q * size
            row += n


def take_first(s_ref, chunks, dst, first, count):
    me, core, zed = s_ref[0], s_ref[1], s_ref[2]
    for (c, m, z), block, row, n, crow in first_chunks():
        if first <= block < first + count:
            piece = chunks[core ^ c, me ^ m, zed ^ z, crow : crow + n, :]
            dst[block - first, row : row + n, :] = piece.astype(F32)


def take_second(s_ref, chunks, dst):
    me, core = s_ref[0], s_ref[1]
    size = 3 * D // 8
    for q in range(8):
        row = q * size
        while row < (q + 1) * size:
            n = min((q + 1) * size, (row // D + 1) * D) - row
            piece = chunks[core ^ (q // 4), me ^ (q % 4), row - q * size : row - q * size + n, :]
            dst[row // D, row % D : row % D + n, :] = piece.astype(F32)
            row += n


def ns_a_kernel(s_ref, ints, coeffs, mom, fx0, fx1, kept, chunks, upd, grd, mat, bufs, kf):
    me, core = s_ref[0], s_ref[1]
    half = fx0.shape[0]
    ndev = kept.shape[0] // KEPT_ROWS

    def kept_rows(first):
        part = [kf[j, pl.ds(first, ndev, stride=KEPT_ROWS), :] for j in range(3)]
        return jnp.concatenate(part, axis=1).astype(BF16)

    for pair, target in (((0, 1), ADALN), ((2, 3), UP)):
        nb = MATS[target][1] // D
        first = MATS[target][2]

        @pl.when((me // 2) == pair[0] // 2)
        def _(target=target, nb=nb):
            if target == ADALN:
                for j in range(3):
                    kf[j] = kept[:, 128 * j : 128 * j + 128].astype(F32)
                sil = jnp.concatenate([kept_rows(12), kept_rows(13)], axis=0)
                for b in range(nb):
                    gm = jnp.concatenate([kept_rows(2 * b), kept_rows(2 * b + 1)], axis=0)
                    grd[b] = mm(sil, gm, 0, 0)
            else:
                take_first(s_ref, chunks, grd, 1, nb)

        for t in pair:
            for _, block, r0, n, crow, frow, stride in [p for p in shard_pieces(t, 4) if p[0] == target]:
                b = block - first

                @pl.when(me == t)
                def _(b=b, r0=r0, n=n, frow=frow, stride=stride):
                    for j in range(3):
                        cs = slice(128 * j, 128 * j + 128)
                        m = mom[pl.ds(frow + j, n, stride=stride), :]
                        mat[b, r0 : r0 + n, cs] = MOMENTUM_RATE * m + grd[b, r0 : r0 + n, cs]

                cuts = sorted({crow, crow + n} | {c for c in (half,) if crow < c < crow + n})
                for lo, hi in zip(cuts[:-1], cuts[1:]):
                    h = lo // half
                    for mine in (True, False):

                        @pl.when(jnp.logical_and(me == (t ^ 1), (core == h) if mine else (core != h)))
                        def _(b=b, r0=r0, lo=lo, hi=hi, h=h, crow=crow, mine=mine):
                            src = fx0 if mine else fx1
                            dst = slice(r0 + lo - crow, r0 + hi - crow)
                            m = src[lo - h * half : hi - h * half, :].astype(F32)
                            mat[b, dst, :] = MOMENTUM_RATE * m + grd[b, dst, :]

    low = me < 2
    npairs = jnp.where(low, 3, 2)
    factor = jnp.where(low, update_scale(ADALN), update_scale(UP))
    newton_schulz(ints, coeffs, mat, upd, bufs, npairs, jnp.bool_(False), factor)


def ns_a(sidx, tables, mom, fx0, fx1, kept, chunks):
    sd = jax.ShapeDtypeStruct((6, D, D), F32)
    return pl.pallas_call(
        ns_a_kernel,
        out_shape=(sd, sd),
        in_specs=[sspec()] * 3 + [vspec()] * 5,
        out_specs=(vspec(), vspec()),
        scratch_shapes=[
            pltpu.VMEM((6, D, D), F32),
            pltpu.VMEM((4, D, D), F32),
            pltpu.VMEM((3, kept.shape[0], 128), F32),
        ],
        compiler_params=params_of(),
        cost_estimate=pl.CostEstimate(flops=8_000_000_000, bytes_accessed=12_000_000, transcendentals=0),
        name="ns_a",
    )(sidx, *tables, mom, fx0, fx1, kept, chunks)


OWNER = ((QKV, 1, 2), (OUTW, 2, 1), (DOWN, 3, 2))


def final_kernel(
    s_ref, ints, coeffs, par, mom, chunks, chunks2, upa, grda, ograd, onew, omom, upb, gb, mat, bufs
):
    me = s_ref[0]
    for target, t, npairs in OWNER:

        @pl.when(me == t)
        def _(target=target, t=t, npairs=npairs):
            first = MATS[target][2]
            count = MATS[target][0] * MATS[target][1] // (D * D)
            if target == QKV:
                take_second(s_ref, chunks2, gb)
            else:
                take_first(s_ref, chunks, gb, first - 9 if target == OUTW else 5, count)
            for b in range(count, 2 * npairs):
                mat[b] = jnp.zeros((D, D), F32)
            for _, block, r0, n, crow, frow, stride in [p for p in shard_pieces(t, 4) if p[0] == target]:
                b = block - first
                for j in range(3):
                    cs = slice(128 * j, 128 * j + 128)
                    m = mom[pl.ds(frow + j, n, stride=stride), :]
                    mat[b, r0 : r0 + n, cs] = MOMENTUM_RATE * m + gb[b, r0 : r0 + n, cs]

    @pl.when(me > 0)
    def _():
        npairs = jnp.where(me == 2, 1, 2)
        factor = jnp.where(
            me == 1, update_scale(QKV), jnp.where(me == 2, update_scale(OUTW), update_scale(DOWN))
        )
        newton_schulz(ints, coeffs, mat, upb, bufs, npairs, me == 3, factor)

    for t in range(4):

        @pl.when(me == t)
        def _(t=t):
            for mat_id, block, r0, n, crow, frow, stride in shard_pieces(t, 4):
                b = block - MATS[mat_id][2]
                gref, uref = (grda, upa) if mat_id in (ADALN, UP) else (gb, upb)
                for j in range(3):
                    cs = slice(128 * j, 128 * j + 128)
                    fl = pl.ds(frow + j, n, stride=stride)
                    g = gref[b, r0 : r0 + n, cs]
                    ograd[fl, :] = g
                    omom[fl, :] = MOMENTUM_RATE * mom[fl, :] + g
                    onew[fl, :] = par[fl, :] - uref[b, r0 : r0 + n, cs]


def final_call(sidx, tables, par, mom, chunks, chunks2, upa, grda):
    sd = jax.ShapeDtypeStruct(par.shape, F32)
    block4 = pltpu.VMEM((4, D, D), F32)
    return pl.pallas_call(
        final_kernel,
        out_shape=(sd, sd, sd),
        in_specs=[sspec()] * 3 + [vspec()] * 6,
        out_specs=(vspec(),) * 3,
        scratch_shapes=[block4, block4, block4, block4],
        compiler_params=params_of(),
        cost_estimate=pl.CostEstimate(flops=8_000_000_000, bytes_accessed=24_000_000, transcendentals=0),
        name="finish",
    )(sidx, *tables, par, mom, chunks, chunks2, upa, grda)


def swap(x, axis, mask):
    count = lax.axis_size(axis)
    return lax.ppermute(x, axis, [(i, i ^ mask) for i in range(count)])


def rows_at(x, start, n):
    return lax.dynamic_slice_in_dim(x, start, n, 0)


def more_rows(x, hops):
    for axis, mask in hops:
        x = jnp.concatenate([x, swap(x, axis, mask)], axis=0)
    return x


def wide_sum(parts):
    total = None
    for p in parts:
        total = p.astype(F32) if total is None else total + p.astype(F32)
    return total


def plane_scatter(x, me):
    mine = lax.dynamic_index_in_dim(x, me, 0, keepdims=False)
    got = [swap(lax.dynamic_index_in_dim(x, me ^ m, 0, keepdims=False), "fsdp", m) for m in (1, 2, 3)]
    return wide_sum([mine] + got)


def core_sum(g, core):
    half = g.shape[0] // 2
    mine = rows_at(g, core * half, half)
    return mine + swap(rows_at(g, (1 - core) * half, half), "rep", 1)


def fast_device(tokens, conditions, assignment, params, momentum, cotangent):
    me = lax.axis_index("fsdp")
    rep = lax.axis_index("rep")
    core, zed = rep % 2, rep // 2
    lat = tokens.shape[0]
    rows = lat * SEQ
    par = params.reshape(-1, 128)
    mom = momentum.reshape(-1, 128)
    dev = me * lax.axis_size("rep") + rep
    pick = ((assignment // lat) ^ dev) * lat + assignment % lat
    sidx = jnp.concatenate([jnp.stack([me, core, zed]), pick]).astype(jnp.int32)

    wc, mc = prep(sidx, par, mom, 4)
    half = wc.shape[0] // 2
    quarter = half // 2
    wh = rows_at(wc, core * half, half)
    conditions, wh = lax.optimization_barrier((conditions, wh))
    rx, ry = swap(wh, "fsdp", 1), swap(wh, "fsdp", 2)
    table = more_rows(conditions, (("rep", 1), ("rep", 2), ("rep", 4)))
    rx, ry, table = lax.optimization_barrier((rx, ry, table))
    table = more_rows(table, (("fsdp", 1), ("fsdp", 2)))
    rda, rdb = swap(rx[:quarter], "fsdp", 2), swap(ry[quarter:], "fsdp", 1)
    px, py = swap(rx, "rep", 1), swap(ry, "rep", 1)
    pda, pdb = swap(rda, "rep", 1), swap(rdb, "rep", 1)
    bufs = (wc, rx, ry, rda, rdb, px, py, pda, pdb)

    tok2, cot2 = tokens.reshape(rows, D), cotangent.reshape(rows, D)
    (blend, qkv, probs, ai, gafter, gmx, mods, gmod1, silu, wqkv, g1) = main_call(
        sidx, table, tok2, cot2, bufs, True
    )
    fx0 = swap(rows_at(mc, core * half, half), "fsdp", 1)
    fx1 = swap(fx0, "rep", 1)

    h1 = core_sum(g1, core).astype(BF16)
    s1 = plane_scatter(h1.reshape(4, GRAD_ROWS // 8, D), me).astype(BF16)
    piece = s1.shape[0] // 4
    s1 = s1.reshape(4, piece, D)
    mine = lax.dynamic_index_in_dim(s1, zed, 0, keepdims=False)
    got = [
        swap(lax.dynamic_index_in_dim(s1, zed ^ m, 0, keepdims=False), "rep", 2 * m) for m in (1, 2, 3)
    ]
    zsum = wide_sum([mine] + got).astype(BF16)
    col = jnp.stack([zsum] + [swap(zsum, "rep", 2 * m) for m in (1, 2, 3)])
    plane = jnp.stack([col] + [swap(col, "fsdp", m) for m in (1, 2, 3)])
    both = jnp.stack([plane, swap(plane, "rep", 1)])

    gtok, g2, keep = heads_call(tok2, qkv, probs, ai, gafter, gmx, mods, gmod1, silu, wqkv)

    h2 = core_sum(g2, core).astype(BF16).reshape(4, 3 * D // 8, D)
    s2 = plane_scatter(h2, me).astype(BF16)
    k2 = jnp.concatenate([keep] + [swap(keep, "fsdp", m) for m in (1, 2, 3)], axis=0)
    msg = jnp.concatenate([s2, k2], axis=0)
    z1, z2, z3 = (swap(msg, "rep", 2 * m) for m in (1, 2, 3))
    ns = s2.shape[0]
    q2 = (wide_sum([s2, z1[:ns]]) + wide_sum([z2[:ns], z3[:ns]])).astype(BF16)
    kz = jnp.concatenate([k2, z1[ns:], z2[ns:], z3[ns:]], axis=0)
    kept = jnp.concatenate([kz, swap(kz, "rep", 1)], axis=0)
    p2 = jnp.stack([q2] + [swap(q2, "fsdp", m) for m in (1, 2, 3)])
    both2 = jnp.stack([p2, swap(p2, "rep", 1)])

    tables = step_tables()
    upa, grda = ns_a(sidx, tables, mom, fx0, fx1, kept, both)
    ograd, onew, omom = final_call(sidx, tables, par, mom, both, both2, upa, grda)
    shape = tokens.shape
    return (
        blend.reshape(shape),
        gtok.reshape(shape),
        ograd.reshape(-1),
        onew.reshape(-1),
        omom.reshape(-1),
    )


def unpack(flat):
    pieces, offset = [], 0
    for rows_count, cols_count, _, _ in MATS:
        pieces.append(flat[offset : offset + rows_count * cols_count].reshape(rows_count, cols_count))
        offset += rows_count * cols_count
    return pieces


def to_blocks(mats):
    out = []
    for matrix, (rows_count, cols_count, _, by_cols) in zip(mats, MATS):
        if by_cols:
            out.append(matrix.reshape(D, cols_count // D, D).transpose(1, 0, 2))
        else:
            out.append(matrix.reshape(rows_count // D, D, D))
    return jnp.concatenate(out, axis=0)


def from_blocks(blocks, by_cols):
    if by_cols:
        return blocks.transpose(1, 0, 2).reshape(-1)
    return blocks.reshape(-1)


def orthogonalize(matrix):
    flipped = matrix.shape[0] > matrix.shape[1]
    current = matrix.T if flipped else matrix
    current = current / (jnp.sqrt(jnp.sum(current * current)) + 1e-07)
    for _ in range(NS_ITERS):
        square = jnp.dot(current, current.T, precision=lax.Precision.HIGHEST)
        polynomial = COEFF_B * square + COEFF_C * jnp.dot(square, square, precision=lax.Precision.HIGHEST)
        current = COEFF_A * current + jnp.dot(polynomial, current, precision=lax.Precision.HIGHEST)
    return current.T if flipped else current


def scaled_update(matrix, factor):
    return (factor * orthogonalize(matrix)).reshape(-1)


def empty_update(matrix, factor):
    return jnp.zeros((matrix.shape[0] * matrix.shape[1],), F32)


def any_device(tokens, conditions, assignment, params, momentum, cotangent):
    lat = tokens.shape[0]
    rows = lat * SEQ
    table = lax.all_gather(conditions, ("fsdp", "rep"), axis=0, tiled=True)
    gathered = lax.all_gather(params.astype(BF16), "fsdp", axis=0, tiled=True)
    blocks = to_blocks(unpack(gathered))
    me = lax.axis_index("fsdp")
    sidx = jnp.concatenate([jnp.stack([me, me, me]), assignment]).astype(jnp.int32)
    tok2, cot2 = tokens.reshape(rows, D), cotangent.reshape(rows, D)
    (blend, qkv, probs, ai, gafter, gmx, mods, gmod1, silu, wqkv, g1) = main_call(
        sidx, table, tok2, cot2, (blocks,), False
    )
    gtok, g2, keep = heads_call(tok2, qkv, probs, ai, gafter, gmx, mods, gmod1, silu, wqkv)
    rest = jnp.concatenate(
        [
            from_blocks(g2.reshape(3, D, D), True),
            g1[:D].reshape(-1),
            from_blocks(g1[D : 5 * D].reshape(4, D, D), True),
            g1[5 * D : 9 * D].reshape(-1),
        ]
    )
    kept = lax.all_gather(keep, ("fsdp", "rep"), axis=0, tiled=True).reshape(-1, KEPT_ROWS, D)
    silu_all = kept[:, 6 * lat : 7 * lat].reshape(-1, D)
    mod_all = kept[:, : 6 * lat].reshape(-1, 6, lat, D).transpose(0, 2, 1, 3).reshape(-1, 6 * D)
    adaln = lax.dot_general(silu_all, mod_all, (((0,), (0,)), ((), ())), preferred_element_type=F32)
    shard_len = params.shape[0]
    head = jnp.concatenate([adaln.reshape(-1), jnp.zeros_like(rest)])
    flat = jnp.concatenate([jnp.zeros((D * 6 * D,), F32), rest])
    part = lax.psum_scatter(flat, "fsdp", scatter_dimension=0, tiled=True)
    full_grad = lax.psum(part, "rep") + lax.dynamic_slice_in_dim(head, me * shard_len, shard_len, 0)
    new_momentum = MOMENTUM_RATE * momentum + full_grad
    whole_mom = lax.all_gather(new_momentum, "fsdp", axis=0, tiled=True)
    group_size = lax.axis_size("fsdp")
    updates, offset = [], 0
    for mat, piece in enumerate(unpack(whole_mom)):
        factor = F32(update_scale(mat))
        owner = (offset // shard_len + group_size // 2) % group_size
        updates.append(lax.cond(me == owner, scaled_update, empty_update, piece, factor))
        offset += piece.size
    update = lax.psum_scatter(jnp.concatenate(updates), "fsdp", scatter_dimension=0, tiled=True)
    shape = tokens.shape
    return (blend.reshape(shape), gtok.reshape(shape), full_grad, params - update, new_momentum)


def solution(mesh):
    both = ("fsdp", "rep")
    in_specs = (P(both, None, None), P(both, None), P(both), P("fsdp"), P("fsdp"), P(both, None, None))
    out_specs = (P(both, None, None), P(both, None, None), P("fsdp"), P("fsdp"), P("fsdp"))
    small = dict(mesh.shape) == {"fsdp": 4, "rep": 8}
    return jax.shard_map(
        fast_device if small else any_device,
        mesh=mesh,
        in_specs=in_specs,
        out_specs=out_specs,
        check_vma=False,
    )
```

profile of v0, /device:TPU:3, one launch (start us, length us, event | category | flops | bytes accessed | tf_op | source)
XLA Modules:
  0.0 212.5 jit_solution(17954457696969348280)
XLA Ops:
  1.9 4.6 %prep.1 = (bf16[1728,384]{1,0:T(8,128)(2,1)}, bf16[1728,384]{1,0:T(8,128)(2,1)}) custom-call(s32[5]{0:T(128)} %pad_add_fusion.s_ref, f32[5184,128]{1,0:T(8,128)} %bitcast.64, f32[5184,128]{1,0:T(8,128)} %bitcast.66), custom_call_target="tpu_custom_call" | custom-call | tf_op jit(solution)/shard_map/prep/pallas_call | solution.py:102
  14.2 2.4 %collective-permute-start.4 = (bf16[8,384]{1,0:T(8,128)(2,1)S(1)}, bf16[8,384]{1,0:T(8,128)(2,1)S(1)}, u32[]{:S(2)}, u32[]{:S(2)}) collective-permute-start(bf16[8,384]{1,0:T(8,128)(2,1)S(1)} %pad_maximum_fusion.8), channel_id=1, source_target_pairs={{0,4},{1,5},{2,6},{3,7},{4,0},{5,1},{6,2},{7,3},{8,12},{9,13},{10,... | collective-permute-start | bytes 18440 | tf_op jit(solution)/shard_map/ppermute | solution.py:643
  17.6 5.9 %collective-permute-done.1.refs_2_ = bf16[864,384]{1,0:T(8,128)(2,1)S(1)} collective-permute-done((bf16[864,384]{1,0:T(8,128)(2,1)S(1)}, bf16[864,384]{1,0:T(8,128)(2,1)S(1)}, u32[]{:S(2)}, u32[]{:S(2)}) %collective-permute-start.1) | collective-permute-done | bytes 663584 | tf_op jit(solution)/shard_map/ppermute | solution.py:643
  25.4 2.1 collective-permute-start.9
  27.4 4.7 %collective-permute-done.8.refs_4_ = bf16[432,384]{1,0:T(8,128)(2,1)S(1)} collective-permute-done((bf16[432,384]{1,0:T(8,128)(2,1)S(1)}, bf16[432,384]{1,0:T(8,128)(2,1)S(1)}, u32[]{:S(2)}, u32[]{:S(2)}) %collective-permute-start.8) | collective-permute-done | bytes 331808 | tf_op jit(solution)/shard_map/ppermute | solution.py:643
  32.1 2.7 %collective-permute-start.12 = (bf16[432,384]{1,0:T(8,128)(2,1)S(1)}, bf16[432,384]{1,0:T(8,128)(2,1)}, u32[]{:S(2)}, u32[]{:S(2)}) collective-permute-start(bf16[432,384]{1,0:T(8,128)(2,1)S(1)} %collective-permute-done.8.refs_4_), channel_id=1, source_target_pairs={{0,1},{1,0},{2,3},{3,2},{4,5},{5,4},{6,7},{7,6},{8,9},{9,8},{10,11... | collective-permute-start | bytes 995336 | tf_op jit(solution)/shard_map/ppermute | solution.py:643
  38.1 2.3 %collective-permute-done.6 = bf16[32,384]{1,0:T(8,128)(2,1)S(1)} collective-permute-done((bf16[32,384]{1,0:T(8,128)(2,1)S(1)}, bf16[32,384]{1,0:T(8,128)(2,1)S(1)}, u32[]{:S(2)}, u32[]{:S(2)}) %collective-permute-start.6) | collective-permute-done | bytes 24608 | tf_op jit(solution)/shard_map/ppermute | solution.py:643
  42.1 19.4 %main.1 = (bf16[512,384]{1,0:T(8,128)(2,1)}, bf16[3,512,384]{2,1,0:T(8,128)(2,1)}, f32[12,256,256]{2,1,0:T(8,128)}, bf16[512,384]{1,0:T(8,128)(2,1)}, f32[512,38...) custom-call(s32[5]{0:T(128)} %pad_add_fusion.s_ref, ...), custom_call_target="tpu_custom_call" | custom-call | flops 20000000000 | bytes 30000000 | tf_op jit(solution)/shard_map/main/pallas_call | solution.py:298
  61.6 2.0 constant_dynamic-slice_fusion.2
  63.6 2.4 %collective-permute-start.13 = (f32[1792,384]{1,0:T(8,128)S(1)}, f32[1792,384]{1,0:T(8,128)}, u32[]{:S(2)}, u32[]{:S(2)}) collective-permute-start(f32[1792,384]{1,0:T(8,128)S(1)} %constant_dynamic-slice_fusion.2), channel_id=1, source_target_pairs={{0,1},{1,0},{2,3},{3,2},{4,5},{5,4},{6,7},{7,6},{8,9},{9,8},{10,11... | collective-permute-start | bytes 8257544 | tf_op jit(solution)/shard_map/ppermute | solution.py:643
  66.0 11.2 %heads.1 = (f32[512,384]{1,0:T(8,128)}, f32[1152,384]{1,0:T(8,128)}, bf16[16,384]{1,0:T(8,128)(2,1)}) custom-call(bf16[512,384]{1,0:T(8,128)(2,1)} %bitcast.88, bf16[3,512,384]{2,1,0:T(8,128)(2,1)} %get-tuple-element.38.qkv, f32[12,256,256]{2,1,0:T(8,128)} %get-tuple-element.39.probs, bf16[512,384]{1,0:T(8,128)(2,1)} %get-tuple-element.40.ai, ...), custom_call_target="tpu_custom_call" | custom-call | flops 12000000000 | bytes 12000000 | tf_op jit(solution)/shard_map/heads/pallas_call | solution.py:367
  77.2 2.1 %constant_dynamic-slice_fusion.1 = f32[576,384]{1,0:T(8,128)} fusion(f32[1152,384]{1,0:T(8,128)} %get-tuple-element.49, s32[]{:T(128)S(6)} %select_n.85), kind=kLoop, calls=%fused_computation.54 | loop fusion | bytes 1769476 | tf_op jit(solution)/shard_map/dynamic_slice | solution.py:647
  79.4 3.0 %add_convert_fusion = bf16[1792,384]{1,0:T(8,128)(2,1)S(1)} fusion(f32[1792,384]{1,0:T(8,128)} %collective-permute-done.13, f32[3584,384]{1,0:T(8,128)} %get-tuple-element.48, s32[]{:T(128)S(6)} %select_n.74), kind=kLoop, calls=%fused_computation.1 | loop fusion | flops 1376256 | bytes 6881284 | tf_op jit(solution)/shard_map/convert_element_type | solution.py:708
  89.6 3.3 %collective-permute-done.14 = bf16[448,384]{1,0:T(8,128)(2,1)S(1)} collective-permute-done((bf16[448,384]{1,0:T(8,128)(2,1)}, bf16[448,384]{1,0:T(8,128)(2,1)S(1)}, u32[]{:S(2)}, u32[]{:S(2)}) %collective-permute-start.14) | collective-permute-done | bytes 344096 | tf_op jit(solution)/shard_map/ppermute | solution.py:643
  92.9 7.4 %collective-permute-done.16 = bf16[448,384]{1,0:T(8,128)(2,1)} collective-permute-done((bf16[448,384]{1,0:T(8,128)(2,1)}, bf16[448,384]{1,0:T(8,128)(2,1)}, u32[]{:S(2)}, u32[]{:S(2)}) %collective-permute-start.16) | collective-permute-done | bytes 344096 | tf_op jit(solution)/shard_map/ppermute | solution.py:643
  102.9 2.2 %collective-permute-start.19 = (bf16[112,384]{1,0:T(8,128)(2,1)S(1)}, bf16[112,384]{1,0:T(8,128)(2,1)S(1)}, u32[]{:S(2)}, u32[]{:S(2)}) collective-permute-start(bf16[112,384]{1,0:T(8,128)(2,1)S(1)} %get-tuple-element.72), channel_id=1, source_target_pairs={{0,6},{1,7},{2,4},{3,5},{4,2},{5,3},{6,0},{7,1},{8,14},{9,15},{10,... | collective-permute-start | bytes 258056 | tf_op jit(solution)/shard_map/ppermute | solution.py:643
  106.5 1.7 collective-permute-done.19
  108.1 2.0 collective-permute-start.30
  110.1 1.9 collective-permute-done.18
  113.3 3.5 %collective-permute-done.28 = bf16[144,384]{1,0:T(8,128)(2,1)S(1)} collective-permute-done((bf16[144,384]{1,0:T(8,128)(2,1)S(1)}, bf16[144,384]{1,0:T(8,128)(2,1)S(1)}, u32[]{:S(2)}, u32[]{:S(2)}) %collective-permute-start.28) | collective-permute-done | bytes 110624 | tf_op jit(solution)/shard_map/ppermute | solution.py:643
  116.8 3.3 %collective-permute-start.22 = (bf16[112,384]{1,0:T(8,128)(2,1)S(1)}, bf16[112,384]{1,0:T(8,128)(2,1)S(1)}, u32[]{:S(2)}, u32[]{:S(2)}) collective-permute-start(bf16[112,384]{1,0:T(8,128)(2,1)S(1)} %fusion.8), channel_id=1, source_target_pairs={{0,6},{1,7},{2,4},{3,5},{4,2},{5,3},{6,0},{7,1},{8,14},{9,15},{10,... | collective-permute-start | bytes 258056 | tf_op jit(solution)/shard_map/ppermute | solution.py:643
  123.9 4.3 %collective-permute-done.21 = bf16[112,384]{1,0:T(8,128)(2,1)S(1)} collective-permute-done((bf16[112,384]{1,0:T(8,128)(2,1)S(1)}, bf16[112,384]{1,0:T(8,128)(2,1)S(1)}, u32[]{:S(2)}, u32[]{:S(2)}) %collective-permute-start.21) | collective-permute-done | bytes 86048 | tf_op jit(solution)/shard_map/ppermute | solution.py:643
  132.1 13.5 %collective-permute-done.33 = bf16[16,384]{1,0:T(8,128)(2,1)S(1)} collective-permute-done((bf16[16,384]{1,0:T(8,128)(2,1)S(1)}, bf16[16,384]{1,0:T(8,128)(2,1)S(1)}, u32[]{:S(2)}, u32[]{:S(2)}) %collective-permute-start.33) | collective-permute-done | bytes 12320 | tf_op jit(solution)/shard_map/ppermute | solution.py:643
  145.7 2.6 %collective-permute-start.36 = (bf16[208,384]{1,0:T(8,128)(2,1)S(1)}, bf16[208,384]{1,0:T(8,128)(2,1)S(1)}, u32[]{:S(2)}, u32[]{:S(2)}) collective-permute-start(bf16[208,384]{1,0:T(8,128)(2,1)S(1)} %get-tuple-element.82), channel_id=1, source_target_pairs={{0,6},{1,7},{2,4},{3,5},{4,2},{5,3},{6,0},{7,1},{8,14},{9,15},{10,... | collective-permute-start | bytes 479240 | tf_op jit(solution)/shard_map/ppermute | solution.py:643
  149.3 2.9 %collective-permute-start.42 = (bf16[864,384]{1,0:T(8,128)(2,1)}, bf16[864,384]{1,0:T(8,128)(2,1)S(1)}, u32[]{:S(2)}, u32[]{:S(2)}) collective-permute-start(bf16[864,384]{1,0:T(8,128)(2,1)} %collective-permute-done.41.fx0), channel_id=1, source_target_pairs={{0,1},{1,0},{2,3},{3,2},{4,5},{5,4},{6,7},{7,6},{8,9},{9,8},{10,11... | collective-permute-start | bytes 1990664 | tf_op jit(solution)/shard_map/ppermute | solution.py:643
  152.6 8.0 %collective-permute-done.35 = bf16[208,384]{1,0:T(8,128)(2,1)S(1)} collective-permute-done((bf16[208,384]{1,0:T(8,128)(2,1)S(1)}, bf16[208,384]{1,0:T(8,128)(2,1)S(1)}, u32[]{:S(2)}, u32[]{:S(2)}) %collective-permute-start.35) | collective-permute-done | bytes 159776 | tf_op jit(solution)/shard_map/ppermute | solution.py:643
  163.5 1.9 collective-permute-done.39
  168.2 2.0 collective-permute-start.40
  170.3 1.6 collective-permute-done.43
  173.0 1.9 pad_maximum_fusion.chunks
  175.8 16.9 %ns_a.1 = (f32[6,384,384]{2,1,0:T(8,128)}, f32[6,384,384]{2,1,0:T(8,128)}) custom-call(s32[5]{0:T(128)} %pad_add_fusion.s_ref, s32[27]{0:T(128)} %constant.103.clone.ints, f32[27]{0:T(128)} %constant.104.clone.coeffs, f32[5184,128]{1,0:T(8,128)} %bitcast.67, bf16[864,384]{1,0:T(8,128)(2,1)} %collective-permute-done.41.fx0, bf16[864,384]{1,0:T(8,128)(2,1)} %copy-done.7, ...), custom_call_target="tpu_custom_call" | custom-call | flops 8000000000 | bytes 12000000 | tf_op jit(solution)/shard_map/ns_a/pallas_call | solution.py:560
  192.7 19.8 %finish.1 = (f32[5184,128]{1,0:T(8,128)}, f32[5184,128]{1,0:T(8,128)}, f32[5184,128]{1,0:T(8,128)}) custom-call(s32[5]{0:T(128)} %pad_add_fusion.s_ref, s32[27]{0:T(128)} %constant.103.clone.ints, f32[27]{0:T(128)} %constant.104.clone.coeffs, f32[5184,128]{1,0:T(8,128)} %bitcast.65, f32[5184,128]{1,0:T(8,128)} %bitcast.68, ...), custom_call_target="tpu_custom_call" | custom-call | flops 8000000000 | bytes 24000000 | tf_op jit(solution)/shard_map/finish/pallas_call | solution.py:629
  (120 shorter events, 46.2 us)
Async XLA Ops:
  7.6 15.9 %collective-permute-start.1 = (bf16[864,384]{1,0:T(8,128)(2,1)S(1)}, bf16[864,384]{1,0:T(8,128)(2,1)S(1)}, u32[]{:S(2)}, u32[]{:S(2)}) collective-permute-start(bf16[864,384]{1,0:T(8,128)(2,1)S(1)} %constant_dynamic-slice_fusion.3), channel_id=1, source_target_pairs={{0,16},{8,24},{16,0},{24,8},{1,17},{9,25},{17,1},{25,9},{2,18},{10... | collective-permute-start | bytes 1990664 | tf_op jit(solution)/shard_map/ppermute | solution.py:643
  8.9 15.5 %collective-permute-start = (bf16[864,384]{1,0:T(8,128)(2,1)S(1)}, bf16[864,384]{1,0:T(8,128)(2,1)S(1)}, u32[]{:S(2)}, u32[]{:S(2)}) collective-permute-start(bf16[864,384]{1,0:T(8,128)(2,1)S(1)} %constant_dynamic-slice_fusion.3), channel_id=1, source_target_pairs={{0,8},{8,0},{16,24},{24,16},{1,9},{9,1},{17,25},{25,17},{2,10},{10... | collective-permute-start | bytes 1990664 | tf_op jit(solution)/shard_map/ppermute | solution.py:643
  24.5 7.6 %collective-permute-start.8 = (bf16[432,384]{1,0:T(8,128)(2,1)S(1)}, bf16[432,384]{1,0:T(8,128)(2,1)S(1)}, u32[]{:S(2)}, u32[]{:S(2)}) collective-permute-start(bf16[432,384]{1,0:T(8,128)(2,1)S(1)} %slice.25), channel_id=1, source_target_pairs={{0,8},{8,0},{16,24},{24,16},{1,9},{9,1},{17,25},{25,17},{2,10},{10... | collective-permute-start | bytes 995336 | tf_op jit(solution)/shard_map/ppermute | solution.py:643
  24.9 9.9 %collective-permute-start.7 = (bf16[432,384]{1,0:T(8,128)(2,1)S(1)}, bf16[432,384]{1,0:T(8,128)(2,1)S(1)}, u32[]{:S(2)}, u32[]{:S(2)}) collective-permute-start(bf16[432,384]{1,0:T(8,128)(2,1)S(1)} %slice.24), channel_id=1, source_target_pairs={{0,16},{8,24},{16,0},{24,8},{1,17},{9,25},{17,1},{25,9},{2,18},{10... | collective-permute-start | bytes 995336 | tf_op jit(solution)/shard_map/ppermute | solution.py:643
  25.4 15.7 %collective-permute-start.9 = (bf16[864,384]{1,0:T(8,128)(2,1)S(1)}, bf16[864,384]{1,0:T(8,128)(2,1)S(1)}, u32[]{:S(2)}, u32[]{:S(2)}) collective-permute-start(bf16[864,384]{1,0:T(8,128)(2,1)S(1)} %collective-permute-done.refs_1_), channel_id=1, source_target_pairs={{0,1},{1,0},{2,3},{3,2},{4,5},{5,4},{6,7},{7,6},{8,9},{9,8},{10,11... | collective-permute-start | bytes 1990664 | tf_op jit(solution)/shard_map/ppermute | solution.py:643
  27.4 13.6 %collective-permute-start.10 = (bf16[864,384]{1,0:T(8,128)(2,1)S(1)}, bf16[864,384]{1,0:T(8,128)(2,1)S(1)}, u32[]{:S(2)}, u32[]{:S(2)}) collective-permute-start(bf16[864,384]{1,0:T(8,128)(2,1)S(1)} %collective-permute-done.1.refs_2_), channel_id=1, source_target_pairs={{0,1},{1,0},{2,3},{3,2},{4,5},{5,4},{6,7},{7,6},{8,9},{9,8},{10,11... | collective-permute-start | bytes 1990664 | tf_op jit(solution)/shard_map/ppermute | solution.py:643
  32.1 8.9 %collective-permute-start.12 = (bf16[432,384]{1,0:T(8,128)(2,1)S(1)}, bf16[432,384]{1,0:T(8,128)(2,1)}, u32[]{:S(2)}, u32[]{:S(2)}) collective-permute-start(bf16[432,384]{1,0:T(8,128)(2,1)S(1)} %collective-permute-done.8.refs_4_), channel_id=1, source_target_pairs={{0,1},{1,0},{2,3},{3,2},{4,5},{5,4},{6,7},{7,6},{8,9},{9,8},{10,11... | collective-permute-start | bytes 995336 | tf_op jit(solution)/shard_map/ppermute | solution.py:643
  34.8 6.3 %collective-permute-start.11 = (bf16[432,384]{1,0:T(8,128)(2,1)S(1)}, bf16[432,384]{1,0:T(8,128)(2,1)}, u32[]{:S(2)}, u32[]{:S(2)}) collective-permute-start(bf16[432,384]{1,0:T(8,128)(2,1)S(1)} %collective-permute-done.7.refs_3_), channel_id=1, source_target_pairs={{0,1},{1,0},{2,3},{3,2},{4,5},{5,4},{6,7},{7,6},{8,9},{9,8},{10,11... | collective-permute-start | bytes 995336 | tf_op jit(solution)/shard_map/ppermute | solution.py:643
  63.6 15.8 %collective-permute-start.13 = (f32[1792,384]{1,0:T(8,128)S(1)}, f32[1792,384]{1,0:T(8,128)}, u32[]{:S(2)}, u32[]{:S(2)}) collective-permute-start(f32[1792,384]{1,0:T(8,128)S(1)} %constant_dynamic-slice_fusion.2), channel_id=1, source_target_pairs={{0,1},{1,0},{2,3},{3,2},{4,5},{5,4},{6,7},{7,6},{8,9},{9,8},{10,11... | collective-permute-start | bytes 8257544 | tf_op jit(solution)/shard_map/ppermute | solution.py:643
  79.3 8.7 %collective-permute-start.27 = (f32[576,384]{1,0:T(8,128)}, f32[576,384]{1,0:T(8,128)}, u32[]{:S(2)}, u32[]{:S(2)}) collective-permute-start(f32[576,384]{1,0:T(8,128)} %constant_dynamic-slice_fusion.1), channel_id=1, source_target_pairs={{0,1},{1,0},{2,3},{3,2},{4,5},{5,4},{6,7},{7,6},{8,9},{9,8},{10,11... | collective-permute-start | bytes 2654216 | tf_op jit(solution)/shard_map/ppermute | solution.py:643
  83.4 9.5 %collective-permute-start.14 = (bf16[448,384]{1,0:T(8,128)(2,1)}, bf16[448,384]{1,0:T(8,128)(2,1)S(1)}, u32[]{:S(2)}, u32[]{:S(2)}) collective-permute-start(bf16[448,384]{1,0:T(8,128)(2,1)} %get-tuple-element.61), channel_id=1, source_target_pairs={{0,8},{8,0},{16,24},{24,16},{1,9},{9,1},{17,25},{25,17},{2,10},{10... | collective-permute-start | bytes 1032200 | tf_op jit(solution)/shard_map/ppermute | solution.py:643
  84.5 15.8 %collective-permute-start.16 = (bf16[448,384]{1,0:T(8,128)(2,1)}, bf16[448,384]{1,0:T(8,128)(2,1)}, u32[]{:S(2)}, u32[]{:S(2)}) collective-permute-start(bf16[448,384]{1,0:T(8,128)(2,1)} %get-tuple-element.62), channel_id=1, source_target_pairs={{0,24},{8,16},{16,8},{24,0},{1,25},{9,17},{17,9},{25,1},{2,26},{10... | collective-permute-start | bytes 1032200 | tf_op jit(solution)/shard_map/ppermute | solution.py:643
  84.9 15.4 %collective-permute-start.15 = (bf16[448,384]{1,0:T(8,128)(2,1)}, bf16[448,384]{1,0:T(8,128)(2,1)}, u32[]{:S(2)}, u32[]{:S(2)}) collective-permute-start(bf16[448,384]{1,0:T(8,128)(2,1)} %get-tuple-element.63), channel_id=1, source_target_pairs={{0,16},{8,24},{16,0},{24,8},{1,17},{9,25},{17,1},{25,9},{2,18},{10... | collective-permute-start | bytes 1032200 | tf_op jit(solution)/shard_map/ppermute | solution.py:643
  87.0 61.3 %collective-permute-start.41 = (bf16[864,384]{1,0:T(8,128)(2,1)}, bf16[864,384]{1,0:T(8,128)(2,1)}, u32[]{:S(2)}, u32[]{:S(2)}) collective-permute-start(bf16[864,384]{1,0:T(8,128)(2,1)} %constant_dynamic-slice_fusion), channel_id=1, source_target_pairs={{0,8},{8,0},{16,24},{24,16},{1,9},{9,1},{17,25},{25,17},{2,10},{10... | collective-permute-start | bytes 1990664 | tf_op jit(solution)/shard_map/ppermute | solution.py:643
  88.0 43.1 %collective-permute-start.32 = (bf16[16,384]{1,0:T(8,128)(2,1)S(1)}, bf16[16,384]{1,0:T(8,128)(2,1)S(1)}, u32[]{:S(2)}, u32[]{:S(2)}) collective-permute-start(bf16[16,384]{1,0:T(8,128)(2,1)S(1)} %copy-done.5), channel_id=1, source_target_pairs={{0,16},{8,24},{16,0},{24,8},{1,17},{9,25},{17,1},{25,9},{2,18},{10... | collective-permute-start | bytes 36872 | tf_op jit(solution)/shard_map/ppermute | solution.py:643
  105.1 6.9 %collective-permute-start.18 = (bf16[112,384]{1,0:T(8,128)(2,1)S(1)}, bf16[112,384]{1,0:T(8,128)(2,1)S(1)}, u32[]{:S(2)}, u32[]{:S(2)}) collective-permute-start(bf16[112,384]{1,0:T(8,128)(2,1)S(1)} %get-tuple-element.73), channel_id=1, source_target_pairs={{0,4},{1,5},{2,6},{3,7},{4,0},{5,1},{6,2},{7,3},{8,12},{9,13},{10,... | collective-permute-start | bytes 258056 | tf_op jit(solution)/shard_map/ppermute | solution.py:643
  105.4 11.4 %collective-permute-start.28 = (bf16[144,384]{1,0:T(8,128)(2,1)S(1)}, bf16[144,384]{1,0:T(8,128)(2,1)S(1)}, u32[]{:S(2)}, u32[]{:S(2)}) collective-permute-start(bf16[144,384]{1,0:T(8,128)(2,1)S(1)} %get-tuple-element.66), channel_id=1, source_target_pairs={{0,8},{8,0},{16,24},{24,16},{1,9},{9,1},{17,25},{25,17},{2,10},{10... | collective-permute-start | bytes 331784 | tf_op jit(solution)/shard_map/ppermute | solution.py:643
  108.1 11.9 %collective-permute-start.30 = (bf16[144,384]{1,0:T(8,128)(2,1)S(1)}, bf16[144,384]{1,0:T(8,128)(2,1)S(1)}, u32[]{:S(2)}, u32[]{:S(2)}) collective-permute-start(bf16[144,384]{1,0:T(8,128)(2,1)S(1)} %get-tuple-element.67), channel_id=1, source_target_pairs={{0,24},{8,16},{16,8},{24,0},{1,25},{9,17},{17,9},{25,1},{2,26},{10... | collective-permute-start | bytes 331784 | tf_op jit(solution)/shard_map/ppermute | solution.py:643
  112.0 9.4 %collective-permute-start.29 = (bf16[144,384]{1,0:T(8,128)(2,1)S(1)}, bf16[144,384]{1,0:T(8,128)(2,1)S(1)}, u32[]{:S(2)}, u32[]{:S(2)}) collective-permute-start(bf16[144,384]{1,0:T(8,128)(2,1)S(1)} %get-tuple-element.68), channel_id=1, source_target_pairs={{0,16},{8,24},{16,0},{24,8},{1,17},{9,25},{17,1},{25,9},{2,18},{10... | collective-permute-start | bytes 331784 | tf_op jit(solution)/shard_map/ppermute | solution.py:643
  116.8 6.0 %collective-permute-start.22 = (bf16[112,384]{1,0:T(8,128)(2,1)S(1)}, bf16[112,384]{1,0:T(8,128)(2,1)S(1)}, u32[]{:S(2)}, u32[]{:S(2)}) collective-permute-start(bf16[112,384]{1,0:T(8,128)(2,1)S(1)} %fusion.8), channel_id=1, source_target_pairs={{0,6},{1,7},{2,4},{3,5},{4,2},{5,3},{6,0},{7,1},{8,14},{9,15},{10,... | collective-permute-start | bytes 258056 | tf_op jit(solution)/shard_map/ppermute | solution.py:643
  120.1 8.2 %collective-permute-start.21 = (bf16[112,384]{1,0:T(8,128)(2,1)S(1)}, bf16[112,384]{1,0:T(8,128)(2,1)S(1)}, u32[]{:S(2)}, u32[]{:S(2)}) collective-permute-start(bf16[112,384]{1,0:T(8,128)(2,1)S(1)} %fusion.8), channel_id=1, source_target_pairs={{0,4},{1,5},{2,6},{3,7},{4,0},{5,1},{6,2},{7,3},{8,12},{9,13},{10,... | collective-permute-start | bytes 258056 | tf_op jit(solution)/shard_map/ppermute | solution.py:643
  121.4 6.8 %collective-permute-start.20 = (bf16[112,384]{1,0:T(8,128)(2,1)S(1)}, bf16[112,384]{1,0:T(8,128)(2,1)S(1)}, u32[]{:S(2)}, u32[]{:S(2)}) collective-permute-start(bf16[112,384]{1,0:T(8,128)(2,1)S(1)} %fusion.8), channel_id=1, source_target_pairs={{0,2},{1,3},{2,0},{3,1},{4,6},{5,7},{6,4},{7,5},{8,10},{9,11},{10,... | collective-permute-start | bytes 258056 | tf_op jit(solution)/shard_map/ppermute | solution.py:643
  122.8 6.9 %collective-permute-start.31 = (bf16[16,384]{1,0:T(8,128)(2,1)S(1)}, bf16[16,384]{1,0:T(8,128)(2,1)S(1)}, u32[]{:S(2)}, u32[]{:S(2)}) collective-permute-start(bf16[16,384]{1,0:T(8,128)(2,1)S(1)} %copy-done.5), channel_id=1, source_target_pairs={{0,8},{8,0},{16,24},{24,16},{1,9},{9,1},{17,25},{25,17},{2,10},{10... | collective-permute-start | bytes 36872 | tf_op jit(solution)/shard_map/ppermute | solution.py:643
  128.4 19.9 %collective-permute-start.24 = (bf16[4,112,384]{2,1,0:T(8,128)(2,1)S(1)}, bf16[4,112,384]{2,1,0:T(8,128)(2,1)S(1)}, u32[]{:S(2)}, u32[]{:S(2)}) collective-permute-start(bf16[4,112,384]{2,1,0:T(8,128)(2,1)S(1)} %get-tuple-element.70), channel_id=1, source_target_pairs={{0,16},{8,24},{16,0},{24,8},{1,17},{9,25},{17,1},{25,9},{2,18},{10... | collective-permute-start | bytes 1032200 | tf_op jit(solution)/shard_map/ppermute | solution.py:643
  128.6 20.7 %collective-permute-start.23 = (bf16[4,112,384]{2,1,0:T(8,128)(2,1)S(1)}, bf16[4,112,384]{2,1,0:T(8,128)(2,1)S(1)}, u32[]{:S(2)}, u32[]{:S(2)}) collective-permute-start(bf16[4,112,384]{2,1,0:T(8,128)(2,1)S(1)} %get-tuple-element.70), channel_id=1, source_target_pairs={{0,8},{8,0},{16,24},{24,16},{1,9},{9,1},{17,25},{25,17},{2,10},{10... | collective-permute-start | bytes 1032200 | tf_op jit(solution)/shard_map/ppermute | solution.py:643
  129.7 22.5 %collective-permute-start.25 = (bf16[4,112,384]{2,1,0:T(8,128)(2,1)S(1)}, bf16[4,112,384]{2,1,0:T(8,128)(2,1)S(1)}, u32[]{:S(2)}, u32[]{:S(2)}) collective-permute-start(bf16[4,112,384]{2,1,0:T(8,128)(2,1)S(1)} %get-tuple-element.70), channel_id=1, source_target_pairs={{0,24},{8,16},{16,8},{24,0},{1,25},{9,17},{17,9},{25,1},{2,26},{10... | collective-permute-start | bytes 1032200 | tf_op jit(solution)/shard_map/ppermute | solution.py:643
  131.1 14.6 %collective-permute-start.33 = (bf16[16,384]{1,0:T(8,128)(2,1)S(1)}, bf16[16,384]{1,0:T(8,128)(2,1)S(1)}, u32[]{:S(2)}, u32[]{:S(2)}) collective-permute-start(bf16[16,384]{1,0:T(8,128)(2,1)S(1)} %copy-done.5), channel_id=1, source_target_pairs={{0,24},{8,16},{16,8},{24,0},{1,25},{9,17},{17,9},{25,1},{2,26},{10... | collective-permute-start | bytes 36872 | tf_op jit(solution)/shard_map/ppermute | solution.py:643
  145.7 6.9 %collective-permute-start.36 = (bf16[208,384]{1,0:T(8,128)(2,1)S(1)}, bf16[208,384]{1,0:T(8,128)(2,1)S(1)}, u32[]{:S(2)}, u32[]{:S(2)}) collective-permute-start(bf16[208,384]{1,0:T(8,128)(2,1)S(1)} %get-tuple-element.82), channel_id=1, source_target_pairs={{0,6},{1,7},{2,4},{3,5},{4,2},{5,3},{6,0},{7,1},{8,14},{9,15},{10,... | collective-permute-start | bytes 479240 | tf_op jit(solution)/shard_map/ppermute | solution.py:643
  148.3 12.3 %collective-permute-start.35 = (bf16[208,384]{1,0:T(8,128)(2,1)S(1)}, bf16[208,384]{1,0:T(8,128)(2,1)S(1)}, u32[]{:S(2)}, u32[]{:S(2)}) collective-permute-start(bf16[208,384]{1,0:T(8,128)(2,1)S(1)} %get-tuple-element.82), channel_id=1, source_target_pairs={{0,4},{1,5},{2,6},{3,7},{4,0},{5,1},{6,2},{7,3},{8,12},{9,13},{10,... | collective-permute-start | bytes 479240 | tf_op jit(solution)/shard_map/ppermute | solution.py:643
  148.3 12.3 %collective-permute-start.34 = (bf16[208,384]{1,0:T(8,128)(2,1)S(1)}, bf16[208,384]{1,0:T(8,128)(2,1)S(1)}, u32[]{:S(2)}, u32[]{:S(2)}) collective-permute-start(bf16[208,384]{1,0:T(8,128)(2,1)S(1)} %get-tuple-element.82), channel_id=1, source_target_pairs={{0,2},{1,3},{2,0},{3,1},{4,6},{5,7},{6,4},{7,5},{8,10},{9,11},{10,... | collective-permute-start | bytes 479240 | tf_op jit(solution)/shard_map/ppermute | solution.py:643
  149.3 25.6 %collective-permute-start.42 = (bf16[864,384]{1,0:T(8,128)(2,1)}, bf16[864,384]{1,0:T(8,128)(2,1)S(1)}, u32[]{:S(2)}, u32[]{:S(2)}) collective-permute-start(bf16[864,384]{1,0:T(8,128)(2,1)} %collective-permute-done.41.fx0), channel_id=1, source_target_pairs={{0,1},{1,0},{2,3},{3,2},{4,5},{5,4},{6,7},{7,6},{8,9},{9,8},{10,11... | collective-permute-start | bytes 1990664 | tf_op jit(solution)/shard_map/ppermute | solution.py:643
  152.5 20.5 %collective-permute-start.26 = (bf16[4,4,112,384]{3,2,1,0:T(8,128)(2,1)S(1)}, bf16[4,4,112,384]{3,2,1,0:T(8,128)(2,1)S(1)}, u32[]{:S(2)}, u32[]{:S(2)}) collective-permute-start(bf16[4,4,112,384]{3,2,1,0:T(8,128)(2,1)S(1)} %get-tuple-element.60), channel_id=1, source_target_pairs={{0,1},{1,0},{2,3},{3,2},{4,5},{5,4},{6,7},{7,6},{8,9},{9,8},{10,11... | collective-permute-start | bytes 4128776 | tf_op jit(solution)/shard_map/ppermute | solution.py:643
  (24 other events, 123.8 us)
where the time goes:
time: 213 us
  Pallas kernels  71.9 us (34%)
  waiting for transfers between devices  68.7 us (32%)
  starting transfers between devices  50.6 us (24%)
  other arithmetic  11 us (5%)
  local copies, waits for them, and re-layouts  9.38 us (4%)
    ppermute x44, waiting for transfers between devices, swap(): return lax.ppermute(x, axis, [(i, i ^ mask) for i in range(count)])  68.7 us
    ppermute x44, starting transfers between devices, swap(): return lax.ppermute(x, axis, [(i, i ^ mask) for i in range(count)])  50.6 us
    pallas_call x1, Pallas kernels, final_call(): pl.pallas_call(final_kernel, out_shape=(sd, sd, sd), in_specs=[sspec()] *...  19.8 us
    pallas_call x1, Pallas kernels, main_call(): pl.pallas_call(functools.partial(main_kernel, len(bufs), fast, rows), out...  19.4 us
    pallas_call x1, Pallas kernels, ns_a(): pl.pallas_call(ns_a_kernel, out_shape=(sd, sd), in_specs=[sspec()] * 3 +...  16.9 us
    pallas_call x1, Pallas kernels, heads_call(): pl.pallas_call(functools.partial(heads_kernel, rows), out_shape=outs, in_...  11.2 us
    dynamic_slice x4, local copies, waits for them, and re-layouts, rows_at(): return lax.dynamic_slice_in_dim(x, start, n, 0)  6.16 us
    pallas_call x1, Pallas kernels, prep(): pl.pallas_call(functools.partial(prep_kernel, count), out_shape=(out, out...  4.55 us
  transfers between devices with their start and end apart: 44, of which 21 were waited for; matrix products, arithmetic and copies ran while one was open for 7% of the time, Pallas kernels for 5%

commit v1 on v0

--- a/solution.py
+++ b/solution.py
@@ -8,6 +8,7 @@
 from jax.experimental.pallas import tpu as pltpu
 from jax.sharding import PartitionSpec as P
 
+
 D = 384
 HEADS = 6
 HD = 64
@@ -31,7 +32,6 @@
 NBLOCKS = 18
 ADALN, QKV, OUTW, UP, DOWN = range(5)
 P_SIZE = sum(m[0] * m[1] for m in MATS)
-GRAD_ROWS = 3584
 KEPT_ROWS = 16
 
 
@@ -84,7 +84,7 @@
     return pltpu.CompilerParams(vmem_limit_bytes=VMEM_LIMIT, **kw)
 
 
-def prep_kernel(count, s_ref, p_ref, m_ref, w_ref, mo_ref):
+def prep_kernel(count, s_ref, p_ref, m_ref, w_ref, wh_ref, mh_ref, mo_ref):
     for shard in range(count):
 
         @pl.when(s_ref[0] == shard)
@@ -95,15 +95,22 @@
                     w_ref[crow : crow + n, 128 * j : 128 * j + 128] = p_ref[src, :].astype(BF16)
                     mo_ref[crow : crow + n, 128 * j : 128 * j + 128] = m_ref[src, :].astype(BF16)
 
+    half = wh_ref.shape[0]
+    mine = pl.ds(pl.multiple_of(s_ref[1] * half, half), half)
+    wh_ref[...] = w_ref[mine, :]
+    mh_ref[...] = mo_ref[mine, :]
+
 
 def prep(sidx, params, momentum, count):
     rows = P_SIZE // count // D
     out = jax.ShapeDtypeStruct((rows, D), BF16)
+    part = jax.ShapeDtypeStruct((rows // 2, D), BF16)
     return pl.pallas_call(
         functools.partial(prep_kernel, count),
-        out_shape=(out, out),
+        out_shape=(out, part, part),
         in_specs=[sspec(), vspec(), vspec()],
-        out_specs=(vspec(), vspec()),
+        out_specs=(vspec(),) * 3,
+        scratch_shapes=[pltpu.VMEM((rows, D), BF16)],
         compiler_params=params_of(),
         name="prep",
     )(sidx, params, momentum)
@@ -165,10 +172,16 @@
                     pltpu.make_async_copy(src, dst, sems.at[q]).start()
 
 
+def by_core(value, core):
+    half = value.shape[0] // 2
+    top, bottom = value[:half], value[half:]
+    return jnp.where(core == 0, top, bottom), jnp.where(core == 0, bottom, top)
+
+
 def main_kernel(nbuf, fast, rows, s_ref, table, tok, cot, *refs):
     bufs = refs[:nbuf]
-    (blend, qkv, probs, amix_in, gafter, gmx, mods, gmod, silu, wqkv, grads) = refs[nbuf : nbuf + 11]
-    wts, ao_s, aa_s, amix, minp, gmi, mo, sems = refs[nbuf + 11 :]
+    (blend, qkv, probs, amix_in, gafter, gmx, mods, gmod, silu, wqkv, gout, keep1, send1) = refs[nbuf : nbuf + 13]
+    wts, ao_s, aa_s, amix, minp, gmi, mo, sems = refs[nbuf + 13 :]
     lat = rows // SEQ
     if fast:
         load_weights_fast(s_ref, bufs, wts, sems, True)
@@ -192,7 +205,6 @@
         mods[b] = mm(sc, wts[b])[:8]
     for j in range(3):
         wqkv[j] = wts[6 + j]
-    grads[9 * D :, :] = jnp.zeros((GRAD_ROWS - 9 * D, D), F32)
 
     def mod(b, l):
         return mods[b, l : l + 1, :]
@@ -239,6 +251,15 @@
     gmi[...] = jnp.zeros_like(gmi)
     mo[...] = jnp.zeros_like(mo)
 
+    me, core = s_ref[0], s_ref[1]
+
+    def put(value, members, j):
+        mine, other = by_core(value, core)
+        for i, member in enumerate(members):
+            rs = pl.ds(pl.multiple_of(j * 96, 96), 96)
+            keep1[member ^ me, rs, :] = mine[96 * i : 96 * i + 96]
+            send1[member ^ me, rs, :] = other[96 * i : 96 * i + 96].astype(BF16)
+
     def mlp(j, carry):
         wu, wd = wts[10 + j], wts[14 + j]
         u = mm(minp[...], wu)
@@ -251,8 +272,8 @@
         mo[...] += mm(act, wd)
         gmo = gmx[...]
         gp = (mm(gmo, wd, 1, 1) * slope).astype(BF16)
-        grads[pl.ds(pl.multiple_of((5 + j) * D, D), D), :] = mm(act, gmo, 0, 0)
-        grads[pl.ds(pl.multiple_of((1 + j) * D, D), D), :] = mm(minp[...], gp, 0, 0)
+        put(mm(act, gmo, 0, 0), (3, 1), j)
+        put(mm(minp[...], gp, 0, 0), (2, 0), j)
         gmi[...] += mm(gp, wu, 1, 1)
         return carry
 
@@ -273,7 +294,7 @@
         gmod[2, l : l + 1, :] = jnp.sum(ga * ao_s[rs, :], axis=0, keepdims=True)
         minp[rs, :] = (ga * mod(2, l)).astype(BF16)
     gao = minp[...]
-    grads[0:D, :] = mm(amix[...], gao, 0, 0)
+    gout[...] = mm(amix[...], gao, 0, 0)
     gmx[...] = mm(gao, wts[9], 1, 1).astype(BF16)
 
 
@@ -292,7 +313,9 @@
         sd((6, 8, D), F32),
         sd((16, D), F32),
         sd((3, D, D), BF16),
-        sd((GRAD_ROWS, D), F32),
+        sd((D, D), F32),
+        sd((4, D, D), F32),
+        sd((4, D, D), BF16),
     )
     nsem = len(gather_plan(4)) if fast else 1
     return pl.pallas_call(
@@ -316,7 +339,7 @@
     )(sidx, table, tokens, cotangent, *bufs)
 
 
-def heads_kernel(rows, tok, qkv, probs, ai, gafter, gmx, mods, gmod1, silu, wqkv, gtok, gq, keep, gqkv, srow):
+def heads_kernel(rows, qkv, probs, gmx, gqkv):
     lat = rows // SEQ
     low = lax.broadcasted_iota(jnp.int32, (SEQ, 128), 1) < HD
     zero = jnp.zeros((SEQ, 128), BF16)
@@ -341,11 +364,37 @@
         return carry
 
     lax.fori_loop(0, lat, back, 0)
+
+
+def heads_call(qkv, probs, gmx):
+    rows = gmx.shape[0]
+    return pl.pallas_call(
+        functools.partial(heads_kernel, rows),
+        out_shape=jax.ShapeDtypeStruct((3, rows, D), BF16),
+        in_specs=[vspec()] * 3,
+        out_specs=vspec(),
+        compiler_params=params_of(),
+        cost_estimate=pl.CostEstimate(flops=6_000_000_000, bytes_accessed=6_000_000, transcendentals=0),
+        name="heads",
+    )(qkv, probs, gmx)
+
+
+def input_kernel(rows, s_ref, tok, gqkv, ai, gafter, mods, gmod1, silu, wqkv, gout, gtok, keep2, send2, keep, srow):
+    me, core = s_ref[0], s_ref[1]
+    lat = rows // SEQ
     gai = None
-    for j in range(3):
-        part = mm(gqkv[j], wqkv[j], 1, 1)
-        gai = part if gai is None else gai + part
-        gq[j * D : (j + 1) * D, :] = mm(ai[...], gqkv[j], 0, 0)
+    for j in range(4):
+        if j < 3:
+            part = mm(gqkv[j], wqkv[j], 1, 1)
+            gai = part if gai is None else gai + part
+            value = mm(ai[...], gqkv[j], 0, 0)
+        else:
+            value = gout[...]
+        mine, other = by_core(value, core)
+        for m in range(4):
+            rs = slice(48 * j, 48 * j + 48)
+            keep2[m ^ me, rs, :] = mine[48 * m : 48 * m + 48]
+            send2[m ^ me, rs, :] = other[48 * m : 48 * m + 48].astype(BF16)
     srow[...] = jnp.zeros_like(srow)
     for l in range(lat):
         rs = slice(l * SEQ, (l + 1) * SEQ)
@@ -360,20 +409,20 @@
     keep[...] = srow[...].astype(BF16)
 
 
-def heads_call(tokens, qkv, probs, ai, gafter, gmx, mods, gmod1, silu, wqkv):
+def input_call(sidx, tokens, gqkv, ai, gafter, mods, gmod1, silu, wqkv, gout):
     rows = tokens.shape[0]
     sd = jax.ShapeDtypeStruct
-    outs = (sd((rows, D), F32), sd((3 * D, D), F32), sd((KEPT_ROWS, D), BF16))
+    outs = (sd((rows, D), F32), sd((4, D // 2, D), F32), sd((4, D // 2, D), BF16), sd((KEPT_ROWS, D), BF16))
     return pl.pallas_call(
-        functools.partial(heads_kernel, rows),
+        functools.partial(input_kernel, rows),
         out_shape=outs,
-        in_specs=[vspec()] * 10,
-        out_specs=(vspec(),) * 3,
-        scratch_shapes=[pltpu.VMEM((3, rows, D), BF16), pltpu.VMEM((KEPT_ROWS, D), F32)],
+        in_specs=[sspec()] + [vspec()] * 9,
+        out_specs=(vspec(),) * 4,
+        scratch_shapes=[pltpu.VMEM((KEPT_ROWS, D), F32)],
         compiler_params=params_of(),
-        cost_estimate=pl.CostEstimate(flops=12_000_000_000, bytes_accessed=12_000_000, transcendentals=0),
-        name="heads",
-    )(tokens, qkv, probs, ai, gafter, gmx, mods, gmod1, silu, wqkv)
+        cost_estimate=pl.CostEstimate(flops=6_000_000_000, bytes_accessed=6_000_000, transcendentals=0),
+        name="input",
+    )(sidx, tokens, gqkv, ai, gafter, mods, gmod1, silu, wqkv, gout)
 
 
 def split(x):
@@ -402,21 +451,29 @@
     return ints, coeffs
 
 
+def either(flipped, tall, wide):
+    if flipped is None:
+        wide()
+    else:
+        pl.when(flipped)(tall)
+        pl.when(jnp.logical_not(flipped))(wide)
+
+
 def newton_schulz(ints, coeffs, mat_ref, upd_ref, bufs, npairs, flipped, factor):
     bufs[0] = jnp.zeros((D, D), F32)
 
     def gram(b, carry):
         x0, x1 = mat_ref[2 * b].astype(BF16), mat_ref[2 * b + 1].astype(BF16)
 
-        @pl.when(flipped)
-        def _():
+        def tall():
             x = jnp.concatenate([x0, x1], axis=0)
             bufs[0] += mm(x, x, 0, 0)
 
-        @pl.when(jnp.logical_not(flipped))
-        def _():
+        def wide():
             x = jnp.concatenate([x0, x1], axis=1)
             bufs[0] += mm(x, x, 1, 1)
+
+        either(flipped, tall, wide)
 
         return carry
 
@@ -449,16 +506,14 @@
         wh, wl = split(bufs[0])
         xs = [mat_ref[2 * b + i] for i in range(2)]
 
-        @pl.when(flipped)
-        def _():
+        def tall():
             for i in range(2):
                 xh, xl = split(xs[i])
                 upd_ref[2 * b + i] = mm(
                     jnp.concatenate([xh, xl, xh], axis=1), jnp.concatenate([wh, wh, wl], axis=0)
                 )
 
-        @pl.when(jnp.logical_not(flipped))
-        def _():
+        def wide():
             (h0, l0), (h1, l1) = split(xs[0]), split(xs[1])
             xh = jnp.concatenate([h0, h1], axis=1)
             xl = jnp.concatenate([l0, l1], axis=1)
@@ -466,146 +521,150 @@
             upd_ref[2 * b] = out[:, :D]
             upd_ref[2 * b + 1] = out[:, D:]
 
+        either(flipped, tall, wide)
         return carry
 
     lax.fori_loop(0, npairs, apply, 0)
 
 
-def first_chunks():
-    for q in range(32):
-        size = GRAD_ROWS // 32
-        row = q * size
-        while row < min((q + 1) * size, 9 * D):
-            n = min((q + 1) * size, (row // D + 1) * D) - row
-            yield (q // 16, q // 4 % 4, q % 4), row // D, row % D, n, row - q * size
-            row += n
-
-
-def take_first(s_ref, chunks, dst, first, count):
+def take_first(s_ref, chunks, dst):
     me, core, zed = s_ref[0], s_ref[1], s_ref[2]
-    for (c, m, z), block, row, n, crow in first_chunks():
-        if first <= block < first + count:
-            piece = chunks[core ^ c, me ^ m, zed ^ z, crow : crow + n, :]
-            dst[block - first, row : row + n, :] = piece.astype(F32)
+    for c, ref in enumerate(chunks):
+        for y in range(2):
+            part = ((me // 2) ^ 1) ^ y
+            rs = pl.ds(pl.multiple_of((core ^ c) * 192 + part * 96, 96), 96)
+            for z in range(4):
+                dst[zed ^ z, rs, :] = ref[y, z].astype(F32)
 
 
 def take_second(s_ref, chunks, dst):
-    me, core = s_ref[0], s_ref[1]
-    size = 3 * D // 8
-    for q in range(8):
-        row = q * size
-        while row < (q + 1) * size:
-            n = min((q + 1) * size, (row // D + 1) * D) - row
-            piece = chunks[core ^ (q // 4), me ^ (q % 4), row - q * size : row - q * size + n, :]
-            dst[row // D, row % D : row % D + n, :] = piece.astype(F32)
-            row += n
-
-
-def ns_a_kernel(s_ref, ints, coeffs, mom, fx0, fx1, kept, chunks, upd, grd, mat, bufs, kf):
-    me, core = s_ref[0], s_ref[1]
-    half = fx0.shape[0]
-    ndev = kept.shape[0] // KEPT_ROWS
-
-    def kept_rows(first):
+    me, core, zed = s_ref[0], s_ref[1], s_ref[2]
+    for c, ref in enumerate(chunks):
+        for m in range(4):
+            rs = pl.ds(pl.multiple_of((core ^ c) * 192 + (me ^ m) * 48, 48), 48)
+            for z in range(4):
+                dst[zed ^ z, rs, :] = ref[m, z].astype(F32)
+
+
+def adaln_grads(kept, grd, kf):
+    ndev = 2 * kept[0].shape[0] // KEPT_ROWS
+    for i, ref in enumerate(kept):
+        n = ref.shape[0]
+        for j in range(3):
+            kf[j, i * n : (i + 1) * n, :] = ref[:, 128 * j : 128 * j + 128].astype(F32)
+
+    def rows(first):
         part = [kf[j, pl.ds(first, ndev, stride=KEPT_ROWS), :] for j in range(3)]
         return jnp.concatenate(part, axis=1).astype(BF16)
 
-    for pair, target in (((0, 1), ADALN), ((2, 3), UP)):
-        nb = MATS[target][1] // D
-        first = MATS[target][2]
-
-        @pl.when((me // 2) == pair[0] // 2)
-        def _(target=target, nb=nb):
-            if target == ADALN:
-                for j in range(3):
-                    kf[j] = kept[:, 128 * j : 128 * j + 128].astype(F32)
-                sil = jnp.concatenate([kept_rows(12), kept_rows(13)], axis=0)
-                for b in range(nb):
-                    gm = jnp.concatenate([kept_rows(2 * b), kept_rows(2 * b + 1)], axis=0)
-                    grd[b] = mm(sil, gm, 0, 0)
-            else:
-                take_first(s_ref, chunks, grd, 1, nb)
-
-        for t in pair:
-            for _, block, r0, n, crow, frow, stride in [p for p in shard_pieces(t, 4) if p[0] == target]:
-                b = block - first
-
-                @pl.when(me == t)
-                def _(b=b, r0=r0, n=n, frow=frow, stride=stride):
-                    for j in range(3):
-                        cs = slice(128 * j, 128 * j + 128)
-                        m = mom[pl.ds(frow + j, n, stride=stride), :]
-                        mat[b, r0 : r0 + n, cs] = MOMENTUM_RATE * m + grd[b, r0 : r0 + n, cs]
-
-                cuts = sorted({crow, crow + n} | {c for c in (half,) if crow < c < crow + n})
-                for lo, hi in zip(cuts[:-1], cuts[1:]):
-                    h = lo // half
-                    for mine in (True, False):
-
-                        @pl.when(jnp.logical_and(me == (t ^ 1), (core == h) if mine else (core != h)))
-                        def _(b=b, r0=r0, lo=lo, hi=hi, h=h, crow=crow, mine=mine):
-                            src = fx0 if mine else fx1
-                            dst = slice(r0 + lo - crow, r0 + hi - crow)
-                            m = src[lo - h * half : hi - h * half, :].astype(F32)
-                            mat[b, dst, :] = MOMENTUM_RATE * m + grd[b, dst, :]
-
-    low = me < 2
-    npairs = jnp.where(low, 3, 2)
-    factor = jnp.where(low, update_scale(ADALN), update_scale(UP))
-    newton_schulz(ints, coeffs, mat, upd, bufs, npairs, jnp.bool_(False), factor)
-
-
-def ns_a(sidx, tables, mom, fx0, fx1, kept, chunks):
+    sil = jnp.concatenate([rows(12), rows(13)], axis=0)
+    for b in range(6):
+        gm = jnp.concatenate([rows(2 * b), rows(2 * b + 1)], axis=0)
+        grd[b] = mm(sil, gm, 0, 0)
+
+
+def add_momentum(t, target, mom, grd, mat, base=0):
+    first = MATS[target][2]
+    for _, block, r0, n, _, frow, stride in [p for p in shard_pieces(t, 4) if p[0] == target]:
+        b = block - first
+        for j in range(3):
+            cs = slice(128 * j, 128 * j + 128)
+            m = mom[pl.ds(frow + j, n, stride=stride), :]
+            mat[b, r0 : r0 + n, cs] = MOMENTUM_RATE * m + grd[base + b, r0 : r0 + n, cs]
+
+
+def add_foreign(s_ref, t, target, foreign, grd, mat):
+    core = s_ref[1]
+    half = foreign[0].shape[0]
+    for _, block, r0, n, crow, _, _ in [p for p in shard_pieces(t ^ 1, 4) if p[0] == target]:
+        b = block - MATS[target][2]
+        cuts = sorted({crow, crow + n} | {c for c in (half,) if crow < c < crow + n})
+        for lo, hi in zip(cuts[:-1], cuts[1:]):
+            h = lo // half
+            for mine, src in enumerate(foreign):
+
+                @pl.when(core == (h ^ mine))
+                def _(b=b, r0=r0, lo=lo, hi=hi, h=h, crow=crow, src=src):
+                    dst = slice(r0 + lo - crow, r0 + hi - crow)
+                    m = src[lo - h * half : hi - h * half, :].astype(F32)
+                    mat[b, dst, :] = MOMENTUM_RATE * m + grd[b, dst, :]
+
+
+TAIL = 48
+
+
+def ns_a_kernel(s_ref, ints, coeffs, mom, fx0, fx1, kz0, kz1, ch0, ch1, upd, grd, tail, mat, bufs, kf):
+    me = s_ref[0]
+
+    @pl.when(me < 2)
+    def _():
+        adaln_grads((kz0, kz1), grd, kf)
+
+    @pl.when(me >= 2)
+    def _():
+        take_first(s_ref, (ch0, ch1), grd)
+
+    for t, target in enumerate((ADALN, ADALN, UP, DOWN)):
+
+        @pl.when(me == t)
+        def _(t=t, target=target):
+            add_momentum(t, target, mom, grd, mat)
+            if target != DOWN:
+                add_foreign(s_ref, t, target, (fx0, fx1), grd, mat)
+
+    npairs = jnp.where(me < 2, 3, 2)
+    factor = jnp.where(me < 2, update_scale(ADALN), update_scale(UP))
+    newton_schulz(ints, coeffs, mat, upd, bufs, npairs, me == 3, factor)
+
+    for b in range(4):
+        rs = slice(TAIL * b, TAIL * b + TAIL)
+        tail[0, rs, :] = grd[b, D - TAIL :, :].astype(BF16)
+        tail[1, rs, :] = upd[b, D - TAIL :, :].astype(BF16)
+
+
+def ns_a(sidx, tables, mom, foreign, kept, chunks):
     sd = jax.ShapeDtypeStruct((6, D, D), F32)
     return pl.pallas_call(
         ns_a_kernel,
-        out_shape=(sd, sd),
-        in_specs=[sspec()] * 3 + [vspec()] * 5,
-        out_specs=(vspec(), vspec()),
+        out_shape=(sd, sd, jax.ShapeDtypeStruct((2, 4 * TAIL, D), BF16)),
+        in_specs=[sspec()] * 3 + [vspec()] * 7,
+        out_specs=(vspec(),) * 3,
         scratch_shapes=[
             pltpu.VMEM((6, D, D), F32),
             pltpu.VMEM((4, D, D), F32),
-            pltpu.VMEM((3, kept.shape[0], 128), F32),
+            pltpu.VMEM((3, 2 * kept[0].shape[0], 128), F32),
         ],
         compiler_params=params_of(),
         cost_estimate=pl.CostEstimate(flops=8_000_000_000, bytes_accessed=12_000_000, transcendentals=0),
         name="ns_a",
-    )(sidx, *tables, mom, fx0, fx1, kept, chunks)
-
-
-OWNER = ((QKV, 1, 2), (OUTW, 2, 1), (DOWN, 3, 2))
+    )(sidx, *tables, mom, *foreign, *kept, *chunks)
 
 
 def final_kernel(
-    s_ref, ints, coeffs, par, mom, chunks, chunks2, upa, grda, ograd, onew, omom, upb, gb, mat, bufs
+    s_ref, ints, coeffs, par, mom, ch0, ch1, upa, grda, tail, ograd, onew, omom, upb, gb, mat, bufs
 ):
     me = s_ref[0]
-    for target, t, npairs in OWNER:
-
-        @pl.when(me == t)
-        def _(target=target, t=t, npairs=npairs):
-            first = MATS[target][2]
-            count = MATS[target][0] * MATS[target][1] // (D * D)
-            if target == QKV:
-                take_second(s_ref, chunks2, gb)
-            else:
-                take_first(s_ref, chunks, gb, first - 9 if target == OUTW else 5, count)
-            for b in range(count, 2 * npairs):
-                mat[b] = jnp.zeros((D, D), F32)
-            for _, block, r0, n, crow, frow, stride in [p for p in shard_pieces(t, 4) if p[0] == target]:
-                b = block - first
-                for j in range(3):
-                    cs = slice(128 * j, 128 * j + 128)
-                    m = mom[pl.ds(frow + j, n, stride=stride), :]
-                    mat[b, r0 : r0 + n, cs] = MOMENTUM_RATE * m + gb[b, r0 : r0 + n, cs]
-
-    @pl.when(me > 0)
+    inner = jnp.logical_or(me == 1, me == 2)
+
+    @pl.when(inner)
     def _():
-        npairs = jnp.where(me == 2, 1, 2)
-        factor = jnp.where(
-            me == 1, update_scale(QKV), jnp.where(me == 2, update_scale(OUTW), update_scale(DOWN))
-        )
-        newton_schulz(ints, coeffs, mat, upb, bufs, npairs, me == 3, factor)
+        take_second(s_ref, (ch0, ch1), gb)
+        for b in range(1, 4):
+            mat[b] = jnp.zeros((D, D), F32)
+
+    @pl.when(me == 1)
+    def _():
+        add_momentum(1, QKV, mom, gb, mat)
+
+    @pl.when(me == 2)
+    def _():
+        add_momentum(2, OUTW, mom, gb, mat, 3)
+
+    @pl.when(inner)
+    def _():
+        npairs = jnp.where(me == 1, 2, 1)
+        factor = jnp.where(me == 1, update_scale(QKV), update_scale(OUTW))
+        newton_schulz(ints, coeffs, mat, upb, bufs, npairs, None, factor)
 
     for t in range(4):
 
@@ -613,38 +672,42 @@
         def _(t=t):
             for mat_id, block, r0, n, crow, frow, stride in shard_pieces(t, 4):
                 b = block - MATS[mat_id][2]
-                gref, uref = (grda, upa) if mat_id in (ADALN, UP) else (gb, upb)
                 for j in range(3):
                     cs = slice(128 * j, 128 * j + 128)
                     fl = pl.ds(frow + j, n, stride=stride)
-                    g = gref[b, r0 : r0 + n, cs]
+                    if mat_id == UP and t == 3:
+                        assert r0 == D - TAIL and n == TAIL
+                        g = tail[0, TAIL * b : TAIL * b + TAIL, cs].astype(F32)
+                        u = tail[1, TAIL * b : TAIL * b + TAIL, cs].astype(F32)
+                    elif mat_id in (QKV, OUTW):
+                        g = gb[b + 3 * (mat_id == OUTW), r0 : r0 + n, cs]
+                        u = upb[b, r0 : r0 + n, cs]
+                    else:
+                        g = grda[b, r0 : r0 + n, cs]
+                        u = upa[b, r0 : r0 + n, cs]
                     ograd[fl, :] = g
                     omom[fl, :] = MOMENTUM_RATE * mom[fl, :] + g
-                    onew[fl, :] = par[fl, :] - uref[b, r0 : r0 + n, cs]
-
-
-def final_call(sidx, tables, par, mom, chunks, chunks2, upa, grda):
+                    onew[fl, :] = par[fl, :] - u
+
+
+def final_call(sidx, tables, par, mom, chunks, upa, grda, tail):
     sd = jax.ShapeDtypeStruct(par.shape, F32)
     block4 = pltpu.VMEM((4, D, D), F32)
     return pl.pallas_call(
         final_kernel,
         out_shape=(sd, sd, sd),
-        in_specs=[sspec()] * 3 + [vspec()] * 6,
+        in_specs=[sspec()] * 3 + [vspec()] * 7,
         out_specs=(vspec(),) * 3,
         scratch_shapes=[block4, block4, block4, block4],
         compiler_params=params_of(),
         cost_estimate=pl.CostEstimate(flops=8_000_000_000, bytes_accessed=24_000_000, transcendentals=0),
         name="finish",
-    )(sidx, *tables, par, mom, chunks, chunks2, upa, grda)
+    )(sidx, *tables, par, mom, *chunks, upa, grda, tail)
 
 
 def swap(x, axis, mask):
     count = lax.axis_size(axis)
     return lax.ppermute(x, axis, [(i, i ^ mask) for i in range(count)])
-
-
-def rows_at(x, start, n):
-    return lax.dynamic_slice_in_dim(x, start, n, 0)
 
 
 def more_rows(x, hops):
@@ -660,19 +723,37 @@
     return total
 
 
-def plane_scatter(x, me):
-    mine = lax.dynamic_index_in_dim(x, me, 0, keepdims=False)
-    got = [swap(lax.dynamic_index_in_dim(x, me ^ m, 0, keepdims=False), "fsdp", m) for m in (1, 2, 3)]
-    return wide_sum([mine] + got)
-
-
-def core_sum(g, core):
-    half = g.shape[0] // 2
-    mine = rows_at(g, core * half, half)
-    return mine + swap(rows_at(g, (1 - core) * half, half), "rep", 1)
+def at(x, i):
+    return lax.dynamic_index_in_dim(x, i, 0, keepdims=False)
+
+
+def z_scatter(s, zed, extra=None):
+    size = s.shape[0] // 4
+    blocks = s.reshape(4, size, D)
+    got = []
+    for m in (1, 2, 3):
+        piece = at(blocks, zed ^ m).astype(BF16)
+        if extra is not None:
+            piece = jnp.concatenate([piece, extra], axis=0)
+        got.append(swap(piece, "rep", 2 * m))
+    total = wide_sum([at(blocks, zed)] + [g[:size] for g in got]).astype(BF16)
+    if extra is None:
+        return total
+    return total, jnp.concatenate([extra] + [g[size:] for g in got], axis=0)
+
+
+def fan(x, axis, masks):
+    got = [x]
+    for m in masks:
+        got.append(swap(x, axis, m))
+    return jnp.stack(got)
 
 
 def fast_device(tokens, conditions, assignment, params, momentum, cotangent):
+    return fast_body(tokens, conditions, assignment, params, momentum, cotangent)
+
+
+def fast_body(tokens, conditions, assignment, params, momentum, cotangent):
     me = lax.axis_index("fsdp")
     rep = lax.axis_index("rep")
     core, zed = rep % 2, rep // 2
@@ -680,61 +761,61 @@
     rows = lat * SEQ
     par = params.reshape(-1, 128)
     mom = momentum.reshape(-1, 128)
-    dev = me * lax.axis_size("rep") + rep
-    pick = ((assignment // lat) ^ dev) * lat + assignment % lat
+    source = assignment // lat
+    apart = ((source // 8) ^ me) + 4 * ((source % 8) ^ rep)
+    pick = apart * lat + assignment % lat
     sidx = jnp.concatenate([jnp.stack([me, core, zed]), pick]).astype(jnp.int32)
 
-    wc, mc = prep(sidx, par, mom, 4)
-    half = wc.shape[0] // 2
-    quarter = half // 2
-    wh = rows_at(wc, core * half, half)
-    conditions, wh = lax.optimization_barrier((conditions, wh))
-    rx, ry = swap(wh, "fsdp", 1), swap(wh, "fsdp", 2)
-    table = more_rows(conditions, (("rep", 1), ("rep", 2), ("rep", 4)))
+    hop = swap(conditions, "fsdp", 1)
+    wc, wh, mh = prep(sidx, par, mom, 4)
+    table = jnp.concatenate([conditions, hop], axis=0)
+    table, wh = lax.optimization_barrier((table, wh))
+    hop = swap(table, "fsdp", 2)
+    rx = swap(wh, "fsdp", 1)
+    ry = swap(wh, "fsdp", 2)
+    table = jnp.concatenate([table, hop], axis=0)
+    table = more_rows(table, (("rep", 1), ("rep", 2), ("rep", 4)))
     rx, ry, table = lax.optimization_barrier((rx, ry, table))
-    table = more_rows(table, (("fsdp", 1), ("fsdp", 2)))
+    quarter = wh.shape[0] // 2
     rda, rdb = swap(rx[:quarter], "fsdp", 2), swap(ry[quarter:], "fsdp", 1)
     px, py = swap(rx, "rep", 1), swap(ry, "rep", 1)
     pda, pdb = swap(rda, "rep", 1), swap(rdb, "rep", 1)
     bufs = (wc, rx, ry, rda, rdb, px, py, pda, pdb)
+    fx0 = swap(mh, "fsdp", 1)
 
     tok2, cot2 = tokens.reshape(rows, D), cotangent.reshape(rows, D)
-    (blend, qkv, probs, ai, gafter, gmx, mods, gmod1, silu, wqkv, g1) = main_call(
+    (blend, qkv, probs, ai, gafter, gmx, mods, gmod1, silu, wqkv, gout, keep1, send1) = main_call(
         sidx, table, tok2, cot2, bufs, True
     )
-    fx0 = swap(rows_at(mc, core * half, half), "fsdp", 1)
     fx1 = swap(fx0, "rep", 1)
 
-    h1 = core_sum(g1, core).astype(BF16)
-    s1 = plane_scatter(h1.reshape(4, GRAD_ROWS // 8, D), me).astype(BF16)
-    piece = s1.shape[0] // 4
-    s1 = s1.reshape(4, piece, D)
-    mine = lax.dynamic_index_in_dim(s1, zed, 0, keepdims=False)
-    got = [
-        swap(lax.dynamic_index_in_dim(s1, zed ^ m, 0, keepdims=False), "rep", 2 * m) for m in (1, 2, 3)
-    ]
-    zsum = wide_sum([mine] + got).astype(BF16)
-    col = jnp.stack([zsum] + [swap(zsum, "rep", 2 * m) for m in (1, 2, 3)])
-    plane = jnp.stack([col] + [swap(col, "fsdp", m) for m in (1, 2, 3)])
-    both = jnp.stack([plane, swap(plane, "rep", 1)])
-
-    gtok, g2, keep = heads_call(tok2, qkv, probs, ai, gafter, gmx, mods, gmod1, silu, wqkv)
-
-    h2 = core_sum(g2, core).astype(BF16).reshape(4, 3 * D // 8, D)
-    s2 = plane_scatter(h2, me).astype(BF16)
-    k2 = jnp.concatenate([keep] + [swap(keep, "fsdp", m) for m in (1, 2, 3)], axis=0)
-    msg = jnp.concatenate([s2, k2], axis=0)
-    z1, z2, z3 = (swap(msg, "rep", 2 * m) for m in (1, 2, 3))
-    ns = s2.shape[0]
-    q2 = (wide_sum([s2, z1[:ns]]) + wide_sum([z2[:ns], z3[:ns]])).astype(BF16)
-    kz = jnp.concatenate([k2, z1[ns:], z2[ns:], z3[ns:]], axis=0)
-    kept = jnp.concatenate([kz, swap(kz, "rep", 1)], axis=0)
-    p2 = jnp.stack([q2] + [swap(q2, "fsdp", m) for m in (1, 2, 3)])
-    both2 = jnp.stack([p2, swap(p2, "rep", 1)])
+    other = swap(send1, "rep", 1)
+    gqkv = heads_call(qkv, probs, gmx)
+    got = []
+    for m in (1, 2, 3):
+        got.append(swap((keep1[m] + other[m].astype(F32)).astype(BF16), "fsdp", m))
+    gtok, keep2, send2, keep = input_call(sidx, tok2, gqkv, ai, gafter, mods, gmod1, silu, wqkv, gout)
+    s1 = wide_sum([keep1[0] + other[0].astype(F32)] + got)
+    col = fan(z_scatter(s1, zed), "rep", (2, 4, 6))
+    pair = fan(col, "fsdp", (2,))
+    pairs = (pair, swap(pair, "rep", 1))
+
+    other = swap(send2, "rep", 1)
+    got = []
+    for m in (1, 2, 3):
+        part = (keep2[m] + other[m].astype(F32)).astype(BF16)
+        got.append(swap(jnp.concatenate([part, keep], axis=0), "fsdp", m))
+    size = keep2.shape[1]
+    s2 = wide_sum([keep2[0] + other[0].astype(F32)] + [g[:size] for g in got])
+    q2, kz = z_scatter(s2, zed, jnp.concatenate([keep] + [g[size:] for g in got], axis=0))
+    kept = (kz, swap(kz, "rep", 1))
+    quad = fan(fan(q2, "rep", (2, 4, 6)), "fsdp", (1, 2, 3))
+    quads = (quad, swap(quad, "rep", 1))
 
     tables = step_tables()
-    upa, grda = ns_a(sidx, tables, mom, fx0, fx1, kept, both)
-    ograd, onew, omom = final_call(sidx, tables, par, mom, both, both2, upa, grda)
+    upa, grda, tail = ns_a(sidx, tables, mom, (fx0, fx1), kept, pairs)
+    tail = swap(tail, "fsdp", 1)
+    ograd, onew, omom = final_call(sidx, tables, par, mom, quads, upa, grda, tail)
     shape = tokens.shape
     return (
         blend.reshape(shape),
@@ -795,19 +876,20 @@
     gathered = lax.all_gather(params.astype(BF16), "fsdp", axis=0, tiled=True)
     blocks = to_blocks(unpack(gathered))
     me = lax.axis_index("fsdp")
-    sidx = jnp.concatenate([jnp.stack([me, me, me]), assignment]).astype(jnp.int32)
+    sidx = jnp.concatenate([jnp.zeros((3,), jnp.int32), assignment.astype(jnp.int32)])
     tok2, cot2 = tokens.reshape(rows, D), cotangent.reshape(rows, D)
-    (blend, qkv, probs, ai, gafter, gmx, mods, gmod1, silu, wqkv, g1) = main_call(
+    (blend, qkv, probs, ai, gafter, gmx, mods, gmod1, silu, wqkv, gout, keep1, send1) = main_call(
         sidx, table, tok2, cot2, (blocks,), False
     )
-    gtok, g2, keep = heads_call(tok2, qkv, probs, ai, gafter, gmx, mods, gmod1, silu, wqkv)
+    gqkv = heads_call(qkv, probs, gmx)
+    gtok, keep2, send2, keep = input_call(sidx, tok2, gqkv, ai, gafter, mods, gmod1, silu, wqkv, gout)
+    halves1 = jnp.stack([keep1, send1.astype(F32)]).reshape(2, 4, 4, 96, D)
+    up = halves1[:, jnp.array([2, 0])].transpose(2, 0, 1, 3, 4).reshape(4, D, D)
+    down = halves1[:, jnp.array([3, 1])].transpose(2, 0, 1, 3, 4).reshape(4, D, D)
+    halves2 = jnp.stack([keep2, send2.astype(F32)]).reshape(2, 4, 4, 48, D)
+    last = halves2.transpose(2, 0, 1, 3, 4).reshape(4, D, D)
     rest = jnp.concatenate(
-        [
-            from_blocks(g2.reshape(3, D, D), True),
-            g1[:D].reshape(-1),
-            from_blocks(g1[D : 5 * D].reshape(4, D, D), True),
-            g1[5 * D : 9 * D].reshape(-1),
-        ]
+        [from_blocks(last[:3], True), last[3].reshape(-1), from_blocks(up, True), down.reshape(-1)]
     )
     kept = lax.all_gather(keep, ("fsdp", "rep"), axis=0, tiled=True).reshape(-1, KEPT_ROWS, D)
     silu_all = kept[:, 6 * lat : 7 * lat].reshape(-1, D)

time: 213 us -> 219 us (1.028)
  starting transfers between devices: 50.6 us -> 56.5 us
  other arithmetic: 11 us -> 6.05 us
  Pallas kernels: 71.9 us -> 74.4 us
  waiting for transfers between devices: 68.7 us -> 71 us
    dynamic_slice x4 -> x0, local copies, waits for them, and re-layouts: 6.16 us -> none  [rows_at(): return lax.dynamic_slice_in_dim(x, start, n, 0)]
    ppermute x44 -> x43, starting transfers between devices: 50.6 us -> 56.5 us  [swap(): return lax.ppermute(x, axis, [(i, i ^ mask) for i in range(count)])]
    unnamed x30 -> x47, local copies, waits for them, and re-layouts: 1.97 us -> 6.84 us
    convert_element_type x5 -> x4, other arithmetic: 5.6 us -> 1.46 us  [the longest x1 1.22 us: fast_body(): part = (keep2[m] + other[m].astype(F32)).astype(BF16)]
    pallas_call x3 -> x4, Pallas kernels: 32.6 us -> 36.1 us  [the longest x1 17.8 us: ns_a(): pl.pallas_call(ns_a_kernel, out_shape=(sd, sd, jax.ShapeDtypeStruct((2, 4...]
    another operation x5 -> x4, other arithmetic: 3.43 us -> 0.27 us  [fan(): return jnp.stack(got)]
    concatenate x2, local copies, waits for them, and re-layouts: 0.05 us -> 2.44 us  [the longest x1 2.43 us: more_rows(): x = jnp.concatenate([x, swap(x, axis, mask)], axis=0)]
    ppermute x44 -> x43, waiting for transfers between devices: 68.7 us -> 71 us  [swap(): return lax.ppermute(x, axis, [(i, i ^ mask) for i in range(count)])]
  transfers between devices with their start and end apart: 44 -> 43, of which waited for: 21 -> 19; matrix products, arithmetic and copies ran while one was open for 7% -> 5% of each run, Pallas kernels for 5% -> 10%
where the time goes in v1:
time: 219 us; the launch traced here: 218 us
  Pallas kernels  74.4 us (34%)
  waiting for transfers between devices  71 us (32%)
  starting transfers between devices  56.5 us (26%)
  local copies, waits for them, and re-layouts  9.39 us (4%)
  other arithmetic  6.05 us (3%)
    ppermute x43, waiting for transfers between devices, swap(): return lax.ppermute(x, axis, [(i, i ^ mask) for i in range(count)])  71 us
    ppermute x43, starting transfers between devices, swap(): return lax.ppermute(x, axis, [(i, i ^ mask) for i in range(count)])  56.5 us
    pallas_call x1, Pallas kernels, main_call(): pl.pallas_call(functools.partial(main_kernel, len(bufs), fast, rows), out...  19.5 us
    pallas_call x1, Pallas kernels, final_call(): pl.pallas_call(final_kernel, out_shape=(sd, sd, sd), in_specs=[sspec()] *...  18.8 us
    pallas_call x1, Pallas kernels, ns_a(): pl.pallas_call(ns_a_kernel, out_shape=(sd, sd, jax.ShapeDtypeStruct((2, 4...  17.8 us
    pallas_call x1, Pallas kernels, heads_call(): pl.pallas_call(functools.partial(heads_kernel, rows), out_shape=jax.Shape...  8.33 us
    unnamed x47, local copies, waits for them, and re-layouts  6.84 us
    pallas_call x1, Pallas kernels, input_call(): pl.pallas_call(functools.partial(input_kernel, rows), out_shape=outs, in_...  5.39 us
  transfers between devices with their start and end apart: 43, of which 19 were waited for; matrix products, arithmetic and copies ran while one was open for 5% of the time, Pallas kernels for 10%

profile of v1, /device:TPU:3, one launch (start us, length us, event | category | flops | bytes accessed | tf_op | source)
XLA Modules:
  0.0 218.3 jit_solution(18046527376023756852)
XLA Ops:
  2.1 4.5 %prep.1 = (bf16[1728,384]{1,0:T(8,128)(2,1)}, bf16[864,384]{1,0:T(8,128)(2,1)}, bf16[864,384]{1,0:T(8,128)(2,1)}) custom-call(s32[5]{0:T(128)} %pad_add_fusion.s_ref, f32[5184,128]{1,0:T(8,128)} %bitcast.88, f32[5184,128]{1,0:T(8,128)} %bitcast.90), custom_call_target="tpu_custom_call" | custom-call | tf_op jit(solution)/shard_map/prep/pallas_call | solution.py:108
  9.6 14.0 %collective-permute-done.3 = bf16[4,384]{1,0:T(4,128)(2,1)S(1)} collective-permute-done((bf16[4,384]{1,0:T(4,128)(2,1)S(1)}, bf16[4,384]{1,0:T(4,128)(2,1)S(1)}, u32[]{:S(2)}, u32[]{:S(2)}) %collective-permute-start.3) | collective-permute-done | bytes 3104 | tf_op jit(solution)/shard_map/ppermute | solution.py:710
  23.6 2.2 collective-permute-start.4
  29.3 2.4 %collective-permute-start.6 = (bf16[32,384]{1,0:T(8,128)(2,1)S(1)}, bf16[32,384]{1,0:T(8,128)(2,1)S(1)}, u32[]{:S(2)}, u32[]{:S(2)}) collective-permute-start(bf16[32,384]{1,0:T(8,128)(2,1)S(1)} %pad_maximum_fusion.7), channel_id=1, source_target_pairs={{0,4},{1,5},{2,6},{3,7},{4,0},{5,1},{6,2},{7,3},{8,12},{9,13},{10,... | collective-permute-start | bytes 73736 | tf_op jit(solution)/shard_map/ppermute | solution.py:710
  32.9 2.4 %concatenate.52.table = bf16[64,384]{1,0:T(8,128)(2,1)} concatenate(bf16[4,384]{1,0:T(4,128)(2,1)S(1)} %pad_maximum_fusion.10, bf16[4,384]{1,0:T(4,128)(2,1)S(1)} %collective-permute-done.3, bf16[8,384]{1,0:T(8,128)(2,1)S(1)} %collective-permute-done.4, bf16[16,384]{1,0:T(8,128)(2,1)S(1)} %collective-permute-done.5, bf16[32,384]{1,0:T(8,128)(2,1)S(1)} %collective-permute-done.6), dimensions={0} | concatenate | bytes 98304 | tf_op jit(solution)/shard_map/concatenate | solution.py:715
  35.4 2.7 %collective-permute-start.9 = (bf16[864,384]{1,0:T(8,128)(2,1)S(1)}, bf16[864,384]{1,0:T(8,128)(2,1)S(1)}, u32[]{:S(2)}, u32[]{:S(2)}) collective-permute-start(bf16[864,384]{1,0:T(8,128)(2,1)S(1)} %collective-permute-done.1.refs_1_), channel_id=1, source_target_pairs={{0,1},{1,0},{2,3},{3,2},{4,5},{5,4},{6,7},{7,6},{8,9},{9,8},{10,11... | collective-permute-start | bytes 1990664 | tf_op jit(solution)/shard_map/ppermute | solution.py:710
  40.1 7.3 %collective-permute-done.7.refs_3_ = bf16[432,384]{1,0:T(8,128)(2,1)S(1)} collective-permute-done((bf16[432,384]{1,0:T(8,128)(2,1)S(1)}, bf16[432,384]{1,0:T(8,128)(2,1)S(1)}, u32[]{:S(2)}, u32[]{:S(2)}) %collective-permute-start.7) | collective-permute-done | bytes 331808 | tf_op jit(solution)/shard_map/ppermute | solution.py:710
  52.1 19.5 %main.1 = (bf16[512,384]{1,0:T(8,128)(2,1)}, bf16[3,512,384]{2,1,0:T(8,128)(2,1)}, f32[12,256,256]{2,1,0:T(8,128)}, bf16[512,384]{1,0:T(8,128)(2,1)}, f32[512,38...) custom-call(s32[5]{0:T(128)} %pad_add_fusion.s_ref, ...), custom_call_target="tpu_custom_call" | custom-call | flops 20000000000 | bytes 30000000 | tf_op jit(solution)/shard_map/main/pallas_call | solution.py:321
  71.7 8.3 %heads.1.gqkv = bf16[3,512,384]{2,1,0:T(8,128)(2,1)} custom-call(bf16[3,512,384]{2,1,0:T(8,128)(2,1)} %get-tuple-element.44.qkv, f32[12,256,256]{2,1,0:T(8,128)} %get-tuple-element.45.probs, bf16[512,384]{1,0:T(8,128)(2,1)} %get-tuple-element.46.gmx), custom_call_target="tpu_custom_call" | custom-call | flops 6000000000 | bytes 6000000 | tf_op jit(solution)/shard_map/heads/pallas_call | solution.py:371
  80.0 5.4 %input.1 = (f32[512,384]{1,0:T(8,128)}, f32[4,192,384]{2,1,0:T(8,128)}, bf16[4,192,384]{2,1,0:T(8,128)(2,1)}, bf16[16,384]{1,0:T(8,128)(2,1)}) custom-call(s32[5]{0:T(128)} %pad_add_fusion.s_ref, bf16[512,384]{1,0:T(8,128)(2,1)} %bitcast.111, bf16[3,512,384]{2,1,0:T(8,128)(2,1)} %heads.1.gqkv, bf16[512,384]{1,0:T(8,128)(2,1)} %get-tuple-element.47.ai, ...), custom_call_target="tpu_custom_call" | custom-call | flops 6000000000 | bytes 6000000 | tf_op jit(solution)/shard_map/input/pallas_call | solution.py:416
  86.1 1.5 collective-permute-done.13
  89.6 1.5 pad_maximum_fusion.5
  93.8 8.5 %collective-permute-done.27.fx0 = bf16[864,384]{1,0:T(8,128)(2,1)} collective-permute-done((bf16[864,384]{1,0:T(8,128)(2,1)}, bf16[864,384]{1,0:T(8,128)(2,1)}, u32[]{:S(2)}, u32[]{:S(2)}) %collective-permute-start.27) | collective-permute-done | bytes 663584 | tf_op jit(solution)/shard_map/ppermute | solution.py:710
  102.3 2.1 collective-permute-start.28
  105.6 3.5 %collective-permute-done.14 = bf16[208,384]{1,0:T(8,128)(2,1)} collective-permute-done((bf16[208,384]{1,0:T(8,128)(2,1)}, bf16[208,384]{1,0:T(8,128)(2,1)}, u32[]{:S(2)}, u32[]{:S(2)}) %collective-permute-start.14) | collective-permute-done | bytes 159776 | tf_op jit(solution)/shard_map/ppermute | solution.py:710
  114.1 4.9 %collective-permute-done.33 = bf16[384,384]{1,0:T(8,128)(2,1)S(1)} collective-permute-done((bf16[384,384]{1,0:T(8,128)(2,1)S(1)}, bf16[384,384]{1,0:T(8,128)(2,1)S(1)}, u32[]{:S(2)}, u32[]{:S(2)}) %collective-permute-start.33) | collective-permute-done | bytes 294944 | tf_op jit(solution)/shard_map/ppermute | solution.py:710
  119.1 6.2 %collective-permute-done.32 = bf16[384,384]{1,0:T(8,128)(2,1)S(1)} collective-permute-done((bf16[384,384]{1,0:T(8,128)(2,1)S(1)}, bf16[384,384]{1,0:T(8,128)(2,1)S(1)}, u32[]{:S(2)}, u32[]{:S(2)}) %collective-permute-start.32) | collective-permute-done | bytes 294944 | tf_op jit(solution)/shard_map/ppermute | solution.py:710
  125.4 3.6 %collective-permute-start.36 = (bf16[96,384]{1,0:T(8,128)(2,1)S(1)}, bf16[96,384]{1,0:T(8,128)(2,1)S(1)}, u32[]{:S(2)}, u32[]{:S(2)}) collective-permute-start(bf16[96,384]{1,0:T(8,128)(2,1)S(1)} %get-tuple-element.74), channel_id=1, source_target_pairs={{0,6},{1,7},{2,4},{3,5},{4,2},{5,3},{6,0},{7,1},{8,14},{9,15},{10,... | collective-permute-start | bytes 221192 | tf_op jit(solution)/shard_map/ppermute | solution.py:710
  130.8 4.6 %collective-permute-done.35 = bf16[96,384]{1,0:T(8,128)(2,1)S(1)} collective-permute-done((bf16[96,384]{1,0:T(8,128)(2,1)S(1)}, bf16[96,384]{1,0:T(8,128)(2,1)S(1)}, u32[]{:S(2)}, u32[]{:S(2)}) %collective-permute-start.35) | collective-permute-done | bytes 73760 | tf_op jit(solution)/shard_map/ppermute | solution.py:710
  136.2 2.9 %collective-permute-start.37 = (bf16[96,384]{1,0:T(8,128)(2,1)S(1)}, bf16[96,384]{1,0:T(8,128)(2,1)S(1)}, u32[]{:S(2)}, u32[]{:S(2)}) collective-permute-start(bf16[96,384]{1,0:T(8,128)(2,1)S(1)} %fusion.12), channel_id=1, source_target_pairs={{0,2},{1,3},{2,0},{3,1},{4,6},{5,7},{6,4},{7,5},{8,10},{9,11},{10,... | collective-permute-start | bytes 221192 | tf_op jit(solution)/shard_map/ppermute | solution.py:710
  140.9 2.4 %collective-permute-start.17 = (bf16[112,384]{1,0:T(8,128)(2,1)S(1)}, bf16[112,384]{1,0:T(8,128)(2,1)S(1)}, u32[]{:S(2)}, u32[]{:S(2)}) collective-permute-start(bf16[112,384]{1,0:T(8,128)(2,1)S(1)} %get-tuple-element.84), channel_id=1, source_target_pairs={{0,2},{1,3},{2,0},{3,1},{4,6},{5,7},{6,4},{7,5},{8,10},{9,11},{10,... | collective-permute-start | bytes 258056 | tf_op jit(solution)/shard_map/ppermute | solution.py:710
  143.4 4.1 %collective-permute-start.40 = (bf16[4,96,384]{2,1,0:T(8,128)(2,1)S(1)}, bf16[4,96,384]{2,1,0:T(8,128)(2,1)S(1)}, u32[]{:S(2)}, u32[]{:S(2)}) collective-permute-start(bf16[4,96,384]{2,1,0:T(8,128)(2,1)S(1)} %get-tuple-element.77), channel_id=1, source_target_pairs={{0,16},{8,24},{16,0},{24,8},{1,17},{9,25},{17,1},{25,9},{2,18},{10... | collective-permute-start | bytes 884744 | tf_op jit(solution)/shard_map/ppermute | solution.py:710
  147.4 3.0 %collective-permute-done.18 = bf16[112,384]{1,0:T(8,128)(2,1)S(1)} collective-permute-done((bf16[112,384]{1,0:T(8,128)(2,1)S(1)}, bf16[112,384]{1,0:T(8,128)(2,1)S(1)}, u32[]{:S(2)}, u32[]{:S(2)}) %collective-permute-start.18) | collective-permute-done | bytes 86048 | tf_op jit(solution)/shard_map/ppermute | solution.py:710
  151.6 2.5 %collective-permute-start.20 = (bf16[48,384]{1,0:T(8,128)(2,1)S(1)}, bf16[48,384]{1,0:T(8,128)(2,1)S(1)}, u32[]{:S(2)}, u32[]{:S(2)}) collective-permute-start(bf16[48,384]{1,0:T(8,128)(2,1)S(1)} %fusion.18), channel_id=1, source_target_pairs={{0,2},{1,3},{2,0},{3,1},{4,6},{5,7},{6,4},{7,5},{8,10},{9,11},{10,... | collective-permute-start | bytes 110600 | tf_op jit(solution)/shard_map/ppermute | solution.py:710
  154.2 4.2 %collective-permute-start.41 = (bf16[2,4,96,384]{3,2,1,0:T(8,128)(2,1)S(1)}, bf16[2,4,96,384]{3,2,1,0:T(8,128)(2,1)S(1)}, u32[]{:S(2)}, u32[]{:S(2)}) collective-permute-start(bf16[2,4,96,384]{3,2,1,0:T(8,128)(2,1)S(1)} %pad_maximum_fusion.1.ch0), channel_id=1, source_target_pairs={{0,1},{1,0},{2,3},{3,2},{4,5},{5,4},{6,7},{7,6},{8,9},{9,8},{10,11... | collective-permute-start | bytes 1769480 | tf_op jit(solution)/shard_map/ppermute | solution.py:710
  158.5 1.9 collective-permute-start.25
  161.7 1.8 collective-permute-done.25
  163.6 4.5 %collective-permute-start.29 = (bf16[256,384]{1,0:T(8,128)(2,1)S(1)}, bf16[256,384]{1,0:T(8,128)(2,1)S(1)}, u32[]{:S(2)}, u32[]{:S(2)}) collective-permute-start(bf16[256,384]{1,0:T(8,128)(2,1)S(1)} %slice_dynamic-update-slice_fusion.kz0), channel_id=1, source_target_pairs={{0,1},{1,0},{2,3},{3,2},{4,5},{5,4},{6,7},{7,6},{8,9},{9,8},{10,11... | collective-permute-start | bytes 589832 | tf_op jit(solution)/shard_map/ppermute | solution.py:710
  168.1 1.7 collective-permute-start.26
  172.2 17.8 %ns_a.1 = (f32[6,384,384]{2,1,0:T(8,128)}, f32[6,384,384]{2,1,0:T(8,128)}, bf16[2,192,384]{2,1,0:T(8,128)(2,1)}) custom-call(s32[5]{0:T(128)} %pad_add_fusion.s_ref, s32[27]{0:T(128)} %constant.98.clone.ints, f32[27]{0:T(128)} %constant.99.clone.coeffs, f32[5184,128]{1,0:T(8,128)} %bitcast.91, bf16[864,384]{1,0:T(8,128)(2,1)} %collective-permute-done.27.fx0, ...), custom_call_target="tpu_custom_call" | custom-call | flops 8000000000 | bytes 12000000 | tf_op jit(solution)/shard_map/ns_a/pallas_call | solution.py:627
  191.3 7.5 %collective-permute-done.42.tail = bf16[2,192,384]{2,1,0:T(8,128)(2,1)S(1)} collective-permute-done((bf16[2,192,384]{2,1,0:T(8,128)(2,1)}, bf16[2,192,384]{2,1,0:T(8,128)(2,1)S(1)}, u32[]{:S(2)}, u32[]{:S(2)}) %collective-permute-start.42) | collective-permute-done | bytes 294944 | tf_op jit(solution)/shard_map/ppermute | solution.py:710
  199.5 18.8 %finish.1 = (f32[5184,128]{1,0:T(8,128)}, f32[5184,128]{1,0:T(8,128)}, f32[5184,128]{1,0:T(8,128)}) custom-call(s32[5]{0:T(128)} %pad_add_fusion.s_ref, s32[27]{0:T(128)} %constant.98.clone.ints, f32[27]{0:T(128)} %constant.99.clone.coeffs, f32[5184,128]{1,0:T(8,128)} %bitcast.89, f32[5184,128]{1,0:T(8,128)} %bitcast.92, bf16[4,4,48,384]{3,2,1,0:T(8,128)(2,1)} %copy-done.3, ...), custom_call_target="tpu_custom_call" | custom-call | flops 8000000000 | bytes 24000000 | tf_op jit(solution)/shard_map/finish/pallas_call | solution.py:696
  (129 shorter events, 38.9 us)
Async XLA Ops:
  6.6 28.7 %collective-permute-start.1 = (bf16[864,384]{1,0:T(8,128)(2,1)}, bf16[864,384]{1,0:T(8,128)(2,1)S(1)}, u32[]{:S(2)}, u32[]{:S(2)}) collective-permute-start(bf16[864,384]{1,0:T(8,128)(2,1)} %get-tuple-element.37), channel_id=1, source_target_pairs={{0,8},{8,0},{16,24},{24,16},{1,9},{9,1},{17,25},{25,17},{2,10},{10... | collective-permute-start | bytes 1990664 | tf_op jit(solution)/shard_map/ppermute | solution.py:710
  8.1 27.2 %collective-permute-start.2 = (bf16[864,384]{1,0:T(8,128)(2,1)}, bf16[864,384]{1,0:T(8,128)(2,1)S(1)}, u32[]{:S(2)}, u32[]{:S(2)}) collective-permute-start(bf16[864,384]{1,0:T(8,128)(2,1)} %get-tuple-element.37), channel_id=1, source_target_pairs={{0,16},{8,24},{16,0},{24,8},{1,17},{9,25},{17,1},{25,9},{2,18},{10... | collective-permute-start | bytes 1990664 | tf_op jit(solution)/shard_map/ppermute | solution.py:710
  9.4 14.2 %collective-permute-start.3 = (bf16[4,384]{1,0:T(4,128)(2,1)S(1)}, bf16[4,384]{1,0:T(4,128)(2,1)S(1)}, u32[]{:S(2)}, u32[]{:S(2)}) collective-permute-start(bf16[4,384]{1,0:T(4,128)(2,1)S(1)} %pad_maximum_fusion.10), channel_id=1, source_target_pairs={{0,16},{8,24},{16,0},{24,8},{1,17},{9,25},{17,1},{25,9},{2,18},{10... | collective-permute-start | bytes 9224 | tf_op jit(solution)/shard_map/ppermute | solution.py:710
  35.4 14.7 %collective-permute-start.9 = (bf16[864,384]{1,0:T(8,128)(2,1)S(1)}, bf16[864,384]{1,0:T(8,128)(2,1)S(1)}, u32[]{:S(2)}, u32[]{:S(2)}) collective-permute-start(bf16[864,384]{1,0:T(8,128)(2,1)S(1)} %collective-permute-done.1.refs_1_), channel_id=1, source_target_pairs={{0,1},{1,0},{2,3},{3,2},{4,5},{5,4},{6,7},{7,6},{8,9},{9,8},{10,11... | collective-permute-start | bytes 1990664 | tf_op jit(solution)/shard_map/ppermute | solution.py:710
  38.1 9.3 %collective-permute-start.7 = (bf16[432,384]{1,0:T(8,128)(2,1)S(1)}, bf16[432,384]{1,0:T(8,128)(2,1)S(1)}, u32[]{:S(2)}, u32[]{:S(2)}) collective-permute-start(bf16[432,384]{1,0:T(8,128)(2,1)S(1)} %slice.90), channel_id=1, source_target_pairs={{0,16},{8,24},{16,0},{24,8},{1,17},{9,25},{17,1},{25,9},{2,18},{10... | collective-permute-start | bytes 995336 | tf_op jit(solution)/shard_map/ppermute | solution.py:710
  39.5 10.6 %collective-permute-start.10 = (bf16[864,384]{1,0:T(8,128)(2,1)S(1)}, bf16[864,384]{1,0:T(8,128)(2,1)S(1)}, u32[]{:S(2)}, u32[]{:S(2)}) collective-permute-start(bf16[864,384]{1,0:T(8,128)(2,1)S(1)} %collective-permute-done.2.refs_2_), channel_id=1, source_target_pairs={{0,1},{1,0},{2,3},{3,2},{4,5},{5,4},{6,7},{7,6},{8,9},{9,8},{10,11... | collective-permute-start | bytes 1990664 | tf_op jit(solution)/shard_map/ppermute | solution.py:710
  39.9 9.2 %collective-permute-start.8 = (bf16[432,384]{1,0:T(8,128)(2,1)S(1)}, bf16[432,384]{1,0:T(8,128)(2,1)S(1)}, u32[]{:S(2)}, u32[]{:S(2)}) collective-permute-start(bf16[432,384]{1,0:T(8,128)(2,1)S(1)} %slice.91), channel_id=1, source_target_pairs={{0,8},{8,0},{16,24},{24,16},{1,9},{9,1},{17,25},{25,17},{2,10},{10... | collective-permute-start | bytes 995336 | tf_op jit(solution)/shard_map/ppermute | solution.py:710
  85.7 24.7 %collective-permute-start.30 = (bf16[4,384,384]{2,1,0:T(8,128)(2,1)}, bf16[4,384,384]{2,1,0:T(8,128)(2,1)S(1)}, u32[]{:S(2)}, u32[]{:S(2)}) collective-permute-start(bf16[4,384,384]{2,1,0:T(8,128)(2,1)} %get-tuple-element.60), channel_id=1, source_target_pairs={{0,1},{1,0},{2,3},{3,2},{4,5},{5,4},{6,7},{7,6},{8,9},{9,8},{10,11... | collective-permute-start | bytes 3538952 | tf_op jit(solution)/shard_map/ppermute | solution.py:710
  85.9 16.4 %collective-permute-start.27 = (bf16[864,384]{1,0:T(8,128)(2,1)}, bf16[864,384]{1,0:T(8,128)(2,1)}, u32[]{:S(2)}, u32[]{:S(2)}) collective-permute-start(bf16[864,384]{1,0:T(8,128)(2,1)} %get-tuple-element.58), channel_id=1, source_target_pairs={{0,8},{8,0},{16,24},{24,16},{1,9},{9,1},{17,25},{25,17},{2,10},{10... | collective-permute-start | bytes 1990664 | tf_op jit(solution)/shard_map/ppermute | solution.py:710
  91.2 14.4 %collective-permute-start.16 = (bf16[208,384]{1,0:T(8,128)(2,1)}, bf16[208,384]{1,0:T(8,128)(2,1)}, u32[]{:S(2)}, u32[]{:S(2)}) collective-permute-start(bf16[208,384]{1,0:T(8,128)(2,1)} %get-tuple-element.101), channel_id=1, source_target_pairs={{0,24},{8,16},{16,8},{24,0},{1,25},{9,17},{17,9},{25,1},{2,26},{10... | collective-permute-start | bytes 479240 | tf_op jit(solution)/shard_map/ppermute | solution.py:710
  91.2 14.4 %collective-permute-start.15 = (bf16[208,384]{1,0:T(8,128)(2,1)}, bf16[208,384]{1,0:T(8,128)(2,1)}, u32[]{:S(2)}, u32[]{:S(2)}) collective-permute-start(bf16[208,384]{1,0:T(8,128)(2,1)} %get-tuple-element.100), channel_id=1, source_target_pairs={{0,16},{8,24},{16,0},{24,8},{1,17},{9,25},{17,1},{25,9},{2,18},{10... | collective-permute-start | bytes 479240 | tf_op jit(solution)/shard_map/ppermute | solution.py:710
  92.5 16.6 %collective-permute-start.14 = (bf16[208,384]{1,0:T(8,128)(2,1)}, bf16[208,384]{1,0:T(8,128)(2,1)}, u32[]{:S(2)}, u32[]{:S(2)}) collective-permute-start(bf16[208,384]{1,0:T(8,128)(2,1)} %get-tuple-element.99), channel_id=1, source_target_pairs={{0,8},{8,0},{16,24},{24,16},{1,9},{9,1},{17,25},{25,17},{2,10},{10... | collective-permute-start | bytes 479240 | tf_op jit(solution)/shard_map/ppermute | solution.py:710
  102.3 67.6 %collective-permute-start.28 = (bf16[864,384]{1,0:T(8,128)(2,1)}, bf16[864,384]{1,0:T(8,128)(2,1)S(1)}, u32[]{:S(2)}, u32[]{:S(2)}) collective-permute-start(bf16[864,384]{1,0:T(8,128)(2,1)} %collective-permute-done.27.fx0), channel_id=1, source_target_pairs={{0,1},{1,0},{2,3},{3,2},{4,5},{5,4},{6,7},{7,6},{8,9},{9,8},{10,11... | collective-permute-start | bytes 1990664 | tf_op jit(solution)/shard_map/ppermute | solution.py:710
  110.7 8.4 %collective-permute-start.33 = (bf16[384,384]{1,0:T(8,128)(2,1)S(1)}, bf16[384,384]{1,0:T(8,128)(2,1)S(1)}, u32[]{:S(2)}, u32[]{:S(2)}) collective-permute-start(bf16[384,384]{1,0:T(8,128)(2,1)S(1)} %get-tuple-element.68), channel_id=1, source_target_pairs={{0,24},{8,16},{16,8},{24,0},{1,25},{9,17},{17,9},{25,1},{2,26},{10... | collective-permute-start | bytes 884744 | tf_op jit(solution)/shard_map/ppermute | solution.py:710
  110.7 14.5 %collective-permute-start.32 = (bf16[384,384]{1,0:T(8,128)(2,1)S(1)}, bf16[384,384]{1,0:T(8,128)(2,1)S(1)}, u32[]{:S(2)}, u32[]{:S(2)}) collective-permute-start(bf16[384,384]{1,0:T(8,128)(2,1)S(1)} %get-tuple-element.69), channel_id=1, source_target_pairs={{0,16},{8,24},{16,0},{24,8},{1,17},{9,25},{17,1},{25,9},{2,18},{10... | collective-permute-start | bytes 884744 | tf_op jit(solution)/shard_map/ppermute | solution.py:710
  112.1 13.2 %collective-permute-start.31 = (bf16[384,384]{1,0:T(8,128)(2,1)S(1)}, bf16[384,384]{1,0:T(8,128)(2,1)S(1)}, u32[]{:S(2)}, u32[]{:S(2)}) collective-permute-start(bf16[384,384]{1,0:T(8,128)(2,1)S(1)} %get-tuple-element.67), channel_id=1, source_target_pairs={{0,8},{8,0},{16,24},{24,16},{1,9},{9,1},{17,25},{25,17},{2,10},{10... | collective-permute-start | bytes 884744 | tf_op jit(solution)/shard_map/ppermute | solution.py:710
  129.1 6.3 %collective-permute-start.35 = (bf16[96,384]{1,0:T(8,128)(2,1)S(1)}, bf16[96,384]{1,0:T(8,128)(2,1)S(1)}, u32[]{:S(2)}, u32[]{:S(2)}) collective-permute-start(bf16[96,384]{1,0:T(8,128)(2,1)S(1)} %get-tuple-element.75), channel_id=1, source_target_pairs={{0,4},{1,5},{2,6},{3,7},{4,0},{5,1},{6,2},{7,3},{8,12},{9,13},{10,... | collective-permute-start | bytes 221192 | tf_op jit(solution)/shard_map/ppermute | solution.py:710
  129.1 6.3 %collective-permute-start.34 = (bf16[96,384]{1,0:T(8,128)(2,1)S(1)}, bf16[96,384]{1,0:T(8,128)(2,1)S(1)}, u32[]{:S(2)}, u32[]{:S(2)}) collective-permute-start(bf16[96,384]{1,0:T(8,128)(2,1)S(1)} %get-tuple-element.73), channel_id=1, source_target_pairs={{0,2},{1,3},{2,0},{3,1},{4,6},{5,7},{6,4},{7,5},{8,10},{9,11},{10,... | collective-permute-start | bytes 221192 | tf_op jit(solution)/shard_map/ppermute | solution.py:710
  136.2 7.1 %collective-permute-start.37 = (bf16[96,384]{1,0:T(8,128)(2,1)S(1)}, bf16[96,384]{1,0:T(8,128)(2,1)S(1)}, u32[]{:S(2)}, u32[]{:S(2)}) collective-permute-start(bf16[96,384]{1,0:T(8,128)(2,1)S(1)} %fusion.12), channel_id=1, source_target_pairs={{0,2},{1,3},{2,0},{3,1},{4,6},{5,7},{6,4},{7,5},{8,10},{9,11},{10,... | collective-permute-start | bytes 221192 | tf_op jit(solution)/shard_map/ppermute | solution.py:710
  139.8 7.7 %collective-permute-start.19 = (bf16[112,384]{1,0:T(8,128)(2,1)S(1)}, bf16[112,384]{1,0:T(8,128)(2,1)S(1)}, u32[]{:S(2)}, u32[]{:S(2)}) collective-permute-start(bf16[112,384]{1,0:T(8,128)(2,1)S(1)} %get-tuple-element.83), channel_id=1, source_target_pairs={{0,6},{1,7},{2,4},{3,5},{4,2},{5,3},{6,0},{7,1},{8,14},{9,15},{10,... | collective-permute-start | bytes 258056 | tf_op jit(solution)/shard_map/ppermute | solution.py:710
  140.7 9.8 %collective-permute-start.18 = (bf16[112,384]{1,0:T(8,128)(2,1)S(1)}, bf16[112,384]{1,0:T(8,128)(2,1)S(1)}, u32[]{:S(2)}, u32[]{:S(2)}) collective-permute-start(bf16[112,384]{1,0:T(8,128)(2,1)S(1)} %get-tuple-element.82), channel_id=1, source_target_pairs={{0,4},{1,5},{2,6},{3,7},{4,0},{5,1},{6,2},{7,3},{8,12},{9,13},{10,... | collective-permute-start | bytes 258056 | tf_op jit(solution)/shard_map/ppermute | solution.py:710
  140.9 9.5 %collective-permute-start.17 = (bf16[112,384]{1,0:T(8,128)(2,1)S(1)}, bf16[112,384]{1,0:T(8,128)(2,1)S(1)}, u32[]{:S(2)}, u32[]{:S(2)}) collective-permute-start(bf16[112,384]{1,0:T(8,128)(2,1)S(1)} %get-tuple-element.84), channel_id=1, source_target_pairs={{0,2},{1,3},{2,0},{3,1},{4,6},{5,7},{6,4},{7,5},{8,10},{9,11},{10,... | collective-permute-start | bytes 258056 | tf_op jit(solution)/shard_map/ppermute | solution.py:710
  143.4 10.7 %collective-permute-start.40 = (bf16[4,96,384]{2,1,0:T(8,128)(2,1)S(1)}, bf16[4,96,384]{2,1,0:T(8,128)(2,1)S(1)}, u32[]{:S(2)}, u32[]{:S(2)}) collective-permute-start(bf16[4,96,384]{2,1,0:T(8,128)(2,1)S(1)} %get-tuple-element.77), channel_id=1, source_target_pairs={{0,16},{8,24},{16,0},{24,8},{1,17},{9,25},{17,1},{25,9},{2,18},{10... | collective-permute-start | bytes 884744 | tf_op jit(solution)/shard_map/ppermute | solution.py:710
  150.5 8.0 %collective-permute-start.22 = (bf16[48,384]{1,0:T(8,128)(2,1)S(1)}, bf16[48,384]{1,0:T(8,128)(2,1)S(1)}, u32[]{:S(2)}, u32[]{:S(2)}) collective-permute-start(bf16[48,384]{1,0:T(8,128)(2,1)S(1)} %fusion.18), channel_id=1, source_target_pairs={{0,6},{1,7},{2,4},{3,5},{4,2},{5,3},{6,0},{7,1},{8,14},{9,15},{10,... | collective-permute-start | bytes 110600 | tf_op jit(solution)/shard_map/ppermute | solution.py:710
  151.6 6.9 %collective-permute-start.21 = (bf16[48,384]{1,0:T(8,128)(2,1)S(1)}, bf16[48,384]{1,0:T(8,128)(2,1)S(1)}, u32[]{:S(2)}, u32[]{:S(2)}) collective-permute-start(bf16[48,384]{1,0:T(8,128)(2,1)S(1)} %fusion.18), channel_id=1, source_target_pairs={{0,4},{1,5},{2,6},{3,7},{4,0},{5,1},{6,2},{7,3},{8,12},{9,13},{10,... | collective-permute-start | bytes 110600 | tf_op jit(solution)/shard_map/ppermute | solution.py:710
  151.6 6.9 %collective-permute-start.20 = (bf16[48,384]{1,0:T(8,128)(2,1)S(1)}, bf16[48,384]{1,0:T(8,128)(2,1)S(1)}, u32[]{:S(2)}, u32[]{:S(2)}) collective-permute-start(bf16[48,384]{1,0:T(8,128)(2,1)S(1)} %fusion.18), channel_id=1, source_target_pairs={{0,2},{1,3},{2,0},{3,1},{4,6},{5,7},{6,4},{7,5},{8,10},{9,11},{10,... | collective-permute-start | bytes 110600 | tf_op jit(solution)/shard_map/ppermute | solution.py:710
  154.2 16.5 %collective-permute-start.41 = (bf16[2,4,96,384]{3,2,1,0:T(8,128)(2,1)S(1)}, bf16[2,4,96,384]{3,2,1,0:T(8,128)(2,1)S(1)}, u32[]{:S(2)}, u32[]{:S(2)}) collective-permute-start(bf16[2,4,96,384]{3,2,1,0:T(8,128)(2,1)S(1)} %pad_maximum_fusion.1.ch0), channel_id=1, source_target_pairs={{0,1},{1,0},{2,3},{3,2},{4,5},{5,4},{6,7},{7,6},{8,9},{9,8},{10,11... | collective-permute-start | bytes 1769480 | tf_op jit(solution)/shard_map/ppermute | solution.py:710
  160.5 7.5 %collective-permute-start.24 = (bf16[4,48,384]{2,1,0:T(8,128)(2,1)S(1)}, bf16[4,48,384]{2,1,0:T(8,128)(2,1)S(1)}, u32[]{:S(2)}, u32[]{:S(2)}) collective-permute-start(bf16[4,48,384]{2,1,0:T(8,128)(2,1)S(1)} %get-tuple-element.94), channel_id=1, source_target_pairs={{0,16},{8,24},{16,0},{24,8},{1,17},{9,25},{17,1},{25,9},{2,18},{10... | collective-permute-start | bytes 442376 | tf_op jit(solution)/shard_map/ppermute | solution.py:710
  161.7 6.3 %collective-permute-start.23 = (bf16[4,48,384]{2,1,0:T(8,128)(2,1)S(1)}, bf16[4,48,384]{2,1,0:T(8,128)(2,1)S(1)}, u32[]{:S(2)}, u32[]{:S(2)}) collective-permute-start(bf16[4,48,384]{2,1,0:T(8,128)(2,1)S(1)} %get-tuple-element.94), channel_id=1, source_target_pairs={{0,8},{8,0},{16,24},{24,16},{1,9},{9,1},{17,25},{25,17},{2,10},{10... | collective-permute-start | bytes 442376 | tf_op jit(solution)/shard_map/ppermute | solution.py:710
  163.6 6.3 %collective-permute-start.29 = (bf16[256,384]{1,0:T(8,128)(2,1)S(1)}, bf16[256,384]{1,0:T(8,128)(2,1)S(1)}, u32[]{:S(2)}, u32[]{:S(2)}) collective-permute-start(bf16[256,384]{1,0:T(8,128)(2,1)S(1)} %slice_dynamic-update-slice_fusion.kz0), channel_id=1, source_target_pairs={{0,1},{1,0},{2,3},{3,2},{4,5},{5,4},{6,7},{7,6},{8,9},{9,8},{10,11... | collective-permute-start | bytes 589832 | tf_op jit(solution)/shard_map/ppermute | solution.py:710
  168.1 23.1 %collective-permute-start.26 = (bf16[4,4,48,384]{3,2,1,0:T(8,128)(2,1)S(1)}, bf16[4,4,48,384]{3,2,1,0:T(8,128)(2,1)S(1)}, u32[]{:S(2)}, u32[]{:S(2)}) collective-permute-start(bf16[4,4,48,384]{3,2,1,0:T(8,128)(2,1)S(1)} %pad_maximum_fusion.ch0), channel_id=1, source_target_pairs={{0,1},{1,0},{2,3},{3,2},{4,5},{5,4},{6,7},{7,6},{8,9},{9,8},{10,11... | collective-permute-start | bytes 1769480 | tf_op jit(solution)/shard_map/ppermute | solution.py:710
  190.0 8.7 %collective-permute-start.42 = (bf16[2,192,384]{2,1,0:T(8,128)(2,1)}, bf16[2,192,384]{2,1,0:T(8,128)(2,1)S(1)}, u32[]{:S(2)}, u32[]{:S(2)}) collective-permute-start(bf16[2,192,384]{2,1,0:T(8,128)(2,1)} %get-tuple-element.63), channel_id=1, source_target_pairs={{0,8},{8,0},{16,24},{24,16},{1,9},{9,1},{17,25},{25,17},{2,10},{10... | collective-permute-start | bytes 884744 | tf_op jit(solution)/shard_map/ppermute | solution.py:710
  (31 other events, 196.8 us)

commit v2 on v1

--- a/solution.py
+++ b/solution.py
@@ -26,7 +26,6 @@
 F32 = jnp.float32
 BF16 = jnp.bfloat16
 ANY = pl.ANY
-VMEM_LIMIT = 60 * 1024 * 1024
 
 MATS = ((D, 6 * D, 0, True), (D, 3 * D, 6, True), (D, D, 9, True), (D, FF, 10, True), (FF, D, 14, False))
 NBLOCKS = 18
@@ -80,8 +79,8 @@
     return pl.BlockSpec(memory_space=pltpu.SMEM)
 
 
-def params_of(**kw):
-    return pltpu.CompilerParams(vmem_limit_bytes=VMEM_LIMIT, **kw)
+def params_of(mib):
+    return pltpu.CompilerParams(vmem_limit_bytes=mib * 1024 * 1024)
 
 
 def prep_kernel(count, s_ref, p_ref, m_ref, w_ref, wh_ref, mh_ref, mo_ref):
@@ -111,7 +110,7 @@
         in_specs=[sspec(), vspec(), vspec()],
         out_specs=(vspec(),) * 3,
         scratch_shapes=[pltpu.VMEM((rows, D), BF16)],
-        compiler_params=params_of(),
+        compiler_params=params_of(12),
         name="prep",
     )(sidx, params, momentum)
 
@@ -333,7 +332,7 @@
             pltpu.VMEM((rows, D), F32),
             pltpu.SemaphoreType.DMA((nsem,)),
         ],
-        compiler_params=params_of(),
+        compiler_params=params_of(34),
         cost_estimate=pl.CostEstimate(flops=20_000_000_000, bytes_accessed=30_000_000, transcendentals=0),
         name="main",
     )(sidx, table, tokens, cotangent, *bufs)
@@ -373,7 +372,7 @@
         out_shape=jax.ShapeDtypeStruct((3, rows, D), BF16),
         in_specs=[vspec()] * 3,
         out_specs=vspec(),
-        compiler_params=params_of(),
+        compiler_params=params_of(12),
         cost_estimate=pl.CostEstimate(flops=6_000_000_000, bytes_accessed=6_000_000, transcendentals=0),
         name="heads",
     )(qkv, probs, gmx)
@@ -419,7 +418,7 @@
         in_specs=[sspec()] + [vspec()] * 9,
         out_specs=(vspec(),) * 4,
         scratch_shapes=[pltpu.VMEM((KEPT_ROWS, D), F32)],
-        compiler_params=params_of(),
+        compiler_params=params_of(12),
         cost_estimate=pl.CostEstimate(flops=6_000_000_000, bytes_accessed=6_000_000, transcendentals=0),
         name="input",
     )(sidx, tokens, gqkv, ai, gafter, mods, gmod1, silu, wqkv, gout)
@@ -433,21 +432,21 @@
 POLY = (COEFF_C, COEFF_B, COEFF_A)
 PLAIN = (1.0, 0.0, 0.0)
 STEPS = (
-    (0, 0, 2, POLY),
-    (2, 0, 3, PLAIN),
-    (3, 2, 0, PLAIN),
-    (0, 0, 1, POLY),
-    (1, 2, 2, PLAIN),
-    (1, 0, 3, PLAIN),
-    (3, 1, 0, PLAIN),
-    (0, 0, 1, POLY),
-    (1, 2, 2, PLAIN),
+    (0, 0, 2, 1, POLY),
+    (2, 0, 3, 2, PLAIN),
+    (3, 2, 0, 2, PLAIN),
+    (0, 0, 1, 1, POLY),
+    (1, 2, 2, 3, PLAIN),
+    (1, 0, 3, 2, PLAIN),
+    (3, 1, 0, 2, PLAIN),
+    (0, 0, 1, 3, POLY),
+    (1, 2, 2, 3, PLAIN),
 )
 
 
 def step_tables():
-    ints = jnp.array([x for st in STEPS for x in st[:3]], jnp.int32)
-    coeffs = jnp.array([x for st in STEPS for x in st[3]], F32)
+    ints = jnp.array([x for st in STEPS for x in st[:4]], jnp.int32)
+    coeffs = jnp.array([x for st in STEPS for x in st[4]], F32)
     return ints, coeffs
 
 
@@ -488,15 +487,22 @@
     bufs[0] = g * (inv * inv)
 
     def step(k, carry):
-        i, j, d = ints[3 * k], ints[3 * k + 1], ints[3 * k + 2]
-        x = bufs[i]
-        xh, xl = split(x)
-        yh, yl = split(bufs[j])
-        prod = mm(jnp.concatenate([xh, xl, xh], axis=1), jnp.concatenate([yh, yh, yl], axis=0))
-        r0 = lax.broadcasted_iota(jnp.int32, (D, D), 0)
-        r1 = lax.broadcasted_iota(jnp.int32, (D, D), 1)
-        ident = jnp.where(r0 == r1, coeffs[3 * k + 2], 0.0)
-        bufs[d] = coeffs[3 * k] * prod + (coeffs[3 * k + 1] * x + ident)
+        i, j, d, passes = (ints[4 * k + n] for n in range(4))
+
+        def product(count):
+            x = bufs[i]
+            xh, xl = split(x)
+            yh, yl = split(bufs[j])
+            lhs = (xh, xl, xh)[:count]
+            rhs = (yh, yh, yl)[:count]
+            prod = mm(jnp.concatenate(lhs, axis=1), jnp.concatenate(rhs, axis=0))
+            r0 = lax.broadcasted_iota(jnp.int32, (D, D), 0)
+            r1 = lax.broadcasted_iota(jnp.int32, (D, D), 1)
+            ident = jnp.where(r0 == r1, coeffs[3 * k + 2], 0.0)
+            bufs[d] = coeffs[3 * k] * prod + (coeffs[3 * k + 1] * x + ident)
+
+        for count in (1, 2, 3):
+            pl.when(passes == count)(functools.partial(product, count))
         return carry
 
     lax.fori_loop(0, len(STEPS), step, 0)
@@ -508,16 +514,14 @@
 
         def tall():
             for i in range(2):
-                xh, xl = split(xs[i])
+                x = xs[i].astype(BF16)
                 upd_ref[2 * b + i] = mm(
-                    jnp.concatenate([xh, xl, xh], axis=1), jnp.concatenate([wh, wh, wl], axis=0)
+                    jnp.concatenate([x, x], axis=1), jnp.concatenate([wh, wl], axis=0)
                 )
 
         def wide():
-            (h0, l0), (h1, l1) = split(xs[0]), split(xs[1])
-            xh = jnp.concatenate([h0, h1], axis=1)
-            xl = jnp.concatenate([l0, l1], axis=1)
-            out = mm(jnp.concatenate([wh, wl, wh], axis=1), jnp.concatenate([xh, xh, xl], axis=0))
+            x = jnp.concatenate([xs[0].astype(BF16), xs[1].astype(BF16)], axis=1)
+            out = mm(jnp.concatenate([wh, wl], axis=1), jnp.concatenate([x, x], axis=0))
             upd_ref[2 * b] = out[:, :D]
             upd_ref[2 * b + 1] = out[:, D:]
 
@@ -634,7 +638,7 @@
             pltpu.VMEM((4, D, D), F32),
             pltpu.VMEM((3, 2 * kept[0].shape[0], 128), F32),
         ],
-        compiler_params=params_of(),
+        compiler_params=params_of(26),
         cost_estimate=pl.CostEstimate(flops=8_000_000_000, bytes_accessed=12_000_000, transcendentals=0),
         name="ns_a",
     )(sidx, *tables, mom, *foreign, *kept, *chunks)
@@ -699,7 +703,7 @@
         in_specs=[sspec()] * 3 + [vspec()] * 7,
         out_specs=(vspec(),) * 3,
         scratch_shapes=[block4, block4, block4, block4],
-        compiler_params=params_of(),
+        compiler_params=params_of(38),
         cost_estimate=pl.CostEstimate(flops=8_000_000_000, bytes_accessed=24_000_000, transcendentals=0),
         name="finish",
     )(sidx, *tables, par, mom, *chunks, upa, grda, tail)
@@ -814,7 +818,7 @@
 
     tables = step_tables()
     upa, grda, tail = ns_a(sidx, tables, mom, (fx0, fx1), kept, pairs)
-    tail = swap(tail, "fsdp", 1)
+    tail = lax.ppermute(tail, "fsdp", [(2, 3)])
     ograd, onew, omom = final_call(sidx, tables, par, mom, quads, upa, grda, tail)
     shape = tokens.shape
     return (

time: 219 us -> 203 us (0.927)
  the two profiles are of different devices: /device:TPU:3 before, /device:TPU:4 now
where the time goes in v2:
time: 203 us
  waiting for transfers between devices  84.7 us (42%)
  Pallas kernels  54.8 us (27%)
  starting transfers between devices  45.2 us (22%)
  local copies, waits for them, and re-layouts  11.2 us (6%)
  other arithmetic  5.76 us (3%)
    ppermute x42, waiting for transfers between devices, swap(): return lax.ppermute(x, axis, [(i, i ^ mask) for i in range(count)])  78 us
    ppermute x42, starting transfers between devices, swap(): return lax.ppermute(x, axis, [(i, i ^ mask) for i in range(count)])  41.8 us
    pallas_call x1, Pallas kernels, main_call(): pl.pallas_call(functools.partial(main_kernel, len(bufs), fast, rows), out...  23.4 us
    pallas_call x1, Pallas kernels, final_call(): pl.pallas_call(final_kernel, out_shape=(sd, sd, sd), in_specs=[sspec()] *...  11.5 us
    unnamed x35, local copies, waits for them, and re-layouts  11 us
    pallas_call x1, Pallas kernels, ns_a(): pl.pallas_call(ns_a_kernel, out_shape=(sd, sd, jax.ShapeDtypeStruct((2, 4...  9.89 us
    ppermute x1, waiting for transfers between devices, fast_body(): tail = lax.ppermute(tail, 'fsdp', [(2, 3)])  6.72 us
    pallas_call x1, Pallas kernels, heads_call(): pl.pallas_call(functools.partial(heads_kernel, rows), out_shape=jax.Shape...  4.83 us
  transfers between devices with their start and end apart: 43, of which 25 were waited for; matrix products, arithmetic and copies ran while one was open for 4% of the time, Pallas kernels for 6%

profile of v2, /device:TPU:4, one launch (start us, length us, event | category | flops | bytes accessed | tf_op | source)
XLA Modules:
  0.0 202.7 jit_solution(10263576552549269166)
XLA Ops:
  3.0 1.7 copy-done
  4.7 1.7 copy-done.2
  6.5 2.1 %prep.1 = (bf16[1728,384]{1,0:T(8,128)(2,1)S(1)}, bf16[864,384]{1,0:T(8,128)(2,1)S(1)}, bf16[864,384]{1,0:T(8,128)(2,1)}) custom-call(s32[5]{0:T(128)S(1)} %pad_add_fusion.s_ref, f32[5184,128]{1,0:T(8,128)S(1)} %bitcast.88, f32[5184,128]{1,0:T(8,128)S(1)} %bitcast.90), custom_call_target="tpu_custom_call" | custom-call | tf_op jit(solution)/shard_map/prep/pallas_call | solution.py:107
  10.2 2.0 collective-permute-start.3
  12.2 14.1 %collective-permute-done.3 = bf16[4,384]{1,0:T(4,128)(2,1)S(1)} collective-permute-done((bf16[4,384]{1,0:T(4,128)(2,1)S(1)}, bf16[4,384]{1,0:T(4,128)(2,1)S(1)}, u32[]{:S(2)}, u32[]{:S(2)}) %collective-permute-start.3) | collective-permute-done | bytes 3104 | tf_op jit(solution)/shard_map/ppermute | solution.py:714
  29.2 2.1 %collective-permute-done.5 = bf16[16,384]{1,0:T(8,128)(2,1)S(1)} collective-permute-done((bf16[16,384]{1,0:T(8,128)(2,1)S(1)}, bf16[16,384]{1,0:T(8,128)(2,1)S(1)}, u32[]{:S(2)}, u32[]{:S(2)}) %collective-permute-start.5) | collective-permute-done | bytes 12320 | tf_op jit(solution)/shard_map/ppermute | solution.py:714
  31.3 2.7 %collective-permute-start.6 = (bf16[32,384]{1,0:T(8,128)(2,1)S(1)}, bf16[32,384]{1,0:T(8,128)(2,1)S(1)}, u32[]{:S(2)}, u32[]{:S(2)}) collective-permute-start(bf16[32,384]{1,0:T(8,128)(2,1)S(1)} %pad_maximum_fusion.7), channel_id=1, source_target_pairs={{0,4},{1,5},{2,6},{3,7},{4,0},{5,1},{6,2},{7,3},{8,12},{9,13},{10,... | collective-permute-start | bytes 73736 | tf_op jit(solution)/shard_map/ppermute | solution.py:714
  34.0 2.1 %collective-permute-done.6 = bf16[32,384]{1,0:T(8,128)(2,1)S(1)} collective-permute-done((bf16[32,384]{1,0:T(8,128)(2,1)S(1)}, bf16[32,384]{1,0:T(8,128)(2,1)S(1)}, u32[]{:S(2)}, u32[]{:S(2)}) %collective-permute-start.6) | collective-permute-done | bytes 24608 | tf_op jit(solution)/shard_map/ppermute | solution.py:714
  38.6 7.9 %collective-permute-done.7.refs_3_ = bf16[432,384]{1,0:T(8,128)(2,1)S(1)} collective-permute-done((bf16[432,384]{1,0:T(8,128)(2,1)S(1)}, bf16[432,384]{1,0:T(8,128)(2,1)S(1)}, u32[]{:S(2)}, u32[]{:S(2)}) %collective-permute-start.7) | collective-permute-done | bytes 331808 | tf_op jit(solution)/shard_map/ppermute | solution.py:714
  52.1 23.4 %main.1 = (bf16[512,384]{1,0:T(8,128)(2,1)}, bf16[3,512,384]{2,1,0:T(8,128)(2,1)S(1)}, f32[12,256,256]{2,1,0:T(8,128)S(1)}, bf16[512,384]{1,0:T(8,128)(2,1)S(1)}...) custom-call(s32[5]{0:T(128)S(1)} %pad_add_fusion.s_ref, ...), custom_call_target="tpu_custom_call" | custom-call | flops 20000000000 | bytes 30000000 | tf_op jit(solution)/shard_map/main/pallas_call | solution.py:320
  75.5 4.8 %heads.1.gqkv = bf16[3,512,384]{2,1,0:T(8,128)(2,1)S(1)} custom-call(bf16[3,512,384]{2,1,0:T(8,128)(2,1)S(1)} %get-tuple-element.44.qkv, f32[12,256,256]{2,1,0:T(8,128)S(1)} %get-tuple-element.45.probs, bf16[512,384]{1,0:T(8,128)(2,1)S(1)} %get-tuple-element.46.gmx), custom_call_target="tpu_custom_call" | custom-call | flops 6000000000 | bytes 6000000 | tf_op jit(solution)/shard_map/heads/pallas_call | solution.py:370
  80.3 3.2 %input.1 = (f32[512,384]{1,0:T(8,128)}, f32[4,192,384]{2,1,0:T(8,128)S(1)}, bf16[4,192,384]{2,1,0:T(8,128)(2,1)S(1)}, bf16[16,384]{1,0:T(8,128)(2,1)S(1)}) custom-call(s32[5]{0:T(128)S(1)} %pad_add_fusion.s_ref, bf16[512,384]{1,0:T(8,128)(2,1)S(1)} %bitcast.95, bf16[3,512,384]{2,1,0:T(8,128)(2,1)S(1)} %heads.1.gqkv, ...), custom_call_target="tpu_custom_call" | custom-call | flops 6000000000 | bytes 6000000 | tf_op jit(solution)/shard_map/input/pallas_call | solution.py:415
  87.4 2.6 %collective-permute-start.16 = (bf16[208,384]{1,0:T(8,128)(2,1)}, bf16[208,384]{1,0:T(8,128)(2,1)}, u32[]{:S(2)}, u32[]{:S(2)}) collective-permute-start(bf16[208,384]{1,0:T(8,128)(2,1)} %get-tuple-element.101), channel_id=1, source_target_pairs={{0,24},{8,16},{16,8},{24,0},{1,25},{9,17},{17,9},{25,1},{2,26},{10... | collective-permute-start | bytes 479240 | tf_op jit(solution)/shard_map/ppermute | solution.py:714
  90.9 11.2 %collective-permute-done.27.fx0 = bf16[864,384]{1,0:T(8,128)(2,1)} collective-permute-done((bf16[864,384]{1,0:T(8,128)(2,1)}, bf16[864,384]{1,0:T(8,128)(2,1)}, u32[]{:S(2)}, u32[]{:S(2)}) %collective-permute-start.27) | collective-permute-done | bytes 663584 | tf_op jit(solution)/shard_map/ppermute | solution.py:714
  102.1 4.6 %collective-permute-done.16 = bf16[208,384]{1,0:T(8,128)(2,1)} collective-permute-done((bf16[208,384]{1,0:T(8,128)(2,1)}, bf16[208,384]{1,0:T(8,128)(2,1)}, u32[]{:S(2)}, u32[]{:S(2)}) %collective-permute-start.16) | collective-permute-done | bytes 159776 | tf_op jit(solution)/shard_map/ppermute | solution.py:714
  110.7 2.8 %collective-permute-start.33 = (bf16[384,384]{1,0:T(8,128)(2,1)S(1)}, bf16[384,384]{1,0:T(8,128)(2,1)S(1)}, u32[]{:S(2)}, u32[]{:S(2)}) collective-permute-start(bf16[384,384]{1,0:T(8,128)(2,1)S(1)} %get-tuple-element.68), channel_id=1, source_target_pairs={{0,24},{8,16},{16,8},{24,0},{1,25},{9,17},{17,9},{25,1},{2,26},{10... | collective-permute-start | bytes 884744 | tf_op jit(solution)/shard_map/ppermute | solution.py:714
  115.0 6.6 %collective-permute-done.33 = bf16[384,384]{1,0:T(8,128)(2,1)S(1)} collective-permute-done((bf16[384,384]{1,0:T(8,128)(2,1)S(1)}, bf16[384,384]{1,0:T(8,128)(2,1)S(1)}, u32[]{:S(2)}, u32[]{:S(2)}) %collective-permute-start.33) | collective-permute-done | bytes 294944 | tf_op jit(solution)/shard_map/ppermute | solution.py:714
  121.6 4.6 %collective-permute-done.32 = bf16[384,384]{1,0:T(8,128)(2,1)S(1)} collective-permute-done((bf16[384,384]{1,0:T(8,128)(2,1)S(1)}, bf16[384,384]{1,0:T(8,128)(2,1)S(1)}, u32[]{:S(2)}, u32[]{:S(2)}) %collective-permute-start.32) | collective-permute-done | bytes 294944 | tf_op jit(solution)/shard_map/ppermute | solution.py:714
  127.8 3.8 %collective-permute-start.36 = (bf16[96,384]{1,0:T(8,128)(2,1)S(1)}, bf16[96,384]{1,0:T(8,128)(2,1)S(1)}, u32[]{:S(2)}, u32[]{:S(2)}) collective-permute-start(bf16[96,384]{1,0:T(8,128)(2,1)S(1)} %get-tuple-element.74), channel_id=1, source_target_pairs={{0,6},{1,7},{2,4},{3,5},{4,2},{5,3},{6,0},{7,1},{8,14},{9,15},{10,... | collective-permute-start | bytes 221192 | tf_op jit(solution)/shard_map/ppermute | solution.py:714
  134.7 3.0 %collective-permute-done.35 = bf16[96,384]{1,0:T(8,128)(2,1)S(1)} collective-permute-done((bf16[96,384]{1,0:T(8,128)(2,1)S(1)}, bf16[96,384]{1,0:T(8,128)(2,1)S(1)}, u32[]{:S(2)}, u32[]{:S(2)}) %collective-permute-start.35) | collective-permute-done | bytes 73760 | tf_op jit(solution)/shard_map/ppermute | solution.py:714
  137.7 2.8 %collective-permute-start.39 = (bf16[96,384]{1,0:T(8,128)(2,1)S(1)}, bf16[96,384]{1,0:T(8,128)(2,1)S(1)}, u32[]{:S(2)}, u32[]{:S(2)}) collective-permute-start(bf16[96,384]{1,0:T(8,128)(2,1)S(1)} %fusion.12), channel_id=1, source_target_pairs={{0,6},{1,7},{2,4},{3,5},{4,2},{5,3},{6,0},{7,1},{8,14},{9,15},{10,... | collective-permute-start | bytes 221192 | tf_op jit(solution)/shard_map/ppermute | solution.py:714
  142.9 2.7 %collective-permute-start.19 = (bf16[112,384]{1,0:T(8,128)(2,1)S(1)}, bf16[112,384]{1,0:T(8,128)(2,1)S(1)}, u32[]{:S(2)}, u32[]{:S(2)}) collective-permute-start(bf16[112,384]{1,0:T(8,128)(2,1)S(1)} %get-tuple-element.83), channel_id=1, source_target_pairs={{0,6},{1,7},{2,4},{3,5},{4,2},{5,3},{6,0},{7,1},{8,14},{9,15},{10,... | collective-permute-start | bytes 258056 | tf_op jit(solution)/shard_map/ppermute | solution.py:714
  145.9 4.9 %collective-permute-done.38 = bf16[96,384]{1,0:T(8,128)(2,1)S(1)} collective-permute-done((bf16[96,384]{1,0:T(8,128)(2,1)S(1)}, bf16[96,384]{1,0:T(8,128)(2,1)S(1)}, u32[]{:S(2)}, u32[]{:S(2)}) %collective-permute-start.38) | collective-permute-done | bytes 73760 | tf_op jit(solution)/shard_map/ppermute | solution.py:714
  152.5 2.2 %collective-permute-done.18 = bf16[112,384]{1,0:T(8,128)(2,1)S(1)} collective-permute-done((bf16[112,384]{1,0:T(8,128)(2,1)S(1)}, bf16[112,384]{1,0:T(8,128)(2,1)S(1)}, u32[]{:S(2)}, u32[]{:S(2)}) %collective-permute-start.18) | collective-permute-done | bytes 86048 | tf_op jit(solution)/shard_map/ppermute | solution.py:714
  155.6 2.0 collective-permute-start.22
  157.6 2.4 %collective-permute-start.20 = (bf16[48,384]{1,0:T(8,128)(2,1)S(1)}, bf16[48,384]{1,0:T(8,128)(2,1)S(1)}, u32[]{:S(2)}, u32[]{:S(2)}) collective-permute-start(bf16[48,384]{1,0:T(8,128)(2,1)S(1)} %fusion.18), channel_id=1, source_target_pairs={{0,2},{1,3},{2,0},{3,1},{4,6},{5,7},{6,4},{7,5},{8,10},{9,11},{10,... | collective-permute-start | bytes 110600 | tf_op jit(solution)/shard_map/ppermute | solution.py:714
  163.0 2.4 %collective-permute-start.24 = (bf16[4,48,384]{2,1,0:T(8,128)(2,1)S(1)}, bf16[4,48,384]{2,1,0:T(8,128)(2,1)S(1)}, u32[]{:S(2)}, u32[]{:S(2)}) collective-permute-start(bf16[4,48,384]{2,1,0:T(8,128)(2,1)S(1)} %get-tuple-element.94), channel_id=1, source_target_pairs={{0,16},{8,24},{16,0},{24,8},{1,17},{9,25},{17,1},{25,9},{2,18},{10... | collective-permute-start | bytes 442376 | tf_op jit(solution)/shard_map/ppermute | solution.py:714
  166.1 3.2 %collective-permute-done.25 = bf16[4,48,384]{2,1,0:T(8,128)(2,1)S(1)} collective-permute-done((bf16[4,48,384]{2,1,0:T(8,128)(2,1)S(1)}, bf16[4,48,384]{2,1,0:T(8,128)(2,1)S(1)}, u32[]{:S(2)}, u32[]{:S(2)}) %collective-permute-start.25) | collective-permute-done | bytes 147488 | tf_op jit(solution)/shard_map/ppermute | solution.py:714
  171.1 9.9 %ns_a.1 = (f32[6,384,384]{2,1,0:T(8,128)S(1)}, f32[6,384,384]{2,1,0:T(8,128)S(1)}, bf16[2,192,384]{2,1,0:T(8,128)(2,1)S(1)}) custom-call(s32[5]{0:T(128)S(1)} %pad_add_fusion.s_ref, s32[36]{0:T(128)S(1)} %copy-done.10, f32[27]{0:T(128)S(1)} %copy-done.11, f32[5184,128]{1,0:T(8,128)S(1)} %bitcast.91, bf16[864,384]{1,0:T(8,128)(2,1)} %collective-permute-done.27.fx0, ...), custom_call_target="tpu_custom_call" | custom-call | flops 8000000000 | bytes 12000000 | tf_op jit(solution)/shard_map/ns_a/pallas_call | solution.py:631
  181.0 3.4 %collective-permute-start.42 = (bf16[2,192,384]{2,1,0:T(8,128)(2,1)S(1)}, bf16[2,192,384]{2,1,0:T(8,128)(2,1)S(1)}, u32[]{:S(2)}, u32[]{:S(2)}) collective-permute-start(bf16[2,192,384]{2,1,0:T(8,128)(2,1)S(1)} %get-tuple-element.63), channel_id=1, source_target_pairs={{16,24},{17,25},{18,26},{19,27},{20,28},{21,29},{22,30},{23,31}} | collective-permute-start | bytes 884744 | tf_op jit(solution)/shard_map/ppermute | solution.py:821
  184.5 6.7 %collective-permute-done.42.tail = bf16[2,192,384]{2,1,0:T(8,128)(2,1)S(1)} collective-permute-done((bf16[2,192,384]{2,1,0:T(8,128)(2,1)S(1)}, bf16[2,192,384]{2,1,0:T(8,128)(2,1)S(1)}, u32[]{:S(2)}, u32[]{:S(2)}) %collective-permute-start.42) | collective-permute-done | bytes 294944 | tf_op jit(solution)/shard_map/ppermute | solution.py:821
  191.2 11.5 %finish.1 = (f32[5184,128]{1,0:T(8,128)}, f32[5184,128]{1,0:T(8,128)}, f32[5184,128]{1,0:T(8,128)}) custom-call(s32[5]{0:T(128)S(1)} %pad_add_fusion.s_ref, s32[36]{0:T(128)S(1)} %copy-done.10, f32[27]{0:T(128)S(1)} %copy-done.11, f32[5184,128]{1,0:T(8,128)S(1)} %bitcast.89, f32[5184,128]{1,0:T(8,128)S(1)} %bitcast.92, ...), custom_call_target="tpu_custom_call" | custom-call | flops 8000000000 | bytes 24000000 | tf_op jit(solution)/shard_map/finish/pallas_call | solution.py:700
  (117 shorter events, 40.5 us)
Async XLA Ops:
  0.6 9.0 %collective-permute-start = (bf16[2,384]{1,0:T(2,128)(2,1)}, bf16[2,384]{1,0:T(2,128)(2,1)S(1)}, u32[]{:S(2)}, u32[]{:S(2)}) collective-permute-start(bf16[2,384]{1,0:T(2,128)(2,1)} %param.9), channel_id=1, source_target_pairs={{0,8},{8,0},{16,24},{24,16},{1,9},{9,1},{17,25},{25,17},{2,10},{10... | collective-permute-start | bytes 4616 | tf_op jit(solution)/shard_map/ppermute | solution.py:714
  9.6 26.6 %collective-permute-start.1 = (bf16[864,384]{1,0:T(8,128)(2,1)S(1)}, bf16[864,384]{1,0:T(8,128)(2,1)S(1)}, u32[]{:S(2)}, u32[]{:S(2)}) collective-permute-start(bf16[864,384]{1,0:T(8,128)(2,1)S(1)} %get-tuple-element.37), channel_id=1, source_target_pairs={{0,8},{8,0},{16,24},{24,16},{1,9},{9,1},{17,25},{25,17},{2,10},{10... | collective-permute-start | bytes 1990664 | tf_op jit(solution)/shard_map/ppermute | solution.py:714
  10.1 26.1 %collective-permute-start.2 = (bf16[864,384]{1,0:T(8,128)(2,1)S(1)}, bf16[864,384]{1,0:T(8,128)(2,1)S(1)}, u32[]{:S(2)}, u32[]{:S(2)}) collective-permute-start(bf16[864,384]{1,0:T(8,128)(2,1)S(1)} %get-tuple-element.37), channel_id=1, source_target_pairs={{0,16},{8,24},{16,0},{24,8},{1,17},{9,25},{17,1},{25,9},{2,18},{10... | collective-permute-start | bytes 1990664 | tf_op jit(solution)/shard_map/ppermute | solution.py:714
  10.2 16.1 %collective-permute-start.3 = (bf16[4,384]{1,0:T(4,128)(2,1)S(1)}, bf16[4,384]{1,0:T(4,128)(2,1)S(1)}, u32[]{:S(2)}, u32[]{:S(2)}) collective-permute-start(bf16[4,384]{1,0:T(4,128)(2,1)S(1)} %pad_maximum_fusion.10), channel_id=1, source_target_pairs={{0,16},{8,24},{16,0},{24,8},{1,17},{9,25},{17,1},{25,9},{2,18},{10... | collective-permute-start | bytes 9224 | tf_op jit(solution)/shard_map/ppermute | solution.py:714
  36.2 10.8 %collective-permute-start.9 = (bf16[864,384]{1,0:T(8,128)(2,1)S(1)}, bf16[864,384]{1,0:T(8,128)(2,1)S(1)}, u32[]{:S(2)}, u32[]{:S(2)}) collective-permute-start(bf16[864,384]{1,0:T(8,128)(2,1)S(1)} %collective-permute-done.1.refs_1_), channel_id=1, source_target_pairs={{0,1},{1,0},{2,3},{3,2},{4,5},{5,4},{6,7},{7,6},{8,9},{9,8},{10,11... | collective-permute-start | bytes 1990664 | tf_op jit(solution)/shard_map/ppermute | solution.py:714
  36.3 10.2 %collective-permute-start.7 = (bf16[432,384]{1,0:T(8,128)(2,1)S(1)}, bf16[432,384]{1,0:T(8,128)(2,1)S(1)}, u32[]{:S(2)}, u32[]{:S(2)}) collective-permute-start(bf16[432,384]{1,0:T(8,128)(2,1)S(1)} %slice.90), channel_id=1, source_target_pairs={{0,16},{8,24},{16,0},{24,8},{1,17},{9,25},{17,1},{25,9},{2,18},{10... | collective-permute-start | bytes 995336 | tf_op jit(solution)/shard_map/ppermute | solution.py:714
  36.8 10.3 %collective-permute-start.10 = (bf16[864,384]{1,0:T(8,128)(2,1)S(1)}, bf16[864,384]{1,0:T(8,128)(2,1)S(1)}, u32[]{:S(2)}, u32[]{:S(2)}) collective-permute-start(bf16[864,384]{1,0:T(8,128)(2,1)S(1)} %collective-permute-done.2.refs_2_), channel_id=1, source_target_pairs={{0,1},{1,0},{2,3},{3,2},{4,5},{5,4},{6,7},{7,6},{8,9},{9,8},{10,11... | collective-permute-start | bytes 1990664 | tf_op jit(solution)/shard_map/ppermute | solution.py:714
  37.0 10.1 %collective-permute-start.8 = (bf16[432,384]{1,0:T(8,128)(2,1)S(1)}, bf16[432,384]{1,0:T(8,128)(2,1)S(1)}, u32[]{:S(2)}, u32[]{:S(2)}) collective-permute-start(bf16[432,384]{1,0:T(8,128)(2,1)S(1)} %slice.91), channel_id=1, source_target_pairs={{0,8},{8,0},{16,24},{24,16},{1,9},{9,1},{17,25},{25,17},{2,10},{10... | collective-permute-start | bytes 995336 | tf_op jit(solution)/shard_map/ppermute | solution.py:714
  83.6 25.7 %collective-permute-start.30 = (bf16[4,384,384]{2,1,0:T(8,128)(2,1)}, bf16[4,384,384]{2,1,0:T(8,128)(2,1)}, u32[]{:S(2)}, u32[]{:S(2)}) collective-permute-start(bf16[4,384,384]{2,1,0:T(8,128)(2,1)} %get-tuple-element.60), channel_id=1, source_target_pairs={{0,1},{1,0},{2,3},{3,2},{4,5},{5,4},{6,7},{7,6},{8,9},{9,8},{10,11... | collective-permute-start | bytes 3538952 | tf_op jit(solution)/shard_map/ppermute | solution.py:714
  84.0 18.1 %collective-permute-start.27 = (bf16[864,384]{1,0:T(8,128)(2,1)}, bf16[864,384]{1,0:T(8,128)(2,1)}, u32[]{:S(2)}, u32[]{:S(2)}) collective-permute-start(bf16[864,384]{1,0:T(8,128)(2,1)} %get-tuple-element.58), channel_id=1, source_target_pairs={{0,8},{8,0},{16,24},{24,16},{1,9},{9,1},{17,25},{25,17},{2,10},{10... | collective-permute-start | bytes 1990664 | tf_op jit(solution)/shard_map/ppermute | solution.py:714
  87.4 19.3 %collective-permute-start.16 = (bf16[208,384]{1,0:T(8,128)(2,1)}, bf16[208,384]{1,0:T(8,128)(2,1)}, u32[]{:S(2)}, u32[]{:S(2)}) collective-permute-start(bf16[208,384]{1,0:T(8,128)(2,1)} %get-tuple-element.101), channel_id=1, source_target_pairs={{0,24},{8,16},{16,8},{24,0},{1,25},{9,17},{17,9},{25,1},{2,26},{10... | collective-permute-start | bytes 479240 | tf_op jit(solution)/shard_map/ppermute | solution.py:714
  90.0 16.7 %collective-permute-start.15 = (bf16[208,384]{1,0:T(8,128)(2,1)}, bf16[208,384]{1,0:T(8,128)(2,1)}, u32[]{:S(2)}, u32[]{:S(2)}) collective-permute-start(bf16[208,384]{1,0:T(8,128)(2,1)} %get-tuple-element.100), channel_id=1, source_target_pairs={{0,16},{8,24},{16,0},{24,8},{1,17},{9,25},{17,1},{25,9},{2,18},{10... | collective-permute-start | bytes 479240 | tf_op jit(solution)/shard_map/ppermute | solution.py:714
  90.4 17.7 %collective-permute-start.14 = (bf16[208,384]{1,0:T(8,128)(2,1)}, bf16[208,384]{1,0:T(8,128)(2,1)}, u32[]{:S(2)}, u32[]{:S(2)}) collective-permute-start(bf16[208,384]{1,0:T(8,128)(2,1)} %get-tuple-element.99), channel_id=1, source_target_pairs={{0,8},{8,0},{16,24},{24,16},{1,9},{9,1},{17,25},{25,17},{2,10},{10... | collective-permute-start | bytes 479240 | tf_op jit(solution)/shard_map/ppermute | solution.py:714
  102.1 69.0 %collective-permute-start.28 = (bf16[864,384]{1,0:T(8,128)(2,1)}, bf16[864,384]{1,0:T(8,128)(2,1)S(1)}, u32[]{:S(2)}, u32[]{:S(2)}) collective-permute-start(bf16[864,384]{1,0:T(8,128)(2,1)} %collective-permute-done.27.fx0), channel_id=1, source_target_pairs={{0,1},{1,0},{2,3},{3,2},{4,5},{5,4},{6,7},{7,6},{8,9},{9,8},{10,11... | collective-permute-start | bytes 1990664 | tf_op jit(solution)/shard_map/ppermute | solution.py:714
  110.7 10.9 %collective-permute-start.33 = (bf16[384,384]{1,0:T(8,128)(2,1)S(1)}, bf16[384,384]{1,0:T(8,128)(2,1)S(1)}, u32[]{:S(2)}, u32[]{:S(2)}) collective-permute-start(bf16[384,384]{1,0:T(8,128)(2,1)S(1)} %get-tuple-element.68), channel_id=1, source_target_pairs={{0,24},{8,16},{16,8},{24,0},{1,25},{9,17},{17,9},{25,1},{2,26},{10... | collective-permute-start | bytes 884744 | tf_op jit(solution)/shard_map/ppermute | solution.py:714
  113.5 12.7 %collective-permute-start.32 = (bf16[384,384]{1,0:T(8,128)(2,1)S(1)}, bf16[384,384]{1,0:T(8,128)(2,1)S(1)}, u32[]{:S(2)}, u32[]{:S(2)}) collective-permute-start(bf16[384,384]{1,0:T(8,128)(2,1)S(1)} %get-tuple-element.69), channel_id=1, source_target_pairs={{0,16},{8,24},{16,0},{24,8},{1,17},{9,25},{17,1},{25,9},{2,18},{10... | collective-permute-start | bytes 884744 | tf_op jit(solution)/shard_map/ppermute | solution.py:714
  113.9 12.7 %collective-permute-start.31 = (bf16[384,384]{1,0:T(8,128)(2,1)S(1)}, bf16[384,384]{1,0:T(8,128)(2,1)S(1)}, u32[]{:S(2)}, u32[]{:S(2)}) collective-permute-start(bf16[384,384]{1,0:T(8,128)(2,1)S(1)} %get-tuple-element.67), channel_id=1, source_target_pairs={{0,8},{8,0},{16,24},{24,16},{1,9},{9,1},{17,25},{25,17},{2,10},{10... | collective-permute-start | bytes 884744 | tf_op jit(solution)/shard_map/ppermute | solution.py:714
  127.8 6.9 %collective-permute-start.36 = (bf16[96,384]{1,0:T(8,128)(2,1)S(1)}, bf16[96,384]{1,0:T(8,128)(2,1)S(1)}, u32[]{:S(2)}, u32[]{:S(2)}) collective-permute-start(bf16[96,384]{1,0:T(8,128)(2,1)S(1)} %get-tuple-element.74), channel_id=1, source_target_pairs={{0,6},{1,7},{2,4},{3,5},{4,2},{5,3},{6,0},{7,1},{8,14},{9,15},{10,... | collective-permute-start | bytes 221192 | tf_op jit(solution)/shard_map/ppermute | solution.py:714
  131.6 6.1 %collective-permute-start.35 = (bf16[96,384]{1,0:T(8,128)(2,1)S(1)}, bf16[96,384]{1,0:T(8,128)(2,1)S(1)}, u32[]{:S(2)}, u32[]{:S(2)}) collective-permute-start(bf16[96,384]{1,0:T(8,128)(2,1)S(1)} %get-tuple-element.75), channel_id=1, source_target_pairs={{0,4},{1,5},{2,6},{3,7},{4,0},{5,1},{6,2},{7,3},{8,12},{9,13},{10,... | collective-permute-start | bytes 221192 | tf_op jit(solution)/shard_map/ppermute | solution.py:714
  131.6 6.1 %collective-permute-start.34 = (bf16[96,384]{1,0:T(8,128)(2,1)S(1)}, bf16[96,384]{1,0:T(8,128)(2,1)S(1)}, u32[]{:S(2)}, u32[]{:S(2)}) collective-permute-start(bf16[96,384]{1,0:T(8,128)(2,1)S(1)} %get-tuple-element.73), channel_id=1, source_target_pairs={{0,2},{1,3},{2,0},{3,1},{4,6},{5,7},{6,4},{7,5},{8,10},{9,11},{10,... | collective-permute-start | bytes 221192 | tf_op jit(solution)/shard_map/ppermute | solution.py:714
  137.7 7.9 %collective-permute-start.39 = (bf16[96,384]{1,0:T(8,128)(2,1)S(1)}, bf16[96,384]{1,0:T(8,128)(2,1)S(1)}, u32[]{:S(2)}, u32[]{:S(2)}) collective-permute-start(bf16[96,384]{1,0:T(8,128)(2,1)S(1)} %fusion.12), channel_id=1, source_target_pairs={{0,6},{1,7},{2,4},{3,5},{4,2},{5,3},{6,0},{7,1},{8,14},{9,15},{10,... | collective-permute-start | bytes 221192 | tf_op jit(solution)/shard_map/ppermute | solution.py:714
  140.5 10.2 %collective-permute-start.38 = (bf16[96,384]{1,0:T(8,128)(2,1)S(1)}, bf16[96,384]{1,0:T(8,128)(2,1)S(1)}, u32[]{:S(2)}, u32[]{:S(2)}) collective-permute-start(bf16[96,384]{1,0:T(8,128)(2,1)S(1)} %fusion.12), channel_id=1, source_target_pairs={{0,4},{1,5},{2,6},{3,7},{4,0},{5,1},{6,2},{7,3},{8,12},{9,13},{10,... | collective-permute-start | bytes 221192 | tf_op jit(solution)/shard_map/ppermute | solution.py:714
  140.5 10.3 %collective-permute-start.37 = (bf16[96,384]{1,0:T(8,128)(2,1)S(1)}, bf16[96,384]{1,0:T(8,128)(2,1)S(1)}, u32[]{:S(2)}, u32[]{:S(2)}) collective-permute-start(bf16[96,384]{1,0:T(8,128)(2,1)S(1)} %fusion.12), channel_id=1, source_target_pairs={{0,2},{1,3},{2,0},{3,1},{4,6},{5,7},{6,4},{7,5},{8,10},{9,11},{10,... | collective-permute-start | bytes 221192 | tf_op jit(solution)/shard_map/ppermute | solution.py:714
  142.9 9.6 %collective-permute-start.19 = (bf16[112,384]{1,0:T(8,128)(2,1)S(1)}, bf16[112,384]{1,0:T(8,128)(2,1)S(1)}, u32[]{:S(2)}, u32[]{:S(2)}) collective-permute-start(bf16[112,384]{1,0:T(8,128)(2,1)S(1)} %get-tuple-element.83), channel_id=1, source_target_pairs={{0,6},{1,7},{2,4},{3,5},{4,2},{5,3},{6,0},{7,1},{8,14},{9,15},{10,... | collective-permute-start | bytes 258056 | tf_op jit(solution)/shard_map/ppermute | solution.py:714
  145.6 9.1 %collective-permute-start.18 = (bf16[112,384]{1,0:T(8,128)(2,1)S(1)}, bf16[112,384]{1,0:T(8,128)(2,1)S(1)}, u32[]{:S(2)}, u32[]{:S(2)}) collective-permute-start(bf16[112,384]{1,0:T(8,128)(2,1)S(1)} %get-tuple-element.82), channel_id=1, source_target_pairs={{0,4},{1,5},{2,6},{3,7},{4,0},{5,1},{6,2},{7,3},{8,12},{9,13},{10,... | collective-permute-start | bytes 258056 | tf_op jit(solution)/shard_map/ppermute | solution.py:714
  150.8 9.3 %collective-permute-start.40 = (bf16[4,96,384]{2,1,0:T(8,128)(2,1)S(1)}, bf16[4,96,384]{2,1,0:T(8,128)(2,1)S(1)}, u32[]{:S(2)}, u32[]{:S(2)}) collective-permute-start(bf16[4,96,384]{2,1,0:T(8,128)(2,1)S(1)} %get-tuple-element.77), channel_id=1, source_target_pairs={{0,16},{8,24},{16,0},{24,8},{1,17},{9,25},{17,1},{25,9},{2,18},{10... | collective-permute-start | bytes 884744 | tf_op jit(solution)/shard_map/ppermute | solution.py:714
  155.6 5.8 %collective-permute-start.22 = (bf16[48,384]{1,0:T(8,128)(2,1)S(1)}, bf16[48,384]{1,0:T(8,128)(2,1)S(1)}, u32[]{:S(2)}, u32[]{:S(2)}) collective-permute-start(bf16[48,384]{1,0:T(8,128)(2,1)S(1)} %fusion.18), channel_id=1, source_target_pairs={{0,6},{1,7},{2,4},{3,5},{4,2},{5,3},{6,0},{7,1},{8,14},{9,15},{10,... | collective-permute-start | bytes 110600 | tf_op jit(solution)/shard_map/ppermute | solution.py:714
  160.2 10.9 %collective-permute-start.41 = (bf16[2,4,96,384]{3,2,1,0:T(8,128)(2,1)S(1)}, bf16[2,4,96,384]{3,2,1,0:T(8,128)(2,1)S(1)}, u32[]{:S(2)}, u32[]{:S(2)}) collective-permute-start(bf16[2,4,96,384]{3,2,1,0:T(8,128)(2,1)S(1)} %pad_maximum_fusion.1.ch0), channel_id=1, source_target_pairs={{0,1},{1,0},{2,3},{3,2},{4,5},{5,4},{6,7},{7,6},{8,9},{9,8},{10,11... | collective-permute-start | bytes 1769480 | tf_op jit(solution)/shard_map/ppermute | solution.py:714
  162.5 6.7 %collective-permute-start.25 = (bf16[4,48,384]{2,1,0:T(8,128)(2,1)S(1)}, bf16[4,48,384]{2,1,0:T(8,128)(2,1)S(1)}, u32[]{:S(2)}, u32[]{:S(2)}) collective-permute-start(bf16[4,48,384]{2,1,0:T(8,128)(2,1)S(1)} %get-tuple-element.94), channel_id=1, source_target_pairs={{0,24},{8,16},{16,8},{24,0},{1,25},{9,17},{17,9},{25,1},{2,26},{10... | collective-permute-start | bytes 442376 | tf_op jit(solution)/shard_map/ppermute | solution.py:714
  163.0 7.7 %collective-permute-start.24 = (bf16[4,48,384]{2,1,0:T(8,128)(2,1)S(1)}, bf16[4,48,384]{2,1,0:T(8,128)(2,1)S(1)}, u32[]{:S(2)}, u32[]{:S(2)}) collective-permute-start(bf16[4,48,384]{2,1,0:T(8,128)(2,1)S(1)} %get-tuple-element.94), channel_id=1, source_target_pairs={{0,16},{8,24},{16,0},{24,8},{1,17},{9,25},{17,1},{25,9},{2,18},{10... | collective-permute-start | bytes 442376 | tf_op jit(solution)/shard_map/ppermute | solution.py:714
  171.0 13.5 %collective-permute-start.26 = (bf16[4,4,48,384]{3,2,1,0:T(8,128)(2,1)S(1)}, bf16[4,4,48,384]{3,2,1,0:T(8,128)(2,1)S(1)}, u32[]{:S(2)}, u32[]{:S(2)}) collective-permute-start(bf16[4,4,48,384]{3,2,1,0:T(8,128)(2,1)S(1)} %pad_maximum_fusion.ch0), channel_id=1, source_target_pairs={{0,1},{1,0},{2,3},{3,2},{4,5},{5,4},{6,7},{7,6},{8,9},{9,8},{10,11... | collective-permute-start | bytes 1769480 | tf_op jit(solution)/shard_map/ppermute | solution.py:714
  181.0 10.2 %collective-permute-start.42 = (bf16[2,192,384]{2,1,0:T(8,128)(2,1)S(1)}, bf16[2,192,384]{2,1,0:T(8,128)(2,1)S(1)}, u32[]{:S(2)}, u32[]{:S(2)}) collective-permute-start(bf16[2,192,384]{2,1,0:T(8,128)(2,1)S(1)} %get-tuple-element.63), channel_id=1, source_target_pairs={{16,24},{17,25},{18,26},{19,27},{20,28},{21,29},{22,30},{23,31}} | collective-permute-start | bytes 884744 | tf_op jit(solution)/shard_map/ppermute | solution.py:821
  (25 other events, 238.3 us)

commit v3 on v2

--- a/solution.py
+++ b/solution.py
@@ -83,7 +83,7 @@
     return pltpu.CompilerParams(vmem_limit_bytes=mib * 1024 * 1024)
 
 
-def prep_kernel(count, s_ref, p_ref, m_ref, w_ref, wh_ref, mh_ref, mo_ref):
+def prep_kernel(count, s_ref, p_ref, w_ref, half_ref):
     for shard in range(count):
 
         @pl.when(s_ref[0] == shard)
@@ -92,27 +92,23 @@
                 for j in range(3):
                     src = pl.ds(frow + j, n, stride=stride)
                     w_ref[crow : crow + n, 128 * j : 128 * j + 128] = p_ref[src, :].astype(BF16)
-                    mo_ref[crow : crow + n, 128 * j : 128 * j + 128] = m_ref[src, :].astype(BF16)
-
-    half = wh_ref.shape[0]
-    mine = pl.ds(pl.multiple_of(s_ref[1] * half, half), half)
-    wh_ref[...] = w_ref[mine, :]
-    mh_ref[...] = mo_ref[mine, :]
-
-
-def prep(sidx, params, momentum, count):
+
+    half = half_ref.shape[0]
+    half_ref[...] = w_ref[pl.ds(pl.multiple_of(s_ref[1] * half, half), half), :]
+
+
+def prep(sidx, flat, count):
     rows = P_SIZE // count // D
-    out = jax.ShapeDtypeStruct((rows, D), BF16)
-    part = jax.ShapeDtypeStruct((rows // 2, D), BF16)
+    out = (jax.ShapeDtypeStruct((rows, D), BF16), jax.ShapeDtypeStruct((rows // 2, D), BF16))
     return pl.pallas_call(
         functools.partial(prep_kernel, count),
-        out_shape=(out, part, part),
-        in_specs=[sspec(), vspec(), vspec()],
-        out_specs=(vspec(),) * 3,
-        scratch_shapes=[pltpu.VMEM((rows, D), BF16)],
-        compiler_params=params_of(12),
+        out_shape=out,
+        in_specs=[sspec(), vspec()],
+        out_specs=(vspec(), vspec()),
+        compiler_params=params_of(4),
+        cost_estimate=pl.CostEstimate(flops=0, bytes_accessed=4_000_000, transcendentals=0),
         name="prep",
-    )(sidx, params, momentum)
+    )(sidx, flat)
 
 
 def layer_norm(h):
@@ -140,35 +136,47 @@
     return plan
 
 
-def load_weights_fast(s_ref, bufs, wts, sems, start):
+def load_weights_fast(s_ref, bufs, wts, own_ready):
     own, rx, ry, rda, rdb, px, py, pda, pdb = bufs
     me, core = s_ref[0], s_ref[1]
     half = own.shape[0] // 2
     quarter = half // 2
-    for q, (shard, h, r, n, block, br) in enumerate(gather_plan(4)):
-        dst = wts.at[block, br : br + n]
-        if not start:
-            pltpu.make_async_copy(own.at[0:n], dst, sems.at[q]).wait()
-            continue
-        for m in range(4):
-            for mine in (True, False):
-                if m == 0 and not mine:
-                    continue
-                cond = me == (shard ^ m)
-                if m > 0:
-                    cond = jnp.logical_and(cond, (core == h) if mine else (core != h))
-                if m == 0:
-                    src = own.at[h * half + r : h * half + r + n]
-                elif m < 3:
-                    src = ((rx, ry) if mine else (px, py))[m - 1].at[r : r + n]
-                else:
-                    pair = (rda, rdb) if mine else (pda, pdb)
-                    k = r // quarter
-                    src = pair[k].at[r - k * quarter : r - k * quarter + n]
-
-                @pl.when(cond)
-                def _(src=src, dst=dst, q=q):
-                    pltpu.make_async_copy(src, dst, sems.at[q]).start()
+    plan = gather_plan(4)
+
+    def move(src, row, n, block, brow):
+        size = 96 if n % 96 == 0 else 48
+
+        def chunk(i, carry):
+            a = pl.multiple_of(row + i * size, 16)
+            b = pl.multiple_of(brow + i * size, 16)
+            wts[block, pl.ds(b, size), :] = src[pl.ds(a, size), :]
+            return carry
+
+        lax.fori_loop(0, n // size, chunk, 0)
+
+    for shard in range(4):
+        for h in range(2):
+            pieces = [p for p in plan if p[0] == shard and p[1] == h]
+            for m in (1, 2, 3):
+                for mine in (True, False):
+
+                    @pl.when(jnp.logical_and(me == (shard ^ m), (core == h) if mine else (core != h)))
+                    def _(pieces=pieces, m=m, mine=mine):
+                        for _, _, r, n, block, br in pieces:
+                            if m < 3:
+                                move(((rx, ry) if mine else (px, py))[m - 1], r, n, block, br)
+                            else:
+                                k = r // quarter
+                                pair = (rda, rdb) if mine else (pda, pdb)
+                                move(pair[k], r - k * quarter, n, block, br)
+
+    own_ready()
+    for shard in range(4):
+
+        @pl.when(me == shard)
+        def _(shard=shard):
+            for _, h, r, n, block, br in [p for p in plan if p[0] == shard]:
+                move(own, h * half + r, n, block, br)
 
 
 def by_core(value, core):
@@ -177,16 +185,23 @@
     return jnp.where(core == 0, top, bottom), jnp.where(core == 0, bottom, top)
 
 
-def main_kernel(nbuf, fast, rows, s_ref, table, tok, cot, *refs):
+def main_kernel(nbuf, fast, rows, s_ref, table, tok_hbm, cot_hbm, *refs):
     bufs = refs[:nbuf]
     (blend, qkv, probs, amix_in, gafter, gmx, mods, gmod, silu, wqkv, gout, keep1, send1) = refs[nbuf : nbuf + 13]
-    wts, ao_s, aa_s, amix, minp, gmi, mo, sems = refs[nbuf + 13 :]
+    wts, ao_s, aa_s, amix, minp, gmi, mo, tok, cot, own, sems = refs[nbuf + 13 :]
     lat = rows // SEQ
+    get_tok = pltpu.make_async_copy(tok_hbm, tok, sems.at[1])
+    get_cot = pltpu.make_async_copy(cot_hbm, cot, sems.at[2])
+    first = pltpu.make_async_copy(bufs[0], own if fast else wts, sems.at[0])
+    first.start()
+    get_tok.start()
+    get_cot.start()
     if fast:
-        load_weights_fast(s_ref, bufs, wts, sems, True)
+        load_weights_fast(s_ref, (own,) + bufs[1:], wts, first.wait)
     else:
-        whole = pltpu.make_async_copy(bufs[0], wts, sems.at[0])
-        whole.start()
+        first.wait()
+    get_tok.wait()
+    get_cot.wait()
     nt = table.shape[0]
     lanes = lax.broadcasted_iota(jnp.int32, (16, nt), 1)
     rws = lax.broadcasted_iota(jnp.int32, (16, nt), 0)
@@ -196,10 +211,6 @@
     cond = mm(pick.astype(F32).astype(BF16), table[...])
     sc = (cond * (1.0 / (1.0 + jnp.exp(-cond)))).astype(BF16)
     silu[...] = sc.astype(F32)
-    if fast:
-        load_weights_fast(s_ref, bufs, wts, sems, False)
-    else:
-        whole.wait()
     for b in range(6):
         mods[b] = mm(sc, wts[b])[:8]
     for j in range(3):
@@ -316,11 +327,10 @@
         sd((4, D, D), F32),
         sd((4, D, D), BF16),
     )
-    nsem = len(gather_plan(4)) if fast else 1
     return pl.pallas_call(
         functools.partial(main_kernel, len(bufs), fast, rows),
         out_shape=outs,
-        in_specs=[sspec(), vspec(), vspec(), vspec()] + [aspec()] * len(bufs),
+        in_specs=[sspec(), vspec(), aspec(), aspec(), aspec()] + [vspec()] * (len(bufs) - 1),
         out_specs=(vspec(),) * len(outs),
         scratch_shapes=[
             pltpu.VMEM((NBLOCKS, D, D), BF16),
@@ -330,9 +340,12 @@
             pltpu.VMEM((rows, D), BF16),
             pltpu.VMEM((rows, D), F32),
             pltpu.VMEM((rows, D), F32),
-            pltpu.SemaphoreType.DMA((nsem,)),
+            pltpu.VMEM((rows, D), BF16),
+            pltpu.VMEM((rows, D), BF16),
+            pltpu.VMEM(bufs[0].shape if fast else (16, D), BF16),
+            pltpu.SemaphoreType.DMA((3,)),
         ],
-        compiler_params=params_of(34),
+        compiler_params=params_of(20),
         cost_estimate=pl.CostEstimate(flops=20_000_000_000, bytes_accessed=30_000_000, transcendentals=0),
         name="main",
     )(sidx, table, tokens, cotangent, *bufs)
@@ -372,7 +385,7 @@
         out_shape=jax.ShapeDtypeStruct((3, rows, D), BF16),
         in_specs=[vspec()] * 3,
         out_specs=vspec(),
-        compiler_params=params_of(12),
+        compiler_params=params_of(4),
         cost_estimate=pl.CostEstimate(flops=6_000_000_000, bytes_accessed=6_000_000, transcendentals=0),
         name="heads",
     )(qkv, probs, gmx)
@@ -418,7 +431,7 @@
         in_specs=[sspec()] + [vspec()] * 9,
         out_specs=(vspec(),) * 4,
         scratch_shapes=[pltpu.VMEM((KEPT_ROWS, D), F32)],
-        compiler_params=params_of(12),
+        compiler_params=params_of(6),
         cost_estimate=pl.CostEstimate(flops=6_000_000_000, bytes_accessed=6_000_000, transcendentals=0),
         name="input",
     )(sidx, tokens, gqkv, ai, gafter, mods, gmod1, silu, wqkv, gout)
@@ -638,7 +651,7 @@
             pltpu.VMEM((4, D, D), F32),
             pltpu.VMEM((3, 2 * kept[0].shape[0], 128), F32),
         ],
-        compiler_params=params_of(26),
+        compiler_params=params_of(14),
         cost_estimate=pl.CostEstimate(flops=8_000_000_000, bytes_accessed=12_000_000, transcendentals=0),
         name="ns_a",
     )(sidx, *tables, mom, *foreign, *kept, *chunks)
@@ -703,7 +716,7 @@
         in_specs=[sspec()] * 3 + [vspec()] * 7,
         out_specs=(vspec(),) * 3,
         scratch_shapes=[block4, block4, block4, block4],
-        compiler_params=params_of(38),
+        compiler_params=params_of(20),
         cost_estimate=pl.CostEstimate(flops=8_000_000_000, bytes_accessed=24_000_000, transcendentals=0),
         name="finish",
     )(sidx, *tables, par, mom, *chunks, upa, grda, tail)
@@ -771,7 +784,7 @@
     sidx = jnp.concatenate([jnp.stack([me, core, zed]), pick]).astype(jnp.int32)
 
     hop = swap(conditions, "fsdp", 1)
-    wc, wh, mh = prep(sidx, par, mom, 4)
+    wc, wh = prep(sidx, par, 4)
     table = jnp.concatenate([conditions, hop], axis=0)
     table, wh = lax.optimization_barrier((table, wh))
     hop = swap(table, "fsdp", 2)
@@ -785,6 +798,7 @@
     px, py = swap(rx, "rep", 1), swap(ry, "rep", 1)
     pda, pdb = swap(rda, "rep", 1), swap(rdb, "rep", 1)
     bufs = (wc, rx, ry, rda, rdb, px, py, pda, pdb)
+    _, mh = prep(sidx, mom, 4)
     fx0 = swap(mh, "fsdp", 1)
 
     tok2, cot2 = tokens.reshape(rows, D), cotangent.reshape(rows, D)

time: 203 us -> 200 us (0.985)
  Pallas kernels: 54.8 us -> 50.2 us
  local copies, waits for them, and re-layouts: 11.2 us -> 8.96 us
    pallas_call x1, Pallas kernels: 23.4 us -> 16.7 us  [main_call(): pl.pallas_call(functools.partial(main_kernel, len(bufs), fast, rows), out...]
    unnamed x35, local copies, waits for them, and re-layouts: 11 us -> 8.77 us
  transfers between devices with their start and end apart: 43 -> 43, of which waited for: 25 -> 24; matrix products, arithmetic and copies ran while one was open for 4% -> 4% of each run, Pallas kernels for 6% -> 7%
where the time goes in v3:
time: 200 us
  waiting for transfers between devices  86.4 us (43%)
  Pallas kernels  50.2 us (25%)
  starting transfers between devices  46.7 us (23%)
  local copies, waits for them, and re-layouts  8.96 us (4%)
  other arithmetic  6.34 us (3%)
    ppermute x42, waiting for transfers between devices, swap(): return lax.ppermute(x, axis, [(i, i ^ mask) for i in range(count)])  79.7 us
    ppermute x42, starting transfers between devices, swap(): return lax.ppermute(x, axis, [(i, i ^ mask) for i in range(count)])  43.1 us
    pallas_call x1, Pallas kernels, main_call(): pl.pallas_call(functools.partial(main_kernel, len(bufs), fast, rows), out...  16.7 us
    pallas_call x1, Pallas kernels, final_call(): pl.pallas_call(final_kernel, out_shape=(sd, sd, sd), in_specs=[sspec()] *...  11.8 us
    pallas_call x1, Pallas kernels, ns_a(): pl.pallas_call(ns_a_kernel, out_shape=(sd, sd, jax.ShapeDtypeStruct((2, 4...  9.68 us
    unnamed x35, local copies, waits for them, and re-layouts  8.77 us
    ppermute x1, waiting for transfers between devices, fast_body(): tail = lax.ppermute(tail, 'fsdp', [(2, 3)])  6.71 us
    pallas_call x1, Pallas kernels, heads_call(): pl.pallas_call(functools.partial(heads_kernel, rows), out_shape=jax.Shape...  4.85 us
  transfers between devices with their start and end apart: 43, of which 24 were waited for; matrix products, arithmetic and copies ran while one was open for 4% of the time, Pallas kernels for 7%

profile of v3, /device:TPU:4, one launch (start us, length us, event | category | flops | bytes accessed | tf_op | source)
XLA Modules:
  0.0 199.6 jit_solution(17206196110645860277)
XLA Ops:
  8.2 2.0 collective-permute-start.3
  10.1 14.3 %collective-permute-done.3 = bf16[4,384]{1,0:T(4,128)(2,1)S(1)} collective-permute-done((bf16[4,384]{1,0:T(4,128)(2,1)S(1)}, bf16[4,384]{1,0:T(4,128)(2,1)S(1)}, u32[]{:S(2)}, u32[]{:S(2)}) %collective-permute-start.3) | collective-permute-done | bytes 3104 | tf_op jit(solution)/shard_map/ppermute | solution.py:727
  27.4 2.1 %collective-permute-done.5 = bf16[16,384]{1,0:T(8,128)(2,1)S(1)} collective-permute-done((bf16[16,384]{1,0:T(8,128)(2,1)S(1)}, bf16[16,384]{1,0:T(8,128)(2,1)S(1)}, u32[]{:S(2)}, u32[]{:S(2)}) %collective-permute-start.5) | collective-permute-done | bytes 12320 | tf_op jit(solution)/shard_map/ppermute | solution.py:727
  29.5 2.7 %collective-permute-start.6 = (bf16[32,384]{1,0:T(8,128)(2,1)S(1)}, bf16[32,384]{1,0:T(8,128)(2,1)S(1)}, u32[]{:S(2)}, u32[]{:S(2)}) collective-permute-start(bf16[32,384]{1,0:T(8,128)(2,1)S(1)} %pad_maximum_fusion.7), channel_id=1, source_target_pairs={{0,4},{1,5},{2,6},{3,7},{4,0},{5,1},{6,2},{7,3},{8,12},{9,13},{10,... | collective-permute-start | bytes 73736 | tf_op jit(solution)/shard_map/ppermute | solution.py:727
  32.2 2.1 %collective-permute-done.6 = bf16[32,384]{1,0:T(8,128)(2,1)S(1)} collective-permute-done((bf16[32,384]{1,0:T(8,128)(2,1)S(1)}, bf16[32,384]{1,0:T(8,128)(2,1)S(1)}, u32[]{:S(2)}, u32[]{:S(2)}) %collective-permute-start.6) | collective-permute-done | bytes 24608 | tf_op jit(solution)/shard_map/ppermute | solution.py:727
  36.8 7.9 %collective-permute-done.7.refs_3_ = bf16[432,384]{1,0:T(8,128)(2,1)S(1)} collective-permute-done((bf16[432,384]{1,0:T(8,128)(2,1)S(1)}, bf16[432,384]{1,0:T(8,128)(2,1)S(1)}, u32[]{:S(2)}, u32[]{:S(2)}) %collective-permute-start.7) | collective-permute-done | bytes 331808 | tf_op jit(solution)/shard_map/ppermute | solution.py:727
  51.3 16.7 %main.1 = (bf16[512,384]{1,0:T(8,128)(2,1)}, bf16[3,512,384]{2,1,0:T(8,128)(2,1)S(1)}, f32[12,256,256]{2,1,0:T(8,128)S(1)}, bf16[512,384]{1,0:T(8,128)(2,1)S(1)}...) custom-call(s32[5]{0:T(128)S(1)} %pad_add_fusion.s_ref, ...), custom_call_target="tpu_custom_call" | custom-call | flops 20000000000 | bytes 30000000 | tf_op jit(solution)/shard_map/main/pallas_call | solution.py:330
  68.0 4.8 %heads.1.gqkv = bf16[3,512,384]{2,1,0:T(8,128)(2,1)S(1)} custom-call(bf16[3,512,384]{2,1,0:T(8,128)(2,1)S(1)} %get-tuple-element.44.qkv, f32[12,256,256]{2,1,0:T(8,128)S(1)} %get-tuple-element.45.probs, bf16[512,384]{1,0:T(8,128)(2,1)S(1)} %get-tuple-element.46.gmx), custom_call_target="tpu_custom_call" | custom-call | flops 6000000000 | bytes 6000000 | tf_op jit(solution)/shard_map/heads/pallas_call | solution.py:383
  72.9 3.2 %input.1 = (f32[512,384]{1,0:T(8,128)}, f32[4,192,384]{2,1,0:T(8,128)S(1)}, bf16[4,192,384]{2,1,0:T(8,128)(2,1)S(1)}, bf16[16,384]{1,0:T(8,128)(2,1)S(1)}) custom-call(s32[5]{0:T(128)S(1)} %pad_add_fusion.s_ref, bf16[512,384]{1,0:T(8,128)(2,1)S(1)} %bitcast.95, bf16[3,512,384]{2,1,0:T(8,128)(2,1)S(1)} %heads.1.gqkv, ...), custom_call_target="tpu_custom_call" | custom-call | flops 6000000000 | bytes 6000000 | tf_op jit(solution)/shard_map/input/pallas_call | solution.py:428
  76.6 2.3 %prep.3 = (bf16[1728,384]{1,0:T(8,128)(2,1)}, bf16[864,384]{1,0:T(8,128)(2,1)}) custom-call(s32[5]{0:T(128)S(1)} %pad_add_fusion.s_ref, f32[5184,128]{1,0:T(8,128)S(1)} %bitcast.90), custom_call_target="tpu_custom_call" | custom-call | bytes 4000000 | tf_op jit(solution)/shard_map/prep/pallas_call | solution.py:103
  84.9 12.1 %collective-permute-done.27.fx0 = bf16[864,384]{1,0:T(8,128)(2,1)} collective-permute-done((bf16[864,384]{1,0:T(8,128)(2,1)}, bf16[864,384]{1,0:T(8,128)(2,1)}, u32[]{:S(2)}, u32[]{:S(2)}) %collective-permute-start.27) | collective-permute-done | bytes 663584 | tf_op jit(solution)/shard_map/ppermute | solution.py:727
  97.0 4.4 %collective-permute-done.16 = bf16[208,384]{1,0:T(8,128)(2,1)S(1)} collective-permute-done((bf16[208,384]{1,0:T(8,128)(2,1)}, bf16[208,384]{1,0:T(8,128)(2,1)S(1)}, u32[]{:S(2)}, u32[]{:S(2)}) %collective-permute-start.16) | collective-permute-done | bytes 159776 | tf_op jit(solution)/shard_map/ppermute | solution.py:727
  104.2 1.9 fusion.2
  106.1 2.7 %collective-permute-start.33 = (bf16[384,384]{1,0:T(8,128)(2,1)S(1)}, bf16[384,384]{1,0:T(8,128)(2,1)S(1)}, u32[]{:S(2)}, u32[]{:S(2)}) collective-permute-start(bf16[384,384]{1,0:T(8,128)(2,1)S(1)} %get-tuple-element.68), channel_id=1, source_target_pairs={{0,24},{8,16},{16,8},{24,0},{1,25},{9,17},{17,9},{25,1},{2,26},{10... | collective-permute-start | bytes 884744 | tf_op jit(solution)/shard_map/ppermute | solution.py:727
  110.4 6.6 %collective-permute-done.33 = bf16[384,384]{1,0:T(8,128)(2,1)S(1)} collective-permute-done((bf16[384,384]{1,0:T(8,128)(2,1)S(1)}, bf16[384,384]{1,0:T(8,128)(2,1)S(1)}, u32[]{:S(2)}, u32[]{:S(2)}) %collective-permute-start.33) | collective-permute-done | bytes 294944 | tf_op jit(solution)/shard_map/ppermute | solution.py:727
  117.0 4.6 %collective-permute-done.32 = bf16[384,384]{1,0:T(8,128)(2,1)S(1)} collective-permute-done((bf16[384,384]{1,0:T(8,128)(2,1)S(1)}, bf16[384,384]{1,0:T(8,128)(2,1)S(1)}, u32[]{:S(2)}, u32[]{:S(2)}) %collective-permute-start.32) | collective-permute-done | bytes 294944 | tf_op jit(solution)/shard_map/ppermute | solution.py:727
  123.2 3.8 %collective-permute-start.36 = (bf16[96,384]{1,0:T(8,128)(2,1)S(1)}, bf16[96,384]{1,0:T(8,128)(2,1)S(1)}, u32[]{:S(2)}, u32[]{:S(2)}) collective-permute-start(bf16[96,384]{1,0:T(8,128)(2,1)S(1)} %get-tuple-element.74), channel_id=1, source_target_pairs={{0,6},{1,7},{2,4},{3,5},{4,2},{5,3},{6,0},{7,1},{8,14},{9,15},{10,... | collective-permute-start | bytes 221192 | tf_op jit(solution)/shard_map/ppermute | solution.py:727
  129.9 3.5 %collective-permute-done.35 = bf16[96,384]{1,0:T(8,128)(2,1)S(1)} collective-permute-done((bf16[96,384]{1,0:T(8,128)(2,1)S(1)}, bf16[96,384]{1,0:T(8,128)(2,1)S(1)}, u32[]{:S(2)}, u32[]{:S(2)}) %collective-permute-start.35) | collective-permute-done | bytes 73760 | tf_op jit(solution)/shard_map/ppermute | solution.py:727
  133.4 2.6 %collective-permute-start.39 = (bf16[96,384]{1,0:T(8,128)(2,1)S(1)}, bf16[96,384]{1,0:T(8,128)(2,1)S(1)}, u32[]{:S(2)}, u32[]{:S(2)}) collective-permute-start(bf16[96,384]{1,0:T(8,128)(2,1)S(1)} %fusion.12), channel_id=1, source_target_pairs={{0,6},{1,7},{2,4},{3,5},{4,2},{5,3},{6,0},{7,1},{8,14},{9,15},{10,... | collective-permute-start | bytes 221192 | tf_op jit(solution)/shard_map/ppermute | solution.py:727
  135.9 1.9 collective-permute-start.37
  137.8 2.6 %collective-permute-start.19 = (bf16[112,384]{1,0:T(8,128)(2,1)S(1)}, bf16[112,384]{1,0:T(8,128)(2,1)S(1)}, u32[]{:S(2)}, u32[]{:S(2)}) collective-permute-start(bf16[112,384]{1,0:T(8,128)(2,1)S(1)} %get-tuple-element.83), channel_id=1, source_target_pairs={{0,6},{1,7},{2,4},{3,5},{4,2},{5,3},{6,0},{7,1},{8,14},{9,15},{10,... | collective-permute-start | bytes 258056 | tf_op jit(solution)/shard_map/ppermute | solution.py:727
  140.4 1.8 collective-permute-start.18
  142.2 4.0 %collective-permute-done.38 = bf16[96,384]{1,0:T(8,128)(2,1)S(1)} collective-permute-done((bf16[96,384]{1,0:T(8,128)(2,1)S(1)}, bf16[96,384]{1,0:T(8,128)(2,1)S(1)}, u32[]{:S(2)}, u32[]{:S(2)}) %collective-permute-start.38) | collective-permute-done | bytes 73760 | tf_op jit(solution)/shard_map/ppermute | solution.py:727
  147.9 2.3 %collective-permute-done.18 = bf16[112,384]{1,0:T(8,128)(2,1)S(1)} collective-permute-done((bf16[112,384]{1,0:T(8,128)(2,1)S(1)}, bf16[112,384]{1,0:T(8,128)(2,1)S(1)}, u32[]{:S(2)}, u32[]{:S(2)}) %collective-permute-start.18) | collective-permute-done | bytes 86048 | tf_op jit(solution)/shard_map/ppermute | solution.py:727
  151.1 2.5 %collective-permute-start.22 = (bf16[48,384]{1,0:T(8,128)(2,1)S(1)}, bf16[48,384]{1,0:T(8,128)(2,1)S(1)}, u32[]{:S(2)}, u32[]{:S(2)}) collective-permute-start(bf16[48,384]{1,0:T(8,128)(2,1)S(1)} %fusion.18), channel_id=1, source_target_pairs={{0,6},{1,7},{2,4},{3,5},{4,2},{5,3},{6,0},{7,1},{8,14},{9,15},{10,... | collective-permute-start | bytes 110600 | tf_op jit(solution)/shard_map/ppermute | solution.py:727
  153.6 1.9 collective-permute-start.20
  158.9 2.6 %collective-permute-start.24 = (bf16[4,48,384]{2,1,0:T(8,128)(2,1)S(1)}, bf16[4,48,384]{2,1,0:T(8,128)(2,1)S(1)}, u32[]{:S(2)}, u32[]{:S(2)}) collective-permute-start(bf16[4,48,384]{2,1,0:T(8,128)(2,1)S(1)} %get-tuple-element.94), channel_id=1, source_target_pairs={{0,16},{8,24},{16,0},{24,8},{1,17},{9,25},{17,1},{25,9},{2,18},{10... | collective-permute-start | bytes 442376 | tf_op jit(solution)/shard_map/ppermute | solution.py:727
  162.1 3.9 %collective-permute-done.25 = bf16[4,48,384]{2,1,0:T(8,128)(2,1)S(1)} collective-permute-done((bf16[4,48,384]{2,1,0:T(8,128)(2,1)S(1)}, bf16[4,48,384]{2,1,0:T(8,128)(2,1)S(1)}, u32[]{:S(2)}, u32[]{:S(2)}) %collective-permute-start.25) | collective-permute-done | bytes 147488 | tf_op jit(solution)/shard_map/ppermute | solution.py:727
  167.8 9.7 %ns_a.1 = (f32[6,384,384]{2,1,0:T(8,128)S(1)}, f32[6,384,384]{2,1,0:T(8,128)S(1)}, bf16[2,192,384]{2,1,0:T(8,128)(2,1)S(1)}) custom-call(s32[5]{0:T(128)S(1)} %pad_add_fusion.s_ref, s32[36]{0:T(128)S(1)} %copy-done.11, f32[27]{0:T(128)S(1)} %copy-done.12, f32[5184,128]{1,0:T(8,128)S(1)} %bitcast.91, bf16[864,384]{1,0:T(8,128)(2,1)} %collective-permute-done.27.fx0, ...), custom_call_target="tpu_custom_call" | custom-call | flops 8000000000 | bytes 12000000 | tf_op jit(solution)/shard_map/ns_a/pallas_call | solution.py:644
  177.5 3.6 %collective-permute-start.42 = (bf16[2,192,384]{2,1,0:T(8,128)(2,1)S(1)}, bf16[2,192,384]{2,1,0:T(8,128)(2,1)S(1)}, u32[]{:S(2)}, u32[]{:S(2)}) collective-permute-start(bf16[2,192,384]{2,1,0:T(8,128)(2,1)S(1)} %get-tuple-element.63), channel_id=1, source_target_pairs={{16,24},{17,25},{18,26},{19,27},{20,28},{21,29},{22,30},{23,31}} | collective-permute-start | bytes 884744 | tf_op jit(solution)/shard_map/ppermute | solution.py:835
  181.1 6.7 %collective-permute-done.42.tail = bf16[2,192,384]{2,1,0:T(8,128)(2,1)S(1)} collective-permute-done((bf16[2,192,384]{2,1,0:T(8,128)(2,1)S(1)}, bf16[2,192,384]{2,1,0:T(8,128)(2,1)S(1)}, u32[]{:S(2)}, u32[]{:S(2)}) %collective-permute-start.42) | collective-permute-done | bytes 294944 | tf_op jit(solution)/shard_map/ppermute | solution.py:835
  187.8 11.8 %finish.1 = (f32[5184,128]{1,0:T(8,128)}, f32[5184,128]{1,0:T(8,128)}, f32[5184,128]{1,0:T(8,128)}) custom-call(s32[5]{0:T(128)S(1)} %pad_add_fusion.s_ref, s32[36]{0:T(128)S(1)} %copy-done.11, f32[27]{0:T(128)S(1)} %copy-done.12, f32[5184,128]{1,0:T(8,128)S(1)} %bitcast.89, f32[5184,128]{1,0:T(8,128)S(1)} %bitcast.92, ...), custom_call_target="tpu_custom_call" | custom-call | flops 8000000000 | bytes 24000000 | tf_op jit(solution)/shard_map/finish/pallas_call | solution.py:713
  (118 shorter events, 43.2 us)
Async XLA Ops:
  0.6 6.9 %collective-permute-start = (bf16[2,384]{1,0:T(2,128)(2,1)}, bf16[2,384]{1,0:T(2,128)(2,1)S(1)}, u32[]{:S(2)}, u32[]{:S(2)}) collective-permute-start(bf16[2,384]{1,0:T(2,128)(2,1)} %param.9), channel_id=1, source_target_pairs={{0,8},{8,0},{16,24},{24,16},{1,9},{9,1},{17,25},{25,17},{2,10},{10... | collective-permute-start | bytes 4616 | tf_op jit(solution)/shard_map/ppermute | solution.py:727
  7.5 26.9 %collective-permute-start.1 = (bf16[864,384]{1,0:T(8,128)(2,1)}, bf16[864,384]{1,0:T(8,128)(2,1)S(1)}, u32[]{:S(2)}, u32[]{:S(2)}) collective-permute-start(bf16[864,384]{1,0:T(8,128)(2,1)} %get-tuple-element.37), channel_id=1, source_target_pairs={{0,8},{8,0},{16,24},{24,16},{1,9},{9,1},{17,25},{25,17},{2,10},{10... | collective-permute-start | bytes 1990664 | tf_op jit(solution)/shard_map/ppermute | solution.py:727
  8.1 26.3 %collective-permute-start.2 = (bf16[864,384]{1,0:T(8,128)(2,1)}, bf16[864,384]{1,0:T(8,128)(2,1)S(1)}, u32[]{:S(2)}, u32[]{:S(2)}) collective-permute-start(bf16[864,384]{1,0:T(8,128)(2,1)} %get-tuple-element.37), channel_id=1, source_target_pairs={{0,16},{8,24},{16,0},{24,8},{1,17},{9,25},{17,1},{25,9},{2,18},{10... | collective-permute-start | bytes 1990664 | tf_op jit(solution)/shard_map/ppermute | solution.py:727
  8.2 16.3 %collective-permute-start.3 = (bf16[4,384]{1,0:T(4,128)(2,1)S(1)}, bf16[4,384]{1,0:T(4,128)(2,1)S(1)}, u32[]{:S(2)}, u32[]{:S(2)}) collective-permute-start(bf16[4,384]{1,0:T(4,128)(2,1)S(1)} %pad_maximum_fusion.10), channel_id=1, source_target_pairs={{0,16},{8,24},{16,0},{24,8},{1,17},{9,25},{17,1},{25,9},{2,18},{10... | collective-permute-start | bytes 9224 | tf_op jit(solution)/shard_map/ppermute | solution.py:727
  34.4 10.8 %collective-permute-start.9 = (bf16[864,384]{1,0:T(8,128)(2,1)S(1)}, bf16[864,384]{1,0:T(8,128)(2,1)S(1)}, u32[]{:S(2)}, u32[]{:S(2)}) collective-permute-start(bf16[864,384]{1,0:T(8,128)(2,1)S(1)} %collective-permute-done.1.refs_1_), channel_id=1, source_target_pairs={{0,1},{1,0},{2,3},{3,2},{4,5},{5,4},{6,7},{7,6},{8,9},{9,8},{10,11... | collective-permute-start | bytes 1990664 | tf_op jit(solution)/shard_map/ppermute | solution.py:727
  34.5 10.2 %collective-permute-start.7 = (bf16[432,384]{1,0:T(8,128)(2,1)S(1)}, bf16[432,384]{1,0:T(8,128)(2,1)S(1)}, u32[]{:S(2)}, u32[]{:S(2)}) collective-permute-start(bf16[432,384]{1,0:T(8,128)(2,1)S(1)} %slice.90), channel_id=1, source_target_pairs={{0,16},{8,24},{16,0},{24,8},{1,17},{9,25},{17,1},{25,9},{2,18},{10... | collective-permute-start | bytes 995336 | tf_op jit(solution)/shard_map/ppermute | solution.py:727
  35.0 10.3 %collective-permute-start.10 = (bf16[864,384]{1,0:T(8,128)(2,1)S(1)}, bf16[864,384]{1,0:T(8,128)(2,1)S(1)}, u32[]{:S(2)}, u32[]{:S(2)}) collective-permute-start(bf16[864,384]{1,0:T(8,128)(2,1)S(1)} %collective-permute-done.2.refs_2_), channel_id=1, source_target_pairs={{0,1},{1,0},{2,3},{3,2},{4,5},{5,4},{6,7},{7,6},{8,9},{9,8},{10,11... | collective-permute-start | bytes 1990664 | tf_op jit(solution)/shard_map/ppermute | solution.py:727
  35.2 10.1 %collective-permute-start.8 = (bf16[432,384]{1,0:T(8,128)(2,1)S(1)}, bf16[432,384]{1,0:T(8,128)(2,1)S(1)}, u32[]{:S(2)}, u32[]{:S(2)}) collective-permute-start(bf16[432,384]{1,0:T(8,128)(2,1)S(1)} %slice.91), channel_id=1, source_target_pairs={{0,8},{8,0},{16,24},{24,16},{1,9},{9,1},{17,25},{25,17},{2,10},{10... | collective-permute-start | bytes 995336 | tf_op jit(solution)/shard_map/ppermute | solution.py:727
  76.2 28.0 %collective-permute-start.30 = (bf16[4,384,384]{2,1,0:T(8,128)(2,1)}, bf16[4,384,384]{2,1,0:T(8,128)(2,1)}, u32[]{:S(2)}, u32[]{:S(2)}) collective-permute-start(bf16[4,384,384]{2,1,0:T(8,128)(2,1)} %get-tuple-element.60), channel_id=1, source_target_pairs={{0,1},{1,0},{2,3},{3,2},{4,5},{5,4},{6,7},{7,6},{8,9},{9,8},{10,11... | collective-permute-start | bytes 3538952 | tf_op jit(solution)/shard_map/ppermute | solution.py:727
  78.9 18.1 %collective-permute-start.27 = (bf16[864,384]{1,0:T(8,128)(2,1)}, bf16[864,384]{1,0:T(8,128)(2,1)}, u32[]{:S(2)}, u32[]{:S(2)}) collective-permute-start(bf16[864,384]{1,0:T(8,128)(2,1)} %get-tuple-element.58), channel_id=1, source_target_pairs={{0,8},{8,0},{16,24},{24,16},{1,9},{9,1},{17,25},{25,17},{2,10},{10... | collective-permute-start | bytes 1990664 | tf_op jit(solution)/shard_map/ppermute | solution.py:727
  81.5 20.0 %collective-permute-start.16 = (bf16[208,384]{1,0:T(8,128)(2,1)}, bf16[208,384]{1,0:T(8,128)(2,1)S(1)}, u32[]{:S(2)}, u32[]{:S(2)}) collective-permute-start(bf16[208,384]{1,0:T(8,128)(2,1)} %get-tuple-element.101), channel_id=1, source_target_pairs={{0,24},{8,16},{16,8},{24,0},{1,25},{9,17},{17,9},{25,1},{2,26},{10... | collective-permute-start | bytes 479240 | tf_op jit(solution)/shard_map/ppermute | solution.py:727
  82.9 18.5 %collective-permute-start.15 = (bf16[208,384]{1,0:T(8,128)(2,1)}, bf16[208,384]{1,0:T(8,128)(2,1)}, u32[]{:S(2)}, u32[]{:S(2)}) collective-permute-start(bf16[208,384]{1,0:T(8,128)(2,1)} %get-tuple-element.100), channel_id=1, source_target_pairs={{0,16},{8,24},{16,0},{24,8},{1,17},{9,25},{17,1},{25,9},{2,18},{10... | collective-permute-start | bytes 479240 | tf_op jit(solution)/shard_map/ppermute | solution.py:727
  83.3 19.7 %collective-permute-start.14 = (bf16[208,384]{1,0:T(8,128)(2,1)}, bf16[208,384]{1,0:T(8,128)(2,1)}, u32[]{:S(2)}, u32[]{:S(2)}) collective-permute-start(bf16[208,384]{1,0:T(8,128)(2,1)} %get-tuple-element.99), channel_id=1, source_target_pairs={{0,8},{8,0},{16,24},{24,16},{1,9},{9,1},{17,25},{25,17},{2,10},{10... | collective-permute-start | bytes 479240 | tf_op jit(solution)/shard_map/ppermute | solution.py:727
  97.0 70.8 %collective-permute-start.28 = (bf16[864,384]{1,0:T(8,128)(2,1)}, bf16[864,384]{1,0:T(8,128)(2,1)S(1)}, u32[]{:S(2)}, u32[]{:S(2)}) collective-permute-start(bf16[864,384]{1,0:T(8,128)(2,1)} %collective-permute-done.27.fx0), channel_id=1, source_target_pairs={{0,1},{1,0},{2,3},{3,2},{4,5},{5,4},{6,7},{7,6},{8,9},{9,8},{10,11... | collective-permute-start | bytes 1990664 | tf_op jit(solution)/shard_map/ppermute | solution.py:727
  106.1 10.9 %collective-permute-start.33 = (bf16[384,384]{1,0:T(8,128)(2,1)S(1)}, bf16[384,384]{1,0:T(8,128)(2,1)S(1)}, u32[]{:S(2)}, u32[]{:S(2)}) collective-permute-start(bf16[384,384]{1,0:T(8,128)(2,1)S(1)} %get-tuple-element.68), channel_id=1, source_target_pairs={{0,24},{8,16},{16,8},{24,0},{1,25},{9,17},{17,9},{25,1},{2,26},{10... | collective-permute-start | bytes 884744 | tf_op jit(solution)/shard_map/ppermute | solution.py:727
  108.7 12.8 %collective-permute-start.32 = (bf16[384,384]{1,0:T(8,128)(2,1)S(1)}, bf16[384,384]{1,0:T(8,128)(2,1)S(1)}, u32[]{:S(2)}, u32[]{:S(2)}) collective-permute-start(bf16[384,384]{1,0:T(8,128)(2,1)S(1)} %get-tuple-element.69), channel_id=1, source_target_pairs={{0,16},{8,24},{16,0},{24,8},{1,17},{9,25},{17,1},{25,9},{2,18},{10... | collective-permute-start | bytes 884744 | tf_op jit(solution)/shard_map/ppermute | solution.py:727
  109.2 12.6 %collective-permute-start.31 = (bf16[384,384]{1,0:T(8,128)(2,1)S(1)}, bf16[384,384]{1,0:T(8,128)(2,1)S(1)}, u32[]{:S(2)}, u32[]{:S(2)}) collective-permute-start(bf16[384,384]{1,0:T(8,128)(2,1)S(1)} %get-tuple-element.67), channel_id=1, source_target_pairs={{0,8},{8,0},{16,24},{24,16},{1,9},{9,1},{17,25},{25,17},{2,10},{10... | collective-permute-start | bytes 884744 | tf_op jit(solution)/shard_map/ppermute | solution.py:727
  123.2 6.7 %collective-permute-start.36 = (bf16[96,384]{1,0:T(8,128)(2,1)S(1)}, bf16[96,384]{1,0:T(8,128)(2,1)S(1)}, u32[]{:S(2)}, u32[]{:S(2)}) collective-permute-start(bf16[96,384]{1,0:T(8,128)(2,1)S(1)} %get-tuple-element.74), channel_id=1, source_target_pairs={{0,6},{1,7},{2,4},{3,5},{4,2},{5,3},{6,0},{7,1},{8,14},{9,15},{10,... | collective-permute-start | bytes 221192 | tf_op jit(solution)/shard_map/ppermute | solution.py:727
  127.0 6.3 %collective-permute-start.35 = (bf16[96,384]{1,0:T(8,128)(2,1)S(1)}, bf16[96,384]{1,0:T(8,128)(2,1)S(1)}, u32[]{:S(2)}, u32[]{:S(2)}) collective-permute-start(bf16[96,384]{1,0:T(8,128)(2,1)S(1)} %get-tuple-element.75), channel_id=1, source_target_pairs={{0,4},{1,5},{2,6},{3,7},{4,0},{5,1},{6,2},{7,3},{8,12},{9,13},{10,... | collective-permute-start | bytes 221192 | tf_op jit(solution)/shard_map/ppermute | solution.py:727
  127.0 6.3 %collective-permute-start.34 = (bf16[96,384]{1,0:T(8,128)(2,1)S(1)}, bf16[96,384]{1,0:T(8,128)(2,1)S(1)}, u32[]{:S(2)}, u32[]{:S(2)}) collective-permute-start(bf16[96,384]{1,0:T(8,128)(2,1)S(1)} %get-tuple-element.73), channel_id=1, source_target_pairs={{0,2},{1,3},{2,0},{3,1},{4,6},{5,7},{6,4},{7,5},{8,10},{9,11},{10,... | collective-permute-start | bytes 221192 | tf_op jit(solution)/shard_map/ppermute | solution.py:727
  133.4 7.1 %collective-permute-start.39 = (bf16[96,384]{1,0:T(8,128)(2,1)S(1)}, bf16[96,384]{1,0:T(8,128)(2,1)S(1)}, u32[]{:S(2)}, u32[]{:S(2)}) collective-permute-start(bf16[96,384]{1,0:T(8,128)(2,1)S(1)} %fusion.12), channel_id=1, source_target_pairs={{0,6},{1,7},{2,4},{3,5},{4,2},{5,3},{6,0},{7,1},{8,14},{9,15},{10,... | collective-permute-start | bytes 221192 | tf_op jit(solution)/shard_map/ppermute | solution.py:727
  135.9 10.3 %collective-permute-start.38 = (bf16[96,384]{1,0:T(8,128)(2,1)S(1)}, bf16[96,384]{1,0:T(8,128)(2,1)S(1)}, u32[]{:S(2)}, u32[]{:S(2)}) collective-permute-start(bf16[96,384]{1,0:T(8,128)(2,1)S(1)} %fusion.12), channel_id=1, source_target_pairs={{0,4},{1,5},{2,6},{3,7},{4,0},{5,1},{6,2},{7,3},{8,12},{9,13},{10,... | collective-permute-start | bytes 221192 | tf_op jit(solution)/shard_map/ppermute | solution.py:727
  135.9 10.3 %collective-permute-start.37 = (bf16[96,384]{1,0:T(8,128)(2,1)S(1)}, bf16[96,384]{1,0:T(8,128)(2,1)S(1)}, u32[]{:S(2)}, u32[]{:S(2)}) collective-permute-start(bf16[96,384]{1,0:T(8,128)(2,1)S(1)} %fusion.12), channel_id=1, source_target_pairs={{0,2},{1,3},{2,0},{3,1},{4,6},{5,7},{6,4},{7,5},{8,10},{9,11},{10,... | collective-permute-start | bytes 221192 | tf_op jit(solution)/shard_map/ppermute | solution.py:727
  137.8 10.0 %collective-permute-start.19 = (bf16[112,384]{1,0:T(8,128)(2,1)S(1)}, bf16[112,384]{1,0:T(8,128)(2,1)S(1)}, u32[]{:S(2)}, u32[]{:S(2)}) collective-permute-start(bf16[112,384]{1,0:T(8,128)(2,1)S(1)} %get-tuple-element.83), channel_id=1, source_target_pairs={{0,6},{1,7},{2,4},{3,5},{4,2},{5,3},{6,0},{7,1},{8,14},{9,15},{10,... | collective-permute-start | bytes 258056 | tf_op jit(solution)/shard_map/ppermute | solution.py:727
  140.4 9.8 %collective-permute-start.18 = (bf16[112,384]{1,0:T(8,128)(2,1)S(1)}, bf16[112,384]{1,0:T(8,128)(2,1)S(1)}, u32[]{:S(2)}, u32[]{:S(2)}) collective-permute-start(bf16[112,384]{1,0:T(8,128)(2,1)S(1)} %get-tuple-element.82), channel_id=1, source_target_pairs={{0,4},{1,5},{2,6},{3,7},{4,0},{5,1},{6,2},{7,3},{8,12},{9,13},{10,... | collective-permute-start | bytes 258056 | tf_op jit(solution)/shard_map/ppermute | solution.py:727
  146.3 9.3 %collective-permute-start.40 = (bf16[4,96,384]{2,1,0:T(8,128)(2,1)S(1)}, bf16[4,96,384]{2,1,0:T(8,128)(2,1)S(1)}, u32[]{:S(2)}, u32[]{:S(2)}) collective-permute-start(bf16[4,96,384]{2,1,0:T(8,128)(2,1)S(1)} %get-tuple-element.77), channel_id=1, source_target_pairs={{0,16},{8,24},{16,0},{24,8},{1,17},{9,25},{17,1},{25,9},{2,18},{10... | collective-permute-start | bytes 884744 | tf_op jit(solution)/shard_map/ppermute | solution.py:727
  155.6 12.2 %collective-permute-start.41 = (bf16[2,4,96,384]{3,2,1,0:T(8,128)(2,1)S(1)}, bf16[2,4,96,384]{3,2,1,0:T(8,128)(2,1)S(1)}, u32[]{:S(2)}, u32[]{:S(2)}) collective-permute-start(bf16[2,4,96,384]{3,2,1,0:T(8,128)(2,1)S(1)} %pad_maximum_fusion.1.ch0), channel_id=1, source_target_pairs={{0,1},{1,0},{2,3},{3,2},{4,5},{5,4},{6,7},{7,6},{8,9},{9,8},{10,11... | collective-permute-start | bytes 1769480 | tf_op jit(solution)/shard_map/ppermute | solution.py:727
  158.5 7.4 %collective-permute-start.25 = (bf16[4,48,384]{2,1,0:T(8,128)(2,1)S(1)}, bf16[4,48,384]{2,1,0:T(8,128)(2,1)S(1)}, u32[]{:S(2)}, u32[]{:S(2)}) collective-permute-start(bf16[4,48,384]{2,1,0:T(8,128)(2,1)S(1)} %get-tuple-element.94), channel_id=1, source_target_pairs={{0,24},{8,16},{16,8},{24,0},{1,25},{9,17},{17,9},{25,1},{2,26},{10... | collective-permute-start | bytes 442376 | tf_op jit(solution)/shard_map/ppermute | solution.py:727
  158.9 8.6 %collective-permute-start.24 = (bf16[4,48,384]{2,1,0:T(8,128)(2,1)S(1)}, bf16[4,48,384]{2,1,0:T(8,128)(2,1)S(1)}, u32[]{:S(2)}, u32[]{:S(2)}) collective-permute-start(bf16[4,48,384]{2,1,0:T(8,128)(2,1)S(1)} %get-tuple-element.94), channel_id=1, source_target_pairs={{0,16},{8,24},{16,0},{24,8},{1,17},{9,25},{17,1},{25,9},{2,18},{10... | collective-permute-start | bytes 442376 | tf_op jit(solution)/shard_map/ppermute | solution.py:727
  161.5 6.1 %collective-permute-start.23 = (bf16[4,48,384]{2,1,0:T(8,128)(2,1)S(1)}, bf16[4,48,384]{2,1,0:T(8,128)(2,1)S(1)}, u32[]{:S(2)}, u32[]{:S(2)}) collective-permute-start(bf16[4,48,384]{2,1,0:T(8,128)(2,1)S(1)} %get-tuple-element.94), channel_id=1, source_target_pairs={{0,8},{8,0},{16,24},{24,16},{1,9},{9,1},{17,25},{25,17},{2,10},{10... | collective-permute-start | bytes 442376 | tf_op jit(solution)/shard_map/ppermute | solution.py:727
  167.7 13.4 %collective-permute-start.26 = (bf16[4,4,48,384]{3,2,1,0:T(8,128)(2,1)S(1)}, bf16[4,4,48,384]{3,2,1,0:T(8,128)(2,1)S(1)}, u32[]{:S(2)}, u32[]{:S(2)}) collective-permute-start(bf16[4,4,48,384]{3,2,1,0:T(8,128)(2,1)S(1)} %pad_maximum_fusion.ch0), channel_id=1, source_target_pairs={{0,1},{1,0},{2,3},{3,2},{4,5},{5,4},{6,7},{7,6},{8,9},{9,8},{10,11... | collective-permute-start | bytes 1769480 | tf_op jit(solution)/shard_map/ppermute | solution.py:727
  177.5 10.3 %collective-permute-start.42 = (bf16[2,192,384]{2,1,0:T(8,128)(2,1)S(1)}, bf16[2,192,384]{2,1,0:T(8,128)(2,1)S(1)}, u32[]{:S(2)}, u32[]{:S(2)}) collective-permute-start(bf16[2,192,384]{2,1,0:T(8,128)(2,1)S(1)} %get-tuple-element.63), channel_id=1, source_target_pairs={{16,24},{17,25},{18,26},{19,27},{20,28},{21,29},{22,30},{23,31}} | collective-permute-start | bytes 884744 | tf_op jit(solution)/shard_map/ppermute | solution.py:835
  (25 other events, 179.3 us)

commit v4 on v3

--- a/solution.py
+++ b/solution.py
@@ -23,9 +23,9 @@
 COEFF_B = -4.775
 COEFF_C = 2.0315
 
+
 F32 = jnp.float32
 BF16 = jnp.bfloat16
-ANY = pl.ANY
 
 MATS = ((D, 6 * D, 0, True), (D, 3 * D, 6, True), (D, D, 9, True), (D, FF, 10, True), (FF, D, 14, False))
 NBLOCKS = 18
@@ -71,8 +71,12 @@
     return pl.BlockSpec(memory_space=pltpu.VMEM)
 
 
-def aspec():
-    return pl.BlockSpec(memory_space=ANY)
+def hspec():
+    return pl.BlockSpec(memory_space=pltpu.HBM)
+
+
+def in_hbm(x):
+    return pltpu.with_memory_space_constraint(x, pltpu.HBM)
 
 
 def sspec():
@@ -330,7 +334,7 @@
     return pl.pallas_call(
         functools.partial(main_kernel, len(bufs), fast, rows),
         out_shape=outs,
-        in_specs=[sspec(), vspec(), aspec(), aspec(), aspec()] + [vspec()] * (len(bufs) - 1),
+        in_specs=[sspec(), vspec(), hspec(), hspec(), hspec()] + [vspec()] * (len(bufs) - 1),
         out_specs=(vspec(),) * len(outs),
         scratch_shapes=[
             pltpu.VMEM((NBLOCKS, D, D), BF16),
@@ -348,7 +352,7 @@
         compiler_params=params_of(20),
         cost_estimate=pl.CostEstimate(flops=20_000_000_000, bytes_accessed=30_000_000, transcendentals=0),
         name="main",
-    )(sidx, table, tokens, cotangent, *bufs)
+    )(sidx, table, *(in_hbm(x) for x in (tokens, cotangent, bufs[0])), *bufs[1:])
 
 
 def heads_kernel(rows, qkv, probs, gmx, gqkv):

time: 200 us -> 197 us (0.985)
  local copies, waits for them, and re-layouts: 8.96 us -> 5.65 us
    unnamed x35 -> x31, local copies, waits for them, and re-layouts: 8.77 us -> 5.47 us
  transfers between devices with their start and end apart: 43 -> 43, of which waited for: 24 -> 25; matrix products, arithmetic and copies ran while one was open for 4% -> 4% of each run, Pallas kernels for 7% -> 7%
where the time goes in v4:
time: 197 us; the launch traced here: 196 us
  waiting for transfers between devices  86.4 us (44%)
  Pallas kernels  50.1 us (25%)
  starting transfers between devices  46.7 us (24%)
  other arithmetic  6.36 us (3%)
  local copies, waits for them, and re-layouts  5.65 us (3%)
    ppermute x42, waiting for transfers between devices, swap(): return lax.ppermute(x, axis, [(i, i ^ mask) for i in range(count)])  79.7 us
    ppermute x42, starting transfers between devices, swap(): return lax.ppermute(x, axis, [(i, i ^ mask) for i in range(count)])  43.2 us
    pallas_call x1, Pallas kernels, main_call(): pl.pallas_call(functools.partial(main_kernel, len(bufs), fast, rows), out...  16.6 us
    pallas_call x1, Pallas kernels, final_call(): pl.pallas_call(final_kernel, out_shape=(sd, sd, sd), in_specs=[sspec()] *...  11.8 us
    pallas_call x1, Pallas kernels, ns_a(): pl.pallas_call(ns_a_kernel, out_shape=(sd, sd, jax.ShapeDtypeStruct((2, 4...  9.67 us
    ppermute x1, waiting for transfers between devices, fast_body(): tail = lax.ppermute(tail, 'fsdp', [(2, 3)])  6.72 us
    unnamed x31, local copies, waits for them, and re-layouts  5.47 us
    pallas_call x1, Pallas kernels, heads_call(): pl.pallas_call(functools.partial(heads_kernel, rows), out_shape=jax.Shape...  4.87 us
  transfers between devices with their start and end apart: 43, of which 25 were waited for; matrix products, arithmetic and copies ran while one was open for 4% of the time, Pallas kernels for 7%

profile of v4, /device:TPU:4, one launch (start us, length us, event | category | flops | bytes accessed | tf_op | source)
XLA Modules:
  0.0 196.2 jit_solution(9038922031412511642)
XLA Ops:
  8.2 2.0 %collective-permute-start.3 = (bf16[4,384]{1,0:T(4,128)(2,1)S(1)}, bf16[4,384]{1,0:T(4,128)(2,1)S(1)}, u32[]{:S(2)}, u32[]{:S(2)}) collective-permute-start(bf16[4,384]{1,0:T(4,128)(2,1)S(1)} %pad_maximum_fusion.10), channel_id=1, source_target_pairs={{0,16},{8,24},{16,0},{24,8},{1,17},{9,25},{17,1},{25,9},{2,18},{10... | collective-permute-start | bytes 9224 | tf_op jit(solution)/shard_map/ppermute | solution.py:731
  10.1 14.3 %collective-permute-done.3 = bf16[4,384]{1,0:T(4,128)(2,1)S(1)} collective-permute-done((bf16[4,384]{1,0:T(4,128)(2,1)S(1)}, bf16[4,384]{1,0:T(4,128)(2,1)S(1)}, u32[]{:S(2)}, u32[]{:S(2)}) %collective-permute-start.3) | collective-permute-done | bytes 3104 | tf_op jit(solution)/shard_map/ppermute | solution.py:731
  27.4 2.1 %collective-permute-done.5 = bf16[16,384]{1,0:T(8,128)(2,1)S(1)} collective-permute-done((bf16[16,384]{1,0:T(8,128)(2,1)S(1)}, bf16[16,384]{1,0:T(8,128)(2,1)S(1)}, u32[]{:S(2)}, u32[]{:S(2)}) %collective-permute-start.5) | collective-permute-done | bytes 12320 | tf_op jit(solution)/shard_map/ppermute | solution.py:731
  29.5 2.7 %collective-permute-start.6 = (bf16[32,384]{1,0:T(8,128)(2,1)S(1)}, bf16[32,384]{1,0:T(8,128)(2,1)S(1)}, u32[]{:S(2)}, u32[]{:S(2)}) collective-permute-start(bf16[32,384]{1,0:T(8,128)(2,1)S(1)} %pad_maximum_fusion.7), channel_id=1, source_target_pairs={{0,4},{1,5},{2,6},{3,7},{4,0},{5,1},{6,2},{7,3},{8,12},{9,13},{10,... | collective-permute-start | bytes 73736 | tf_op jit(solution)/shard_map/ppermute | solution.py:731
  32.2 2.1 %collective-permute-done.6 = bf16[32,384]{1,0:T(8,128)(2,1)S(1)} collective-permute-done((bf16[32,384]{1,0:T(8,128)(2,1)S(1)}, bf16[32,384]{1,0:T(8,128)(2,1)S(1)}, u32[]{:S(2)}, u32[]{:S(2)}) %collective-permute-start.6) | collective-permute-done | bytes 24608 | tf_op jit(solution)/shard_map/ppermute | solution.py:731
  36.8 7.9 %collective-permute-done.7.refs_3_ = bf16[432,384]{1,0:T(8,128)(2,1)S(1)} collective-permute-done((bf16[432,384]{1,0:T(8,128)(2,1)S(1)}, bf16[432,384]{1,0:T(8,128)(2,1)S(1)}, u32[]{:S(2)}, u32[]{:S(2)}) %collective-permute-start.7) | collective-permute-done | bytes 331808 | tf_op jit(solution)/shard_map/ppermute | solution.py:731
  48.0 16.6 %main.1 = (bf16[512,384]{1,0:T(8,128)(2,1)}, bf16[3,512,384]{2,1,0:T(8,128)(2,1)S(1)}, f32[12,256,256]{2,1,0:T(8,128)S(1)}, bf16[512,384]{1,0:T(8,128)(2,1)S(1)}...) custom-call(s32[5]{0:T(128)S(1)} %pad_add_fusion.s_ref, ...), custom_call_target="tpu_custom_call" | custom-call | flops 20000000000 | bytes 30000000 | tf_op jit(solution)/shard_map/main/pallas_call | solution.py:334
  64.6 4.9 %heads.1.gqkv = bf16[3,512,384]{2,1,0:T(8,128)(2,1)S(1)} custom-call(bf16[3,512,384]{2,1,0:T(8,128)(2,1)S(1)} %get-tuple-element.44.qkv, f32[12,256,256]{2,1,0:T(8,128)S(1)} %get-tuple-element.45.probs, bf16[512,384]{1,0:T(8,128)(2,1)S(1)} %get-tuple-element.46.gmx), custom_call_target="tpu_custom_call" | custom-call | flops 6000000000 | bytes 6000000 | tf_op jit(solution)/shard_map/heads/pallas_call | solution.py:387
  69.5 3.2 %input.1 = (f32[512,384]{1,0:T(8,128)}, f32[4,192,384]{2,1,0:T(8,128)S(1)}, bf16[4,192,384]{2,1,0:T(8,128)(2,1)S(1)}, bf16[16,384]{1,0:T(8,128)(2,1)S(1)}) custom-call(s32[5]{0:T(128)S(1)} %pad_add_fusion.s_ref, bf16[512,384]{1,0:T(8,128)(2,1)S(1)} %bitcast.94, bf16[3,512,384]{2,1,0:T(8,128)(2,1)S(1)} %heads.1.gqkv, ...), custom_call_target="tpu_custom_call" | custom-call | flops 6000000000 | bytes 6000000 | tf_op jit(solution)/shard_map/input/pallas_call | solution.py:432
  73.2 2.3 %prep.3 = (bf16[1728,384]{1,0:T(8,128)(2,1)}, bf16[864,384]{1,0:T(8,128)(2,1)}) custom-call(s32[5]{0:T(128)S(1)} %pad_add_fusion.s_ref, f32[5184,128]{1,0:T(8,128)S(1)} %bitcast.90), custom_call_target="tpu_custom_call" | custom-call | bytes 4000000 | tf_op jit(solution)/shard_map/prep/pallas_call | solution.py:107
  81.5 12.1 %collective-permute-done.27.fx0 = bf16[864,384]{1,0:T(8,128)(2,1)} collective-permute-done((bf16[864,384]{1,0:T(8,128)(2,1)}, bf16[864,384]{1,0:T(8,128)(2,1)}, u32[]{:S(2)}, u32[]{:S(2)}) %collective-permute-start.27) | collective-permute-done | bytes 663584 | tf_op jit(solution)/shard_map/ppermute | solution.py:731
  93.6 4.4 %collective-permute-done.16 = bf16[208,384]{1,0:T(8,128)(2,1)S(1)} collective-permute-done((bf16[208,384]{1,0:T(8,128)(2,1)}, bf16[208,384]{1,0:T(8,128)(2,1)S(1)}, u32[]{:S(2)}, u32[]{:S(2)}) %collective-permute-start.16) | collective-permute-done | bytes 159776 | tf_op jit(solution)/shard_map/ppermute | solution.py:731
  100.8 1.9 fusion.2
  102.7 2.6 %collective-permute-start.33 = (bf16[384,384]{1,0:T(8,128)(2,1)S(1)}, bf16[384,384]{1,0:T(8,128)(2,1)S(1)}, u32[]{:S(2)}, u32[]{:S(2)}) collective-permute-start(bf16[384,384]{1,0:T(8,128)(2,1)S(1)} %get-tuple-element.68), channel_id=1, source_target_pairs={{0,24},{8,16},{16,8},{24,0},{1,25},{9,17},{17,9},{25,1},{2,26},{10... | collective-permute-start | bytes 884744 | tf_op jit(solution)/shard_map/ppermute | solution.py:731
  106.9 6.6 %collective-permute-done.33 = bf16[384,384]{1,0:T(8,128)(2,1)S(1)} collective-permute-done((bf16[384,384]{1,0:T(8,128)(2,1)S(1)}, bf16[384,384]{1,0:T(8,128)(2,1)S(1)}, u32[]{:S(2)}, u32[]{:S(2)}) %collective-permute-start.33) | collective-permute-done | bytes 294944 | tf_op jit(solution)/shard_map/ppermute | solution.py:731
  113.5 4.6 %collective-permute-done.32 = bf16[384,384]{1,0:T(8,128)(2,1)S(1)} collective-permute-done((bf16[384,384]{1,0:T(8,128)(2,1)S(1)}, bf16[384,384]{1,0:T(8,128)(2,1)S(1)}, u32[]{:S(2)}, u32[]{:S(2)}) %collective-permute-start.32) | collective-permute-done | bytes 294944 | tf_op jit(solution)/shard_map/ppermute | solution.py:731
  119.8 3.8 %collective-permute-start.36 = (bf16[96,384]{1,0:T(8,128)(2,1)S(1)}, bf16[96,384]{1,0:T(8,128)(2,1)S(1)}, u32[]{:S(2)}, u32[]{:S(2)}) collective-permute-start(bf16[96,384]{1,0:T(8,128)(2,1)S(1)} %get-tuple-element.74), channel_id=1, source_target_pairs={{0,6},{1,7},{2,4},{3,5},{4,2},{5,3},{6,0},{7,1},{8,14},{9,15},{10,... | collective-permute-start | bytes 221192 | tf_op jit(solution)/shard_map/ppermute | solution.py:731
  126.5 3.4 %collective-permute-done.35 = bf16[96,384]{1,0:T(8,128)(2,1)S(1)} collective-permute-done((bf16[96,384]{1,0:T(8,128)(2,1)S(1)}, bf16[96,384]{1,0:T(8,128)(2,1)S(1)}, u32[]{:S(2)}, u32[]{:S(2)}) %collective-permute-start.35) | collective-permute-done | bytes 73760 | tf_op jit(solution)/shard_map/ppermute | solution.py:731
  129.9 2.6 %collective-permute-start.39 = (bf16[96,384]{1,0:T(8,128)(2,1)S(1)}, bf16[96,384]{1,0:T(8,128)(2,1)S(1)}, u32[]{:S(2)}, u32[]{:S(2)}) collective-permute-start(bf16[96,384]{1,0:T(8,128)(2,1)S(1)} %fusion.12), channel_id=1, source_target_pairs={{0,6},{1,7},{2,4},{3,5},{4,2},{5,3},{6,0},{7,1},{8,14},{9,15},{10,... | collective-permute-start | bytes 221192 | tf_op jit(solution)/shard_map/ppermute | solution.py:731
  132.6 1.8 collective-permute-start.37
  134.4 2.6 %collective-permute-start.19 = (bf16[112,384]{1,0:T(8,128)(2,1)S(1)}, bf16[112,384]{1,0:T(8,128)(2,1)S(1)}, u32[]{:S(2)}, u32[]{:S(2)}) collective-permute-start(bf16[112,384]{1,0:T(8,128)(2,1)S(1)} %get-tuple-element.83), channel_id=1, source_target_pairs={{0,6},{1,7},{2,4},{3,5},{4,2},{5,3},{6,0},{7,1},{8,14},{9,15},{10,... | collective-permute-start | bytes 258056 | tf_op jit(solution)/shard_map/ppermute | solution.py:731
  137.0 1.8 collective-permute-start.18
  138.8 4.0 %collective-permute-done.38 = bf16[96,384]{1,0:T(8,128)(2,1)S(1)} collective-permute-done((bf16[96,384]{1,0:T(8,128)(2,1)S(1)}, bf16[96,384]{1,0:T(8,128)(2,1)S(1)}, u32[]{:S(2)}, u32[]{:S(2)}) %collective-permute-start.38) | collective-permute-done | bytes 73760 | tf_op jit(solution)/shard_map/ppermute | solution.py:731
  144.5 2.3 %collective-permute-done.18 = bf16[112,384]{1,0:T(8,128)(2,1)S(1)} collective-permute-done((bf16[112,384]{1,0:T(8,128)(2,1)S(1)}, bf16[112,384]{1,0:T(8,128)(2,1)S(1)}, u32[]{:S(2)}, u32[]{:S(2)}) %collective-permute-start.18) | collective-permute-done | bytes 86048 | tf_op jit(solution)/shard_map/ppermute | solution.py:731
  147.7 2.5 %collective-permute-start.22 = (bf16[48,384]{1,0:T(8,128)(2,1)S(1)}, bf16[48,384]{1,0:T(8,128)(2,1)S(1)}, u32[]{:S(2)}, u32[]{:S(2)}) collective-permute-start(bf16[48,384]{1,0:T(8,128)(2,1)S(1)} %fusion.18), channel_id=1, source_target_pairs={{0,6},{1,7},{2,4},{3,5},{4,2},{5,3},{6,0},{7,1},{8,14},{9,15},{10,... | collective-permute-start | bytes 110600 | tf_op jit(solution)/shard_map/ppermute | solution.py:731
  150.2 1.9 collective-permute-start.20
  155.5 2.6 %collective-permute-start.24 = (bf16[4,48,384]{2,1,0:T(8,128)(2,1)S(1)}, bf16[4,48,384]{2,1,0:T(8,128)(2,1)S(1)}, u32[]{:S(2)}, u32[]{:S(2)}) collective-permute-start(bf16[4,48,384]{2,1,0:T(8,128)(2,1)S(1)} %get-tuple-element.94), channel_id=1, source_target_pairs={{0,16},{8,24},{16,0},{24,8},{1,17},{9,25},{17,1},{25,9},{2,18},{10... | collective-permute-start | bytes 442376 | tf_op jit(solution)/shard_map/ppermute | solution.py:731
  158.7 3.9 %collective-permute-done.25 = bf16[4,48,384]{2,1,0:T(8,128)(2,1)S(1)} collective-permute-done((bf16[4,48,384]{2,1,0:T(8,128)(2,1)S(1)}, bf16[4,48,384]{2,1,0:T(8,128)(2,1)S(1)}, u32[]{:S(2)}, u32[]{:S(2)}) %collective-permute-start.25) | collective-permute-done | bytes 147488 | tf_op jit(solution)/shard_map/ppermute | solution.py:731
  164.4 9.7 %ns_a.1 = (f32[6,384,384]{2,1,0:T(8,128)S(1)}, f32[6,384,384]{2,1,0:T(8,128)S(1)}, bf16[2,192,384]{2,1,0:T(8,128)(2,1)S(1)}) custom-call(s32[5]{0:T(128)S(1)} %pad_add_fusion.s_ref, s32[36]{0:T(128)S(1)} %copy-done.9, f32[27]{0:T(128)S(1)} %copy-done.10, f32[5184,128]{1,0:T(8,128)S(1)} %bitcast.91, bf16[864,384]{1,0:T(8,128)(2,1)} %collective-permute-done.27.fx0, ...), custom_call_target="tpu_custom_call" | custom-call | flops 8000000000 | bytes 12000000 | tf_op jit(solution)/shard_map/ns_a/pallas_call | solution.py:648
  174.1 3.6 %collective-permute-start.42 = (bf16[2,192,384]{2,1,0:T(8,128)(2,1)S(1)}, bf16[2,192,384]{2,1,0:T(8,128)(2,1)S(1)}, u32[]{:S(2)}, u32[]{:S(2)}) collective-permute-start(bf16[2,192,384]{2,1,0:T(8,128)(2,1)S(1)} %get-tuple-element.63), channel_id=1, source_target_pairs={{16,24},{17,25},{18,26},{19,27},{20,28},{21,29},{22,30},{23,31}} | collective-permute-start | bytes 884744 | tf_op jit(solution)/shard_map/ppermute | solution.py:839
  177.7 6.7 %collective-permute-done.42.tail = bf16[2,192,384]{2,1,0:T(8,128)(2,1)S(1)} collective-permute-done((bf16[2,192,384]{2,1,0:T(8,128)(2,1)S(1)}, bf16[2,192,384]{2,1,0:T(8,128)(2,1)S(1)}, u32[]{:S(2)}, u32[]{:S(2)}) %collective-permute-start.42) | collective-permute-done | bytes 294944 | tf_op jit(solution)/shard_map/ppermute | solution.py:839
  184.4 11.8 %finish.1 = (f32[5184,128]{1,0:T(8,128)}, f32[5184,128]{1,0:T(8,128)}, f32[5184,128]{1,0:T(8,128)}) custom-call(s32[5]{0:T(128)S(1)} %pad_add_fusion.s_ref, s32[36]{0:T(128)S(1)} %copy-done.9, f32[27]{0:T(128)S(1)} %copy-done.10, f32[5184,128]{1,0:T(8,128)S(1)} %bitcast.89, f32[5184,128]{1,0:T(8,128)S(1)} %bitcast.92, ...), custom_call_target="tpu_custom_call" | custom-call | flops 8000000000 | bytes 24000000 | tf_op jit(solution)/shard_map/finish/pallas_call | solution.py:717
  (114 shorter events, 40.0 us)
Async XLA Ops:
  0.6 6.9 %collective-permute-start = (bf16[2,384]{1,0:T(2,128)(2,1)}, bf16[2,384]{1,0:T(2,128)(2,1)S(1)}, u32[]{:S(2)}, u32[]{:S(2)}) collective-permute-start(bf16[2,384]{1,0:T(2,128)(2,1)} %param.9), channel_id=1, source_target_pairs={{0,8},{8,0},{16,24},{24,16},{1,9},{9,1},{17,25},{25,17},{2,10},{10... | collective-permute-start | bytes 4616 | tf_op jit(solution)/shard_map/ppermute | solution.py:731
  7.5 26.9 %collective-permute-start.1 = (bf16[864,384]{1,0:T(8,128)(2,1)}, bf16[864,384]{1,0:T(8,128)(2,1)S(1)}, u32[]{:S(2)}, u32[]{:S(2)}) collective-permute-start(bf16[864,384]{1,0:T(8,128)(2,1)} %get-tuple-element.37), channel_id=1, source_target_pairs={{0,8},{8,0},{16,24},{24,16},{1,9},{9,1},{17,25},{25,17},{2,10},{10... | collective-permute-start | bytes 1990664 | tf_op jit(solution)/shard_map/ppermute | solution.py:731
  8.1 26.3 %collective-permute-start.2 = (bf16[864,384]{1,0:T(8,128)(2,1)}, bf16[864,384]{1,0:T(8,128)(2,1)S(1)}, u32[]{:S(2)}, u32[]{:S(2)}) collective-permute-start(bf16[864,384]{1,0:T(8,128)(2,1)} %get-tuple-element.37), channel_id=1, source_target_pairs={{0,16},{8,24},{16,0},{24,8},{1,17},{9,25},{17,1},{25,9},{2,18},{10... | collective-permute-start | bytes 1990664 | tf_op jit(solution)/shard_map/ppermute | solution.py:731
  8.2 16.3 %collective-permute-start.3 = (bf16[4,384]{1,0:T(4,128)(2,1)S(1)}, bf16[4,384]{1,0:T(4,128)(2,1)S(1)}, u32[]{:S(2)}, u32[]{:S(2)}) collective-permute-start(bf16[4,384]{1,0:T(4,128)(2,1)S(1)} %pad_maximum_fusion.10), channel_id=1, source_target_pairs={{0,16},{8,24},{16,0},{24,8},{1,17},{9,25},{17,1},{25,9},{2,18},{10... | collective-permute-start | bytes 9224 | tf_op jit(solution)/shard_map/ppermute | solution.py:731
  34.4 10.8 %collective-permute-start.9 = (bf16[864,384]{1,0:T(8,128)(2,1)S(1)}, bf16[864,384]{1,0:T(8,128)(2,1)S(1)}, u32[]{:S(2)}, u32[]{:S(2)}) collective-permute-start(bf16[864,384]{1,0:T(8,128)(2,1)S(1)} %collective-permute-done.1.refs_1_), channel_id=1, source_target_pairs={{0,1},{1,0},{2,3},{3,2},{4,5},{5,4},{6,7},{7,6},{8,9},{9,8},{10,11... | collective-permute-start | bytes 1990664 | tf_op jit(solution)/shard_map/ppermute | solution.py:731
  34.5 10.2 %collective-permute-start.7 = (bf16[432,384]{1,0:T(8,128)(2,1)S(1)}, bf16[432,384]{1,0:T(8,128)(2,1)S(1)}, u32[]{:S(2)}, u32[]{:S(2)}) collective-permute-start(bf16[432,384]{1,0:T(8,128)(2,1)S(1)} %slice.90), channel_id=1, source_target_pairs={{0,16},{8,24},{16,0},{24,8},{1,17},{9,25},{17,1},{25,9},{2,18},{10... | collective-permute-start | bytes 995336 | tf_op jit(solution)/shard_map/ppermute | solution.py:731
  35.0 10.3 %collective-permute-start.10 = (bf16[864,384]{1,0:T(8,128)(2,1)S(1)}, bf16[864,384]{1,0:T(8,128)(2,1)S(1)}, u32[]{:S(2)}, u32[]{:S(2)}) collective-permute-start(bf16[864,384]{1,0:T(8,128)(2,1)S(1)} %collective-permute-done.2.refs_2_), channel_id=1, source_target_pairs={{0,1},{1,0},{2,3},{3,2},{4,5},{5,4},{6,7},{7,6},{8,9},{9,8},{10,11... | collective-permute-start | bytes 1990664 | tf_op jit(solution)/shard_map/ppermute | solution.py:731
  35.2 10.1 %collective-permute-start.8 = (bf16[432,384]{1,0:T(8,128)(2,1)S(1)}, bf16[432,384]{1,0:T(8,128)(2,1)S(1)}, u32[]{:S(2)}, u32[]{:S(2)}) collective-permute-start(bf16[432,384]{1,0:T(8,128)(2,1)S(1)} %slice.91), channel_id=1, source_target_pairs={{0,8},{8,0},{16,24},{24,16},{1,9},{9,1},{17,25},{25,17},{2,10},{10... | collective-permute-start | bytes 995336 | tf_op jit(solution)/shard_map/ppermute | solution.py:731
  72.8 28.0 %collective-permute-start.30 = (bf16[4,384,384]{2,1,0:T(8,128)(2,1)}, bf16[4,384,384]{2,1,0:T(8,128)(2,1)}, u32[]{:S(2)}, u32[]{:S(2)}) collective-permute-start(bf16[4,384,384]{2,1,0:T(8,128)(2,1)} %get-tuple-element.60), channel_id=1, source_target_pairs={{0,1},{1,0},{2,3},{3,2},{4,5},{5,4},{6,7},{7,6},{8,9},{9,8},{10,11... | collective-permute-start | bytes 3538952 | tf_op jit(solution)/shard_map/ppermute | solution.py:731
  75.5 18.1 %collective-permute-start.27 = (bf16[864,384]{1,0:T(8,128)(2,1)}, bf16[864,384]{1,0:T(8,128)(2,1)}, u32[]{:S(2)}, u32[]{:S(2)}) collective-permute-start(bf16[864,384]{1,0:T(8,128)(2,1)} %get-tuple-element.58), channel_id=1, source_target_pairs={{0,8},{8,0},{16,24},{24,16},{1,9},{9,1},{17,25},{25,17},{2,10},{10... | collective-permute-start | bytes 1990664 | tf_op jit(solution)/shard_map/ppermute | solution.py:731
  78.1 20.0 %collective-permute-start.16 = (bf16[208,384]{1,0:T(8,128)(2,1)}, bf16[208,384]{1,0:T(8,128)(2,1)S(1)}, u32[]{:S(2)}, u32[]{:S(2)}) collective-permute-start(bf16[208,384]{1,0:T(8,128)(2,1)} %get-tuple-element.101), channel_id=1, source_target_pairs={{0,24},{8,16},{16,8},{24,0},{1,25},{9,17},{17,9},{25,1},{2,26},{10... | collective-permute-start | bytes 479240 | tf_op jit(solution)/shard_map/ppermute | solution.py:731
  79.6 18.5 %collective-permute-start.15 = (bf16[208,384]{1,0:T(8,128)(2,1)}, bf16[208,384]{1,0:T(8,128)(2,1)}, u32[]{:S(2)}, u32[]{:S(2)}) collective-permute-start(bf16[208,384]{1,0:T(8,128)(2,1)} %get-tuple-element.100), channel_id=1, source_target_pairs={{0,16},{8,24},{16,0},{24,8},{1,17},{9,25},{17,1},{25,9},{2,18},{10... | collective-permute-start | bytes 479240 | tf_op jit(solution)/shard_map/ppermute | solution.py:731
  79.9 19.7 %collective-permute-start.14 = (bf16[208,384]{1,0:T(8,128)(2,1)}, bf16[208,384]{1,0:T(8,128)(2,1)}, u32[]{:S(2)}, u32[]{:S(2)}) collective-permute-start(bf16[208,384]{1,0:T(8,128)(2,1)} %get-tuple-element.99), channel_id=1, source_target_pairs={{0,8},{8,0},{16,24},{24,16},{1,9},{9,1},{17,25},{25,17},{2,10},{10... | collective-permute-start | bytes 479240 | tf_op jit(solution)/shard_map/ppermute | solution.py:731
  93.6 70.8 %collective-permute-start.28 = (bf16[864,384]{1,0:T(8,128)(2,1)}, bf16[864,384]{1,0:T(8,128)(2,1)S(1)}, u32[]{:S(2)}, u32[]{:S(2)}) collective-permute-start(bf16[864,384]{1,0:T(8,128)(2,1)} %collective-permute-done.27.fx0), channel_id=1, source_target_pairs={{0,1},{1,0},{2,3},{3,2},{4,5},{5,4},{6,7},{7,6},{8,9},{9,8},{10,11... | collective-permute-start | bytes 1990664 | tf_op jit(solution)/shard_map/ppermute | solution.py:731
  102.7 10.9 %collective-permute-start.33 = (bf16[384,384]{1,0:T(8,128)(2,1)S(1)}, bf16[384,384]{1,0:T(8,128)(2,1)S(1)}, u32[]{:S(2)}, u32[]{:S(2)}) collective-permute-start(bf16[384,384]{1,0:T(8,128)(2,1)S(1)} %get-tuple-element.68), channel_id=1, source_target_pairs={{0,24},{8,16},{16,8},{24,0},{1,25},{9,17},{17,9},{25,1},{2,26},{10... | collective-permute-start | bytes 884744 | tf_op jit(solution)/shard_map/ppermute | solution.py:731
  105.3 12.8 %collective-permute-start.32 = (bf16[384,384]{1,0:T(8,128)(2,1)S(1)}, bf16[384,384]{1,0:T(8,128)(2,1)S(1)}, u32[]{:S(2)}, u32[]{:S(2)}) collective-permute-start(bf16[384,384]{1,0:T(8,128)(2,1)S(1)} %get-tuple-element.69), channel_id=1, source_target_pairs={{0,16},{8,24},{16,0},{24,8},{1,17},{9,25},{17,1},{25,9},{2,18},{10... | collective-permute-start | bytes 884744 | tf_op jit(solution)/shard_map/ppermute | solution.py:731
  105.8 12.6 %collective-permute-start.31 = (bf16[384,384]{1,0:T(8,128)(2,1)S(1)}, bf16[384,384]{1,0:T(8,128)(2,1)S(1)}, u32[]{:S(2)}, u32[]{:S(2)}) collective-permute-start(bf16[384,384]{1,0:T(8,128)(2,1)S(1)} %get-tuple-element.67), channel_id=1, source_target_pairs={{0,8},{8,0},{16,24},{24,16},{1,9},{9,1},{17,25},{25,17},{2,10},{10... | collective-permute-start | bytes 884744 | tf_op jit(solution)/shard_map/ppermute | solution.py:731
  119.8 6.7 %collective-permute-start.36 = (bf16[96,384]{1,0:T(8,128)(2,1)S(1)}, bf16[96,384]{1,0:T(8,128)(2,1)S(1)}, u32[]{:S(2)}, u32[]{:S(2)}) collective-permute-start(bf16[96,384]{1,0:T(8,128)(2,1)S(1)} %get-tuple-element.74), channel_id=1, source_target_pairs={{0,6},{1,7},{2,4},{3,5},{4,2},{5,3},{6,0},{7,1},{8,14},{9,15},{10,... | collective-permute-start | bytes 221192 | tf_op jit(solution)/shard_map/ppermute | solution.py:731
  123.6 6.3 %collective-permute-start.35 = (bf16[96,384]{1,0:T(8,128)(2,1)S(1)}, bf16[96,384]{1,0:T(8,128)(2,1)S(1)}, u32[]{:S(2)}, u32[]{:S(2)}) collective-permute-start(bf16[96,384]{1,0:T(8,128)(2,1)S(1)} %get-tuple-element.75), channel_id=1, source_target_pairs={{0,4},{1,5},{2,6},{3,7},{4,0},{5,1},{6,2},{7,3},{8,12},{9,13},{10,... | collective-permute-start | bytes 221192 | tf_op jit(solution)/shard_map/ppermute | solution.py:731
  123.6 6.3 %collective-permute-start.34 = (bf16[96,384]{1,0:T(8,128)(2,1)S(1)}, bf16[96,384]{1,0:T(8,128)(2,1)S(1)}, u32[]{:S(2)}, u32[]{:S(2)}) collective-permute-start(bf16[96,384]{1,0:T(8,128)(2,1)S(1)} %get-tuple-element.73), channel_id=1, source_target_pairs={{0,2},{1,3},{2,0},{3,1},{4,6},{5,7},{6,4},{7,5},{8,10},{9,11},{10,... | collective-permute-start | bytes 221192 | tf_op jit(solution)/shard_map/ppermute | solution.py:731
  129.9 7.1 %collective-permute-start.39 = (bf16[96,384]{1,0:T(8,128)(2,1)S(1)}, bf16[96,384]{1,0:T(8,128)(2,1)S(1)}, u32[]{:S(2)}, u32[]{:S(2)}) collective-permute-start(bf16[96,384]{1,0:T(8,128)(2,1)S(1)} %fusion.12), channel_id=1, source_target_pairs={{0,6},{1,7},{2,4},{3,5},{4,2},{5,3},{6,0},{7,1},{8,14},{9,15},{10,... | collective-permute-start | bytes 221192 | tf_op jit(solution)/shard_map/ppermute | solution.py:731
  132.6 10.2 %collective-permute-start.38 = (bf16[96,384]{1,0:T(8,128)(2,1)S(1)}, bf16[96,384]{1,0:T(8,128)(2,1)S(1)}, u32[]{:S(2)}, u32[]{:S(2)}) collective-permute-start(bf16[96,384]{1,0:T(8,128)(2,1)S(1)} %fusion.12), channel_id=1, source_target_pairs={{0,4},{1,5},{2,6},{3,7},{4,0},{5,1},{6,2},{7,3},{8,12},{9,13},{10,... | collective-permute-start | bytes 221192 | tf_op jit(solution)/shard_map/ppermute | solution.py:731
  132.6 10.2 %collective-permute-start.37 = (bf16[96,384]{1,0:T(8,128)(2,1)S(1)}, bf16[96,384]{1,0:T(8,128)(2,1)S(1)}, u32[]{:S(2)}, u32[]{:S(2)}) collective-permute-start(bf16[96,384]{1,0:T(8,128)(2,1)S(1)} %fusion.12), channel_id=1, source_target_pairs={{0,2},{1,3},{2,0},{3,1},{4,6},{5,7},{6,4},{7,5},{8,10},{9,11},{10,... | collective-permute-start | bytes 221192 | tf_op jit(solution)/shard_map/ppermute | solution.py:731
  134.4 10.1 %collective-permute-start.19 = (bf16[112,384]{1,0:T(8,128)(2,1)S(1)}, bf16[112,384]{1,0:T(8,128)(2,1)S(1)}, u32[]{:S(2)}, u32[]{:S(2)}) collective-permute-start(bf16[112,384]{1,0:T(8,128)(2,1)S(1)} %get-tuple-element.83), channel_id=1, source_target_pairs={{0,6},{1,7},{2,4},{3,5},{4,2},{5,3},{6,0},{7,1},{8,14},{9,15},{10,... | collective-permute-start | bytes 258056 | tf_op jit(solution)/shard_map/ppermute | solution.py:731
  137.0 9.7 %collective-permute-start.18 = (bf16[112,384]{1,0:T(8,128)(2,1)S(1)}, bf16[112,384]{1,0:T(8,128)(2,1)S(1)}, u32[]{:S(2)}, u32[]{:S(2)}) collective-permute-start(bf16[112,384]{1,0:T(8,128)(2,1)S(1)} %get-tuple-element.82), channel_id=1, source_target_pairs={{0,4},{1,5},{2,6},{3,7},{4,0},{5,1},{6,2},{7,3},{8,12},{9,13},{10,... | collective-permute-start | bytes 258056 | tf_op jit(solution)/shard_map/ppermute | solution.py:731
  142.9 9.3 %collective-permute-start.40 = (bf16[4,96,384]{2,1,0:T(8,128)(2,1)S(1)}, bf16[4,96,384]{2,1,0:T(8,128)(2,1)S(1)}, u32[]{:S(2)}, u32[]{:S(2)}) collective-permute-start(bf16[4,96,384]{2,1,0:T(8,128)(2,1)S(1)} %get-tuple-element.77), channel_id=1, source_target_pairs={{0,16},{8,24},{16,0},{24,8},{1,17},{9,25},{17,1},{25,9},{2,18},{10... | collective-permute-start | bytes 884744 | tf_op jit(solution)/shard_map/ppermute | solution.py:731
  152.2 12.2 %collective-permute-start.41 = (bf16[2,4,96,384]{3,2,1,0:T(8,128)(2,1)S(1)}, bf16[2,4,96,384]{3,2,1,0:T(8,128)(2,1)S(1)}, u32[]{:S(2)}, u32[]{:S(2)}) collective-permute-start(bf16[2,4,96,384]{3,2,1,0:T(8,128)(2,1)S(1)} %pad_maximum_fusion.1.ch0), channel_id=1, source_target_pairs={{0,1},{1,0},{2,3},{3,2},{4,5},{5,4},{6,7},{7,6},{8,9},{9,8},{10,11... | collective-permute-start | bytes 1769480 | tf_op jit(solution)/shard_map/ppermute | solution.py:731
  155.1 7.5 %collective-permute-start.25 = (bf16[4,48,384]{2,1,0:T(8,128)(2,1)S(1)}, bf16[4,48,384]{2,1,0:T(8,128)(2,1)S(1)}, u32[]{:S(2)}, u32[]{:S(2)}) collective-permute-start(bf16[4,48,384]{2,1,0:T(8,128)(2,1)S(1)} %get-tuple-element.94), channel_id=1, source_target_pairs={{0,24},{8,16},{16,8},{24,0},{1,25},{9,17},{17,9},{25,1},{2,26},{10... | collective-permute-start | bytes 442376 | tf_op jit(solution)/shard_map/ppermute | solution.py:731
  155.5 8.6 %collective-permute-start.24 = (bf16[4,48,384]{2,1,0:T(8,128)(2,1)S(1)}, bf16[4,48,384]{2,1,0:T(8,128)(2,1)S(1)}, u32[]{:S(2)}, u32[]{:S(2)}) collective-permute-start(bf16[4,48,384]{2,1,0:T(8,128)(2,1)S(1)} %get-tuple-element.94), channel_id=1, source_target_pairs={{0,16},{8,24},{16,0},{24,8},{1,17},{9,25},{17,1},{25,9},{2,18},{10... | collective-permute-start | bytes 442376 | tf_op jit(solution)/shard_map/ppermute | solution.py:731
  158.1 6.1 %collective-permute-start.23 = (bf16[4,48,384]{2,1,0:T(8,128)(2,1)S(1)}, bf16[4,48,384]{2,1,0:T(8,128)(2,1)S(1)}, u32[]{:S(2)}, u32[]{:S(2)}) collective-permute-start(bf16[4,48,384]{2,1,0:T(8,128)(2,1)S(1)} %get-tuple-element.94), channel_id=1, source_target_pairs={{0,8},{8,0},{16,24},{24,16},{1,9},{9,1},{17,25},{25,17},{2,10},{10... | collective-permute-start | bytes 442376 | tf_op jit(solution)/shard_map/ppermute | solution.py:731
  164.3 13.4 %collective-permute-start.26 = (bf16[4,4,48,384]{3,2,1,0:T(8,128)(2,1)S(1)}, bf16[4,4,48,384]{3,2,1,0:T(8,128)(2,1)S(1)}, u32[]{:S(2)}, u32[]{:S(2)}) collective-permute-start(bf16[4,4,48,384]{3,2,1,0:T(8,128)(2,1)S(1)} %pad_maximum_fusion.ch0), channel_id=1, source_target_pairs={{0,1},{1,0},{2,3},{3,2},{4,5},{5,4},{6,7},{7,6},{8,9},{9,8},{10,11... | collective-permute-start | bytes 1769480 | tf_op jit(solution)/shard_map/ppermute | solution.py:731
  174.1 10.3 %collective-permute-start.42 = (bf16[2,192,384]{2,1,0:T(8,128)(2,1)S(1)}, bf16[2,192,384]{2,1,0:T(8,128)(2,1)S(1)}, u32[]{:S(2)}, u32[]{:S(2)}) collective-permute-start(bf16[2,192,384]{2,1,0:T(8,128)(2,1)S(1)} %get-tuple-element.63), channel_id=1, source_target_pairs={{16,24},{17,25},{18,26},{19,27},{20,28},{21,29},{22,30},{23,31}} | collective-permute-start | bytes 884744 | tf_op jit(solution)/shard_map/ppermute | solution.py:839
  (23 other events, 180.9 us)

commit v5 on v4

--- a/solution.py
+++ b/solution.py
@@ -87,7 +87,8 @@
     return pltpu.CompilerParams(vmem_limit_bytes=mib * 1024 * 1024)
 
 
-def prep_kernel(count, s_ref, p_ref, w_ref, half_ref):
+def prep_kernel(count, parts, s_ref, p_ref, *refs):
+    w_ref = refs[-1]
     for shard in range(count):
 
         @pl.when(s_ref[0] == shard)
@@ -97,18 +98,22 @@
                     src = pl.ds(frow + j, n, stride=stride)
                     w_ref[crow : crow + n, 128 * j : 128 * j + 128] = p_ref[src, :].astype(BF16)
 
-    half = half_ref.shape[0]
-    half_ref[...] = w_ref[pl.ds(pl.multiple_of(s_ref[1] * half, half), half), :]
-
-
-def prep(sidx, flat, count):
+    for i in range(parts):
+        n = refs[i].shape[0]
+        row = s_ref[1] * (n * parts) + i * n
+        refs[i][...] = w_ref[pl.ds(pl.multiple_of(row, n), n), :]
+
+
+def prep(sidx, flat, count, parts):
     rows = P_SIZE // count // D
-    out = (jax.ShapeDtypeStruct((rows, D), BF16), jax.ShapeDtypeStruct((rows // 2, D), BF16))
+    sd = jax.ShapeDtypeStruct
+    outs = (sd((rows // 2 // parts, D), BF16),) * parts if parts else (sd((rows, D), BF16),)
     return pl.pallas_call(
-        functools.partial(prep_kernel, count),
-        out_shape=out,
+        functools.partial(prep_kernel, count, parts),
+        out_shape=outs,
         in_specs=[sspec(), vspec()],
-        out_specs=(vspec(), vspec()),
+        out_specs=(vspec(),) * len(outs),
+        scratch_shapes=[pltpu.VMEM((rows, D), BF16)] if parts else [],
         compiler_params=params_of(4),
         cost_estimate=pl.CostEstimate(flops=0, bytes_accessed=4_000_000, transcendentals=0),
         name="prep",
@@ -141,7 +146,7 @@
 
 
 def load_weights_fast(s_ref, bufs, wts, own_ready):
-    own, rx, ry, rda, rdb, px, py, pda, pdb = bufs
+    own = bufs[0]
     me, core = s_ref[0], s_ref[1]
     half = own.shape[0] // 2
     quarter = half // 2
@@ -167,12 +172,9 @@
                     @pl.when(jnp.logical_and(me == (shard ^ m), (core == h) if mine else (core != h)))
                     def _(pieces=pieces, m=m, mine=mine):
                         for _, _, r, n, block, br in pieces:
-                            if m < 3:
-                                move(((rx, ry) if mine else (px, py))[m - 1], r, n, block, br)
-                            else:
-                                k = r // quarter
-                                pair = (rda, rdb) if mine else (pda, pdb)
-                                move(pair[k], r - k * quarter, n, block, br)
+                            k = r // quarter
+                            src = bufs[(1 if mine else 7) + 2 * (m - 1) + k]
+                            move(src, r - k * quarter, n, block, br)
 
     own_ready()
     for shard in range(4):
@@ -274,8 +276,10 @@
             keep1[member ^ me, rs, :] = mine[96 * i : 96 * i + 96]
             send1[member ^ me, rs, :] = other[96 * i : 96 * i + 96].astype(BF16)
 
-    def mlp(j, carry):
-        wu, wd = wts[10 + j], wts[14 + j]
+    def mlp(jj, carry):
+        j = 2 * jj
+        wu = jnp.concatenate([wts[10 + j], wts[11 + j]], axis=1)
+        wd = jnp.concatenate([wts[14 + j], wts[15 + j]], axis=0)
         u = mm(minp[...], wu)
         c = math.sqrt(2.0 / math.pi)
         u2 = u * u
@@ -286,12 +290,15 @@
         mo[...] += mm(act, wd)
         gmo = gmx[...]
         gp = (mm(gmo, wd, 1, 1) * slope).astype(BF16)
-        put(mm(act, gmo, 0, 0), (3, 1), j)
-        put(mm(minp[...], gp, 0, 0), (2, 0), j)
+        gd = mm(act, gmo, 0, 0)
+        gu = mm(minp[...], gp, 0, 0)
+        for i in range(2):
+            put(gd[i * D : (i + 1) * D], (3, 1), j + i)
+            put(gu[:, i * D : (i + 1) * D], (2, 0), j + i)
         gmi[...] += mm(gp, wu, 1, 1)
         return carry
 
-    lax.fori_loop(0, FF // D, mlp, 0)
+    lax.fori_loop(0, FF // D // 2, mlp, 0)
 
     gmod[...] = jnp.zeros_like(gmod)
     for l in range(lat):
@@ -349,7 +356,7 @@
             pltpu.VMEM(bufs[0].shape if fast else (16, D), BF16),
             pltpu.SemaphoreType.DMA((3,)),
         ],
-        compiler_params=params_of(20),
+        compiler_params=params_of(30),
         cost_estimate=pl.CostEstimate(flops=20_000_000_000, bytes_accessed=30_000_000, transcendentals=0),
         name="main",
     )(sidx, table, *(in_hbm(x) for x in (tokens, cotangent, bufs[0])), *bufs[1:])
@@ -788,21 +795,24 @@
     sidx = jnp.concatenate([jnp.stack([me, core, zed]), pick]).astype(jnp.int32)
 
     hop = swap(conditions, "fsdp", 1)
-    wc, wh = prep(sidx, par, 4)
+    top, bottom = prep(sidx, par, 4, 2)
     table = jnp.concatenate([conditions, hop], axis=0)
-    table, wh = lax.optimization_barrier((table, wh))
+    table, top, bottom = lax.optimization_barrier((table, top, bottom))
     hop = swap(table, "fsdp", 2)
-    rx = swap(wh, "fsdp", 1)
-    ry = swap(wh, "fsdp", 2)
+    x0 = swap(top, "fsdp", 1)
+    y1 = swap(bottom, "fsdp", 2)
+    x1 = swap(bottom, "fsdp", 1)
+    y0 = swap(top, "fsdp", 2)
     table = jnp.concatenate([table, hop], axis=0)
-    table = more_rows(table, (("rep", 1), ("rep", 2), ("rep", 4)))
-    rx, ry, table = lax.optimization_barrier((rx, ry, table))
-    quarter = wh.shape[0] // 2
-    rda, rdb = swap(rx[:quarter], "fsdp", 2), swap(ry[quarter:], "fsdp", 1)
-    px, py = swap(rx, "rep", 1), swap(ry, "rep", 1)
-    pda, pdb = swap(rda, "rep", 1), swap(rdb, "rep", 1)
-    bufs = (wc, rx, ry, rda, rdb, px, py, pda, pdb)
-    _, mh = prep(sidx, mom, 4)
+    table = more_rows(table, (("rep", 1),))
+    table = more_rows(table, (("rep", 2), ("rep", 4)))
+    x0, y1, table = lax.optimization_barrier((x0, y1, table))
+    d0 = swap(x0, "fsdp", 2)
+    d1 = swap(y1, "fsdp", 1)
+    received = (x0, x1, y0, y1, d0, d1)
+    (wc,) = prep(sidx, par, 4, 0)
+    bufs = (wc,) + received + tuple(swap(r, "rep", 1) for r in received)
+    (mh,) = prep(sidx, mom, 4, 1)
     fx0 = swap(mh, "fsdp", 1)
 
     tok2, cot2 = tokens.reshape(rows, D), cotangent.reshape(rows, D)

time: 197 us -> 180 us (0.914)
  waiting for transfers between devices: 86.4 us -> 75.5 us
  starting transfers between devices: 46.7 us -> 42.8 us
    ppermute x42 -> x46, waiting for transfers between devices: 79.7 us -> 68.7 us  [swap(): return lax.ppermute(x, axis, [(i, i ^ mask) for i in range(count)])]
    ppermute x42 -> x46, starting transfers between devices: 43.2 us -> 40 us  [swap(): return lax.ppermute(x, axis, [(i, i ^ mask) for i in range(count)])]
    pallas_call x2 -> x3, Pallas kernels: 4.02 us -> 3.59 us  [prep(): pl.pallas_call(functools.partial(prep_kernel, count, parts), out_shape=ou...]
  transfers between devices with their start and end apart: 43 -> 47, of which waited for: 25 -> 24; matrix products, arithmetic and copies ran while one was open for 4% -> 4% of each run, Pallas kernels for 7% -> 7%
where the time goes in v5:
time: 180 us
  waiting for transfers between devices  75.5 us (42%)
  Pallas kernels  48.9 us (27%)
  starting transfers between devices  42.8 us (24%)
  other arithmetic  6.43 us (4%)
  local copies, waits for them, and re-layouts  5.19 us (3%)
    ppermute x46, waiting for transfers between devices, swap(): return lax.ppermute(x, axis, [(i, i ^ mask) for i in range(count)])  68.7 us
    ppermute x46, starting transfers between devices, swap(): return lax.ppermute(x, axis, [(i, i ^ mask) for i in range(count)])  40 us
    pallas_call x1, Pallas kernels, main_call(): pl.pallas_call(functools.partial(main_kernel, len(bufs), fast, rows), out...  16.1 us
    pallas_call x1, Pallas kernels, final_call(): pl.pallas_call(final_kernel, out_shape=(sd, sd, sd), in_specs=[sspec()] *...  11.7 us
    pallas_call x1, Pallas kernels, ns_a(): pl.pallas_call(ns_a_kernel, out_shape=(sd, sd, jax.ShapeDtypeStruct((2, 4...  9.53 us
    ppermute x1, waiting for transfers between devices, fast_body(): tail = lax.ppermute(tail, 'fsdp', [(2, 3)])  6.86 us
    unnamed x31, local copies, waits for them, and re-layouts  5.08 us
    pallas_call x1, Pallas kernels, heads_call(): pl.pallas_call(functools.partial(heads_kernel, rows), out_shape=jax.Shape...  4.85 us
  transfers between devices with their start and end apart: 47, of which 24 were waited for; matrix products, arithmetic and copies ran while one was open for 4% of the time, Pallas kernels for 7%

profile of v5, /device:TPU:4, one launch (start us, length us, event | category | flops | bytes accessed | tf_op | source)
XLA Modules:
  0.0 179.9 jit_solution(11078284035976920082)
XLA Ops:
  3.0 1.7 copy-done
  4.7 1.7 prep.3
  7.1 1.9 %collective-permute-start.2 = (bf16[432,384]{1,0:T(8,128)(2,1)}, bf16[432,384]{1,0:T(8,128)(2,1)}, u32[]{:S(2)}, u32[]{:S(2)}) collective-permute-start(bf16[432,384]{1,0:T(8,128)(2,1)} %get-tuple-element.39), channel_id=1, source_target_pairs={{0,16},{8,24},{16,0},{24,8},{1,17},{9,25},{17,1},{25,9},{2,18},{10... | collective-permute-start | bytes 995336 | tf_op jit(solution)/shard_map/ppermute | solution.py:738
  11.4 1.6 collective-permute-start.5
  13.0 2.1 %collective-permute-done.5 = bf16[16,384]{1,0:T(8,128)(2,1)S(1)} collective-permute-done((bf16[16,384]{1,0:T(8,128)(2,1)S(1)}, bf16[16,384]{1,0:T(8,128)(2,1)S(1)}, u32[]{:S(2)}, u32[]{:S(2)}) %collective-permute-start.5) | collective-permute-done | bytes 12320 | tf_op jit(solution)/shard_map/ppermute | solution.py:738
  15.2 2.7 %collective-permute-start.6 = (bf16[32,384]{1,0:T(8,128)(2,1)S(1)}, bf16[32,384]{1,0:T(8,128)(2,1)S(1)}, u32[]{:S(2)}, u32[]{:S(2)}) collective-permute-start(bf16[32,384]{1,0:T(8,128)(2,1)S(1)} %pad_maximum_fusion.7), channel_id=1, source_target_pairs={{0,4},{1,5},{2,6},{3,7},{4,0},{5,1},{6,2},{7,3},{8,12},{9,13},{10,... | collective-permute-start | bytes 73736 | tf_op jit(solution)/shard_map/ppermute | solution.py:738
  22.0 6.8 %collective-permute-done.7.refs_2_ = bf16[432,384]{1,0:T(8,128)(2,1)} collective-permute-done((bf16[432,384]{1,0:T(8,128)(2,1)}, bf16[432,384]{1,0:T(8,128)(2,1)}, u32[]{:S(2)}, u32[]{:S(2)}) %collective-permute-start.7) | collective-permute-done | bytes 331808 | tf_op jit(solution)/shard_map/ppermute | solution.py:738
  29.3 4.9 %collective-permute-done.9.refs_5_ = bf16[432,384]{1,0:T(8,128)(2,1)S(1)} collective-permute-done((bf16[432,384]{1,0:T(8,128)(2,1)S(1)}, bf16[432,384]{1,0:T(8,128)(2,1)S(1)}, u32[]{:S(2)}, u32[]{:S(2)}) %collective-permute-start.9) | collective-permute-done | bytes 331808 | tf_op jit(solution)/shard_map/ppermute | solution.py:738
  37.0 16.1 %main.1 = (bf16[512,384]{1,0:T(8,128)(2,1)}, bf16[3,512,384]{2,1,0:T(8,128)(2,1)S(1)}, f32[12,256,256]{2,1,0:T(8,128)S(1)}, bf16[512,384]{1,0:T(8,128)(2,1)S(1)}...) custom-call(s32[5]{0:T(128)S(1)} %pad_add_fusion.s_ref, ...), custom_call_target="tpu_custom_call" | custom-call | flops 20000000000 | bytes 30000000 | tf_op jit(solution)/shard_map/main/pallas_call | solution.py:341
  53.1 4.9 %heads.1.gqkv = bf16[3,512,384]{2,1,0:T(8,128)(2,1)S(1)} custom-call(bf16[3,512,384]{2,1,0:T(8,128)(2,1)S(1)} %get-tuple-element.45.qkv, f32[12,256,256]{2,1,0:T(8,128)S(1)} %get-tuple-element.46.probs, bf16[512,384]{1,0:T(8,128)(2,1)S(1)} %get-tuple-element.47.gmx), custom_call_target="tpu_custom_call" | custom-call | flops 6000000000 | bytes 6000000 | tf_op jit(solution)/shard_map/heads/pallas_call | solution.py:394
  58.0 3.2 %input.1 = (f32[512,384]{1,0:T(8,128)}, f32[4,192,384]{2,1,0:T(8,128)S(1)}, bf16[4,192,384]{2,1,0:T(8,128)(2,1)S(1)}, bf16[16,384]{1,0:T(8,128)(2,1)S(1)}) custom-call(s32[5]{0:T(128)S(1)} %pad_add_fusion.s_ref, bf16[512,384]{1,0:T(8,128)(2,1)S(1)} %bitcast.95, bf16[3,512,384]{2,1,0:T(8,128)(2,1)S(1)} %heads.1.gqkv, ...), custom_call_target="tpu_custom_call" | custom-call | flops 6000000000 | bytes 6000000 | tf_op jit(solution)/shard_map/input/pallas_call | solution.py:439
  69.4 11.3 %collective-permute-done.31.fx0 = bf16[864,384]{1,0:T(8,128)(2,1)} collective-permute-done((bf16[864,384]{1,0:T(8,128)(2,1)S(1)}, bf16[864,384]{1,0:T(8,128)(2,1)}, u32[]{:S(2)}, u32[]{:S(2)}) %collective-permute-start.31) | collective-permute-done | bytes 663584 | tf_op jit(solution)/shard_map/ppermute | solution.py:738
  80.7 3.3 %collective-permute-done.20 = bf16[208,384]{1,0:T(8,128)(2,1)S(1)} collective-permute-done((bf16[208,384]{1,0:T(8,128)(2,1)}, bf16[208,384]{1,0:T(8,128)(2,1)S(1)}, u32[]{:S(2)}, u32[]{:S(2)}) %collective-permute-start.20) | collective-permute-done | bytes 159776 | tf_op jit(solution)/shard_map/ppermute | solution.py:738
  84.0 2.8 %collective-permute-done.18 = bf16[208,384]{1,0:T(8,128)(2,1)} collective-permute-done((bf16[208,384]{1,0:T(8,128)(2,1)}, bf16[208,384]{1,0:T(8,128)(2,1)}, u32[]{:S(2)}, u32[]{:S(2)}) %collective-permute-start.18) | collective-permute-done | bytes 159776 | tf_op jit(solution)/shard_map/ppermute | solution.py:738
  88.1 1.9 %fusion.2 = (bf16[384,384]{1,0:T(8,128)(2,1)S(1)}, bf16[384,384]{1,0:T(8,128)(2,1)S(1)}, bf16[384,384]{1,0:T(8,128)(2,1)S(1)}) fusion(f32[4,384,384]{2,1,0:T(8,128)} %copy-done.4, bf16[4,384,384]{2,1,0:T(8,128)(2,1)} %collective-permute-done.34), kind=kLoop, calls=%fused_computation.8 | loop fusion | flops 1327104 | bytes 3538944 | tf_op jit(solution)/shard_map/convert_element_type | solution.py:828
  91.4 1.6 collective-permute-start.36
  94.2 6.6 %collective-permute-done.37 = bf16[384,384]{1,0:T(8,128)(2,1)S(1)} collective-permute-done((bf16[384,384]{1,0:T(8,128)(2,1)S(1)}, bf16[384,384]{1,0:T(8,128)(2,1)S(1)}, u32[]{:S(2)}, u32[]{:S(2)}) %collective-permute-start.37) | collective-permute-done | bytes 294944 | tf_op jit(solution)/shard_map/ppermute | solution.py:738
  100.8 4.7 %collective-permute-done.36 = bf16[384,384]{1,0:T(8,128)(2,1)S(1)} collective-permute-done((bf16[384,384]{1,0:T(8,128)(2,1)S(1)}, bf16[384,384]{1,0:T(8,128)(2,1)S(1)}, u32[]{:S(2)}, u32[]{:S(2)}) %collective-permute-start.36) | collective-permute-done | bytes 294944 | tf_op jit(solution)/shard_map/ppermute | solution.py:738
  108.3 1.7 collective-permute-start.39
  112.0 1.8 %collective-permute-done.40 = bf16[96,384]{1,0:T(8,128)(2,1)S(1)} collective-permute-done((bf16[96,384]{1,0:T(8,128)(2,1)S(1)}, bf16[96,384]{1,0:T(8,128)(2,1)S(1)}, u32[]{:S(2)}, u32[]{:S(2)}) %collective-permute-start.40) | collective-permute-done | bytes 73760 | tf_op jit(solution)/shard_map/ppermute | solution.py:738
  113.9 3.0 %collective-permute-done.39 = bf16[96,384]{1,0:T(8,128)(2,1)S(1)} collective-permute-done((bf16[96,384]{1,0:T(8,128)(2,1)S(1)}, bf16[96,384]{1,0:T(8,128)(2,1)S(1)}, u32[]{:S(2)}, u32[]{:S(2)}) %collective-permute-start.39) | collective-permute-done | bytes 73760 | tf_op jit(solution)/shard_map/ppermute | solution.py:738
  118.2 3.2 %collective-permute-start.41 = (bf16[96,384]{1,0:T(8,128)(2,1)S(1)}, bf16[96,384]{1,0:T(8,128)(2,1)S(1)}, u32[]{:S(2)}, u32[]{:S(2)}) collective-permute-start(bf16[96,384]{1,0:T(8,128)(2,1)S(1)} %fusion.12), channel_id=1, source_target_pairs={{0,2},{1,3},{2,0},{3,1},{4,6},{5,7},{6,4},{7,5},{8,10},{9,11},{10,... | collective-permute-start | bytes 221192 | tf_op jit(solution)/shard_map/ppermute | solution.py:738
  123.9 4.8 %collective-permute-done.42 = bf16[96,384]{1,0:T(8,128)(2,1)S(1)} collective-permute-done((bf16[96,384]{1,0:T(8,128)(2,1)S(1)}, bf16[96,384]{1,0:T(8,128)(2,1)S(1)}, u32[]{:S(2)}, u32[]{:S(2)}) %collective-permute-start.42) | collective-permute-done | bytes 73760 | tf_op jit(solution)/shard_map/ppermute | solution.py:738
  129.2 3.4 %collective-permute-done.22 = bf16[112,384]{1,0:T(8,128)(2,1)S(1)} collective-permute-done((bf16[112,384]{1,0:T(8,128)(2,1)S(1)}, bf16[112,384]{1,0:T(8,128)(2,1)S(1)}, u32[]{:S(2)}, u32[]{:S(2)}) %collective-permute-start.22) | collective-permute-done | bytes 86048 | tf_op jit(solution)/shard_map/ppermute | solution.py:738
  133.6 2.1 %collective-permute-start.26 = (bf16[48,384]{1,0:T(8,128)(2,1)S(1)}, bf16[48,384]{1,0:T(8,128)(2,1)S(1)}, u32[]{:S(2)}, u32[]{:S(2)}) collective-permute-start(bf16[48,384]{1,0:T(8,128)(2,1)S(1)} %fusion.18), channel_id=1, source_target_pairs={{0,6},{1,7},{2,4},{3,5},{4,2},{5,3},{6,0},{7,1},{8,14},{9,15},{10,... | collective-permute-start | bytes 110600 | tf_op jit(solution)/shard_map/ppermute | solution.py:738
  135.7 2.3 %collective-permute-start.24 = (bf16[48,384]{1,0:T(8,128)(2,1)S(1)}, bf16[48,384]{1,0:T(8,128)(2,1)S(1)}, u32[]{:S(2)}, u32[]{:S(2)}) collective-permute-start(bf16[48,384]{1,0:T(8,128)(2,1)S(1)} %fusion.18), channel_id=1, source_target_pairs={{0,2},{1,3},{2,0},{3,1},{4,6},{5,7},{6,4},{7,5},{8,10},{9,11},{10,... | collective-permute-start | bytes 110600 | tf_op jit(solution)/shard_map/ppermute | solution.py:738
  142.3 1.8 %collective-permute-start.27 = (bf16[4,48,384]{2,1,0:T(8,128)(2,1)S(1)}, bf16[4,48,384]{2,1,0:T(8,128)(2,1)S(1)}, u32[]{:S(2)}, u32[]{:S(2)}) collective-permute-start(bf16[4,48,384]{2,1,0:T(8,128)(2,1)S(1)} %get-tuple-element.94), channel_id=1, source_target_pairs={{0,8},{8,0},{16,24},{24,16},{1,9},{9,1},{17,25},{25,17},{2,10},{10... | collective-permute-start | bytes 442376 | tf_op jit(solution)/shard_map/ppermute | solution.py:738
  144.2 3.0 %collective-permute-done.29 = bf16[4,48,384]{2,1,0:T(8,128)(2,1)S(1)} collective-permute-done((bf16[4,48,384]{2,1,0:T(8,128)(2,1)S(1)}, bf16[4,48,384]{2,1,0:T(8,128)(2,1)S(1)}, u32[]{:S(2)}, u32[]{:S(2)}) %collective-permute-start.29) | collective-permute-done | bytes 147488 | tf_op jit(solution)/shard_map/ppermute | solution.py:738
  148.9 9.5 %ns_a.1 = (f32[6,384,384]{2,1,0:T(8,128)S(1)}, f32[6,384,384]{2,1,0:T(8,128)S(1)}, bf16[2,192,384]{2,1,0:T(8,128)(2,1)S(1)}) custom-call(s32[5]{0:T(128)S(1)} %pad_add_fusion.s_ref, s32[36]{0:T(128)S(1)} %copy-done.8, f32[27]{0:T(128)S(1)} %copy-done.9, f32[5184,128]{1,0:T(8,128)S(1)} %bitcast.92, bf16[864,384]{1,0:T(8,128)(2,1)} %collective-permute-done.31.fx0, ...), custom_call_target="tpu_custom_call" | custom-call | flops 8000000000 | bytes 12000000 | tf_op jit(solution)/shard_map/ns_a/pallas_call | solution.py:655
  158.5 2.8 %collective-permute-start.46 = (bf16[2,192,384]{2,1,0:T(8,128)(2,1)S(1)}, bf16[2,192,384]{2,1,0:T(8,128)(2,1)S(1)}, u32[]{:S(2)}, u32[]{:S(2)}) collective-permute-start(bf16[2,192,384]{2,1,0:T(8,128)(2,1)S(1)} %get-tuple-element.63), channel_id=1, source_target_pairs={{16,24},{17,25},{18,26},{19,27},{20,28},{21,29},{22,30},{23,31}} | collective-permute-start | bytes 884744 | tf_op jit(solution)/shard_map/ppermute | solution.py:849
  161.3 6.9 %collective-permute-done.46.tail = bf16[2,192,384]{2,1,0:T(8,128)(2,1)S(1)} collective-permute-done((bf16[2,192,384]{2,1,0:T(8,128)(2,1)S(1)}, bf16[2,192,384]{2,1,0:T(8,128)(2,1)S(1)}, u32[]{:S(2)}, u32[]{:S(2)}) %collective-permute-start.46) | collective-permute-done | bytes 294944 | tf_op jit(solution)/shard_map/ppermute | solution.py:849
  168.2 11.7 %finish.1 = (f32[5184,128]{1,0:T(8,128)}, f32[5184,128]{1,0:T(8,128)}, f32[5184,128]{1,0:T(8,128)}) custom-call(s32[5]{0:T(128)S(1)} %pad_add_fusion.s_ref, s32[36]{0:T(128)S(1)} %copy-done.8, f32[27]{0:T(128)S(1)} %copy-done.9, f32[5184,128]{1,0:T(8,128)S(1)} %bitcast.90, f32[5184,128]{1,0:T(8,128)S(1)} %bitcast.93, ...), custom_call_target="tpu_custom_call" | custom-call | flops 8000000000 | bytes 24000000 | tf_op jit(solution)/shard_map/finish/pallas_call | solution.py:724
  (121 shorter events, 41.2 us)
Async XLA Ops:
  7.0 13.0 %collective-permute-start.1 = (bf16[432,384]{1,0:T(8,128)(2,1)}, bf16[432,384]{1,0:T(8,128)(2,1)S(1)}, u32[]{:S(2)}, u32[]{:S(2)}) collective-permute-start(bf16[432,384]{1,0:T(8,128)(2,1)} %get-tuple-element.38), channel_id=1, source_target_pairs={{0,8},{8,0},{16,24},{24,16},{1,9},{9,1},{17,25},{25,17},{2,10},{10... | collective-permute-start | bytes 995336 | tf_op jit(solution)/shard_map/ppermute | solution.py:738
  7.1 12.9 %collective-permute-start.2 = (bf16[432,384]{1,0:T(8,128)(2,1)}, bf16[432,384]{1,0:T(8,128)(2,1)}, u32[]{:S(2)}, u32[]{:S(2)}) collective-permute-start(bf16[432,384]{1,0:T(8,128)(2,1)} %get-tuple-element.39), channel_id=1, source_target_pairs={{0,16},{8,24},{16,0},{24,8},{1,17},{9,25},{17,1},{25,9},{2,18},{10... | collective-permute-start | bytes 995336 | tf_op jit(solution)/shard_map/ppermute | solution.py:738
  17.8 11.0 %collective-permute-start.7 = (bf16[432,384]{1,0:T(8,128)(2,1)}, bf16[432,384]{1,0:T(8,128)(2,1)}, u32[]{:S(2)}, u32[]{:S(2)}) collective-permute-start(bf16[432,384]{1,0:T(8,128)(2,1)} %get-tuple-element.39), channel_id=1, source_target_pairs={{0,8},{8,0},{16,24},{24,16},{1,9},{9,1},{17,25},{25,17},{2,10},{10... | collective-permute-start | bytes 995336 | tf_op jit(solution)/shard_map/ppermute | solution.py:738
  18.3 11.0 %collective-permute-start.8 = (bf16[432,384]{1,0:T(8,128)(2,1)}, bf16[432,384]{1,0:T(8,128)(2,1)}, u32[]{:S(2)}, u32[]{:S(2)}) collective-permute-start(bf16[432,384]{1,0:T(8,128)(2,1)} %get-tuple-element.38), channel_id=1, source_target_pairs={{0,16},{8,24},{16,0},{24,8},{1,17},{9,25},{17,1},{25,9},{2,18},{10... | collective-permute-start | bytes 995336 | tf_op jit(solution)/shard_map/ppermute | solution.py:738
  20.0 14.2 %collective-permute-start.9 = (bf16[432,384]{1,0:T(8,128)(2,1)S(1)}, bf16[432,384]{1,0:T(8,128)(2,1)S(1)}, u32[]{:S(2)}, u32[]{:S(2)}) collective-permute-start(bf16[432,384]{1,0:T(8,128)(2,1)S(1)} %collective-permute-done.1.refs_1_), channel_id=1, source_target_pairs={{0,16},{8,24},{16,0},{24,8},{1,17},{9,25},{17,1},{25,9},{2,18},{10... | collective-permute-start | bytes 995336 | tf_op jit(solution)/shard_map/ppermute | solution.py:738
  20.6 13.6 %collective-permute-start.10 = (bf16[432,384]{1,0:T(8,128)(2,1)}, bf16[432,384]{1,0:T(8,128)(2,1)S(1)}, u32[]{:S(2)}, u32[]{:S(2)}) collective-permute-start(bf16[432,384]{1,0:T(8,128)(2,1)} %collective-permute-done.2.refs_4_), channel_id=1, source_target_pairs={{0,8},{8,0},{16,24},{24,16},{1,9},{9,1},{17,25},{25,17},{2,10},{10... | collective-permute-start | bytes 995336 | tf_op jit(solution)/shard_map/ppermute | solution.py:738
  22.0 12.7 %collective-permute-start.11 = (bf16[432,384]{1,0:T(8,128)(2,1)S(1)}, bf16[432,384]{1,0:T(8,128)(2,1)S(1)}, u32[]{:S(2)}, u32[]{:S(2)}) collective-permute-start(bf16[432,384]{1,0:T(8,128)(2,1)S(1)} %collective-permute-done.1.refs_1_), channel_id=1, source_target_pairs={{0,1},{1,0},{2,3},{3,2},{4,5},{5,4},{6,7},{7,6},{8,9},{9,8},{10,11... | collective-permute-start | bytes 995336 | tf_op jit(solution)/shard_map/ppermute | solution.py:738
  28.8 7.9 %collective-permute-start.14 = (bf16[432,384]{1,0:T(8,128)(2,1)}, bf16[432,384]{1,0:T(8,128)(2,1)S(1)}, u32[]{:S(2)}, u32[]{:S(2)}) collective-permute-start(bf16[432,384]{1,0:T(8,128)(2,1)} %collective-permute-done.2.refs_4_), channel_id=1, source_target_pairs={{0,1},{1,0},{2,3},{3,2},{4,5},{5,4},{6,7},{7,6},{8,9},{9,8},{10,11... | collective-permute-start | bytes 995336 | tf_op jit(solution)/shard_map/ppermute | solution.py:738
  29.3 7.4 %collective-permute-start.12 = (bf16[432,384]{1,0:T(8,128)(2,1)}, bf16[432,384]{1,0:T(8,128)(2,1)S(1)}, u32[]{:S(2)}, u32[]{:S(2)}) collective-permute-start(bf16[432,384]{1,0:T(8,128)(2,1)} %collective-permute-done.7.refs_2_), channel_id=1, source_target_pairs={{0,1},{1,0},{2,3},{3,2},{4,5},{5,4},{6,7},{7,6},{8,9},{9,8},{10,11... | collective-permute-start | bytes 995336 | tf_op jit(solution)/shard_map/ppermute | solution.py:738
  61.4 26.7 %collective-permute-start.34 = (bf16[4,384,384]{2,1,0:T(8,128)(2,1)}, bf16[4,384,384]{2,1,0:T(8,128)(2,1)}, u32[]{:S(2)}, u32[]{:S(2)}) collective-permute-start(bf16[4,384,384]{2,1,0:T(8,128)(2,1)} %get-tuple-element.60), channel_id=1, source_target_pairs={{0,1},{1,0},{2,3},{3,2},{4,5},{5,4},{6,7},{7,6},{8,9},{9,8},{10,11... | collective-permute-start | bytes 3538952 | tf_op jit(solution)/shard_map/ppermute | solution.py:738
  62.8 17.9 %collective-permute-start.31 = (bf16[864,384]{1,0:T(8,128)(2,1)S(1)}, bf16[864,384]{1,0:T(8,128)(2,1)}, u32[]{:S(2)}, u32[]{:S(2)}) collective-permute-start(bf16[864,384]{1,0:T(8,128)(2,1)S(1)} %prep.5), channel_id=1, source_target_pairs={{0,8},{8,0},{16,24},{24,16},{1,9},{9,1},{17,25},{25,17},{2,10},{10... | collective-permute-start | bytes 1990664 | tf_op jit(solution)/shard_map/ppermute | solution.py:738
  65.9 18.1 %collective-permute-start.20 = (bf16[208,384]{1,0:T(8,128)(2,1)}, bf16[208,384]{1,0:T(8,128)(2,1)S(1)}, u32[]{:S(2)}, u32[]{:S(2)}) collective-permute-start(bf16[208,384]{1,0:T(8,128)(2,1)} %get-tuple-element.101), channel_id=1, source_target_pairs={{0,24},{8,16},{16,8},{24,0},{1,25},{9,17},{17,9},{25,1},{2,26},{10... | collective-permute-start | bytes 479240 | tf_op jit(solution)/shard_map/ppermute | solution.py:738
  66.4 17.6 %collective-permute-start.19 = (bf16[208,384]{1,0:T(8,128)(2,1)}, bf16[208,384]{1,0:T(8,128)(2,1)}, u32[]{:S(2)}, u32[]{:S(2)}) collective-permute-start(bf16[208,384]{1,0:T(8,128)(2,1)} %get-tuple-element.100), channel_id=1, source_target_pairs={{0,16},{8,24},{16,0},{24,8},{1,17},{9,25},{17,1},{25,9},{2,18},{10... | collective-permute-start | bytes 479240 | tf_op jit(solution)/shard_map/ppermute | solution.py:738
  67.9 18.9 %collective-permute-start.18 = (bf16[208,384]{1,0:T(8,128)(2,1)}, bf16[208,384]{1,0:T(8,128)(2,1)}, u32[]{:S(2)}, u32[]{:S(2)}) collective-permute-start(bf16[208,384]{1,0:T(8,128)(2,1)} %get-tuple-element.99), channel_id=1, source_target_pairs={{0,8},{8,0},{16,24},{24,16},{1,9},{9,1},{17,25},{25,17},{2,10},{10... | collective-permute-start | bytes 479240 | tf_op jit(solution)/shard_map/ppermute | solution.py:738
  80.7 68.2 %collective-permute-start.32 = (bf16[864,384]{1,0:T(8,128)(2,1)}, bf16[864,384]{1,0:T(8,128)(2,1)S(1)}, u32[]{:S(2)}, u32[]{:S(2)}) collective-permute-start(bf16[864,384]{1,0:T(8,128)(2,1)} %collective-permute-done.31.fx0), channel_id=1, source_target_pairs={{0,1},{1,0},{2,3},{3,2},{4,5},{5,4},{6,7},{7,6},{8,9},{9,8},{10,11... | collective-permute-start | bytes 1990664 | tf_op jit(solution)/shard_map/ppermute | solution.py:738
  89.9 10.9 %collective-permute-start.37 = (bf16[384,384]{1,0:T(8,128)(2,1)S(1)}, bf16[384,384]{1,0:T(8,128)(2,1)S(1)}, u32[]{:S(2)}, u32[]{:S(2)}) collective-permute-start(bf16[384,384]{1,0:T(8,128)(2,1)S(1)} %get-tuple-element.68), channel_id=1, source_target_pairs={{0,24},{8,16},{16,8},{24,0},{1,25},{9,17},{17,9},{25,1},{2,26},{10... | collective-permute-start | bytes 884744 | tf_op jit(solution)/shard_map/ppermute | solution.py:738
  91.4 14.1 %collective-permute-start.36 = (bf16[384,384]{1,0:T(8,128)(2,1)S(1)}, bf16[384,384]{1,0:T(8,128)(2,1)S(1)}, u32[]{:S(2)}, u32[]{:S(2)}) collective-permute-start(bf16[384,384]{1,0:T(8,128)(2,1)S(1)} %get-tuple-element.69), channel_id=1, source_target_pairs={{0,16},{8,24},{16,0},{24,8},{1,17},{9,25},{17,1},{25,9},{2,18},{10... | collective-permute-start | bytes 884744 | tf_op jit(solution)/shard_map/ppermute | solution.py:738
  92.9 12.5 %collective-permute-start.35 = (bf16[384,384]{1,0:T(8,128)(2,1)S(1)}, bf16[384,384]{1,0:T(8,128)(2,1)S(1)}, u32[]{:S(2)}, u32[]{:S(2)}) collective-permute-start(bf16[384,384]{1,0:T(8,128)(2,1)S(1)} %get-tuple-element.67), channel_id=1, source_target_pairs={{0,8},{8,0},{16,24},{24,16},{1,9},{9,1},{17,25},{25,17},{2,10},{10... | collective-permute-start | bytes 884744 | tf_op jit(solution)/shard_map/ppermute | solution.py:738
  106.8 7.0 %collective-permute-start.40 = (bf16[96,384]{1,0:T(8,128)(2,1)S(1)}, bf16[96,384]{1,0:T(8,128)(2,1)S(1)}, u32[]{:S(2)}, u32[]{:S(2)}) collective-permute-start(bf16[96,384]{1,0:T(8,128)(2,1)S(1)} %get-tuple-element.74), channel_id=1, source_target_pairs={{0,6},{1,7},{2,4},{3,5},{4,2},{5,3},{6,0},{7,1},{8,14},{9,15},{10,... | collective-permute-start | bytes 221192 | tf_op jit(solution)/shard_map/ppermute | solution.py:738
  108.3 8.6 %collective-permute-start.39 = (bf16[96,384]{1,0:T(8,128)(2,1)S(1)}, bf16[96,384]{1,0:T(8,128)(2,1)S(1)}, u32[]{:S(2)}, u32[]{:S(2)}) collective-permute-start(bf16[96,384]{1,0:T(8,128)(2,1)S(1)} %get-tuple-element.75), channel_id=1, source_target_pairs={{0,4},{1,5},{2,6},{3,7},{4,0},{5,1},{6,2},{7,3},{8,12},{9,13},{10,... | collective-permute-start | bytes 221192 | tf_op jit(solution)/shard_map/ppermute | solution.py:738
  110.0 6.9 %collective-permute-start.38 = (bf16[96,384]{1,0:T(8,128)(2,1)S(1)}, bf16[96,384]{1,0:T(8,128)(2,1)S(1)}, u32[]{:S(2)}, u32[]{:S(2)}) collective-permute-start(bf16[96,384]{1,0:T(8,128)(2,1)S(1)} %get-tuple-element.73), channel_id=1, source_target_pairs={{0,2},{1,3},{2,0},{3,1},{4,6},{5,7},{6,4},{7,5},{8,10},{9,11},{10,... | collective-permute-start | bytes 221192 | tf_op jit(solution)/shard_map/ppermute | solution.py:738
  116.9 7.0 %collective-permute-start.43 = (bf16[96,384]{1,0:T(8,128)(2,1)S(1)}, bf16[96,384]{1,0:T(8,128)(2,1)S(1)}, u32[]{:S(2)}, u32[]{:S(2)}) collective-permute-start(bf16[96,384]{1,0:T(8,128)(2,1)S(1)} %fusion.12), channel_id=1, source_target_pairs={{0,6},{1,7},{2,4},{3,5},{4,2},{5,3},{6,0},{7,1},{8,14},{9,15},{10,... | collective-permute-start | bytes 221192 | tf_op jit(solution)/shard_map/ppermute | solution.py:738
  118.2 10.6 %collective-permute-start.42 = (bf16[96,384]{1,0:T(8,128)(2,1)S(1)}, bf16[96,384]{1,0:T(8,128)(2,1)S(1)}, u32[]{:S(2)}, u32[]{:S(2)}) collective-permute-start(bf16[96,384]{1,0:T(8,128)(2,1)S(1)} %fusion.12), channel_id=1, source_target_pairs={{0,4},{1,5},{2,6},{3,7},{4,0},{5,1},{6,2},{7,3},{8,12},{9,13},{10,... | collective-permute-start | bytes 221192 | tf_op jit(solution)/shard_map/ppermute | solution.py:738
  118.2 10.5 %collective-permute-start.41 = (bf16[96,384]{1,0:T(8,128)(2,1)S(1)}, bf16[96,384]{1,0:T(8,128)(2,1)S(1)}, u32[]{:S(2)}, u32[]{:S(2)}) collective-permute-start(bf16[96,384]{1,0:T(8,128)(2,1)S(1)} %fusion.12), channel_id=1, source_target_pairs={{0,2},{1,3},{2,0},{3,1},{4,6},{5,7},{6,4},{7,5},{8,10},{9,11},{10,... | collective-permute-start | bytes 221192 | tf_op jit(solution)/shard_map/ppermute | solution.py:738
  121.4 7.9 %collective-permute-start.23 = (bf16[112,384]{1,0:T(8,128)(2,1)S(1)}, bf16[112,384]{1,0:T(8,128)(2,1)S(1)}, u32[]{:S(2)}, u32[]{:S(2)}) collective-permute-start(bf16[112,384]{1,0:T(8,128)(2,1)S(1)} %get-tuple-element.83), channel_id=1, source_target_pairs={{0,6},{1,7},{2,4},{3,5},{4,2},{5,3},{6,0},{7,1},{8,14},{9,15},{10,... | collective-permute-start | bytes 258056 | tf_op jit(solution)/shard_map/ppermute | solution.py:738
  123.9 8.8 %collective-permute-start.22 = (bf16[112,384]{1,0:T(8,128)(2,1)S(1)}, bf16[112,384]{1,0:T(8,128)(2,1)S(1)}, u32[]{:S(2)}, u32[]{:S(2)}) collective-permute-start(bf16[112,384]{1,0:T(8,128)(2,1)S(1)} %get-tuple-element.82), channel_id=1, source_target_pairs={{0,4},{1,5},{2,6},{3,7},{4,0},{5,1},{6,2},{7,3},{8,12},{9,13},{10,... | collective-permute-start | bytes 258056 | tf_op jit(solution)/shard_map/ppermute | solution.py:738
  128.8 9.3 %collective-permute-start.44 = (bf16[4,96,384]{2,1,0:T(8,128)(2,1)S(1)}, bf16[4,96,384]{2,1,0:T(8,128)(2,1)S(1)}, u32[]{:S(2)}, u32[]{:S(2)}) collective-permute-start(bf16[4,96,384]{2,1,0:T(8,128)(2,1)S(1)} %get-tuple-element.77), channel_id=1, source_target_pairs={{0,16},{8,24},{16,0},{24,8},{1,17},{9,25},{17,1},{25,9},{2,18},{10... | collective-permute-start | bytes 884744 | tf_op jit(solution)/shard_map/ppermute | solution.py:738
  138.1 10.7 %collective-permute-start.45 = (bf16[2,4,96,384]{3,2,1,0:T(8,128)(2,1)S(1)}, bf16[2,4,96,384]{3,2,1,0:T(8,128)(2,1)S(1)}, u32[]{:S(2)}, u32[]{:S(2)}) collective-permute-start(bf16[2,4,96,384]{3,2,1,0:T(8,128)(2,1)S(1)} %pad_maximum_fusion.1.ch0), channel_id=1, source_target_pairs={{0,1},{1,0},{2,3},{3,2},{4,5},{5,4},{6,7},{7,6},{8,9},{9,8},{10,11... | collective-permute-start | bytes 1769480 | tf_op jit(solution)/shard_map/ppermute | solution.py:738
  140.6 6.6 %collective-permute-start.29 = (bf16[4,48,384]{2,1,0:T(8,128)(2,1)S(1)}, bf16[4,48,384]{2,1,0:T(8,128)(2,1)S(1)}, u32[]{:S(2)}, u32[]{:S(2)}) collective-permute-start(bf16[4,48,384]{2,1,0:T(8,128)(2,1)S(1)} %get-tuple-element.94), channel_id=1, source_target_pairs={{0,24},{8,16},{16,8},{24,0},{1,25},{9,17},{17,9},{25,1},{2,26},{10... | collective-permute-start | bytes 442376 | tf_op jit(solution)/shard_map/ppermute | solution.py:738
  142.2 6.5 %collective-permute-start.28 = (bf16[4,48,384]{2,1,0:T(8,128)(2,1)S(1)}, bf16[4,48,384]{2,1,0:T(8,128)(2,1)S(1)}, u32[]{:S(2)}, u32[]{:S(2)}) collective-permute-start(bf16[4,48,384]{2,1,0:T(8,128)(2,1)S(1)} %get-tuple-element.94), channel_id=1, source_target_pairs={{0,16},{8,24},{16,0},{24,8},{1,17},{9,25},{17,1},{25,9},{2,18},{10... | collective-permute-start | bytes 442376 | tf_op jit(solution)/shard_map/ppermute | solution.py:738
  148.8 12.5 %collective-permute-start.30 = (bf16[4,4,48,384]{3,2,1,0:T(8,128)(2,1)S(1)}, bf16[4,4,48,384]{3,2,1,0:T(8,128)(2,1)S(1)}, u32[]{:S(2)}, u32[]{:S(2)}) collective-permute-start(bf16[4,4,48,384]{3,2,1,0:T(8,128)(2,1)S(1)} %pad_maximum_fusion.ch0), channel_id=1, source_target_pairs={{0,1},{1,0},{2,3},{3,2},{4,5},{5,4},{6,7},{7,6},{8,9},{9,8},{10,11... | collective-permute-start | bytes 1769480 | tf_op jit(solution)/shard_map/ppermute | solution.py:738
  158.5 9.7 %collective-permute-start.46 = (bf16[2,192,384]{2,1,0:T(8,128)(2,1)S(1)}, bf16[2,192,384]{2,1,0:T(8,128)(2,1)S(1)}, u32[]{:S(2)}, u32[]{:S(2)}) collective-permute-start(bf16[2,192,384]{2,1,0:T(8,128)(2,1)S(1)} %get-tuple-element.63), channel_id=1, source_target_pairs={{16,24},{17,25},{18,26},{19,27},{20,28},{21,29},{22,30},{23,31}} | collective-permute-start | bytes 884744 | tf_op jit(solution)/shard_map/ppermute | solution.py:849
  (27 other events, 224.9 us)

commit v6 on v5

--- a/solution.py
+++ b/solution.py
@@ -474,6 +474,15 @@
     return ints, coeffs
 
 
+HALF = 256
+
+
+def symmetric(lhs, rhs):
+    left = mm(lhs, rhs[:, :HALF])
+    corner = mm(lhs[HALF:], rhs[:, HALF:])
+    return jnp.concatenate([left, jnp.concatenate([left[HALF:].T, corner], axis=0)], axis=1)
+
+
 def either(flipped, tall, wide):
     if flipped is None:
         wide()
@@ -490,17 +499,20 @@
 
         def tall():
             x = jnp.concatenate([x0, x1], axis=0)
-            bufs[0] += mm(x, x, 0, 0)
+            bufs[0, :, :HALF] += mm(x, x[:, :HALF], 0, 0)
+            bufs[0, HALF:, HALF:] += mm(x[:, HALF:], x[:, HALF:], 0, 0)
 
         def wide():
             x = jnp.concatenate([x0, x1], axis=1)
-            bufs[0] += mm(x, x, 1, 1)
+            bufs[0, :, :HALF] += mm(x, x[:HALF], 1, 1)
+            bufs[0, HALF:, HALF:] += mm(x[HALF:], x[HALF:], 1, 1)
 
         either(flipped, tall, wide)
 
         return carry
 
     lax.fori_loop(0, npairs, gram, 0)
+    bufs[0, :HALF, HALF:] = bufs[0, HALF:, :HALF].T
     g = bufs[0]
     ri = lax.broadcasted_iota(jnp.int32, (D, D), 0)
     ci = lax.broadcasted_iota(jnp.int32, (D, D), 1)
@@ -519,7 +531,7 @@
             yh, yl = split(bufs[j])
             lhs = (xh, xl, xh)[:count]
             rhs = (yh, yh, yl)[:count]
-            prod = mm(jnp.concatenate(lhs, axis=1), jnp.concatenate(rhs, axis=0))
+            prod = symmetric(jnp.concatenate(lhs, axis=1), jnp.concatenate(rhs, axis=0))
             r0 = lax.broadcasted_iota(jnp.int32, (D, D), 0)
             r1 = lax.broadcasted_iota(jnp.int32, (D, D), 1)
             ident = jnp.where(r0 == r1, coeffs[3 * k + 2], 0.0)
@@ -669,7 +681,8 @@
 
 
 def final_kernel(
-    s_ref, ints, coeffs, par, mom, ch0, ch1, upa, grda, tail, ograd, onew, omom, upb, gb, mat, bufs
+    s_ref, ints, coeffs, par, mom, ch0, ch1, upa, grda, tail, ograd, onew, omom,
+    upb, gb, mat, bufs, og, on, om, sems
 ):
     me = s_ref[0]
     inner = jnp.logical_or(me == 1, me == 2)
@@ -688,6 +701,38 @@
     def _():
         add_momentum(2, OUTW, mom, gb, mat, 3)
 
+    def each(t, body):
+        for mat_id, block, r0, n, _, frow, stride in shard_pieces(t, 4):
+            b = block - MATS[mat_id][2]
+            for j in range(3):
+                cs = slice(128 * j, 128 * j + 128)
+                fl = pl.ds(frow + j, n, stride=stride)
+                if mat_id == UP and t == 3:
+                    assert r0 == D - TAIL and n == TAIL
+                    ts = slice(TAIL * b, TAIL * b + TAIL)
+                    body(fl, lambda: tail[0, ts, cs].astype(F32), lambda: tail[1, ts, cs].astype(F32))
+                    continue
+                rs = slice(r0, r0 + n)
+                if mat_id in (QKV, OUTW):
+                    gb_at = b + 3 * (mat_id == OUTW)
+                    body(fl, lambda: gb[gb_at, rs, cs], lambda: upb[b, rs, cs])
+                else:
+                    body(fl, lambda: grda[b, rs, cs], lambda: upa[b, rs, cs])
+
+    def gradient(fl, g, u):
+        value = g()
+        og[fl, :] = value
+        om[fl, :] = MOMENTUM_RATE * mom[fl, :] + value
+
+    def update(fl, g, u):
+        on[fl, :] = par[fl, :] - u()
+
+    for t in range(4):
+        pl.when(me == t)(functools.partial(each, t, gradient))
+    early = [pltpu.make_async_copy(og, ograd, sems.at[0]), pltpu.make_async_copy(om, omom, sems.at[1])]
+    for copy in early:
+        copy.start()
+
     @pl.when(inner)
     def _():
         npairs = jnp.where(me == 1, 2, 1)
@@ -695,27 +740,11 @@
         newton_schulz(ints, coeffs, mat, upb, bufs, npairs, None, factor)
 
     for t in range(4):
-
-        @pl.when(me == t)
-        def _(t=t):
-            for mat_id, block, r0, n, crow, frow, stride in shard_pieces(t, 4):
-                b = block - MATS[mat_id][2]
-                for j in range(3):
-                    cs = slice(128 * j, 128 * j + 128)
-                    fl = pl.ds(frow + j, n, stride=stride)
-                    if mat_id == UP and t == 3:
-                        assert r0 == D - TAIL and n == TAIL
-                        g = tail[0, TAIL * b : TAIL * b + TAIL, cs].astype(F32)
-                        u = tail[1, TAIL * b : TAIL * b + TAIL, cs].astype(F32)
-                    elif mat_id in (QKV, OUTW):
-                        g = gb[b + 3 * (mat_id == OUTW), r0 : r0 + n, cs]
-                        u = upb[b, r0 : r0 + n, cs]
-                    else:
-                        g = grda[b, r0 : r0 + n, cs]
-                        u = upa[b, r0 : r0 + n, cs]
-                    ograd[fl, :] = g
-                    omom[fl, :] = MOMENTUM_RATE * mom[fl, :] + g
-                    onew[fl, :] = par[fl, :] - u
+        pl.when(me == t)(functools.partial(each, t, update))
+    late = pltpu.make_async_copy(on, onew, sems.at[2])
+    late.start()
+    for copy in early + [late]:
+        copy.wait()
 
 
 def final_call(sidx, tables, par, mom, chunks, upa, grda, tail):
@@ -725,9 +754,9 @@
         final_kernel,
         out_shape=(sd, sd, sd),
         in_specs=[sspec()] * 3 + [vspec()] * 7,
-        out_specs=(vspec(),) * 3,
-        scratch_shapes=[block4, block4, block4, block4],
-        compiler_params=params_of(20),
+        out_specs=(hspec(),) * 3,
+        scratch_shapes=[block4] * 4 + [pltpu.VMEM(par.shape, F32)] * 3 + [pltpu.SemaphoreType.DMA((3,))],
+        compiler_params=params_of(22),
         cost_estimate=pl.CostEstimate(flops=8_000_000_000, bytes_accessed=24_000_000, transcendentals=0),
         name="finish",
     )(sidx, *tables, par, mom, *chunks, upa, grda, tail)
@@ -751,23 +780,78 @@
     return total
 
 
-def at(x, i):
-    return lax.dynamic_index_in_dim(x, i, 0, keepdims=False)
-
-
-def z_scatter(s, zed, extra=None):
-    size = s.shape[0] // 4
-    blocks = s.reshape(4, size, D)
+def join_kernel(own, other, keep, *msgs):
+    n = own.shape[1]
+    for m, msg in enumerate(msgs, 1):
+        msg[:n, :] = (own[m] + other[m].astype(F32)).astype(BF16)
+        msg[n:, :] = keep[...]
+
+
+def join_call(own, other, keep):
+    out = jax.ShapeDtypeStruct((own.shape[1] + keep.shape[0], D), BF16)
+    return pl.pallas_call(
+        join_kernel,
+        out_shape=(out,) * 3,
+        in_specs=[vspec()] * 3,
+        out_specs=(vspec(),) * 3,
+        compiler_params=params_of(4),
+        cost_estimate=pl.CostEstimate(flops=0, bytes_accessed=2_000_000, transcendentals=0),
+        name="join",
+    )(own, other, keep)
+
+
+def piece_kernel(has_keep, s_ref, own, other, *refs):
+    keep = refs[0] if has_keep else None
+    got = refs[has_keep : has_keep + 3]
+    outs = refs[has_keep + 3 :]
+    zed = s_ref[2]
+    n = outs[0].shape[0]
+    size = 4 * n
+    if has_keep:
+        rows = outs[4]
+        kr = keep.shape[0]
+        rows[:kr, :] = keep[...]
+        for m in range(3):
+            rows[kr * (m + 1) : kr * (m + 2), :] = got[m][size:, :]
+    for i in range(4):
+        rs = pl.ds(pl.multiple_of((zed ^ i) * n, n), n)
+        total = own[0, rs, :] + other[0, rs, :].astype(F32)
+        for g in got:
+            total = total + g[rs, :].astype(F32)
+        if i == 0:
+            outs[0][...] = total
+        else:
+            outs[i][:n, :] = total.astype(BF16)
+            if has_keep:
+                outs[i][n:, :] = rows[...]
+
+
+def piece_call(sidx, own, other, got, keep=None):
+    size = own.shape[1]
+    n = size // 4
+    extra = 0 if keep is None else 4 * keep.shape[0]
+    sd = jax.ShapeDtypeStruct
+    outs = (sd((n, D), F32),) + (sd((n + extra, D), BF16),) * 3
+    if extra:
+        outs += (sd((extra, D), BF16),)
+    kept = [] if keep is None else [keep]
+    return pl.pallas_call(
+        functools.partial(piece_kernel, len(kept)),
+        out_shape=outs,
+        in_specs=[sspec()] + [vspec()] * (len(kept) + 5),
+        out_specs=(vspec(),) * len(outs),
+        compiler_params=params_of(6),
+        cost_estimate=pl.CostEstimate(flops=0, bytes_accessed=2_000_000, transcendentals=0),
+        name="piece",
+    )(sidx, own, other, *kept, *got)
+
+
+def z_sum(mine, pieces):
+    n = mine.shape[0]
     got = []
-    for m in (1, 2, 3):
-        piece = at(blocks, zed ^ m).astype(BF16)
-        if extra is not None:
-            piece = jnp.concatenate([piece, extra], axis=0)
+    for m, piece in enumerate(pieces, 1):
         got.append(swap(piece, "rep", 2 * m))
-    total = wide_sum([at(blocks, zed)] + [g[:size] for g in got]).astype(BF16)
-    if extra is None:
-        return total
-    return total, jnp.concatenate([extra] + [g[size:] for g in got], axis=0)
+    return wide_sum([mine] + [g[:n] for g in got]).astype(BF16), [g[n:] for g in got]
 
 
 def fan(x, axis, masks):
@@ -827,19 +911,20 @@
     for m in (1, 2, 3):
         got.append(swap((keep1[m] + other[m].astype(F32)).astype(BF16), "fsdp", m))
     gtok, keep2, send2, keep = input_call(sidx, tok2, gqkv, ai, gafter, mods, gmod1, silu, wqkv, gout)
-    s1 = wide_sum([keep1[0] + other[0].astype(F32)] + got)
-    col = fan(z_scatter(s1, zed), "rep", (2, 4, 6))
+    mine, *pieces = piece_call(sidx, keep1, other, got)
+    total, _ = z_sum(mine, pieces)
+    col = fan(total, "rep", (2, 4, 6))
     pair = fan(col, "fsdp", (2,))
     pairs = (pair, swap(pair, "rep", 1))
 
     other = swap(send2, "rep", 1)
+    msgs = join_call(keep2, other, keep)
     got = []
     for m in (1, 2, 3):
-        part = (keep2[m] + other[m].astype(F32)).astype(BF16)
-        got.append(swap(jnp.concatenate([part, keep], axis=0), "fsdp", m))
-    size = keep2.shape[1]
-    s2 = wide_sum([keep2[0] + other[0].astype(F32)] + [g[:size] for g in got])
-    q2, kz = z_scatter(s2, zed, jnp.concatenate([keep] + [g[size:] for g in got], axis=0))
+        got.append(swap(msgs[m - 1], "fsdp", m))
+    mine, *pieces, rows2 = piece_call(sidx, keep2, other, got, keep)
+    q2, more = z_sum(mine, pieces)
+    kz = jnp.concatenate([rows2] + more, axis=0)
     kept = (kz, swap(kz, "rep", 1))
     quad = fan(fan(q2, "rep", (2, 4, 6)), "fsdp", (1, 2, 3))
     quads = (quad, swap(quad, "rep", 1))

time: 180 us -> 163 us (0.906)
  waiting for transfers between devices: 75.5 us -> 63.9 us
  other arithmetic: 6.43 us -> 1.35 us
  starting transfers between devices: 42.8 us -> 46.6 us
  local copies, waits for them, and re-layouts: 5.19 us -> 2.93 us
  Pallas kernels: 48.9 us -> 46.9 us
    ppermute x46, waiting for transfers between devices: 68.7 us -> 57.1 us  [swap(): return lax.ppermute(x, axis, [(i, i ^ mask) for i in range(count)])]
    ppermute x46, starting transfers between devices: 40 us -> 42.9 us  [swap(): return lax.ppermute(x, axis, [(i, i ^ mask) for i in range(count)])]
    add x2 -> x0, other arithmetic: 2.56 us -> none  [wide_sum(): total = p.astype(F32) if total is None else total + p.astype(F32)]
    unnamed x31 -> x16, local copies, waits for them, and re-layouts: 5.08 us -> 2.84 us
    pallas_call x1, Pallas kernels: 11.7 us -> 9.54 us  [final_call(): pl.pallas_call(final_kernel, out_shape=(sd, sd, sd), in_specs=[sspec()] *...]
  transfers between devices with their start and end apart: 47 -> 47, of which waited for: 24 -> 24; matrix products, arithmetic and copies ran while one was open for 4% -> 1% of each run, Pallas kernels for 7% -> 13%
where the time goes in v6:
time: 163 us
  waiting for transfers between devices  63.9 us (39%)
  Pallas kernels  46.9 us (29%)
  starting transfers between devices  46.6 us (29%)
  local copies, waits for them, and re-layouts  2.93 us (2%)
    ppermute x46, waiting for transfers between devices, swap(): return lax.ppermute(x, axis, [(i, i ^ mask) for i in range(count)])  57.1 us
    ppermute x46, starting transfers between devices, swap(): return lax.ppermute(x, axis, [(i, i ^ mask) for i in range(count)])  42.9 us
    pallas_call x1, Pallas kernels, main_call(): pl.pallas_call(functools.partial(main_kernel, len(bufs), fast, rows), out...  15.8 us
    pallas_call x1, Pallas kernels, final_call(): pl.pallas_call(final_kernel, out_shape=(sd, sd, sd), in_specs=[sspec()] *...  9.54 us
    pallas_call x1, Pallas kernels, ns_a(): pl.pallas_call(ns_a_kernel, out_shape=(sd, sd, jax.ShapeDtypeStruct((2, 4...  8.43 us
    ppermute x1, waiting for transfers between devices, fast_body(): tail = lax.ppermute(tail, 'fsdp', [(2, 3)])  6.86 us
    pallas_call x1, Pallas kernels, heads_call(): pl.pallas_call(functools.partial(heads_kernel, rows), out_shape=jax.Shape...  4.9 us
    ppermute x1, starting transfers between devices, fast_body(): tail = lax.ppermute(tail, 'fsdp', [(2, 3)])  3.62 us
  transfers between devices with their start and end apart: 47, of which 24 were waited for; matrix products, arithmetic and copies ran while one was open for 1% of the time, Pallas kernels for 13%

profile of v6, /device:TPU:4, one launch (start us, length us, event | category | flops | bytes accessed | tf_op | source)
XLA Modules:
  0.0 162.8 jit_solution(11071638940124686581)
XLA Ops:
  3.0 1.7 %copy-done = f32[663552]{0:T(1024)S(1)} copy-done((f32[663552]{0:T(1024)S(1)}, f32[663552]{0:T(1024)}, u32[]{:S(2)}) %copy-start) | copy-done | bytes 2654232
  4.7 1.7 %prep.3 = (bf16[432,384]{1,0:T(8,128)(2,1)}, bf16[432,384]{1,0:T(8,128)(2,1)}) custom-call(s32[5]{0:T(128)S(1)} %pad_add_fusion.s_ref, f32[5184,128]{1,0:T(8,128)S(1)} %bitcast.34), custom_call_target="tpu_custom_call" | custom-call | bytes 4000000 | tf_op jit(solution)/shard_map/prep/pallas_call | solution.py:111
  7.1 1.9 %collective-permute-start.2 = (bf16[432,384]{1,0:T(8,128)(2,1)}, bf16[432,384]{1,0:T(8,128)(2,1)S(1)}, u32[]{:S(2)}, u32[]{:S(2)}) collective-permute-start(bf16[432,384]{1,0:T(8,128)(2,1)} %get-tuple-element.51), channel_id=1, source_target_pairs={{0,16},{8,24},{16,0},{24,8},{1,17},{9,25},{17,1},{25,9},{2,18},{10... | collective-permute-start | bytes 995336 | tf_op jit(solution)/shard_map/ppermute | solution.py:767
  11.4 1.6 %collective-permute-start.5 = (bf16[16,384]{1,0:T(8,128)(2,1)S(1)}, bf16[16,384]{1,0:T(8,128)(2,1)S(1)}, u32[]{:S(2)}, u32[]{:S(2)}) collective-permute-start(bf16[16,384]{1,0:T(8,128)(2,1)S(1)} %pad_maximum_fusion.6), channel_id=1, source_target_pairs={{0,2},{1,3},{2,0},{3,1},{4,6},{5,7},{6,4},{7,5},{8,10},{9,11},{10,... | collective-permute-start | bytes 36872 | tf_op jit(solution)/shard_map/ppermute | solution.py:767
  13.0 2.1 %collective-permute-done.5 = bf16[16,384]{1,0:T(8,128)(2,1)S(1)} collective-permute-done((bf16[16,384]{1,0:T(8,128)(2,1)S(1)}, bf16[16,384]{1,0:T(8,128)(2,1)S(1)}, u32[]{:S(2)}, u32[]{:S(2)}) %collective-permute-start.5) | collective-permute-done | bytes 12320 | tf_op jit(solution)/shard_map/ppermute | solution.py:767
  15.2 2.7 %collective-permute-start.6 = (bf16[32,384]{1,0:T(8,128)(2,1)S(1)}, bf16[32,384]{1,0:T(8,128)(2,1)S(1)}, u32[]{:S(2)}, u32[]{:S(2)}) collective-permute-start(bf16[32,384]{1,0:T(8,128)(2,1)S(1)} %pad_maximum_fusion.5), channel_id=1, source_target_pairs={{0,4},{1,5},{2,6},{3,7},{4,0},{5,1},{6,2},{7,3},{8,12},{9,13},{10,... | collective-permute-start | bytes 73736 | tf_op jit(solution)/shard_map/ppermute | solution.py:767
  22.0 6.8 %collective-permute-done.7.refs_2_ = bf16[432,384]{1,0:T(8,128)(2,1)} collective-permute-done((bf16[432,384]{1,0:T(8,128)(2,1)}, bf16[432,384]{1,0:T(8,128)(2,1)}, u32[]{:S(2)}, u32[]{:S(2)}) %collective-permute-start.7) | collective-permute-done | bytes 331808 | tf_op jit(solution)/shard_map/ppermute | solution.py:767
  29.3 4.8 %collective-permute-done.9.refs_5_ = bf16[432,384]{1,0:T(8,128)(2,1)S(1)} collective-permute-done((bf16[432,384]{1,0:T(8,128)(2,1)S(1)}, bf16[432,384]{1,0:T(8,128)(2,1)S(1)}, u32[]{:S(2)}, u32[]{:S(2)}) %collective-permute-start.9) | collective-permute-done | bytes 331808 | tf_op jit(solution)/shard_map/ppermute | solution.py:767
  36.9 15.8 %main.1 = (bf16[512,384]{1,0:T(8,128)(2,1)}, bf16[3,512,384]{2,1,0:T(8,128)(2,1)S(1)}, f32[12,256,256]{2,1,0:T(8,128)S(1)}, bf16[512,384]{1,0:T(8,128)(2,1)S(1)}...) custom-call(s32[5]{0:T(128)S(1)} %pad_add_fusion.s_ref, ...), custom_call_target="tpu_custom_call" | custom-call | flops 20000000000 | bytes 30000000 | tf_op jit(solution)/shard_map/main/pallas_call | solution.py:341
  53.0 2.6 %collective-permute-done.34.other = bf16[4,384,384]{2,1,0:T(8,128)(2,1)S(1)} collective-permute-done((bf16[4,384,384]{2,1,0:T(8,128)(2,1)S(1)}, bf16[4,384,384]{2,1,0:T(8,128)(2,1)S(1)}, u32[]{:S(2)}, u32[]{:S(2)}) %collective-permute-start.34) | collective-permute-done | bytes 1179680 | tf_op jit(solution)/shard_map/ppermute | solution.py:767
  55.8 1.6 collective-permute-start.35
  59.4 4.9 %heads.1.gqkv = bf16[3,512,384]{2,1,0:T(8,128)(2,1)S(1)} custom-call(bf16[3,512,384]{2,1,0:T(8,128)(2,1)S(1)} %get-tuple-element.57.qkv, f32[12,256,256]{2,1,0:T(8,128)S(1)} %get-tuple-element.58.probs, bf16[512,384]{1,0:T(8,128)(2,1)S(1)} %get-tuple-element.59.gmx), custom_call_target="tpu_custom_call" | custom-call | flops 6000000000 | bytes 6000000 | tf_op jit(solution)/shard_map/heads/pallas_call | solution.py:394
  65.8 6.8 %collective-permute-done.36.refs_1_ = bf16[384,384]{1,0:T(8,128)(2,1)S(1)} collective-permute-done((bf16[384,384]{1,0:T(8,128)(2,1)S(1)}, bf16[384,384]{1,0:T(8,128)(2,1)S(1)}, u32[]{:S(2)}, u32[]{:S(2)}) %collective-permute-start.36) | collective-permute-done | bytes 294944 | tf_op jit(solution)/shard_map/ppermute | solution.py:767
  74.8 1.7 %collective-permute-start.39 = (bf16[96,384]{1,0:T(8,128)(2,1)S(1)}, bf16[96,384]{1,0:T(8,128)(2,1)S(1)}, u32[]{:S(2)}, u32[]{:S(2)}) collective-permute-start(bf16[96,384]{1,0:T(8,128)(2,1)S(1)} %get-tuple-element.83), channel_id=1, source_target_pairs={{0,4},{1,5},{2,6},{3,7},{4,0},{5,1},{6,2},{7,3},{8,12},{9,13},{10,... | collective-permute-start | bytes 221192 | tf_op jit(solution)/shard_map/ppermute | solution.py:767
  77.8 3.1 %input.1 = (f32[512,384]{1,0:T(8,128)}, f32[4,192,384]{2,1,0:T(8,128)S(1)}, bf16[4,192,384]{2,1,0:T(8,128)(2,1)S(1)}, bf16[16,384]{1,0:T(8,128)(2,1)S(1)}) custom-call(s32[5]{0:T(128)S(1)} %pad_add_fusion.s_ref, bf16[512,384]{1,0:T(8,128)(2,1)S(1)} %bitcast.41, bf16[3,512,384]{2,1,0:T(8,128)(2,1)S(1)} %heads.1.gqkv, ...), custom_call_target="tpu_custom_call" | custom-call | flops 6000000000 | bytes 6000000 | tf_op jit(solution)/shard_map/input/pallas_call | solution.py:439
  84.8 2.3 %collective-permute-start.41 = (bf16[96,384]{1,0:T(8,128)(2,1)S(1)}, bf16[96,384]{1,0:T(8,128)(2,1)S(1)}, u32[]{:S(2)}, u32[]{:S(2)}) collective-permute-start(bf16[96,384]{1,0:T(8,128)(2,1)S(1)} %add_convert_fusion.3), channel_id=1, source_target_pairs={{0,2},{1,3},{2,0},{3,1},{4,6},{5,7},{6,4},{7,5},{8,10},{9,11},{10,... | collective-permute-start | bytes 221192 | tf_op jit(solution)/shard_map/ppermute | solution.py:767
  87.1 2.6 %collective-permute-done.43 = bf16[96,384]{1,0:T(8,128)(2,1)S(1)} collective-permute-done((bf16[96,384]{1,0:T(8,128)(2,1)S(1)}, bf16[96,384]{1,0:T(8,128)(2,1)S(1)}, u32[]{:S(2)}, u32[]{:S(2)}) %collective-permute-start.43) | collective-permute-done | bytes 73760 | tf_op jit(solution)/shard_map/ppermute | solution.py:767
  89.8 2.3 %collective-permute-done.42 = bf16[96,384]{1,0:T(8,128)(2,1)S(1)} collective-permute-done((bf16[96,384]{1,0:T(8,128)(2,1)S(1)}, bf16[96,384]{1,0:T(8,128)(2,1)S(1)}, u32[]{:S(2)}, u32[]{:S(2)}) %collective-permute-start.42) | collective-permute-done | bytes 73760 | tf_op jit(solution)/shard_map/ppermute | solution.py:767
  97.1 2.8 %collective-permute-done.31.fx0 = bf16[864,384]{1,0:T(8,128)(2,1)S(1)} collective-permute-done((bf16[864,384]{1,0:T(8,128)(2,1)S(1)}, bf16[864,384]{1,0:T(8,128)(2,1)S(1)}, u32[]{:S(2)}, u32[]{:S(2)}) %collective-permute-start.31) | collective-permute-done | bytes 663584 | tf_op jit(solution)/shard_map/ppermute | solution.py:767
  99.9 3.4 %collective-permute-done.18.refs_1_ = bf16[208,384]{1,0:T(8,128)(2,1)S(1)} collective-permute-done((bf16[208,384]{1,0:T(8,128)(2,1)S(1)}, bf16[208,384]{1,0:T(8,128)(2,1)S(1)}, u32[]{:S(2)}, u32[]{:S(2)}) %collective-permute-start.18) | collective-permute-done | bytes 159776 | tf_op jit(solution)/shard_map/ppermute | solution.py:767
  103.3 4.7 %collective-permute-done.19.refs_2_ = bf16[208,384]{1,0:T(8,128)(2,1)S(1)} collective-permute-done((bf16[208,384]{1,0:T(8,128)(2,1)S(1)}, bf16[208,384]{1,0:T(8,128)(2,1)S(1)}, u32[]{:S(2)}, u32[]{:S(2)}) %collective-permute-start.19) | collective-permute-done | bytes 159776 | tf_op jit(solution)/shard_map/ppermute | solution.py:767
  110.1 3.0 %collective-permute-start.21 = (bf16[112,384]{1,0:T(8,128)(2,1)S(1)}, bf16[112,384]{1,0:T(8,128)(2,1)S(1)}, u32[]{:S(2)}, u32[]{:S(2)}) collective-permute-start(bf16[112,384]{1,0:T(8,128)(2,1)S(1)} %get-tuple-element.75), channel_id=1, source_target_pairs={{0,2},{1,3},{2,0},{3,1},{4,6},{5,7},{6,4},{7,5},{8,10},{9,11},{10,... | collective-permute-start | bytes 258056 | tf_op jit(solution)/shard_map/ppermute | solution.py:767
  113.3 2.8 %collective-permute-done.23 = bf16[112,384]{1,0:T(8,128)(2,1)S(1)} collective-permute-done((bf16[112,384]{1,0:T(8,128)(2,1)S(1)}, bf16[112,384]{1,0:T(8,128)(2,1)S(1)}, u32[]{:S(2)}, u32[]{:S(2)}) %collective-permute-start.23) | collective-permute-done | bytes 86048 | tf_op jit(solution)/shard_map/ppermute | solution.py:767
  116.0 1.8 %collective-permute-done.22 = bf16[112,384]{1,0:T(8,128)(2,1)S(1)} collective-permute-done((bf16[112,384]{1,0:T(8,128)(2,1)S(1)}, bf16[112,384]{1,0:T(8,128)(2,1)S(1)}, u32[]{:S(2)}, u32[]{:S(2)}) %collective-permute-start.22) | collective-permute-done | bytes 86048 | tf_op jit(solution)/shard_map/ppermute | solution.py:767
  117.9 1.9 %collective-permute-start.26 = (bf16[48,384]{1,0:T(8,128)(2,1)S(1)}, bf16[48,384]{1,0:T(8,128)(2,1)S(1)}, u32[]{:S(2)}, u32[]{:S(2)}) collective-permute-start(bf16[48,384]{1,0:T(8,128)(2,1)S(1)} %add_convert_fusion.4), channel_id=1, source_target_pairs={{0,6},{1,7},{2,4},{3,5},{4,2},{5,3},{6,0},{7,1},{8,14},{9,15},{10,... | collective-permute-start | bytes 110600 | tf_op jit(solution)/shard_map/ppermute | solution.py:767
  119.7 2.6 %collective-permute-start.24 = (bf16[48,384]{1,0:T(8,128)(2,1)S(1)}, bf16[48,384]{1,0:T(8,128)(2,1)S(1)}, u32[]{:S(2)}, u32[]{:S(2)}) collective-permute-start(bf16[48,384]{1,0:T(8,128)(2,1)S(1)} %add_convert_fusion.4), channel_id=1, source_target_pairs={{0,2},{1,3},{2,0},{3,1},{4,6},{5,7},{6,4},{7,5},{8,10},{9,11},{10,... | collective-permute-start | bytes 110600 | tf_op jit(solution)/shard_map/ppermute | solution.py:767
  126.3 1.6 collective-permute-start.28
  128.5 3.8 %collective-permute-done.29 = bf16[4,48,384]{2,1,0:T(8,128)(2,1)S(1)} collective-permute-done((bf16[4,48,384]{2,1,0:T(8,128)(2,1)S(1)}, bf16[4,48,384]{2,1,0:T(8,128)(2,1)S(1)}, u32[]{:S(2)}, u32[]{:S(2)}) %collective-permute-start.29) | collective-permute-done | bytes 147488 | tf_op jit(solution)/shard_map/ppermute | solution.py:767
  134.1 8.4 %ns_a.1 = (f32[6,384,384]{2,1,0:T(8,128)S(1)}, f32[6,384,384]{2,1,0:T(8,128)S(1)}, bf16[2,192,384]{2,1,0:T(8,128)(2,1)S(1)}) custom-call(s32[5]{0:T(128)S(1)} %pad_add_fusion.s_ref, s32[36]{0:T(128)S(1)} %copy-done.5, f32[27]{0:T(128)S(1)} %copy-done.6, f32[5184,128]{1,0:T(8,128)S(1)} %bitcast.38, bf16[864,384]{1,0:T(8,128)(2,1)S(1)} %collective-permute-done.31.fx0, ...), custom_call_target="tpu_custom_call" | custom-call | flops 8000000000 | bytes 12000000 | tf_op jit(solution)/shard_map/ns_a/pallas_call | solution.py:667
  142.6 3.6 %collective-permute-start.46 = (bf16[2,192,384]{2,1,0:T(8,128)(2,1)S(1)}, bf16[2,192,384]{2,1,0:T(8,128)(2,1)S(1)}, u32[]{:S(2)}, u32[]{:S(2)}) collective-permute-start(bf16[2,192,384]{2,1,0:T(8,128)(2,1)S(1)} %get-tuple-element.87), channel_id=1, source_target_pairs={{16,24},{17,25},{18,26},{19,27},{20,28},{21,29},{22,30},{23,31}} | collective-permute-start | bytes 884744 | tf_op jit(solution)/shard_map/ppermute | solution.py:934
  146.2 6.9 %collective-permute-done.46.tail = bf16[2,192,384]{2,1,0:T(8,128)(2,1)S(1)} collective-permute-done((bf16[2,192,384]{2,1,0:T(8,128)(2,1)S(1)}, bf16[2,192,384]{2,1,0:T(8,128)(2,1)S(1)}, u32[]{:S(2)}, u32[]{:S(2)}) %collective-permute-start.46) | collective-permute-done | bytes 294944 | tf_op jit(solution)/shard_map/ppermute | solution.py:934
  153.1 9.5 %finish.1 = (f32[5184,128]{1,0:T(8,128)}, f32[5184,128]{1,0:T(8,128)}, f32[5184,128]{1,0:T(8,128)}) custom-call(s32[5]{0:T(128)S(1)} %pad_add_fusion.s_ref, s32[36]{0:T(128)S(1)} %copy-done.5, f32[27]{0:T(128)S(1)} %copy-done.6, f32[5184,128]{1,0:T(8,128)S(1)} %bitcast.36, f32[5184,128]{1,0:T(8,128)S(1)} %bitcast.39, ...), custom_call_target="tpu_custom_call" | custom-call | flops 8000000000 | bytes 24000000 | tf_op jit(solution)/shard_map/finish/pallas_call | solution.py:753
  (107 shorter events, 37.7 us)
Async XLA Ops:
  7.0 13.0 %collective-permute-start.1 = (bf16[432,384]{1,0:T(8,128)(2,1)}, bf16[432,384]{1,0:T(8,128)(2,1)S(1)}, u32[]{:S(2)}, u32[]{:S(2)}) collective-permute-start(bf16[432,384]{1,0:T(8,128)(2,1)} %get-tuple-element.50), channel_id=1, source_target_pairs={{0,8},{8,0},{16,24},{24,16},{1,9},{9,1},{17,25},{25,17},{2,10},{10... | collective-permute-start | bytes 995336 | tf_op jit(solution)/shard_map/ppermute | solution.py:767
  7.1 12.9 %collective-permute-start.2 = (bf16[432,384]{1,0:T(8,128)(2,1)}, bf16[432,384]{1,0:T(8,128)(2,1)S(1)}, u32[]{:S(2)}, u32[]{:S(2)}) collective-permute-start(bf16[432,384]{1,0:T(8,128)(2,1)} %get-tuple-element.51), channel_id=1, source_target_pairs={{0,16},{8,24},{16,0},{24,8},{1,17},{9,25},{17,1},{25,9},{2,18},{10... | collective-permute-start | bytes 995336 | tf_op jit(solution)/shard_map/ppermute | solution.py:767
  17.8 11.0 %collective-permute-start.7 = (bf16[432,384]{1,0:T(8,128)(2,1)}, bf16[432,384]{1,0:T(8,128)(2,1)}, u32[]{:S(2)}, u32[]{:S(2)}) collective-permute-start(bf16[432,384]{1,0:T(8,128)(2,1)} %get-tuple-element.51), channel_id=1, source_target_pairs={{0,8},{8,0},{16,24},{24,16},{1,9},{9,1},{17,25},{25,17},{2,10},{10... | collective-permute-start | bytes 995336 | tf_op jit(solution)/shard_map/ppermute | solution.py:767
  18.3 11.0 %collective-permute-start.8 = (bf16[432,384]{1,0:T(8,128)(2,1)}, bf16[432,384]{1,0:T(8,128)(2,1)}, u32[]{:S(2)}, u32[]{:S(2)}) collective-permute-start(bf16[432,384]{1,0:T(8,128)(2,1)} %get-tuple-element.50), channel_id=1, source_target_pairs={{0,16},{8,24},{16,0},{24,8},{1,17},{9,25},{17,1},{25,9},{2,18},{10... | collective-permute-start | bytes 995336 | tf_op jit(solution)/shard_map/ppermute | solution.py:767
  20.0 14.1 %collective-permute-start.9 = (bf16[432,384]{1,0:T(8,128)(2,1)S(1)}, bf16[432,384]{1,0:T(8,128)(2,1)S(1)}, u32[]{:S(2)}, u32[]{:S(2)}) collective-permute-start(bf16[432,384]{1,0:T(8,128)(2,1)S(1)} %collective-permute-done.1.refs_1_), channel_id=1, source_target_pairs={{0,16},{8,24},{16,0},{24,8},{1,17},{9,25},{17,1},{25,9},{2,18},{10... | collective-permute-start | bytes 995336 | tf_op jit(solution)/shard_map/ppermute | solution.py:767
  20.6 13.5 %collective-permute-start.10 = (bf16[432,384]{1,0:T(8,128)(2,1)S(1)}, bf16[432,384]{1,0:T(8,128)(2,1)S(1)}, u32[]{:S(2)}, u32[]{:S(2)}) collective-permute-start(bf16[432,384]{1,0:T(8,128)(2,1)S(1)} %collective-permute-done.2.refs_4_), channel_id=1, source_target_pairs={{0,8},{8,0},{16,24},{24,16},{1,9},{9,1},{17,25},{25,17},{2,10},{10... | collective-permute-start | bytes 995336 | tf_op jit(solution)/shard_map/ppermute | solution.py:767
  22.0 12.6 %collective-permute-start.11 = (bf16[432,384]{1,0:T(8,128)(2,1)S(1)}, bf16[432,384]{1,0:T(8,128)(2,1)S(1)}, u32[]{:S(2)}, u32[]{:S(2)}) collective-permute-start(bf16[432,384]{1,0:T(8,128)(2,1)S(1)} %collective-permute-done.1.refs_1_), channel_id=1, source_target_pairs={{0,1},{1,0},{2,3},{3,2},{4,5},{5,4},{6,7},{7,6},{8,9},{9,8},{10,11... | collective-permute-start | bytes 995336 | tf_op jit(solution)/shard_map/ppermute | solution.py:767
  28.8 7.8 %collective-permute-start.14 = (bf16[432,384]{1,0:T(8,128)(2,1)S(1)}, bf16[432,384]{1,0:T(8,128)(2,1)S(1)}, u32[]{:S(2)}, u32[]{:S(2)}) collective-permute-start(bf16[432,384]{1,0:T(8,128)(2,1)S(1)} %collective-permute-done.2.refs_4_), channel_id=1, source_target_pairs={{0,1},{1,0},{2,3},{3,2},{4,5},{5,4},{6,7},{7,6},{8,9},{9,8},{10,11... | collective-permute-start | bytes 995336 | tf_op jit(solution)/shard_map/ppermute | solution.py:767
  29.3 7.3 %collective-permute-start.12 = (bf16[432,384]{1,0:T(8,128)(2,1)}, bf16[432,384]{1,0:T(8,128)(2,1)S(1)}, u32[]{:S(2)}, u32[]{:S(2)}) collective-permute-start(bf16[432,384]{1,0:T(8,128)(2,1)} %collective-permute-done.7.refs_2_), channel_id=1, source_target_pairs={{0,1},{1,0},{2,3},{3,2},{4,5},{5,4},{6,7},{7,6},{8,9},{9,8},{10,11... | collective-permute-start | bytes 995336 | tf_op jit(solution)/shard_map/ppermute | solution.py:767
  55.8 9.9 %collective-permute-start.35 = (bf16[384,384]{1,0:T(8,128)(2,1)S(1)}, bf16[384,384]{1,0:T(8,128)(2,1)S(1)}, u32[]{:S(2)}, u32[]{:S(2)}) collective-permute-start(bf16[384,384]{1,0:T(8,128)(2,1)S(1)} %get-tuple-element.93), channel_id=1, source_target_pairs={{0,8},{8,0},{16,24},{24,16},{1,9},{9,1},{17,25},{25,17},{2,10},{10... | collective-permute-start | bytes 884744 | tf_op jit(solution)/shard_map/ppermute | solution.py:767
  57.4 15.1 %collective-permute-start.36 = (bf16[384,384]{1,0:T(8,128)(2,1)S(1)}, bf16[384,384]{1,0:T(8,128)(2,1)S(1)}, u32[]{:S(2)}, u32[]{:S(2)}) collective-permute-start(bf16[384,384]{1,0:T(8,128)(2,1)S(1)} %get-tuple-element.92), channel_id=1, source_target_pairs={{0,16},{8,24},{16,0},{24,8},{1,17},{9,25},{17,1},{25,9},{2,18},{10... | collective-permute-start | bytes 884744 | tf_op jit(solution)/shard_map/ppermute | solution.py:767
  57.9 14.7 %collective-permute-start.37 = (bf16[384,384]{1,0:T(8,128)(2,1)S(1)}, bf16[384,384]{1,0:T(8,128)(2,1)S(1)}, u32[]{:S(2)}, u32[]{:S(2)}) collective-permute-start(bf16[384,384]{1,0:T(8,128)(2,1)S(1)} %get-tuple-element.91), channel_id=1, source_target_pairs={{0,24},{8,16},{16,8},{24,0},{1,25},{9,17},{17,9},{25,1},{2,26},{10... | collective-permute-start | bytes 884744 | tf_op jit(solution)/shard_map/ppermute | solution.py:767
  73.3 9.3 %collective-permute-start.40 = (bf16[96,384]{1,0:T(8,128)(2,1)S(1)}, bf16[96,384]{1,0:T(8,128)(2,1)S(1)}, u32[]{:S(2)}, u32[]{:S(2)}) collective-permute-start(bf16[96,384]{1,0:T(8,128)(2,1)S(1)} %get-tuple-element.84), channel_id=1, source_target_pairs={{0,6},{1,7},{2,4},{3,5},{4,2},{5,3},{6,0},{7,1},{8,14},{9,15},{10,... | collective-permute-start | bytes 221192 | tf_op jit(solution)/shard_map/ppermute | solution.py:767
  74.8 7.8 %collective-permute-start.39 = (bf16[96,384]{1,0:T(8,128)(2,1)S(1)}, bf16[96,384]{1,0:T(8,128)(2,1)S(1)}, u32[]{:S(2)}, u32[]{:S(2)}) collective-permute-start(bf16[96,384]{1,0:T(8,128)(2,1)S(1)} %get-tuple-element.83), channel_id=1, source_target_pairs={{0,4},{1,5},{2,6},{3,7},{4,0},{5,1},{6,2},{7,3},{8,12},{9,13},{10,... | collective-permute-start | bytes 221192 | tf_op jit(solution)/shard_map/ppermute | solution.py:767
  80.9 12.5 %collective-permute-start.17 = (bf16[4,192,384]{2,1,0:T(8,128)(2,1)S(1)}, bf16[4,192,384]{2,1,0:T(8,128)(2,1)S(1)}, u32[]{:S(2)}, u32[]{:S(2)}) collective-permute-start(bf16[4,192,384]{2,1,0:T(8,128)(2,1)S(1)} %get-tuple-element.69), channel_id=1, source_target_pairs={{0,1},{1,0},{2,3},{3,2},{4,5},{5,4},{6,7},{7,6},{8,9},{9,8},{10,11... | collective-permute-start | bytes 1769480 | tf_op jit(solution)/shard_map/ppermute | solution.py:767
  82.0 17.8 %collective-permute-start.31 = (bf16[864,384]{1,0:T(8,128)(2,1)S(1)}, bf16[864,384]{1,0:T(8,128)(2,1)S(1)}, u32[]{:S(2)}, u32[]{:S(2)}) collective-permute-start(bf16[864,384]{1,0:T(8,128)(2,1)S(1)} %prep.5), channel_id=1, source_target_pairs={{0,8},{8,0},{16,24},{24,16},{1,9},{9,1},{17,25},{25,17},{2,10},{10... | collective-permute-start | bytes 1990664 | tf_op jit(solution)/shard_map/ppermute | solution.py:767
  82.7 7.1 %collective-permute-start.43 = (bf16[96,384]{1,0:T(8,128)(2,1)S(1)}, bf16[96,384]{1,0:T(8,128)(2,1)S(1)}, u32[]{:S(2)}, u32[]{:S(2)}) collective-permute-start(bf16[96,384]{1,0:T(8,128)(2,1)S(1)} %add_convert_fusion.3), channel_id=1, source_target_pairs={{0,6},{1,7},{2,4},{3,5},{4,2},{5,3},{6,0},{7,1},{8,14},{9,15},{10,... | collective-permute-start | bytes 221192 | tf_op jit(solution)/shard_map/ppermute | solution.py:767
  84.1 8.0 %collective-permute-start.42 = (bf16[96,384]{1,0:T(8,128)(2,1)S(1)}, bf16[96,384]{1,0:T(8,128)(2,1)S(1)}, u32[]{:S(2)}, u32[]{:S(2)}) collective-permute-start(bf16[96,384]{1,0:T(8,128)(2,1)S(1)} %add_convert_fusion.3), channel_id=1, source_target_pairs={{0,4},{1,5},{2,6},{3,7},{4,0},{5,1},{6,2},{7,3},{8,12},{9,13},{10,... | collective-permute-start | bytes 221192 | tf_op jit(solution)/shard_map/ppermute | solution.py:767
  84.8 7.2 %collective-permute-start.41 = (bf16[96,384]{1,0:T(8,128)(2,1)S(1)}, bf16[96,384]{1,0:T(8,128)(2,1)S(1)}, u32[]{:S(2)}, u32[]{:S(2)}) collective-permute-start(bf16[96,384]{1,0:T(8,128)(2,1)S(1)} %add_convert_fusion.3), channel_id=1, source_target_pairs={{0,2},{1,3},{2,0},{3,1},{4,6},{5,7},{6,4},{7,5},{8,10},{9,11},{10,... | collective-permute-start | bytes 221192 | tf_op jit(solution)/shard_map/ppermute | solution.py:767
  92.2 21.0 %collective-permute-start.44 = (bf16[4,96,384]{2,1,0:T(8,128)(2,1)S(1)}, bf16[4,96,384]{2,1,0:T(8,128)(2,1)S(1)}, u32[]{:S(2)}, u32[]{:S(2)}) collective-permute-start(bf16[4,96,384]{2,1,0:T(8,128)(2,1)S(1)} %get-tuple-element.95), channel_id=1, source_target_pairs={{0,16},{8,24},{16,0},{24,8},{1,17},{9,25},{17,1},{25,9},{2,18},{10... | collective-permute-start | bytes 884744 | tf_op jit(solution)/shard_map/ppermute | solution.py:767
  93.5 9.8 %collective-permute-start.18 = (bf16[208,384]{1,0:T(8,128)(2,1)S(1)}, bf16[208,384]{1,0:T(8,128)(2,1)S(1)}, u32[]{:S(2)}, u32[]{:S(2)}) collective-permute-start(bf16[208,384]{1,0:T(8,128)(2,1)S(1)} %get-tuple-element.71), channel_id=1, source_target_pairs={{0,8},{8,0},{16,24},{24,16},{1,9},{9,1},{17,25},{25,17},{2,10},{10... | collective-permute-start | bytes 479240 | tf_op jit(solution)/shard_map/ppermute | solution.py:767
  94.3 13.7 %collective-permute-start.19 = (bf16[208,384]{1,0:T(8,128)(2,1)S(1)}, bf16[208,384]{1,0:T(8,128)(2,1)S(1)}, u32[]{:S(2)}, u32[]{:S(2)}) collective-permute-start(bf16[208,384]{1,0:T(8,128)(2,1)S(1)} %get-tuple-element.72), channel_id=1, source_target_pairs={{0,16},{8,24},{16,0},{24,8},{1,17},{9,25},{17,1},{25,9},{2,18},{10... | collective-permute-start | bytes 479240 | tf_op jit(solution)/shard_map/ppermute | solution.py:767
  95.9 12.1 %collective-permute-start.20 = (bf16[208,384]{1,0:T(8,128)(2,1)S(1)}, bf16[208,384]{1,0:T(8,128)(2,1)S(1)}, u32[]{:S(2)}, u32[]{:S(2)}) collective-permute-start(bf16[208,384]{1,0:T(8,128)(2,1)S(1)} %get-tuple-element.73), channel_id=1, source_target_pairs={{0,24},{8,16},{16,8},{24,0},{1,25},{9,17},{17,9},{25,1},{2,26},{10... | collective-permute-start | bytes 479240 | tf_op jit(solution)/shard_map/ppermute | solution.py:767
  99.9 34.2 %collective-permute-start.32 = (bf16[864,384]{1,0:T(8,128)(2,1)S(1)}, bf16[864,384]{1,0:T(8,128)(2,1)S(1)}, u32[]{:S(2)}, u32[]{:S(2)}) collective-permute-start(bf16[864,384]{1,0:T(8,128)(2,1)S(1)} %collective-permute-done.31.fx0), channel_id=1, source_target_pairs={{0,1},{1,0},{2,3},{3,2},{4,5},{5,4},{6,7},{7,6},{8,9},{9,8},{10,11... | collective-permute-start | bytes 1990664 | tf_op jit(solution)/shard_map/ppermute | solution.py:767
  108.7 7.4 %collective-permute-start.23 = (bf16[112,384]{1,0:T(8,128)(2,1)S(1)}, bf16[112,384]{1,0:T(8,128)(2,1)S(1)}, u32[]{:S(2)}, u32[]{:S(2)}) collective-permute-start(bf16[112,384]{1,0:T(8,128)(2,1)S(1)} %get-tuple-element.77), channel_id=1, source_target_pairs={{0,6},{1,7},{2,4},{3,5},{4,2},{5,3},{6,0},{7,1},{8,14},{9,15},{10,... | collective-permute-start | bytes 258056 | tf_op jit(solution)/shard_map/ppermute | solution.py:767
  110.1 7.7 %collective-permute-start.22 = (bf16[112,384]{1,0:T(8,128)(2,1)S(1)}, bf16[112,384]{1,0:T(8,128)(2,1)S(1)}, u32[]{:S(2)}, u32[]{:S(2)}) collective-permute-start(bf16[112,384]{1,0:T(8,128)(2,1)S(1)} %get-tuple-element.76), channel_id=1, source_target_pairs={{0,4},{1,5},{2,6},{3,7},{4,0},{5,1},{6,2},{7,3},{8,12},{9,13},{10,... | collective-permute-start | bytes 258056 | tf_op jit(solution)/shard_map/ppermute | solution.py:767
  110.1 7.7 %collective-permute-start.21 = (bf16[112,384]{1,0:T(8,128)(2,1)S(1)}, bf16[112,384]{1,0:T(8,128)(2,1)S(1)}, u32[]{:S(2)}, u32[]{:S(2)}) collective-permute-start(bf16[112,384]{1,0:T(8,128)(2,1)S(1)} %get-tuple-element.75), channel_id=1, source_target_pairs={{0,2},{1,3},{2,0},{3,1},{4,6},{5,7},{6,4},{7,5},{8,10},{9,11},{10,... | collective-permute-start | bytes 258056 | tf_op jit(solution)/shard_map/ppermute | solution.py:767
  113.2 20.9 %collective-permute-start.45 = (bf16[2,4,96,384]{3,2,1,0:T(8,128)(2,1)S(1)}, bf16[2,4,96,384]{3,2,1,0:T(8,128)(2,1)S(1)}, u32[]{:S(2)}, u32[]{:S(2)}) collective-permute-start(bf16[2,4,96,384]{3,2,1,0:T(8,128)(2,1)S(1)} %pad_maximum_fusion.1.ch0), channel_id=1, source_target_pairs={{0,1},{1,0},{2,3},{3,2},{4,5},{5,4},{6,7},{7,6},{8,9},{9,8},{10,11... | collective-permute-start | bytes 1769480 | tf_op jit(solution)/shard_map/ppermute | solution.py:767
  124.8 7.5 %collective-permute-start.29 = (bf16[4,48,384]{2,1,0:T(8,128)(2,1)S(1)}, bf16[4,48,384]{2,1,0:T(8,128)(2,1)S(1)}, u32[]{:S(2)}, u32[]{:S(2)}) collective-permute-start(bf16[4,48,384]{2,1,0:T(8,128)(2,1)S(1)} %get-tuple-element.97), channel_id=1, source_target_pairs={{0,24},{8,16},{16,8},{24,0},{1,25},{9,17},{17,9},{25,1},{2,26},{10... | collective-permute-start | bytes 442376 | tf_op jit(solution)/shard_map/ppermute | solution.py:767
  126.3 7.6 %collective-permute-start.28 = (bf16[4,48,384]{2,1,0:T(8,128)(2,1)S(1)}, bf16[4,48,384]{2,1,0:T(8,128)(2,1)S(1)}, u32[]{:S(2)}, u32[]{:S(2)}) collective-permute-start(bf16[4,48,384]{2,1,0:T(8,128)(2,1)S(1)} %get-tuple-element.97), channel_id=1, source_target_pairs={{0,16},{8,24},{16,0},{24,8},{1,17},{9,25},{17,1},{25,9},{2,18},{10... | collective-permute-start | bytes 442376 | tf_op jit(solution)/shard_map/ppermute | solution.py:767
  134.0 12.2 %collective-permute-start.30 = (bf16[4,4,48,384]{3,2,1,0:T(8,128)(2,1)S(1)}, bf16[4,4,48,384]{3,2,1,0:T(8,128)(2,1)S(1)}, u32[]{:S(2)}, u32[]{:S(2)}) collective-permute-start(bf16[4,4,48,384]{3,2,1,0:T(8,128)(2,1)S(1)} %pad_maximum_fusion.ch0), channel_id=1, source_target_pairs={{0,1},{1,0},{2,3},{3,2},{4,5},{5,4},{6,7},{7,6},{8,9},{9,8},{10,11... | collective-permute-start | bytes 1769480 | tf_op jit(solution)/shard_map/ppermute | solution.py:767
  142.6 10.5 %collective-permute-start.46 = (bf16[2,192,384]{2,1,0:T(8,128)(2,1)S(1)}, bf16[2,192,384]{2,1,0:T(8,128)(2,1)S(1)}, u32[]{:S(2)}, u32[]{:S(2)}) collective-permute-start(bf16[2,192,384]{2,1,0:T(8,128)(2,1)S(1)} %get-tuple-element.87), channel_id=1, source_target_pairs={{16,24},{17,25},{18,26},{19,27},{20,28},{21,29},{22,30},{23,31}} | collective-permute-start | bytes 884744 | tf_op jit(solution)/shard_map/ppermute | solution.py:934
  (23 other events, 165.2 us)

commit v7 on v6

--- a/solution.py
+++ b/solution.py
@@ -851,7 +851,8 @@
     got = []
     for m, piece in enumerate(pieces, 1):
         got.append(swap(piece, "rep", 2 * m))
-    return wide_sum([mine] + [g[:n] for g in got]).astype(BF16), [g[n:] for g in got]
+    total = wide_sum([mine] + [g[:n] for g in got]).astype(BF16)
+    return total, [g[n:] for g in got]
 
 
 def fan(x, axis, masks):
@@ -914,7 +915,8 @@
     mine, *pieces = piece_call(sidx, keep1, other, got)
     total, _ = z_sum(mine, pieces)
     col = fan(total, "rep", (2, 4, 6))
-    pair = fan(col, "fsdp", (2,))
+    across = swap(col, "fsdp", 2)
+    pair = jnp.stack([col, across])
     pairs = (pair, swap(pair, "rep", 1))
 
     other = swap(send2, "rep", 1)

time: 163 us -> 163 us (level)
  no operation moved by 1% of the time
where the time goes in v7:
time: 163 us
  waiting for transfers between devices  63.9 us (39%)
  Pallas kernels  46.9 us (29%)
  starting transfers between devices  46.6 us (29%)
  local copies, waits for them, and re-layouts  2.93 us (2%)
    ppermute x46, waiting for transfers between devices, swap(): return lax.ppermute(x, axis, [(i, i ^ mask) for i in range(count)])  57.1 us
    ppermute x46, starting transfers between devices, swap(): return lax.ppermute(x, axis, [(i, i ^ mask) for i in range(count)])  42.9 us
    pallas_call x1, Pallas kernels, main_call(): pl.pallas_call(functools.partial(main_kernel, len(bufs), fast, rows), out...  15.8 us
    pallas_call x1, Pallas kernels, final_call(): pl.pallas_call(final_kernel, out_shape=(sd, sd, sd), in_specs=[sspec()] *...  9.54 us
    pallas_call x1, Pallas kernels, ns_a(): pl.pallas_call(ns_a_kernel, out_shape=(sd, sd, jax.ShapeDtypeStruct((2, 4...  8.43 us
    ppermute x1, waiting for transfers between devices, fast_body(): tail = lax.ppermute(tail, 'fsdp', [(2, 3)])  6.86 us
    pallas_call x1, Pallas kernels, heads_call(): pl.pallas_call(functools.partial(heads_kernel, rows), out_shape=jax.Shape...  4.9 us
    ppermute x1, starting transfers between devices, fast_body(): tail = lax.ppermute(tail, 'fsdp', [(2, 3)])  3.62 us
  transfers between devices with their start and end apart: 47, of which 24 were waited for; matrix products, arithmetic and copies ran while one was open for 1% of the time, Pallas kernels for 13%

profile of v7, /device:TPU:4, one launch (start us, length us, event | category | flops | bytes accessed | tf_op | source)
XLA Modules:
  0.0 162.8 jit_solution(11071638940124686581)
XLA Ops:
  3.0 1.7 %copy-done = f32[663552]{0:T(1024)S(1)} copy-done((f32[663552]{0:T(1024)S(1)}, f32[663552]{0:T(1024)}, u32[]{:S(2)}) %copy-start) | copy-done | bytes 2654232
  4.7 1.7 %prep.3 = (bf16[432,384]{1,0:T(8,128)(2,1)}, bf16[432,384]{1,0:T(8,128)(2,1)}) custom-call(s32[5]{0:T(128)S(1)} %pad_add_fusion.s_ref, f32[5184,128]{1,0:T(8,128)S(1)} %bitcast.34), custom_call_target="tpu_custom_call" | custom-call | bytes 4000000 | tf_op jit(solution)/shard_map/prep/pallas_call | solution.py:111
  7.1 1.9 %collective-permute-start.2 = (bf16[432,384]{1,0:T(8,128)(2,1)}, bf16[432,384]{1,0:T(8,128)(2,1)S(1)}, u32[]{:S(2)}, u32[]{:S(2)}) collective-permute-start(bf16[432,384]{1,0:T(8,128)(2,1)} %get-tuple-element.51), channel_id=1, source_target_pairs={{0,16},{8,24},{16,0},{24,8},{1,17},{9,25},{17,1},{25,9},{2,18},{10... | collective-permute-start | bytes 995336 | tf_op jit(solution)/shard_map/ppermute | solution.py:767
  11.4 1.6 %collective-permute-start.5 = (bf16[16,384]{1,0:T(8,128)(2,1)S(1)}, bf16[16,384]{1,0:T(8,128)(2,1)S(1)}, u32[]{:S(2)}, u32[]{:S(2)}) collective-permute-start(bf16[16,384]{1,0:T(8,128)(2,1)S(1)} %pad_maximum_fusion.6), channel_id=1, source_target_pairs={{0,2},{1,3},{2,0},{3,1},{4,6},{5,7},{6,4},{7,5},{8,10},{9,11},{10,... | collective-permute-start | bytes 36872 | tf_op jit(solution)/shard_map/ppermute | solution.py:767
  13.0 2.1 %collective-permute-done.5 = bf16[16,384]{1,0:T(8,128)(2,1)S(1)} collective-permute-done((bf16[16,384]{1,0:T(8,128)(2,1)S(1)}, bf16[16,384]{1,0:T(8,128)(2,1)S(1)}, u32[]{:S(2)}, u32[]{:S(2)}) %collective-permute-start.5) | collective-permute-done | bytes 12320 | tf_op jit(solution)/shard_map/ppermute | solution.py:767
  15.2 2.7 %collective-permute-start.6 = (bf16[32,384]{1,0:T(8,128)(2,1)S(1)}, bf16[32,384]{1,0:T(8,128)(2,1)S(1)}, u32[]{:S(2)}, u32[]{:S(2)}) collective-permute-start(bf16[32,384]{1,0:T(8,128)(2,1)S(1)} %pad_maximum_fusion.5), channel_id=1, source_target_pairs={{0,4},{1,5},{2,6},{3,7},{4,0},{5,1},{6,2},{7,3},{8,12},{9,13},{10,... | collective-permute-start | bytes 73736 | tf_op jit(solution)/shard_map/ppermute | solution.py:767
  22.0 6.8 %collective-permute-done.7.refs_2_ = bf16[432,384]{1,0:T(8,128)(2,1)} collective-permute-done((bf16[432,384]{1,0:T(8,128)(2,1)}, bf16[432,384]{1,0:T(8,128)(2,1)}, u32[]{:S(2)}, u32[]{:S(2)}) %collective-permute-start.7) | collective-permute-done | bytes 331808 | tf_op jit(solution)/shard_map/ppermute | solution.py:767
  29.3 4.8 %collective-permute-done.9.refs_5_ = bf16[432,384]{1,0:T(8,128)(2,1)S(1)} collective-permute-done((bf16[432,384]{1,0:T(8,128)(2,1)S(1)}, bf16[432,384]{1,0:T(8,128)(2,1)S(1)}, u32[]{:S(2)}, u32[]{:S(2)}) %collective-permute-start.9) | collective-permute-done | bytes 331808 | tf_op jit(solution)/shard_map/ppermute | solution.py:767
  36.9 15.8 %main.1 = (bf16[512,384]{1,0:T(8,128)(2,1)}, bf16[3,512,384]{2,1,0:T(8,128)(2,1)S(1)}, f32[12,256,256]{2,1,0:T(8,128)S(1)}, bf16[512,384]{1,0:T(8,128)(2,1)S(1)}...) custom-call(s32[5]{0:T(128)S(1)} %pad_add_fusion.s_ref, ...), custom_call_target="tpu_custom_call" | custom-call | flops 20000000000 | bytes 30000000 | tf_op jit(solution)/shard_map/main/pallas_call | solution.py:341
  53.0 2.6 %collective-permute-done.34.other = bf16[4,384,384]{2,1,0:T(8,128)(2,1)S(1)} collective-permute-done((bf16[4,384,384]{2,1,0:T(8,128)(2,1)S(1)}, bf16[4,384,384]{2,1,0:T(8,128)(2,1)S(1)}, u32[]{:S(2)}, u32[]{:S(2)}) %collective-permute-start.34) | collective-permute-done | bytes 1179680 | tf_op jit(solution)/shard_map/ppermute | solution.py:767
  55.8 1.6 collective-permute-start.35
  59.4 4.9 %heads.1.gqkv = bf16[3,512,384]{2,1,0:T(8,128)(2,1)S(1)} custom-call(bf16[3,512,384]{2,1,0:T(8,128)(2,1)S(1)} %get-tuple-element.57.qkv, f32[12,256,256]{2,1,0:T(8,128)S(1)} %get-tuple-element.58.probs, bf16[512,384]{1,0:T(8,128)(2,1)S(1)} %get-tuple-element.59.gmx), custom_call_target="tpu_custom_call" | custom-call | flops 6000000000 | bytes 6000000 | tf_op jit(solution)/shard_map/heads/pallas_call | solution.py:394
  65.8 6.8 %collective-permute-done.36.refs_1_ = bf16[384,384]{1,0:T(8,128)(2,1)S(1)} collective-permute-done((bf16[384,384]{1,0:T(8,128)(2,1)S(1)}, bf16[384,384]{1,0:T(8,128)(2,1)S(1)}, u32[]{:S(2)}, u32[]{:S(2)}) %collective-permute-start.36) | collective-permute-done | bytes 294944 | tf_op jit(solution)/shard_map/ppermute | solution.py:767
  74.8 1.7 %collective-permute-start.39 = (bf16[96,384]{1,0:T(8,128)(2,1)S(1)}, bf16[96,384]{1,0:T(8,128)(2,1)S(1)}, u32[]{:S(2)}, u32[]{:S(2)}) collective-permute-start(bf16[96,384]{1,0:T(8,128)(2,1)S(1)} %get-tuple-element.83), channel_id=1, source_target_pairs={{0,4},{1,5},{2,6},{3,7},{4,0},{5,1},{6,2},{7,3},{8,12},{9,13},{10,... | collective-permute-start | bytes 221192 | tf_op jit(solution)/shard_map/ppermute | solution.py:767
  77.8 3.1 %input.1 = (f32[512,384]{1,0:T(8,128)}, f32[4,192,384]{2,1,0:T(8,128)S(1)}, bf16[4,192,384]{2,1,0:T(8,128)(2,1)S(1)}, bf16[16,384]{1,0:T(8,128)(2,1)S(1)}) custom-call(s32[5]{0:T(128)S(1)} %pad_add_fusion.s_ref, bf16[512,384]{1,0:T(8,128)(2,1)S(1)} %bitcast.41, bf16[3,512,384]{2,1,0:T(8,128)(2,1)S(1)} %heads.1.gqkv, ...), custom_call_target="tpu_custom_call" | custom-call | flops 6000000000 | bytes 6000000 | tf_op jit(solution)/shard_map/input/pallas_call | solution.py:439
  84.8 2.3 %collective-permute-start.41 = (bf16[96,384]{1,0:T(8,128)(2,1)S(1)}, bf16[96,384]{1,0:T(8,128)(2,1)S(1)}, u32[]{:S(2)}, u32[]{:S(2)}) collective-permute-start(bf16[96,384]{1,0:T(8,128)(2,1)S(1)} %add_convert_fusion.3), channel_id=1, source_target_pairs={{0,2},{1,3},{2,0},{3,1},{4,6},{5,7},{6,4},{7,5},{8,10},{9,11},{10,... | collective-permute-start | bytes 221192 | tf_op jit(solution)/shard_map/ppermute | solution.py:767
  87.1 2.6 %collective-permute-done.43 = bf16[96,384]{1,0:T(8,128)(2,1)S(1)} collective-permute-done((bf16[96,384]{1,0:T(8,128)(2,1)S(1)}, bf16[96,384]{1,0:T(8,128)(2,1)S(1)}, u32[]{:S(2)}, u32[]{:S(2)}) %collective-permute-start.43) | collective-permute-done | bytes 73760 | tf_op jit(solution)/shard_map/ppermute | solution.py:767
  89.8 2.3 %collective-permute-done.42 = bf16[96,384]{1,0:T(8,128)(2,1)S(1)} collective-permute-done((bf16[96,384]{1,0:T(8,128)(2,1)S(1)}, bf16[96,384]{1,0:T(8,128)(2,1)S(1)}, u32[]{:S(2)}, u32[]{:S(2)}) %collective-permute-start.42) | collective-permute-done | bytes 73760 | tf_op jit(solution)/shard_map/ppermute | solution.py:767
  97.1 2.8 %collective-permute-done.31.fx0 = bf16[864,384]{1,0:T(8,128)(2,1)S(1)} collective-permute-done((bf16[864,384]{1,0:T(8,128)(2,1)S(1)}, bf16[864,384]{1,0:T(8,128)(2,1)S(1)}, u32[]{:S(2)}, u32[]{:S(2)}) %collective-permute-start.31) | collective-permute-done | bytes 663584 | tf_op jit(solution)/shard_map/ppermute | solution.py:767
  99.9 3.4 %collective-permute-done.18.refs_1_ = bf16[208,384]{1,0:T(8,128)(2,1)S(1)} collective-permute-done((bf16[208,384]{1,0:T(8,128)(2,1)S(1)}, bf16[208,384]{1,0:T(8,128)(2,1)S(1)}, u32[]{:S(2)}, u32[]{:S(2)}) %collective-permute-start.18) | collective-permute-done | bytes 159776 | tf_op jit(solution)/shard_map/ppermute | solution.py:767
  103.3 4.7 %collective-permute-done.19.refs_2_ = bf16[208,384]{1,0:T(8,128)(2,1)S(1)} collective-permute-done((bf16[208,384]{1,0:T(8,128)(2,1)S(1)}, bf16[208,384]{1,0:T(8,128)(2,1)S(1)}, u32[]{:S(2)}, u32[]{:S(2)}) %collective-permute-start.19) | collective-permute-done | bytes 159776 | tf_op jit(solution)/shard_map/ppermute | solution.py:767
  110.1 3.0 %collective-permute-start.21 = (bf16[112,384]{1,0:T(8,128)(2,1)S(1)}, bf16[112,384]{1,0:T(8,128)(2,1)S(1)}, u32[]{:S(2)}, u32[]{:S(2)}) collective-permute-start(bf16[112,384]{1,0:T(8,128)(2,1)S(1)} %get-tuple-element.75), channel_id=1, source_target_pairs={{0,2},{1,3},{2,0},{3,1},{4,6},{5,7},{6,4},{7,5},{8,10},{9,11},{10,... | collective-permute-start | bytes 258056 | tf_op jit(solution)/shard_map/ppermute | solution.py:767
  113.3 2.8 %collective-permute-done.23 = bf16[112,384]{1,0:T(8,128)(2,1)S(1)} collective-permute-done((bf16[112,384]{1,0:T(8,128)(2,1)S(1)}, bf16[112,384]{1,0:T(8,128)(2,1)S(1)}, u32[]{:S(2)}, u32[]{:S(2)}) %collective-permute-start.23) | collective-permute-done | bytes 86048 | tf_op jit(solution)/shard_map/ppermute | solution.py:767
  116.0 1.8 %collective-permute-done.22 = bf16[112,384]{1,0:T(8,128)(2,1)S(1)} collective-permute-done((bf16[112,384]{1,0:T(8,128)(2,1)S(1)}, bf16[112,384]{1,0:T(8,128)(2,1)S(1)}, u32[]{:S(2)}, u32[]{:S(2)}) %collective-permute-start.22) | collective-permute-done | bytes 86048 | tf_op jit(solution)/shard_map/ppermute | solution.py:767
  117.9 1.9 %collective-permute-start.26 = (bf16[48,384]{1,0:T(8,128)(2,1)S(1)}, bf16[48,384]{1,0:T(8,128)(2,1)S(1)}, u32[]{:S(2)}, u32[]{:S(2)}) collective-permute-start(bf16[48,384]{1,0:T(8,128)(2,1)S(1)} %add_convert_fusion.4), channel_id=1, source_target_pairs={{0,6},{1,7},{2,4},{3,5},{4,2},{5,3},{6,0},{7,1},{8,14},{9,15},{10,... | collective-permute-start | bytes 110600 | tf_op jit(solution)/shard_map/ppermute | solution.py:767
  119.7 2.6 %collective-permute-start.24 = (bf16[48,384]{1,0:T(8,128)(2,1)S(1)}, bf16[48,384]{1,0:T(8,128)(2,1)S(1)}, u32[]{:S(2)}, u32[]{:S(2)}) collective-permute-start(bf16[48,384]{1,0:T(8,128)(2,1)S(1)} %add_convert_fusion.4), channel_id=1, source_target_pairs={{0,2},{1,3},{2,0},{3,1},{4,6},{5,7},{6,4},{7,5},{8,10},{9,11},{10,... | collective-permute-start | bytes 110600 | tf_op jit(solution)/shard_map/ppermute | solution.py:767
  126.3 1.6 collective-permute-start.28
  128.5 3.8 %collective-permute-done.29 = bf16[4,48,384]{2,1,0:T(8,128)(2,1)S(1)} collective-permute-done((bf16[4,48,384]{2,1,0:T(8,128)(2,1)S(1)}, bf16[4,48,384]{2,1,0:T(8,128)(2,1)S(1)}, u32[]{:S(2)}, u32[]{:S(2)}) %collective-permute-start.29) | collective-permute-done | bytes 147488 | tf_op jit(solution)/shard_map/ppermute | solution.py:767
  134.1 8.4 %ns_a.1 = (f32[6,384,384]{2,1,0:T(8,128)S(1)}, f32[6,384,384]{2,1,0:T(8,128)S(1)}, bf16[2,192,384]{2,1,0:T(8,128)(2,1)S(1)}) custom-call(s32[5]{0:T(128)S(1)} %pad_add_fusion.s_ref, s32[36]{0:T(128)S(1)} %copy-done.5, f32[27]{0:T(128)S(1)} %copy-done.6, f32[5184,128]{1,0:T(8,128)S(1)} %bitcast.38, bf16[864,384]{1,0:T(8,128)(2,1)S(1)} %collective-permute-done.31.fx0, ...), custom_call_target="tpu_custom_call" | custom-call | flops 8000000000 | bytes 12000000 | tf_op jit(solution)/shard_map/ns_a/pallas_call | solution.py:667
  142.6 3.6 %collective-permute-start.46 = (bf16[2,192,384]{2,1,0:T(8,128)(2,1)S(1)}, bf16[2,192,384]{2,1,0:T(8,128)(2,1)S(1)}, u32[]{:S(2)}, u32[]{:S(2)}) collective-permute-start(bf16[2,192,384]{2,1,0:T(8,128)(2,1)S(1)} %get-tuple-element.87), channel_id=1, source_target_pairs={{16,24},{17,25},{18,26},{19,27},{20,28},{21,29},{22,30},{23,31}} | collective-permute-start | bytes 884744 | tf_op jit(solution)/shard_map/ppermute | solution.py:936
  146.2 6.9 %collective-permute-done.46.tail = bf16[2,192,384]{2,1,0:T(8,128)(2,1)S(1)} collective-permute-done((bf16[2,192,384]{2,1,0:T(8,128)(2,1)S(1)}, bf16[2,192,384]{2,1,0:T(8,128)(2,1)S(1)}, u32[]{:S(2)}, u32[]{:S(2)}) %collective-permute-start.46) | collective-permute-done | bytes 294944 | tf_op jit(solution)/shard_map/ppermute | solution.py:936
  153.1 9.5 %finish.1 = (f32[5184,128]{1,0:T(8,128)}, f32[5184,128]{1,0:T(8,128)}, f32[5184,128]{1,0:T(8,128)}) custom-call(s32[5]{0:T(128)S(1)} %pad_add_fusion.s_ref, s32[36]{0:T(128)S(1)} %copy-done.5, f32[27]{0:T(128)S(1)} %copy-done.6, f32[5184,128]{1,0:T(8,128)S(1)} %bitcast.36, f32[5184,128]{1,0:T(8,128)S(1)} %bitcast.39, ...), custom_call_target="tpu_custom_call" | custom-call | flops 8000000000 | bytes 24000000 | tf_op jit(solution)/shard_map/finish/pallas_call | solution.py:753
  (107 shorter events, 37.7 us)
Async XLA Ops:
  7.0 13.0 %collective-permute-start.1 = (bf16[432,384]{1,0:T(8,128)(2,1)}, bf16[432,384]{1,0:T(8,128)(2,1)S(1)}, u32[]{:S(2)}, u32[]{:S(2)}) collective-permute-start(bf16[432,384]{1,0:T(8,128)(2,1)} %get-tuple-element.50), channel_id=1, source_target_pairs={{0,8},{8,0},{16,24},{24,16},{1,9},{9,1},{17,25},{25,17},{2,10},{10... | collective-permute-start | bytes 995336 | tf_op jit(solution)/shard_map/ppermute | solution.py:767
  7.1 12.9 %collective-permute-start.2 = (bf16[432,384]{1,0:T(8,128)(2,1)}, bf16[432,384]{1,0:T(8,128)(2,1)S(1)}, u32[]{:S(2)}, u32[]{:S(2)}) collective-permute-start(bf16[432,384]{1,0:T(8,128)(2,1)} %get-tuple-element.51), channel_id=1, source_target_pairs={{0,16},{8,24},{16,0},{24,8},{1,17},{9,25},{17,1},{25,9},{2,18},{10... | collective-permute-start | bytes 995336 | tf_op jit(solution)/shard_map/ppermute | solution.py:767
  17.8 11.0 %collective-permute-start.7 = (bf16[432,384]{1,0:T(8,128)(2,1)}, bf16[432,384]{1,0:T(8,128)(2,1)}, u32[]{:S(2)}, u32[]{:S(2)}) collective-permute-start(bf16[432,384]{1,0:T(8,128)(2,1)} %get-tuple-element.51), channel_id=1, source_target_pairs={{0,8},{8,0},{16,24},{24,16},{1,9},{9,1},{17,25},{25,17},{2,10},{10... | collective-permute-start | bytes 995336 | tf_op jit(solution)/shard_map/ppermute | solution.py:767
  18.3 11.0 %collective-permute-start.8 = (bf16[432,384]{1,0:T(8,128)(2,1)}, bf16[432,384]{1,0:T(8,128)(2,1)}, u32[]{:S(2)}, u32[]{:S(2)}) collective-permute-start(bf16[432,384]{1,0:T(8,128)(2,1)} %get-tuple-element.50), channel_id=1, source_target_pairs={{0,16},{8,24},{16,0},{24,8},{1,17},{9,25},{17,1},{25,9},{2,18},{10... | collective-permute-start | bytes 995336 | tf_op jit(solution)/shard_map/ppermute | solution.py:767
  20.0 14.1 %collective-permute-start.9 = (bf16[432,384]{1,0:T(8,128)(2,1)S(1)}, bf16[432,384]{1,0:T(8,128)(2,1)S(1)}, u32[]{:S(2)}, u32[]{:S(2)}) collective-permute-start(bf16[432,384]{1,0:T(8,128)(2,1)S(1)} %collective-permute-done.1.refs_1_), channel_id=1, source_target_pairs={{0,16},{8,24},{16,0},{24,8},{1,17},{9,25},{17,1},{25,9},{2,18},{10... | collective-permute-start | bytes 995336 | tf_op jit(solution)/shard_map/ppermute | solution.py:767
  20.6 13.5 %collective-permute-start.10 = (bf16[432,384]{1,0:T(8,128)(2,1)S(1)}, bf16[432,384]{1,0:T(8,128)(2,1)S(1)}, u32[]{:S(2)}, u32[]{:S(2)}) collective-permute-start(bf16[432,384]{1,0:T(8,128)(2,1)S(1)} %collective-permute-done.2.refs_4_), channel_id=1, source_target_pairs={{0,8},{8,0},{16,24},{24,16},{1,9},{9,1},{17,25},{25,17},{2,10},{10... | collective-permute-start | bytes 995336 | tf_op jit(solution)/shard_map/ppermute | solution.py:767
  22.0 12.6 %collective-permute-start.11 = (bf16[432,384]{1,0:T(8,128)(2,1)S(1)}, bf16[432,384]{1,0:T(8,128)(2,1)S(1)}, u32[]{:S(2)}, u32[]{:S(2)}) collective-permute-start(bf16[432,384]{1,0:T(8,128)(2,1)S(1)} %collective-permute-done.1.refs_1_), channel_id=1, source_target_pairs={{0,1},{1,0},{2,3},{3,2},{4,5},{5,4},{6,7},{7,6},{8,9},{9,8},{10,11... | collective-permute-start | bytes 995336 | tf_op jit(solution)/shard_map/ppermute | solution.py:767
  28.8 7.8 %collective-permute-start.14 = (bf16[432,384]{1,0:T(8,128)(2,1)S(1)}, bf16[432,384]{1,0:T(8,128)(2,1)S(1)}, u32[]{:S(2)}, u32[]{:S(2)}) collective-permute-start(bf16[432,384]{1,0:T(8,128)(2,1)S(1)} %collective-permute-done.2.refs_4_), channel_id=1, source_target_pairs={{0,1},{1,0},{2,3},{3,2},{4,5},{5,4},{6,7},{7,6},{8,9},{9,8},{10,11... | collective-permute-start | bytes 995336 | tf_op jit(solution)/shard_map/ppermute | solution.py:767
  29.3 7.3 %collective-permute-start.12 = (bf16[432,384]{1,0:T(8,128)(2,1)}, bf16[432,384]{1,0:T(8,128)(2,1)S(1)}, u32[]{:S(2)}, u32[]{:S(2)}) collective-permute-start(bf16[432,384]{1,0:T(8,128)(2,1)} %collective-permute-done.7.refs_2_), channel_id=1, source_target_pairs={{0,1},{1,0},{2,3},{3,2},{4,5},{5,4},{6,7},{7,6},{8,9},{9,8},{10,11... | collective-permute-start | bytes 995336 | tf_op jit(solution)/shard_map/ppermute | solution.py:767
  55.8 9.9 %collective-permute-start.35 = (bf16[384,384]{1,0:T(8,128)(2,1)S(1)}, bf16[384,384]{1,0:T(8,128)(2,1)S(1)}, u32[]{:S(2)}, u32[]{:S(2)}) collective-permute-start(bf16[384,384]{1,0:T(8,128)(2,1)S(1)} %get-tuple-element.93), channel_id=1, source_target_pairs={{0,8},{8,0},{16,24},{24,16},{1,9},{9,1},{17,25},{25,17},{2,10},{10... | collective-permute-start | bytes 884744 | tf_op jit(solution)/shard_map/ppermute | solution.py:767
  57.4 15.1 %collective-permute-start.36 = (bf16[384,384]{1,0:T(8,128)(2,1)S(1)}, bf16[384,384]{1,0:T(8,128)(2,1)S(1)}, u32[]{:S(2)}, u32[]{:S(2)}) collective-permute-start(bf16[384,384]{1,0:T(8,128)(2,1)S(1)} %get-tuple-element.92), channel_id=1, source_target_pairs={{0,16},{8,24},{16,0},{24,8},{1,17},{9,25},{17,1},{25,9},{2,18},{10... | collective-permute-start | bytes 884744 | tf_op jit(solution)/shard_map/ppermute | solution.py:767
  57.9 14.7 %collective-permute-start.37 = (bf16[384,384]{1,0:T(8,128)(2,1)S(1)}, bf16[384,384]{1,0:T(8,128)(2,1)S(1)}, u32[]{:S(2)}, u32[]{:S(2)}) collective-permute-start(bf16[384,384]{1,0:T(8,128)(2,1)S(1)} %get-tuple-element.91), channel_id=1, source_target_pairs={{0,24},{8,16},{16,8},{24,0},{1,25},{9,17},{17,9},{25,1},{2,26},{10... | collective-permute-start | bytes 884744 | tf_op jit(solution)/shard_map/ppermute | solution.py:767
  73.3 9.3 %collective-permute-start.40 = (bf16[96,384]{1,0:T(8,128)(2,1)S(1)}, bf16[96,384]{1,0:T(8,128)(2,1)S(1)}, u32[]{:S(2)}, u32[]{:S(2)}) collective-permute-start(bf16[96,384]{1,0:T(8,128)(2,1)S(1)} %get-tuple-element.84), channel_id=1, source_target_pairs={{0,6},{1,7},{2,4},{3,5},{4,2},{5,3},{6,0},{7,1},{8,14},{9,15},{10,... | collective-permute-start | bytes 221192 | tf_op jit(solution)/shard_map/ppermute | solution.py:767
  74.8 7.8 %collective-permute-start.39 = (bf16[96,384]{1,0:T(8,128)(2,1)S(1)}, bf16[96,384]{1,0:T(8,128)(2,1)S(1)}, u32[]{:S(2)}, u32[]{:S(2)}) collective-permute-start(bf16[96,384]{1,0:T(8,128)(2,1)S(1)} %get-tuple-element.83), channel_id=1, source_target_pairs={{0,4},{1,5},{2,6},{3,7},{4,0},{5,1},{6,2},{7,3},{8,12},{9,13},{10,... | collective-permute-start | bytes 221192 | tf_op jit(solution)/shard_map/ppermute | solution.py:767
  80.9 12.5 %collective-permute-start.17 = (bf16[4,192,384]{2,1,0:T(8,128)(2,1)S(1)}, bf16[4,192,384]{2,1,0:T(8,128)(2,1)S(1)}, u32[]{:S(2)}, u32[]{:S(2)}) collective-permute-start(bf16[4,192,384]{2,1,0:T(8,128)(2,1)S(1)} %get-tuple-element.69), channel_id=1, source_target_pairs={{0,1},{1,0},{2,3},{3,2},{4,5},{5,4},{6,7},{7,6},{8,9},{9,8},{10,11... | collective-permute-start | bytes 1769480 | tf_op jit(solution)/shard_map/ppermute | solution.py:767
  82.0 17.8 %collective-permute-start.31 = (bf16[864,384]{1,0:T(8,128)(2,1)S(1)}, bf16[864,384]{1,0:T(8,128)(2,1)S(1)}, u32[]{:S(2)}, u32[]{:S(2)}) collective-permute-start(bf16[864,384]{1,0:T(8,128)(2,1)S(1)} %prep.5), channel_id=1, source_target_pairs={{0,8},{8,0},{16,24},{24,16},{1,9},{9,1},{17,25},{25,17},{2,10},{10... | collective-permute-start | bytes 1990664 | tf_op jit(solution)/shard_map/ppermute | solution.py:767
  82.7 7.1 %collective-permute-start.43 = (bf16[96,384]{1,0:T(8,128)(2,1)S(1)}, bf16[96,384]{1,0:T(8,128)(2,1)S(1)}, u32[]{:S(2)}, u32[]{:S(2)}) collective-permute-start(bf16[96,384]{1,0:T(8,128)(2,1)S(1)} %add_convert_fusion.3), channel_id=1, source_target_pairs={{0,6},{1,7},{2,4},{3,5},{4,2},{5,3},{6,0},{7,1},{8,14},{9,15},{10,... | collective-permute-start | bytes 221192 | tf_op jit(solution)/shard_map/ppermute | solution.py:767
  84.1 8.0 %collective-permute-start.42 = (bf16[96,384]{1,0:T(8,128)(2,1)S(1)}, bf16[96,384]{1,0:T(8,128)(2,1)S(1)}, u32[]{:S(2)}, u32[]{:S(2)}) collective-permute-start(bf16[96,384]{1,0:T(8,128)(2,1)S(1)} %add_convert_fusion.3), channel_id=1, source_target_pairs={{0,4},{1,5},{2,6},{3,7},{4,0},{5,1},{6,2},{7,3},{8,12},{9,13},{10,... | collective-permute-start | bytes 221192 | tf_op jit(solution)/shard_map/ppermute | solution.py:767
  84.8 7.2 %collective-permute-start.41 = (bf16[96,384]{1,0:T(8,128)(2,1)S(1)}, bf16[96,384]{1,0:T(8,128)(2,1)S(1)}, u32[]{:S(2)}, u32[]{:S(2)}) collective-permute-start(bf16[96,384]{1,0:T(8,128)(2,1)S(1)} %add_convert_fusion.3), channel_id=1, source_target_pairs={{0,2},{1,3},{2,0},{3,1},{4,6},{5,7},{6,4},{7,5},{8,10},{9,11},{10,... | collective-permute-start | bytes 221192 | tf_op jit(solution)/shard_map/ppermute | solution.py:767
  92.2 21.0 %collective-permute-start.44 = (bf16[4,96,384]{2,1,0:T(8,128)(2,1)S(1)}, bf16[4,96,384]{2,1,0:T(8,128)(2,1)S(1)}, u32[]{:S(2)}, u32[]{:S(2)}) collective-permute-start(bf16[4,96,384]{2,1,0:T(8,128)(2,1)S(1)} %get-tuple-element.95), channel_id=1, source_target_pairs={{0,16},{8,24},{16,0},{24,8},{1,17},{9,25},{17,1},{25,9},{2,18},{10... | collective-permute-start | bytes 884744 | tf_op jit(solution)/shard_map/ppermute | solution.py:767
  93.5 9.8 %collective-permute-start.18 = (bf16[208,384]{1,0:T(8,128)(2,1)S(1)}, bf16[208,384]{1,0:T(8,128)(2,1)S(1)}, u32[]{:S(2)}, u32[]{:S(2)}) collective-permute-start(bf16[208,384]{1,0:T(8,128)(2,1)S(1)} %get-tuple-element.71), channel_id=1, source_target_pairs={{0,8},{8,0},{16,24},{24,16},{1,9},{9,1},{17,25},{25,17},{2,10},{10... | collective-permute-start | bytes 479240 | tf_op jit(solution)/shard_map/ppermute | solution.py:767
  94.3 13.7 %collective-permute-start.19 = (bf16[208,384]{1,0:T(8,128)(2,1)S(1)}, bf16[208,384]{1,0:T(8,128)(2,1)S(1)}, u32[]{:S(2)}, u32[]{:S(2)}) collective-permute-start(bf16[208,384]{1,0:T(8,128)(2,1)S(1)} %get-tuple-element.72), channel_id=1, source_target_pairs={{0,16},{8,24},{16,0},{24,8},{1,17},{9,25},{17,1},{25,9},{2,18},{10... | collective-permute-start | bytes 479240 | tf_op jit(solution)/shard_map/ppermute | solution.py:767
  95.9 12.1 %collective-permute-start.20 = (bf16[208,384]{1,0:T(8,128)(2,1)S(1)}, bf16[208,384]{1,0:T(8,128)(2,1)S(1)}, u32[]{:S(2)}, u32[]{:S(2)}) collective-permute-start(bf16[208,384]{1,0:T(8,128)(2,1)S(1)} %get-tuple-element.73), channel_id=1, source_target_pairs={{0,24},{8,16},{16,8},{24,0},{1,25},{9,17},{17,9},{25,1},{2,26},{10... | collective-permute-start | bytes 479240 | tf_op jit(solution)/shard_map/ppermute | solution.py:767
  99.9 34.2 %collective-permute-start.32 = (bf16[864,384]{1,0:T(8,128)(2,1)S(1)}, bf16[864,384]{1,0:T(8,128)(2,1)S(1)}, u32[]{:S(2)}, u32[]{:S(2)}) collective-permute-start(bf16[864,384]{1,0:T(8,128)(2,1)S(1)} %collective-permute-done.31.fx0), channel_id=1, source_target_pairs={{0,1},{1,0},{2,3},{3,2},{4,5},{5,4},{6,7},{7,6},{8,9},{9,8},{10,11... | collective-permute-start | bytes 1990664 | tf_op jit(solution)/shard_map/ppermute | solution.py:767
  108.7 7.4 %collective-permute-start.23 = (bf16[112,384]{1,0:T(8,128)(2,1)S(1)}, bf16[112,384]{1,0:T(8,128)(2,1)S(1)}, u32[]{:S(2)}, u32[]{:S(2)}) collective-permute-start(bf16[112,384]{1,0:T(8,128)(2,1)S(1)} %get-tuple-element.77), channel_id=1, source_target_pairs={{0,6},{1,7},{2,4},{3,5},{4,2},{5,3},{6,0},{7,1},{8,14},{9,15},{10,... | collective-permute-start | bytes 258056 | tf_op jit(solution)/shard_map/ppermute | solution.py:767
  110.1 7.7 %collective-permute-start.22 = (bf16[112,384]{1,0:T(8,128)(2,1)S(1)}, bf16[112,384]{1,0:T(8,128)(2,1)S(1)}, u32[]{:S(2)}, u32[]{:S(2)}) collective-permute-start(bf16[112,384]{1,0:T(8,128)(2,1)S(1)} %get-tuple-element.76), channel_id=1, source_target_pairs={{0,4},{1,5},{2,6},{3,7},{4,0},{5,1},{6,2},{7,3},{8,12},{9,13},{10,... | collective-permute-start | bytes 258056 | tf_op jit(solution)/shard_map/ppermute | solution.py:767
  110.1 7.7 %collective-permute-start.21 = (bf16[112,384]{1,0:T(8,128)(2,1)S(1)}, bf16[112,384]{1,0:T(8,128)(2,1)S(1)}, u32[]{:S(2)}, u32[]{:S(2)}) collective-permute-start(bf16[112,384]{1,0:T(8,128)(2,1)S(1)} %get-tuple-element.75), channel_id=1, source_target_pairs={{0,2},{1,3},{2,0},{3,1},{4,6},{5,7},{6,4},{7,5},{8,10},{9,11},{10,... | collective-permute-start | bytes 258056 | tf_op jit(solution)/shard_map/ppermute | solution.py:767
  113.2 20.9 %collective-permute-start.45 = (bf16[2,4,96,384]{3,2,1,0:T(8,128)(2,1)S(1)}, bf16[2,4,96,384]{3,2,1,0:T(8,128)(2,1)S(1)}, u32[]{:S(2)}, u32[]{:S(2)}) collective-permute-start(bf16[2,4,96,384]{3,2,1,0:T(8,128)(2,1)S(1)} %pad_maximum_fusion.1.ch0), channel_id=1, source_target_pairs={{0,1},{1,0},{2,3},{3,2},{4,5},{5,4},{6,7},{7,6},{8,9},{9,8},{10,11... | collective-permute-start | bytes 1769480 | tf_op jit(solution)/shard_map/ppermute | solution.py:767
  124.8 7.5 %collective-permute-start.29 = (bf16[4,48,384]{2,1,0:T(8,128)(2,1)S(1)}, bf16[4,48,384]{2,1,0:T(8,128)(2,1)S(1)}, u32[]{:S(2)}, u32[]{:S(2)}) collective-permute-start(bf16[4,48,384]{2,1,0:T(8,128)(2,1)S(1)} %get-tuple-element.97), channel_id=1, source_target_pairs={{0,24},{8,16},{16,8},{24,0},{1,25},{9,17},{17,9},{25,1},{2,26},{10... | collective-permute-start | bytes 442376 | tf_op jit(solution)/shard_map/ppermute | solution.py:767
  126.3 7.6 %collective-permute-start.28 = (bf16[4,48,384]{2,1,0:T(8,128)(2,1)S(1)}, bf16[4,48,384]{2,1,0:T(8,128)(2,1)S(1)}, u32[]{:S(2)}, u32[]{:S(2)}) collective-permute-start(bf16[4,48,384]{2,1,0:T(8,128)(2,1)S(1)} %get-tuple-element.97), channel_id=1, source_target_pairs={{0,16},{8,24},{16,0},{24,8},{1,17},{9,25},{17,1},{25,9},{2,18},{10... | collective-permute-start | bytes 442376 | tf_op jit(solution)/shard_map/ppermute | solution.py:767
  134.0 12.2 %collective-permute-start.30 = (bf16[4,4,48,384]{3,2,1,0:T(8,128)(2,1)S(1)}, bf16[4,4,48,384]{3,2,1,0:T(8,128)(2,1)S(1)}, u32[]{:S(2)}, u32[]{:S(2)}) collective-permute-start(bf16[4,4,48,384]{3,2,1,0:T(8,128)(2,1)S(1)} %pad_maximum_fusion.ch0), channel_id=1, source_target_pairs={{0,1},{1,0},{2,3},{3,2},{4,5},{5,4},{6,7},{7,6},{8,9},{9,8},{10,11... | collective-permute-start | bytes 1769480 | tf_op jit(solution)/shard_map/ppermute | solution.py:767
  142.6 10.5 %collective-permute-start.46 = (bf16[2,192,384]{2,1,0:T(8,128)(2,1)S(1)}, bf16[2,192,384]{2,1,0:T(8,128)(2,1)S(1)}, u32[]{:S(2)}, u32[]{:S(2)}) collective-permute-start(bf16[2,192,384]{2,1,0:T(8,128)(2,1)S(1)} %get-tuple-element.87), channel_id=1, source_target_pairs={{16,24},{17,25},{18,26},{19,27},{20,28},{21,29},{22,30},{23,31}} | collective-permute-start | bytes 884744 | tf_op jit(solution)/shard_map/ppermute | solution.py:936
  (23 other events, 165.2 us)
